TPU v7x, 32 devices: a whole 2x2x4 slice. The times are simulated.
32 devices in a mesh: dp: 8 (over z, y), enc: 4 (over x, core).
Axes of the slice: x: 2, y: 2, z: 4, core: 2. Of those that a mesh axis runs over, the one named last changes fastest.
Arguments:
- text_embed: bfloat16 [12288, 768], P(('dp', 'enc'))
- region_features: bfloat16 [8192, 2048], P(('dp', 'enc')), may hold values from -6 to 6
- boxes: bfloat16 [4, 8192], P(None, ('dp', 'enc')), may hold values from 0 to 1
- caption_image: int32 [96], P(('dp', 'enc')), may hold values from 0 to 1, as said below
- caption_lengths: int32 [96], P(('dp', 'enc')), may hold values from 1 to 128, as said below
- region_counts: int32 [64], P(('dp', 'enc')), may hold values from 32 to 128, as said below
- region_target: int32 [32, 256], P(('dp', 'enc')), may hold values from 0 to 255, each once within a row
- region_source: int32 [32, 256], P(('dp', 'enc')), may hold values from 0 to 255, as said below
- w_visual: bfloat16 [2048, 768], replicated, may hold values from -0.125 to 0.125
- w_box: bfloat16 [768, 4], replicated, may hold values from -3 to 3
- visual_bias: float32 [768], replicated, may hold values from -3 to 3
- visual_gain: float32 [768], replicated, may hold values from 0.5 to 1.5
- visual_shift: float32 [768], replicated, may hold values from -2 to 2
- w_qkv: bfloat16 [768, 2304], replicated, may hold values from -0.21875 to 0.21875
- qv_bias: float32 [1536], replicated, may hold values from -2 to 2
- w_out: bfloat16 [768, 768], replicated, may hold values from -2.5 to 2.5
- out_bias: float32 [768], replicated, may hold values from -2 to 2
- attn_gain: float32 [768], replicated, may hold values from 0.5 to 1.5
- attn_shift: float32 [768], replicated, may hold values from -2 to 2
- w_up: bfloat16 [768, 3072], replicated, may hold values from -0.21875 to 0.21875
- up_bias: float32 [3072], replicated, may hold values from -2 to 2
- w_down: bfloat16 [3072, 768], replicated, may hold values from -0.15625 to 0.15625
- down_bias: float32 [768], replicated, may hold values from -2 to 2
- ffn_gain: float32 [768], replicated, may hold values from 0.5 to 1.5
- ffn_shift: float32 [768], replicated, may hold values from -2 to 2
- out_grad: bfloat16 [24576, 768], P(('dp', 'enc')), may hold values from -6 to 6
Outputs:
- out_rows: bfloat16 [24576, 768], P(('dp', 'enc'))
- text_grad: float32 [12288, 768], P(('dp', 'enc'))
- feature_grad: float32 [8192, 2048], P(('dp', 'enc'))
- box_grad: float32 [4, 8192], P(None, ('dp', 'enc'))
- rms_values: float32 [3], replicated
- w_visual_grad: float32 [2048, 768], P('dp')
- w_box_grad: float32 [768, 4], P('dp')
- visual_bias_grad: float32 [768], P('dp')
- visual_gain_grad: float32 [768], P('dp')
- visual_shift_grad: float32 [768], P('dp')
- w_qkv_grad: float32 [768, 2304], P('dp')
- qv_bias_grad: float32 [1536], P('dp')
- w_out_grad: float32 [768, 768], P('dp')
- out_bias_grad: float32 [768], P('dp')
- attn_gain_grad: float32 [768], P('dp')
- attn_shift_grad: float32 [768], P('dp')
- w_up_grad: float32 [768, 3072], P('dp')
- up_bias_grad: float32 [3072], P('dp')
- w_down_grad: float32 [3072, 768], P('dp')
- down_bias_grad: float32 [768], P('dp')
- ffn_gain_grad: float32 [768], P('dp')
- ffn_shift_grad: float32 [768], P('dp')
Inputs may be any that keep to these rules, and one draw needn't show every extreme that they name: `caption_image`: among the 3 captions of one device each local image number appears once or twice. `caption_lengths`: the largest length 128 is reached in every draw. `region_counts`: the largest count 128 is reached in every draw. Row s is a permutation; region row r of device s goes to device region_target[s, r] // 8 at place region_target[s, r] % 8 of that device's message. Row d is a permutation; region_source[d, t] % 8 == t % 8, the 8 slots of each aligned block of 8 slots share one source device region_source[d, t] // 8, and each source device serves exactly one block of a row.
All inputs are finite; a program needn't handle non-finite values.
Results may differ from a plain program's by a relative error of at most 0.018.
Values may be sent and summed in bfloat16 or wider, within the bound.
No kernel may reach another device: no remote copies, remote signals or barrier semaphores. Data moves between devices by JAX's collectives and lax.ppermute only.
A program may use at most 256 MiB of HBM per device.

v0:
```python
import jax
import jax.numpy as jnp
from jax import lax
from jax.sharding import PartitionSpec as P

HEADS = 12
HEAD = 64


epsilon = 1e-12
inv_sqrt_two = 0.7071067811865476
inv_sqrt_tau = 0.3989422804014327


def layer_norm(values, gain, shift):
    centre = values - jnp.mean(values, -1, keepdims=True)
    spread = jnp.mean(centre * centre, -1, keepdims=True)
    inv_std = lax.rsqrt(spread + epsilon)
    normed = centre * inv_std
    return (normed * gain + shift, normed, inv_std)


def norm_back(grad, normed, inv_std, gain):
    scaled = grad * gain
    return inv_std * (
        scaled
        - jnp.mean(scaled, -1, keepdims=True)
        - normed * jnp.mean(scaled * normed, -1, keepdims=True)
    )


def col_sum(values):
    return jnp.sum(values.astype(jnp.float32), 0)


def on_device(
    text_embed,
    region_features,
    boxes,
    caption_image,
    caption_lengths,
    region_counts,
    region_target,
    region_source,
    w_visual,
    w_box,
    visual_bias,
    visual_gain,
    visual_shift,
    w_qkv,
    qv_bias,
    w_out,
    out_bias,
    attn_gain,
    attn_shift,
    w_up,
    up_bias,
    w_down,
    down_bias,
    ffn_gain,
    ffn_shift,
    out_grad,
):
    f32 = jnp.float32
    bf16 = jnp.bfloat16
    width = text_embed.shape[1]
    captions = caption_image.shape[0]
    images = region_counts.shape[0]
    region_dev = region_target.shape[1]
    regions = region_dev // images
    text_len = text_embed.shape[0] // captions
    seq_len = text_len + regions
    row_count = captions * seq_len
    flat_target = region_target[0]
    flat_source = region_source[0]
    region_pre = (
        jnp.dot(region_features, w_visual, preferred_element_type=f32)
        + jnp.dot(boxes.T, w_box.T, preferred_element_type=f32)
        + visual_bias
    )
    region_norm, vis_normed, vis_inv = layer_norm(region_pre, visual_gain, visual_shift)
    region_low = region_norm.astype(bf16)
    message = jnp.zeros_like(region_low).at[flat_target].set(region_low)
    arrived = lax.all_to_all(message, ("dp", "enc"), split_axis=0, concat_axis=0, tiled=True)
    local_regions = arrived[flat_source].reshape(images, regions, width)
    image_ids = jnp.arange(images, dtype=jnp.int32)
    select = caption_image[:, None] == image_ids[None, :]
    caption_regions = jnp.einsum(
        "cm,mrd->crd", select.astype(bf16), local_regions, preferred_element_type=f32
    ).astype(bf16)
    seq_rows = jnp.concatenate([text_embed.reshape(captions, text_len, width), caption_regions], 1)
    region_count = jnp.sum(jnp.where(select, region_counts[None, :], 0), 1)
    place = jnp.arange(seq_len, dtype=jnp.int32)[None, :]
    valid_slot = jnp.where(
        place < text_len, place < caption_lengths[:, None], place - text_len < region_count[:, None]
    )
    flat = seq_rows.reshape(row_count, width)
    flat_wide = flat.astype(f32)
    qkv = jnp.dot(flat, w_qkv, preferred_element_type=f32)
    query_low = (
        (qkv[:, :width] + qv_bias[:width]).astype(bf16).reshape(captions, seq_len, HEADS, HEAD)
    )
    key_low = qkv[:, width : 2 * width].astype(bf16).reshape(captions, seq_len, HEADS, HEAD)
    value_low = (
        (qkv[:, 2 * width :] + qv_bias[width:]).astype(bf16).reshape(captions, seq_len, HEADS, HEAD)
    )
    key_mask = valid_slot[:, None, None, :]

    def masked_scores():
        scores = (
            jnp.einsum("cqhe,ckhe->chqk", query_low, key_low, preferred_element_type=f32) * 0.125
        )
        return jnp.where(key_mask, scores, -1e30)

    masked = masked_scores()
    top = jnp.max(masked, -1, keepdims=True)
    log_total = top + jnp.log(jnp.sum(jnp.exp(masked - top), -1, keepdims=True))
    probs_low = jnp.exp(masked - log_total).astype(bf16)
    context_low = (
        jnp.einsum("chqk,ckhe->cqhe", probs_low, value_low, preferred_element_type=f32)
        .astype(bf16)
        .reshape(row_count, width)
    )
    attn_out = jnp.dot(context_low, w_out, preferred_element_type=f32) + out_bias
    hidden, attn_normed, attn_inv = layer_norm(flat_wide + attn_out, attn_gain, attn_shift)
    hidden_low = hidden.astype(bf16)
    upper = jnp.dot(hidden_low, w_up, preferred_element_type=f32) + up_bias
    act_low = jax.nn.gelu(upper, approximate=False).astype(bf16)
    ffn_out = jnp.dot(act_low, w_down, preferred_element_type=f32) + down_bias
    final, ffn_normed, ffn_inv = layer_norm(hidden + ffn_out, ffn_gain, ffn_shift)
    row_mask = valid_slot.reshape(-1, 1).astype(f32)
    out_rows = (final * row_mask).astype(bf16)
    stream_sum, attn_sum, ffn_sum, slot_sum = lax.psum(
        (
            jnp.sum(row_mask * flat_wide * flat_wide),
            jnp.sum(row_mask * attn_out * attn_out),
            jnp.sum(row_mask * ffn_out * ffn_out),
            jnp.sum(row_mask),
        ),
        ("dp", "enc"),
    )
    rms_values = jnp.sqrt(jnp.stack([stream_sum, attn_sum, ffn_sum]) / (slot_sum * width))
    out_cot = out_grad.astype(f32) * row_mask
    g_ffn_gain = jnp.sum(out_cot * ffn_normed, 0)
    g_ffn_shift = jnp.sum(out_cot, 0)
    d_second = norm_back(out_cot, ffn_normed, ffn_inv, ffn_gain)
    d_ffn_low = d_second.astype(bf16)
    g_down_bias = col_sum(d_ffn_low)
    g_w_down = jnp.einsum("rf,rd->fd", act_low, d_ffn_low, preferred_element_type=f32)
    d_act = jnp.einsum("rd,fd->rf", d_ffn_low, w_down, preferred_element_type=f32)
    slope = (
        0.5 * (1.0 + jax.scipy.special.erf(upper * inv_sqrt_two))
        + upper * jnp.exp(-0.5 * upper * upper) * inv_sqrt_tau
    )
    d_upper_low = (d_act * slope).astype(bf16)
    g_up_bias = col_sum(d_upper_low)
    g_w_up = jnp.einsum("rd,rf->df", hidden_low, d_upper_low, preferred_element_type=f32)
    d_hidden = d_second + jnp.einsum("rf,df->rd", d_upper_low, w_up, preferred_element_type=f32)
    g_attn_gain = jnp.sum(d_hidden * attn_normed, 0)
    g_attn_shift = jnp.sum(d_hidden, 0)
    d_resid = norm_back(d_hidden, attn_normed, attn_inv, attn_gain)
    d_attn_low = d_resid.astype(bf16)
    g_out_bias = col_sum(d_attn_low)
    g_w_out = jnp.einsum("rd,re->de", context_low, d_attn_low, preferred_element_type=f32)
    d_context_low = (
        jnp.einsum("re,de->rd", d_attn_low, w_out, preferred_element_type=f32)
        .astype(bf16)
        .reshape(captions, seq_len, HEADS, HEAD)
    )
    probs_again = jnp.exp(masked_scores() - log_total)
    d_probs = jnp.einsum("cqhe,ckhe->chqk", d_context_low, value_low, preferred_element_type=f32)
    inner = jnp.sum(d_probs * probs_again, -1, keepdims=True)
    d_scores_low = (probs_again * (d_probs - inner)).astype(bf16)
    d_query = (
        (jnp.einsum("chqk,ckhe->cqhe", d_scores_low, key_low, preferred_element_type=f32) * 0.125)
        .astype(bf16)
        .reshape(row_count, width)
    )
    d_key = (
        (jnp.einsum("chqk,cqhe->ckhe", d_scores_low, query_low, preferred_element_type=f32) * 0.125)
        .astype(bf16)
        .reshape(row_count, width)
    )
    d_value = (
        jnp.einsum("chqk,cqhe->ckhe", probs_low, d_context_low, preferred_element_type=f32)
        .astype(bf16)
        .reshape(row_count, width)
    )
    d_qkv = jnp.concatenate([d_query, d_key, d_value], 1)
    g_qv_bias = jnp.concatenate([col_sum(d_query), col_sum(d_value)], 0)
    g_w_qkv = jnp.einsum("rd,rk->dk", flat, d_qkv, preferred_element_type=f32)
    d_flat = jnp.einsum("rk,dk->rd", d_qkv, w_qkv, preferred_element_type=f32) + d_resid
    d_seq = d_flat.reshape(captions, seq_len, width)
    text_grad = d_seq[:, :text_len].reshape(captions * text_len, width)
    d_images = jnp.einsum(
        "cm,crd->mrd", select.astype(f32), d_seq[:, text_len:], precision=lax.Precision.HIGHEST
    )
    d_image_low = d_images.reshape(region_dev, width).astype(bf16)
    back_message = jnp.zeros_like(d_image_low).at[flat_source].set(d_image_low)
    returned = lax.all_to_all(back_message, ("dp", "enc"), split_axis=0, concat_axis=0, tiled=True)
    d_region = returned[flat_target].astype(f32)
    g_visual_shift = jnp.sum(d_region, 0)
    g_visual_gain = jnp.sum(d_region * vis_normed, 0)
    d_pre_low = norm_back(d_region, vis_normed, vis_inv, visual_gain).astype(bf16)
    g_visual_bias = col_sum(d_pre_low)
    g_w_visual = jnp.einsum("rf,rd->fd", region_features, d_pre_low, preferred_element_type=f32)
    feature_grad = jnp.einsum("rd,fd->rf", d_pre_low, w_visual, preferred_element_type=f32)
    g_w_box = jnp.einsum("rd,br->db", d_pre_low, boxes, preferred_element_type=f32)
    box_grad = jnp.einsum("rd,db->br", d_pre_low, w_box, preferred_element_type=f32)
    summed = lax.psum(
        (
            g_w_visual,
            g_w_box,
            g_visual_bias,
            g_visual_gain,
            g_visual_shift,
            g_w_qkv,
            g_qv_bias,
            g_w_out,
            g_out_bias,
            g_attn_gain,
            g_attn_shift,
            g_w_up,
            g_up_bias,
            g_w_down,
            g_down_bias,
            g_ffn_gain,
            g_ffn_shift,
        ),
        ("dp", "enc"),
    )
    groups = lax.axis_size("dp")
    position = lax.axis_index("dp")
    shares = tuple(
        (
            lax.dynamic_slice_in_dim(
                whole, position * (whole.shape[0] // groups), whole.shape[0] // groups, 0
            )
            for whole in summed
        )
    )
    return (
        out_rows,
        text_grad,
        feature_grad,
        box_grad,
        rms_values,
        shares[0],
        shares[1],
        shares[2],
        shares[3],
        shares[4],
        shares[5],
        shares[6],
        shares[7],
        shares[8],
        shares[9],
        shares[10],
        shares[11],
        shares[12],
        shares[13],
        shares[14],
        shares[15],
        shares[16],
    )


def solution(mesh):
    return jax.shard_map(
        on_device,
        mesh=mesh,
        in_specs=(
            P(("dp", "enc"), None),
            P(("dp", "enc"), None),
            P(None, ("dp", "enc")),
            P(("dp", "enc")),
            P(("dp", "enc")),
            P(("dp", "enc")),
            P(("dp", "enc"), None),
            P(("dp", "enc"), None),
            P(),
            P(),
            P(),
            P(),
            P(),
            P(),
            P(),
            P(),
            P(),
            P(),
            P(),
            P(),
            P(),
            P(),
            P(),
            P(),
            P(),
            P(("dp", "enc"), None),
        ),
        out_specs=(
            P(("dp", "enc"), None),
            P(("dp", "enc"), None),
            P(("dp", "enc"), None),
            P(None, ("dp", "enc")),
            P(),
            P("dp", None),
            P("dp", None),
            P("dp"),
            P("dp"),
            P("dp"),
            P("dp", None),
            P("dp"),
            P("dp", None),
            P("dp"),
            P("dp"),
            P("dp"),
            P("dp", None),
            P("dp"),
            P("dp", None),
            P("dp"),
            P("dp"),
            P("dp"),
        ),
        check_vma=False,
    )
```

profile of v0, /device:TPU:0, one launch (start us, length us, event | category | flops | bytes accessed | tf_op | source)
XLA Modules:
  0.0 785.0 jit_solution(15910310796388683420)
XLA Ops:
  7.2 3.3 fusion.83
  12.8 3.1 scatter_custom_fusion
  15.9 7.6 all-to-all-start
  26.4 2.4 copy.65
  32.1 4.5 all-to-all-done
  36.6 3.3 gather_fusion
  41.7 5.1 fusion.18
  47.1 2.9 fusion.84
  52.9 4.7 reshape.383
  57.6 4.6 copy.70
  62.1 4.7 reshape.384
  66.8 4.6 copy.71
  71.4 3.8 fusion.16
  75.2 2.4 exponential_reduce_fusion
  79.5 4.7 reshape.382
  84.1 4.7 copy.72
  88.9 6.1 fusion.29
  99.6 25.9 %fusion.2 = (bf16[768,3072]{1,0:T(8,128)(2,1)S(1)}, f32[768,3072]{1,0:T(8,128)}) fusion(f32[3072]{0:T(1024)S(1)} %copy-done.40, bf16[768,3072]{1,0:T(8,128)(2,1)S(1)} %bitcast.125, f32[768,768]{1,0:T(8,128)S(1)} %get-tuple-element.114, f32[768]{0:T(1024)S(1)} %copy-done.21, f32[768]{0:T(1024)S(1)} %copy-done.20, f32[768]{0:T(1024)S(1)} %add_rsqrt_fusion.1, ...), kind=kOutput, calls=%fused_computation.8 | convolution fusion | flops 3782541312 | bytes 21258240 | tf_op jit(solution)/shard_map/dot_general | solution.py:127
  125.5 4.1 fusion.78
  130.9 3.0 multiply_reduce_fusion.1
  134.0 2.7 convert_reduce_fusion.1
  136.6 10.6 %convert_reduce_fusion = (f32[3072]{0:T(1024)}, bf16[768,3072]{1,0:T(8,128)(2,1)S(1)}) fusion(f32[768,3072]{1,0:T(8,128)} %get-tuple-element.128, f32[3072]{0:T(1024)S(1)} %copy-done.40, bf16[3072,768]{1,0:T(8,128)(2,1)S(1)} %bitcast.123, f32[768,768]{1,0:T(8,128)S(1)} %get-tuple-element.102), kind=kOutput, calls=%fused_computation.15 | convolution fusion | flops 3655136256 | bytes 21258240 | tf_op jit(solution)/shard_map/rd,fd->rf/dot_general | solution.py:150
  147.3 7.1 fusion.72
  154.4 5.1 multiply_reduce_fusion.2
  162.5 2.2 convolution_convert_fusion.1
  164.7 4.7 reshape.385
  169.3 4.6 copy.76
  173.9 7.0 convert_reduce_fusion.3
  180.9 6.3 multiply_reduce_fusion
  187.3 3.6 multiply_convert_fusion
  198.8 5.3 fusion.87
  204.1 3.0 convolution_add_fusion
  207.1 2.5 fusion.62
  210.7 2.1 fusion.34
  213.6 2.8 scatter_custom_fusion.1
  216.5 3.3 all-to-all-start.1
  220.1 10.7 %fusion.65 = f32[3072,768]{1,0:T(8,128)} fusion(bf16[768,3072]{1,0:T(8,128)(2,1)} %copy-done.41, f32[768,768]{1,0:T(8,128)} %copy-done.10), kind=kOutput, calls=%fused_computation.160 | convolution fusion | flops 3624468480 | bytes 16515072 | tf_op jit(solution)/shard_map/rf,rd->fd/dot_general | solution.py:149
  230.8 2.2 all-to-all-done.1
  232.9 3.3 gather_fusion.1
  236.3 2.3 fusion.44
  241.5 3.7 convolution_bitcast_fusion
  249.1 43.4 %all-reduce = (f32[1]{0:T(128)}, f32[1]{0:T(128)}, f32[1]{0:T(128)}, f32[]{:T(128)}, f32[768,4]{0,1:T(4,128)}, /*index=5*/f32[768]{0:T(1024)}, f32[768]{0:T(1024...) all-reduce(f32[1]{0:T(128)} %bitcast.22, ...), channel_id=1, replica_groups=mesh['dp'=8,'enc'=4] {'dp','enc'}, use_global_device_ids=true, to_apply=%region_23.24 | all-reduce | flops 14596 | bytes 116768 | tf_op jit(solution)/shard_map/psum | solution.py:133
  307.2 2.5 fusion.61
  312.8 4.4 fusion.85
  317.3 447.5 %all-reduce.4.cloned.1.call-done = (f32[2048,768]{0,1:T(8,128)}, f32[768,2304]{1,0:T(8,128)}, f32[768,768]{1,0:T(8,128)}, f32[768,3072]{1,0:T(8,128)}, f32[3072,768]{1,0:T(8,128)}) async-done(((f32[2048,768]{0,1:T(8,128)}, f32[768,2304]{1,0:T(8,128)}, f32[768,768]{1,0:T(8,128)}, f32[768,3072]{1,0:T(8,128)}, f32[3072,768]{1,0:T(8,128)}), (f32[2048,768]{0,1:T(8,128)}, f32[768,2304]{1,0:T(8,128)}, ...) | async-done | bytes 34603024 | tf_op jit(solution)/shard_map/psum | solution.py:210
  766.8 2.3 copy.90
  769.1 2.4 constant_dynamic-slice_fusion
  771.4 2.4 constant_dynamic-slice_fusion.1
  (173 shorter events, 63.9 us)
Async XLA Ops:
  7.2 39.9 %copy-start = (bf16[768,2304]{1,0:T(8,128)(2,1)S(1)}, bf16[768,2304]{1,0:T(8,128)(2,1)}, u32[]{:S(2)}) copy-start(bf16[768,2304]{1,0:T(8,128)(2,1)} %param.39) | copy-start | bytes 10616836
  7.2 3.4 copy-start.30
  7.2 3.4 copy-start.26
  7.2 3.4 copy-start.34
  10.6 1.6 copy-start.36
  10.6 1.6 copy-start.37
  10.6 2.1 copy-start.22
  10.6 2.1 copy-start.35
  11.1 14.5 %copy-start.24 = (f32[256]{0:T(256)}, f32[256]{0:T(256)S(1)}, u32[]{:S(2)}) copy-start(f32[256]{0:T(256)S(1)} %broadcast_multiply_fusion.8) | copy-start | bytes 3076
  12.2 13.4 %copy-start.29 = (f32[256]{0:T(256)}, f32[256]{0:T(256)S(1)}, u32[]{:S(2)}) copy-start(f32[256]{0:T(256)S(1)} %add_rsqrt_fusion.2) | copy-start | bytes 3076
  15.9 20.7 %all-to-all-start = ((bf16[32,8,768]{2,1,0:T(8,128)(2,1)}), bf16[32,8,768]{2,1,0:T(8,128)(2,1)}, u32[]{:S(2)}, u32[]{:S(2)}) async-start(bf16[32,8,768]{2,1,0:T(8,128)(2,1)} %bitcast.109), calls=%async_computation | async-start | bytes 786432 | tf_op jit(solution)/shard_map/all_to_all | solution.py:84
  39.9 1.8 copy-start.9
  47.0 3.0 copy-start.13
  75.2 3.7 copy-start.1
  95.0 1.4 copy-start.14
  95.0 1.4 copy-start.32
  95.0 1.6 copy-start.39
  96.4 1.7 copy-start.16
  96.4 2.7 slice-start.5
  96.7 2.4 slice-start.6
  96.7 28.8 %slice-start.3 = ((s8[4718592]{0:T(1024)(128)(4,1)}), s8[4194304]{0:T(1024)(128)(4,1)S(1)}, s32[]{:S(2)}) async-start(s8[4718592]{0:T(1024)(128)(4,1)} %bitcast.122), calls=%async_computation.6 | async-start | bytes 8388608
  98.0 1.5 copy-start.20
  98.1 1.5 copy-start.21
  98.1 1.5 copy-start.40
  99.6 25.9 %copy-start.31 = (f32[768]{0:T(1024)S(1)}, f32[768]{0:T(1024)}, u32[]{:S(2)}) copy-start(f32[768]{0:T(1024)} %param.48) | copy-start | bytes 9220
  99.6 25.9 %slice-start.4 = ((s8[4718592]{0:T(1024)(128)(4,1)}), s8[524288]{0:T(1024)(128)(4,1)S(1)}, s32[]{:S(2)}) async-start(s8[4718592]{0:T(1024)(128)(4,1)} %bitcast.122), calls=%async_computation.7 | async-start | bytes 1048576
  125.4 4.2 copy-start.41
  129.7 1.3 copy-start.8
  130.9 3.1 copy-start.33
  136.6 17.7 %copy-start.10 = (f32[768,768]{1,0:T(8,128)}, f32[768,768]{1,0:T(8,128)S(1)}, u32[]{:S(2)}) copy-start(f32[768,768]{1,0:T(8,128)S(1)} %get-tuple-element.102) | copy-start | bytes 7077892
  161.1 1.5 copy-start.11
  173.9 7.0 copy-start.6
  173.9 7.0 copy-start.7
  173.9 7.0 copy-start.19
  173.9 13.4 %slice-start = ((s8[9437184]{0:T(1024)(128)(4,1)}), s8[4194304]{0:T(1024)(128)(4,1)S(1)}, s32[]{:S(2)}) async-start(s8[9437184]{0:T(1024)(128)(4,1)} %bitcast.98), calls=%async_computation.3 | async-start | bytes 8388608
  180.9 6.4 slice-start.1
  180.9 6.4 slice-start.2
  187.3 3.6 copy-start.3
  190.9 1.5 copy-start.4
  197.5 1.3 copy-start.15
  198.8 5.3 copy-start.12
  204.1 3.0 copy-start.17
  216.5 16.5 %all-to-all-start.1 = ((bf16[32,8,768]{2,1,0:T(8,128)(2,1)}), bf16[32,8,768]{2,1,0:T(8,128)(2,1)}, u32[]{:S(2)}, u32[]{:S(2)}) async-start(bf16[32,8,768]{2,1,0:T(8,128)(2,1)} %bitcast.108), calls=%async_computation.1 | async-start | bytes 786432 | tf_op jit(solution)/shard_map/all_to_all | solution.py:200
  219.8 545.0 %all-reduce.4.cloned.1.call-start = ((), (), s32[]{:S(2)}) async-start(), calls=%async_computation.2 | async-start | bytes 69206016 | tf_op jit(solution)/shard_map/psum | solution.py:210
  230.8 5.5 copy-start.23
  230.8 5.5 copy-start.25
  236.3 5.2 copy-start.18
  245.2 3.9 copy-start.28
  (4 other events, 4.1 us)
Sparse Core Ops, SparseCore 0:
  245.3 519.3 all-reduce.3
where the time goes:
time: 790 us; the launch traced here: 785 us
  waiting for transfers between devices  454 us (57%)
  matrix products  125 us (16%)
  local copies, waits for them, and re-layouts  96.6 us (12%)
  blocking collectives  43.4 us (5%)
  other arithmetic  38.5 us (5%)
  between operations  15.9 us (2%)
  starting transfers between devices  11.2 us (1%)
    psum x1, waiting for transfers between devices, on_device(): lax.psum((g_w_visual, g_w_box, g_visual_bias, g_visual_gain, g_visual_shi...  447 us
    psum x1, blocking collectives, on_device(): lax.psum((jnp.sum(row_mask * flat_wide * flat_wide), jnp.sum(row_mask * a...  43.4 us
    dynamic_slice x17, local copies, waits for them, and re-layouts, on_device(): lax.dynamic_slice_in_dim(whole, position * (whole.shape[0] // groups), wh...  26 us
    dot_general x1, matrix products, on_device(): upper = jnp.dot(hidden_low, w_up, preferred_element_type=f32) + up_bias  25.9 us
  transfers between devices with their start and end apart: 3, of which 3 were waited for; matrix products, arithmetic and copies ran while one was open for 6% of the time, Pallas kernels for 0%

commit v1 on v0

--- a/solution.py
+++ b/solution.py
@@ -130,16 +130,14 @@
     final, ffn_normed, ffn_inv = layer_norm(hidden + ffn_out, ffn_gain, ffn_shift)
     row_mask = valid_slot.reshape(-1, 1).astype(f32)
     out_rows = (final * row_mask).astype(bf16)
-    stream_sum, attn_sum, ffn_sum, slot_sum = lax.psum(
-        (
+    stats = jnp.stack(
+        [
             jnp.sum(row_mask * flat_wide * flat_wide),
             jnp.sum(row_mask * attn_out * attn_out),
             jnp.sum(row_mask * ffn_out * ffn_out),
             jnp.sum(row_mask),
-        ),
-        ("dp", "enc"),
-    )
-    rms_values = jnp.sqrt(jnp.stack([stream_sum, attn_sum, ffn_sum]) / (slot_sum * width))
+        ]
+    )
     out_cot = out_grad.astype(f32) * row_mask
     g_ffn_gain = jnp.sum(out_cot * ffn_normed, 0)
     g_ffn_shift = jnp.sum(out_cot, 0)
@@ -207,62 +205,157 @@
     feature_grad = jnp.einsum("rd,fd->rf", d_pre_low, w_visual, preferred_element_type=f32)
     g_w_box = jnp.einsum("rd,br->db", d_pre_low, boxes, preferred_element_type=f32)
     box_grad = jnp.einsum("rd,db->br", d_pre_low, w_box, preferred_element_type=f32)
-    summed = lax.psum(
-        (
-            g_w_visual,
-            g_w_box,
-            g_visual_bias,
-            g_visual_gain,
-            g_visual_shift,
-            g_w_qkv,
-            g_qv_bias,
-            g_w_out,
-            g_out_bias,
-            g_attn_gain,
-            g_attn_shift,
-            g_w_up,
-            g_up_bias,
-            g_w_down,
-            g_down_bias,
-            g_ffn_gain,
-            g_ffn_shift,
-        ),
-        ("dp", "enc"),
-    )
     groups = lax.axis_size("dp")
-    position = lax.axis_index("dp")
-    shares = tuple(
-        (
-            lax.dynamic_slice_in_dim(
-                whole, position * (whole.shape[0] // groups), whole.shape[0] // groups, 0
-            )
-            for whole in summed
-        )
-    )
+    low = lambda t: t.astype(bf16)
+
+    def cols(whole):
+        return whole.reshape(groups, -1)
+
+    smalls = jnp.concatenate(
+        [
+            cols(g_visual_bias),
+            cols(g_visual_gain),
+            cols(g_visual_shift),
+            cols(g_out_bias),
+            cols(g_attn_gain),
+            cols(g_attn_shift),
+            cols(g_down_bias),
+            cols(g_ffn_gain),
+            cols(g_ffn_shift),
+            cols(g_qv_bias),
+            cols(g_up_bias),
+            cols(g_w_box),
+        ],
+        1,
+    )
+    quarter = smalls.shape[1] // 4
+    smalls = smalls.reshape(groups, 4, quarter)
+    smalls = jnp.concatenate([smalls, jnp.broadcast_to(stats, (groups, 4, 4))], 2)
+    smalls = jnp.pad(smalls, ((0, 0), (0, 0), (0, 8 * (width // 2) - quarter - 4)))
+    smalls = smalls.reshape(groups, 2, 2, 8, width // 2).transpose(0, 1, 3, 2, 4)
+    smalls = smalls.reshape(groups, 2, 8, width)
+
+    vis_rows = g_w_visual.shape[0] // groups // 2
+    vis = low(g_w_visual).reshape(groups, 2, vis_rows, width)
+    vis = jnp.concatenate([vis, low(smalls)], 2).reshape(-1, width)
+    down = low(g_w_down)
+    up = low(g_w_up)
+    qkvo = jnp.concatenate([low(g_w_qkv), low(g_w_out)], 1)
+    down = reduce_tall(down, 0)
+    up = reduce_wide(up, 1)
+    qkvo = reduce_wide(qkvo, 0)
+    vis = reduce_tall(vis, 1)
+    vis = vis.reshape(2, vis_rows + 8, width)
+    share_vis = vis[:, :vis_rows].reshape(-1, width)
+    tail = vis[:, vis_rows:].reshape(2, 8, 2, width // 2).transpose(0, 2, 1, 3)
+    tail = tail.reshape(4, 4 * width)
+    total = tail[0, quarter : quarter + 4]
+    rms_values = jnp.sqrt(total[:3] / (total[3] * width))
+    tail = tail[:, :quarter].reshape(-1)
+    small = []
+    at = 0
+    for size in [width // groups] * 9 + [2 * width // groups, 4 * width // groups, 4 * width // groups]:
+        small.append(tail[at : at + size])
+        at += size
     return (
         out_rows,
         text_grad,
         feature_grad,
         box_grad,
         rms_values,
-        shares[0],
-        shares[1],
-        shares[2],
-        shares[3],
-        shares[4],
-        shares[5],
-        shares[6],
-        shares[7],
-        shares[8],
-        shares[9],
-        shares[10],
-        shares[11],
-        shares[12],
-        shares[13],
-        shares[14],
-        shares[15],
-        shares[16],
-    )
+        share_vis,
+        small[11].reshape(-1, 4),
+        small[0],
+        small[1],
+        small[2],
+        qkvo[:, : 3 * width],
+        small[9],
+        qkvo[:, 3 * width :],
+        small[3],
+        small[4],
+        small[5],
+        up,
+        small[10],
+        down,
+        small[6],
+        small[7],
+        small[8],
+    )
+
+
+def device_bit(bit):
+    me = lax.axis_index("dp") * lax.axis_size("enc") + lax.axis_index("enc")
+    return lax.rem(me // bit, 2)
+
+
+def swap(values, bit):
+    count = lax.axis_size("dp") * lax.axis_size("enc")
+    return lax.ppermute(values, ("dp", "enc"), [(i, i ^ bit) for i in range(count)])
+
+
+def halve(values, bit, axis):
+    mine = device_bit(bit)
+    size = values.shape[axis] // 2
+    sent = lax.dynamic_slice_in_dim(values, (1 - mine) * size, size, axis)
+    kept = lax.dynamic_slice_in_dim(values, mine * size, size, axis)
+    return kept + swap(sent, bit)
+
+
+def halve_lead(values, bit, axis):
+    mine = device_bit(bit)
+    sent = lax.dynamic_index_in_dim(values, 1 - mine, axis, keepdims=False)
+    kept = lax.dynamic_index_in_dim(values, mine, axis, keepdims=False)
+    return kept + swap(sent, bit)
+
+
+def double(values, bit, axis):
+    mine = device_bit(bit)
+    other = swap(values, bit)
+    low_half = jnp.where(mine == 0, values, other)
+    high_half = jnp.where(mine == 0, other, values)
+    return jnp.concatenate([low_half, high_half], axis)
+
+
+def reduce_tall(values, first):
+    groups = lax.axis_size("dp")
+    bits = groups.bit_length() - 1
+    rows = values.shape[0] // groups // 2
+    values = halve(values, 1, 1)
+    width = values.shape[1]
+    values = values.reshape((2,) * (bits + 1) + (rows, width))
+    if first == 0:
+        values = halve_lead(values, 2, bits)
+        values = halve_lead(values, 4, bits - 1)
+    else:
+        values = halve_lead(values, 4, bits - 1)
+        values = halve_lead(values, 2, bits - 1)
+    for b in range(1, bits):
+        values = halve_lead(values, 4 << b, bits - 1 - b)
+    values = double(values, 2, 0)
+    return double(values, 1, 1).astype(jnp.float32)
+
+
+def reduce_wide(values, first):
+    groups = lax.axis_size("dp")
+    bits = groups.bit_length() - 1
+    rows = values.shape[0] // groups
+    values = halve(values, 1, 1)
+
+    def by_row(values, b):
+        shape = values.shape
+        values = values.reshape((2,) * (bits - b) + (rows, shape[-1]))
+        return halve_lead(values, 4 << b, bits - 1 - b)
+
+    if first == 0:
+        values = halve(values, 2, 1)
+        values = by_row(values, 0)
+    else:
+        values = by_row(values, 0)
+        values = halve(values, 2, values.ndim - 1)
+    for b in range(1, bits):
+        values = by_row(values, b)
+    values = double(values, 2, 1)
+    return double(values, 1, 1).astype(jnp.float32)
 
 
 def solution(mesh):

time: 790 us -> 421 us (0.53)
  waiting for transfers between devices: 454 us -> 84.4 us
  blocking collectives: 43.4 us -> 0 us
  starting transfers between devices: 11.2 us -> 39.2 us
  other arithmetic: 38.5 us -> 61.5 us
  local copies, waits for them, and re-layouts: 96.6 us -> 113 us
  between operations: 15.9 us -> 2.92 us
  matrix products: 125 us -> 115 us
    psum x1 -> x0, waiting for transfers between devices: 447 us -> none  [on_device(): lax.psum((g_w_visual, g_w_box, g_visual_bias, g_visual_gain, g_visual_shi...]
    ppermute x0 -> x28, waiting for transfers between devices: none -> 79.3 us  [swap(): lax.ppermute(values, ('dp', 'enc'), [(i, i ^ bit) for i in range(count)])]
    psum x1 -> x0, blocking collectives: 43.4 us -> none  [on_device(): lax.psum((jnp.sum(row_mask * flat_wide * flat_wide), jnp.sum(row_mask * a...]
    ppermute x0 -> x28, starting transfers between devices: none -> 28.3 us  [swap(): lax.ppermute(values, ('dp', 'enc'), [(i, i ^ bit) for i in range(count)])]
    dynamic_slice x17 -> x7, local copies, waits for them, and re-layouts: 26 us -> 3.95 us  [the longest x5 3.58 us: halve(): sent = lax.dynamic_slice_in_dim(values, (1 - mine) * size, size, axis)]
    reshape x0 -> x15, local copies, waits for them, and re-layouts: none -> 20.4 us  [the longest x11 13.3 us: cols(): return whole.reshape(groups, -1)]
    add x0 -> x20, other arithmetic: none -> 12.4 us  [the longest x6 8.64 us: halve(): return kept + swap(sent, bit)]
  transfers between devices with their start and end apart: 3 -> 30, of which waited for: 3 -> 14; matrix products, arithmetic and copies ran while one was open for 6% -> 24% of each run, Pallas kernels for 0% -> 0%
where the time goes in v1:
time: 421 us; the launch traced here: 415 us
  matrix products  115 us (27%)
  local copies, waits for them, and re-layouts  113 us (27%)
  waiting for transfers between devices  84.4 us (20%)
  other arithmetic  61.5 us (15%)
  starting transfers between devices  39.2 us (9%)
    ppermute x28, waiting for transfers between devices, swap(): lax.ppermute(values, ('dp', 'enc'), [(i, i ^ bit) for i in range(count)])  79.3 us
    ppermute x28, starting transfers between devices, swap(): lax.ppermute(values, ('dp', 'enc'), [(i, i ^ bit) for i in range(count)])  28.3 us
    dot_general x1, matrix products, on_device(): upper = jnp.dot(hidden_low, w_up, preferred_element_type=f32) + up_bias  25.5 us
    reshape x11, local copies, waits for them, and re-layouts, cols(): return whole.reshape(groups, -1)  13.3 us
    unnamed x146, local copies, waits for them, and re-layouts  12.8 us
    dot_general x1, matrix products, on_device(): jnp.einsum('rd,fd->rf', d_ffn_low, w_down, preferred_element_type=f32)  9.84 us
    reshape x2, local copies, waits for them, and re-layouts, on_device(): (qkv[:, 2 * width:] + qv_bias[width:]).astype(bf16)  9.68 us
    reshape x2, local copies, waits for them, and re-layouts, on_device(): d_context_low = jnp.einsum('re,de->rd', d_attn_low, w_out, preferred_elem...  9.62 us
  transfers between devices with their start and end apart: 30, of which 14 were waited for; matrix products, arithmetic and copies ran while one was open for 24% of the time, Pallas kernels for 0%

profile of v1, /device:TPU:0, one launch (start us, length us, event | category | flops | bytes accessed | tf_op | source)
XLA Modules:
  0.0 415.5 jit_solution(6304354112683405465)
XLA Ops:
  0.7 3.3 fusion.91
  6.2 3.1 scatter_custom_fusion
  9.3 7.6 %all-to-all-start = ((bf16[32,8,768]{2,1,0:T(8,128)(2,1)}), bf16[32,8,768]{2,1,0:T(8,128)(2,1)}, u32[]{:S(2)}, u32[]{:S(2)}) async-start(bf16[32,8,768]{2,1,0:T(8,128)(2,1)} %bitcast.217), calls=%async_computation | async-start | bytes 786432 | tf_op jit(solution)/shard_map/all_to_all | solution.py:84
  25.0 5.1 %all-to-all-done = bf16[32,8,768]{2,1,0:T(8,128)(2,1)} async-done(((bf16[32,8,768]{2,1,0:T(8,128)(2,1)}), bf16[32,8,768]{2,1,0:T(8,128)(2,1)}, u32[]{:S(2)}, u32[]{:S(2)}) %all-to-all-start) | async-done | bytes 393248 | tf_op jit(solution)/shard_map/all_to_all | solution.py:84
  30.1 3.3 gather_fusion
  35.2 5.2 %fusion.18 = (bf16[]{:T(256)}, bf16[3,256,768]{2,0,1:T(4,128)(2,1)S(1)}) fusion(f32[3,256]{0,1:T(8,128)} %copy.123, bf16[3,128,768]{2,0,1:T(4,128)(2,1)S(1)} %convolution_convert_fusion.8, bf16[3,128,768]{2,0,1:T(4,128)(2,1)S(1)} %copy-done.15), kind=kLoop, calls=%fused_computation.49 | loop fusion | flops 4718591 | bytes 2362370 | tf_op jit(solution)/shard_map/reduce_sum | solution.py:135
  40.5 2.9 fusion.92
  46.4 4.7 %reshape.508 = bf16[3,256,12,64]{3,2,1,0:T(8,128)(2,1)} reshape(bf16[768,768]{1,0:T(8,128)(2,1)} %get-tuple-element.97) | data formatting | bytes 2359296 | tf_op jit(solution)/shard_map/reshape | solution.py:101
  51.1 4.6 %copy.103 = bf16[3,256,12,64]{1,3,2,0:T(8,128)(2,1)} copy(bf16[3,256,12,64]{3,2,1,0:T(8,128)(2,1)} %reshape.508) | data formatting | bytes 2359296 | tf_op jit(solution)/shard_map/reshape | solution.py:101
  55.6 4.7 %reshape.509 = bf16[3,256,12,64]{3,2,1,0:T(8,128)(2,1)} reshape(bf16[768,768]{1,0:T(8,128)(2,1)} %slice.151) | data formatting | bytes 2359296 | tf_op jit(solution)/shard_map/reshape | solution.py:103
  60.3 4.6 %copy.104 = bf16[3,256,12,64]{1,3,2,0:T(8,128)(2,1)} copy(bf16[3,256,12,64]{3,2,1,0:T(8,128)(2,1)} %reshape.509) | data formatting | bytes 2359296 | tf_op jit(solution)/shard_map/reshape | solution.py:103
  64.9 3.8 fusion.16
  73.0 5.1 %reshape.507 = bf16[3,256,12,64]{3,2,1,0:T(8,128)(2,1)} reshape(bf16[768,768]{1,0:T(8,128)(2,1)} %get-tuple-element.98) | data formatting | bytes 2359296 | tf_op jit(solution)/shard_map/reshape | solution.py:105
  78.1 4.6 %copy.105 = bf16[3,256,12,64]{1,3,2,0:T(8,128)(2,1)} copy(bf16[3,256,12,64]{3,2,1,0:T(8,128)(2,1)} %reshape.507) | data formatting | bytes 2359296 | tf_op jit(solution)/shard_map/reshape | solution.py:105
  82.7 6.1 %fusion.33 = bf16[3,256,12,64]{1,3,2,0:T(8,128)(2,1)S(1)} fusion(bf16[3,256,12,64]{1,3,2,0:T(8,128)(2,1)} %copy.105, f32[3,12,256,256]{2,3,1,0:T(8,128)} %copy-done.1, f32[3,12,256]{2,1,0:T(8,128)} %log_add_fusion, pred[3,256]{1,0:T(4,128)(4,1)S(1)} %get-tuple-element.86), kind=kOutput, calls=%fused_computation.95 | convolution fusion | flops 312016896 | bytes 11834112 | tf_op jit(solution)/shard_map/chqk,ckhe->cqhe/dot_general | solution.py:120
  93.3 25.5 %fusion.2 = (bf16[768,3072]{1,0:T(8,128)(2,1)S(1)}, f32[768,3072]{1,0:T(8,128)}) fusion(f32[3072]{0:T(1024)S(1)} %copy-done.52, bf16[768,3072]{1,0:T(8,128)(2,1)S(1)} %bitcast.240, f32[768,768]{1,0:T(8,128)S(1)} %get-tuple-element.96, f32[768]{0:T(1024)S(1)} %copy-done.53, f32[768]{0:T(1024)S(1)} %copy-done.41, f32[768]{0:T(1024)S(1)} %add_rsqrt_fusion.1, ...), kind=kOutput, calls=%fused_computation.8 | convolution fusion | flops 3782541312 | bytes 21258240 | tf_op jit(solution)/shard_map/dot_general | solution.py:127
  118.9 4.2 %fusion.82 = (f32[768]{0:T(1024)S(1)}, f32[768,768]{1,0:T(8,128)S(1)}, f32[768,768]{1,0:T(8,128)S(1)}) fusion(f32[768]{0:T(1024)S(1)} %copy-done.45, f32[768]{0:T(1024)S(1)} %copy-done.53, f32[768]{0:T(1024)S(1)} %copy-done.41, f32[768]{0:T(1024)S(1)} %add_rsqrt_fusion.1, f32[768,768]{1,0:T(8,128)S(1)} %get-tuple-element.96, ...), kind=kOutput, calls=%fused_computation.240 | convolution fusion | flops 3628006656 | bytes 16533504 | tf_op jit(solution)/shard_map/dot_general | solution.py:129
  124.3 3.9 fusion.20
  129.8 5.9 %convolution_convert_fusion.1 = bf16[3072,768]{1,0:T(8,128)(2,1)} fusion(bf16[768,3072]{1,0:T(8,128)(2,1)S(1)} %get-tuple-element.137, f32[768,768]{1,0:T(8,128)S(1)} %get-tuple-element.88), kind=kOutput, calls=%fused_computation.39 | convolution fusion | flops 3626827776 | bytes 11796480 | tf_op jit(solution)/shard_map/rf,rd->fd/dot_general | solution.py:147
  135.7 9.8 %fusion.90 = (bf16[3072]{0:T(1024)(128)(2,1)}, bf16[768,3072]{1,0:T(8,128)(2,1)S(1)}) fusion(f32[768,3072]{1,0:T(8,128)} %get-tuple-element.138, f32[3072]{0:T(1024)S(1)} %copy-done.52, bf16[3072,768]{1,0:T(8,128)(2,1)S(1)} %bitcast.238, f32[768,768]{1,0:T(8,128)S(1)} %get-tuple-element.88), kind=kOutput, calls=%fused_computation.248 | convolution fusion | flops 3652776960 | bytes 21252096 | tf_op jit(solution)/shard_map/rd,fd->rf/dot_general | solution.py:148
  145.5 6.5 %convolution_convert_fusion.2 = bf16[768,3072]{1,0:T(8,128)(2,1)} fusion(bf16[768,3072]{1,0:T(8,128)(2,1)S(1)} %get-tuple-element.148, f32[768,768]{1,0:T(8,128)S(1)} %get-tuple-element.96, f32[768]{0:T(1024)S(1)} %copy-done.53, f32[768]{0:T(1024)S(1)} %copy-done.41, f32[768]{0:T(1024)S(1)} %add_rsqrt_fusion.1, f32[768]{0:T(1024)S(1)} %broadcast_multiply_fusion.5), kind=kOutput, calls=%fused_computation.40 | convolution fusion | flops 3629187072 | bytes 11808768 | tf_op jit(solution)/shard_map/rd,rf->df/dot_general | solution.py:155
  152.0 5.1 %multiply_reduce_fusion.2 = (bf16[768]{0:T(1024)(128)(2,1)}, f32[768]{0:T(1024)S(1)}, f32[768]{0:T(1024)S(1)}, bf16[768]{0:T(1024)(128)(2,1)}, f32[768,768]{1,0:T(8,128)S(1)}) fusion(f32[768,768]{1,0:T(8,128)S(1)} %get-tuple-element.96, f32[768]{0:T(1024)S(1)} %add_rsqrt_fusion.1, f32[768]{0:T(1024)S(1)} %broadcast_multiply_fusion.5, ...), kind=kOutput, calls=%fused_computation.64 | convolution fusion | flops 3629773824 | bytes 16533504 | tf_op jit(solution)/shard_map/rf,df->rd/dot_general | solution.py:156
  161.6 4.7 %reshape.510 = bf16[3,256,12,64]{3,2,1,0:T(8,128)(2,1)} reshape(bf16[768,768]{1,0:T(8,128)(2,1)} %convolution_convert_fusion.6) | data formatting | bytes 2359296 | tf_op jit(solution)/shard_map/reshape | solution.py:166
  166.3 4.9 %copy.109 = bf16[3,256,12,64]{1,3,2,0:T(8,128)(2,1)} copy(bf16[3,256,12,64]{3,2,1,0:T(8,128)(2,1)} %reshape.510) | data formatting | bytes 2359296 | tf_op jit(solution)/shard_map/reshape | solution.py:166
  171.3 7.0 %fusion.88 = (bf16[12,64]{1,0:T(8,128)(2,1)}, bf16[3,256,12,64]{1,3,2,0:T(8,128)(2,1)S(1)}) fusion(bf16[3,256,12,64]{1,3,2,0:T(8,128)(2,1)} %copy.109, f32[3,12,256,256]{2,3,1,0:T(8,128)} %copy-done.1, f32[3,12,256]{2,1,0:T(8,128)} %log_add_fusion, pred[3,256]{1,0:T(4,128)(4,1)S(1)} %get-tuple-element.86), kind=kOutput, calls=%fused_computation.246 | convolution fusion | flops 312605952 | bytes 11835648 | tf_op jit(solution)/shard_map/chqk,cqhe->ckhe/dot_general | solution.py:183
  178.3 6.3 %multiply_reduce_fusion = (f32[3,12,256]{2,1,0:T(8,128)S(1)}, f32[3,12,256,256]{2,3,1,0:T(8,128)S(1)}) fusion(f32[3,12,256,256]{2,3,1,0:T(8,128)} %copy-done.1, f32[3,12,256]{2,1,0:T(8,128)S(1)} %copy-done.30, pred[3,256]{1,0:T(4,128)(4,1)S(1)} %get-tuple-element.86, bf16[3,256,12,64]{1,3,2,0:T(8,128)(2,1)S(1)} %copy-done.10, ...), kind=kOutput, calls=%fused_computation.16 | convolution fusion | flops 313777152 | bytes 21308160 | tf_op jit(solution)/shard_map/cqhe,ckhe->chqk/dot_general | solution.py:169
  184.7 3.4 multiply_convert_fusion
  196.0 4.7 %convolution_convert_fusion = bf16[768,2304]{1,0:T(8,128)(2,1)} fusion(bf16[768,768]{1,0:T(8,128)(2,1)S(1)} %bitcast.221, bf16[768,2304]{0,1:T(8,128)(2,1)S(1)} %constant_dynamic-update-slice_fusion), kind=kOutput, calls=%fused_computation.38 | convolution fusion | flops 2719678464 | bytes 8257536 | tf_op jit(solution)/shard_map/rd,rk->dk/dot_general | solution.py:189
  200.7 3.0 convolution_add_fusion
  211.5 2.8 scatter_custom_fusion.1
  214.3 3.3 all-to-all-start.1
  217.7 3.3 convolution_convert_fusion.4
  233.2 2.7 maximum_convert_fusion.5
  237.8 3.3 gather_fusion.1
  246.5 2.7 fusion.19
  249.2 4.8 %copy.136 = bf16[2048,768]{1,0:T(8,128)(2,1)} copy(bf16[2048,768]{0,1:T(8,128)(2,1)} %fusion.19) | data formatting | bytes 6291456 | tf_op jit(solution)/shard_map/reshape | solution.py:239
  280.3 2.5 dynamic-slice_add_fusion.1
  285.6 2.8 fusion.24
  288.9 16.0 %collective-permute-done.1 = bf16[2,2,2,136,384]{4,3,2,1,0:T(8,128)(2,1)S(1)} collective-permute-done((bf16[2,2,2,136,384]{4,3,2,1,0:T(8,128)(2,1)S(1)}, bf16[2,2,2,136,384]{4,3,2,1,0:T(8,128)(2,1)S(1)}, u32[]{:S(2)}, u32[]{:S(2)}) %collective-permute-start.1) | collective-permute-done | bytes 835616 | tf_op jit(solution)/shard_map/ppermute | solution.py:293
  309.3 31.8 %collective-permute-done.2 = bf16[2,2,136,384]{3,2,1,0:T(8,128)(2,1)S(1)} collective-permute-done((bf16[2,2,136,384]{3,2,1,0:T(8,128)(2,1)S(1)}, bf16[2,2,136,384]{3,2,1,0:T(8,128)(2,1)S(1)}, u32[]{:S(2)}, u32[]{:S(2)}) %collective-permute-start.2) | collective-permute-done | bytes 417824 | tf_op jit(solution)/shard_map/ppermute | solution.py:293
  344.6 3.4 collective-permute-done.3
  348.1 2.5 collective-permute-start.4
  350.9 3.9 collective-permute-done.4
  364.0 4.9 %collective-permute-done.9 = bf16[2,2,96,768]{3,2,1,0:T(8,128)(2,1)S(1)} collective-permute-done((bf16[2,2,96,768]{3,2,1,0:T(8,128)(2,1)S(1)}, bf16[2,2,96,768]{3,2,1,0:T(8,128)(2,1)S(1)}, u32[]{:S(2)}, u32[]{:S(2)}) %collective-permute-start.9) | collective-permute-done | bytes 589856 | tf_op jit(solution)/shard_map/ppermute | solution.py:293
  384.2 3.1 collective-permute-start.25
  389.5 3.0 collective-permute-start.11
  392.5 6.2 %collective-permute-done.25 = bf16[192,384]{1,0:T(8,128)(2,1)S(1)} collective-permute-done((bf16[192,384]{1,0:T(8,128)(2,1)S(1)}, bf16[192,384]{1,0:T(8,128)(2,1)S(1)}, u32[]{:S(2)}, u32[]{:S(2)}) %collective-permute-start.25) | collective-permute-done | bytes 147488 | tf_op jit(solution)/shard_map/ppermute | solution.py:293
  404.6 4.6 %collective-permute-done.12 = bf16[96,768]{1,0:T(8,128)(2,1)S(1)} collective-permute-done((bf16[96,768]{1,0:T(8,128)(2,1)S(1)}, bf16[96,768]{1,0:T(8,128)(2,1)S(1)}, u32[]{:S(2)}, u32[]{:S(2)}) %collective-permute-start.12) | collective-permute-done | bytes 147488 | tf_op jit(solution)/shard_map/ppermute | solution.py:293
  (344 shorter events, 141.5 us)
Async XLA Ops:
  0.7 39.9 %copy-start = (bf16[768,2304]{1,0:T(8,128)(2,1)S(1)}, bf16[768,2304]{1,0:T(8,128)(2,1)}, u32[]{:S(2)}) copy-start(bf16[768,2304]{1,0:T(8,128)(2,1)} %param.39) | copy-start | bytes 10616836
  4.5 14.5 %copy-start.34 = (f32[256]{0:T(256)}, f32[256]{0:T(256)S(1)}, u32[]{:S(2)}) copy-start(f32[256]{0:T(256)S(1)} %broadcast_multiply_fusion.8) | copy-start | bytes 3076
  5.7 13.4 %copy-start.38 = (f32[256]{0:T(256)}, f32[256]{0:T(256)S(1)}, u32[]{:S(2)}) copy-start(f32[256]{0:T(256)S(1)} %add_rsqrt_fusion.2) | copy-start | bytes 3076
  9.3 14.3 %copy-start.47 = (s32[256,1]{0,1:T(1,128)S(1)}, s32[256,1]{0,1:T(1,128)}, u32[]{:S(2)}) copy-start(s32[256,1]{0,1:T(1,128)} %get-tuple-element.149) | copy-start | bytes 3076
  9.3 20.8 %all-to-all-start = ((bf16[32,8,768]{2,1,0:T(8,128)(2,1)}), bf16[32,8,768]{2,1,0:T(8,128)(2,1)}, u32[]{:S(2)}, u32[]{:S(2)}) async-start(bf16[32,8,768]{2,1,0:T(8,128)(2,1)} %bitcast.217), calls=%async_computation | async-start | bytes 786432 | tf_op jit(solution)/shard_map/all_to_all | solution.py:84
  90.4 28.4 %slice-start.11 = ((s8[4718592]{0:T(1024)(128)(4,1)}), s8[4194304]{0:T(1024)(128)(4,1)S(1)}, s32[]{:S(2)}) async-start(s8[4718592]{0:T(1024)(128)(4,1)} %bitcast.237), calls=%async_computation.13 | async-start | bytes 8388608
  93.3 25.5 %copy-start.45 = (f32[768]{0:T(1024)S(1)}, f32[768]{0:T(1024)}, u32[]{:S(2)}) copy-start(f32[768]{0:T(1024)} %param.48) | copy-start | bytes 9220
  93.3 25.5 %slice-start.12 = ((s8[4718592]{0:T(1024)(128)(4,1)}), s8[524288]{0:T(1024)(128)(4,1)S(1)}, s32[]{:S(2)}) async-start(s8[4718592]{0:T(1024)(128)(4,1)} %bitcast.237), calls=%async_computation.14 | async-start | bytes 1048576
  171.3 13.4 %slice-start = ((s8[9437184]{0:T(1024)(128)(4,1)}), s8[4194304]{0:T(1024)(128)(4,1)S(1)}, s32[]{:S(2)}) async-start(s8[9437184]{0:T(1024)(128)(4,1)} %bitcast.184), calls=%async_computation.2 | async-start | bytes 8388608
  196.0 7.6 %slice-start.7 = ((s8[4718592]{0:T(1024)(128)(4,1)}), s8[4194304]{0:T(1024)(128)(4,1)S(1)}, s32[]{:S(2)}) async-start(s8[4718592]{0:T(1024)(128)(4,1)} %bitcast.202), calls=%async_computation.9 | async-start | bytes 8388608
  196.0 9.3 %slice-start.3 = ((s8[4718592]{0:T(1024)(128)(4,1)}), s8[524288]{0:T(1024)(128)(4,1)S(1)}, s32[]{:S(2)}) async-start(s8[4718592]{0:T(1024)(128)(4,1)} %bitcast.198), calls=%async_computation.5 | async-start | bytes 1048576
  205.3 70.4 %collective-permute-start.21 = (bf16[3072,384]{1,0:T(8,128)(2,1)}, bf16[3072,384]{1,0:T(8,128)(2,1)}, u32[]{:S(2)}, u32[]{:S(2)}) collective-permute-start(bf16[3072,384]{1,0:T(8,128)(2,1)} %constant_dynamic-slice_fusion.2), channel_id=1, source_target_pairs={{0,1},{1,0},{2,3},{3,2},{4,5},{5,4},{6,7},{7,6},{8,9},{9,8},{10,11... | collective-permute-start | bytes 7077896 | tf_op jit(solution)/shard_map/ppermute | solution.py:293
  206.9 73.3 %collective-permute-start.14 = (bf16[768,1536]{1,0:T(8,128)(2,1)}, bf16[768,1536]{1,0:T(8,128)(2,1)}, u32[]{:S(2)}, u32[]{:S(2)}) collective-permute-start(bf16[768,1536]{1,0:T(8,128)(2,1)} %constant_dynamic-slice_fusion.4), channel_id=1, source_target_pairs={{0,1},{1,0},{2,3},{3,2},{4,5},{5,4},{6,7},{7,6},{8,9},{9,8},{10,11... | collective-permute-start | bytes 7077896 | tf_op jit(solution)/shard_map/ppermute | solution.py:293
  214.3 23.5 %all-to-all-start.1 = ((bf16[32,8,768]{2,1,0:T(8,128)(2,1)}), bf16[32,8,768]{2,1,0:T(8,128)(2,1)}, u32[]{:S(2)}, u32[]{:S(2)}) async-start(bf16[32,8,768]{2,1,0:T(8,128)(2,1)} %bitcast.216), calls=%async_computation.1 | async-start | bytes 786432 | tf_op jit(solution)/shard_map/all_to_all | solution.py:198
  223.1 18.0 %copy-start.33 = (f32[768]{0:T(1024)S(1)}, f32[768]{0:T(1024)}, u32[]{:S(2)}) copy-start(f32[768]{0:T(1024)} %param.37) | copy-start | bytes 9220
  223.1 18.0 %copy-start.35 = (f32[256]{0:T(256)S(1)}, f32[256]{0:T(256)}, u32[]{:S(2)}) copy-start(f32[256]{0:T(256)} %copy-done.34) | copy-start | bytes 3076
  223.1 62.5 %collective-permute-start.7 = (bf16[768,1536]{1,0:T(8,128)(2,1)}, bf16[768,1536]{1,0:T(8,128)(2,1)}, u32[]{:S(2)}, u32[]{:S(2)}) collective-permute-start(bf16[768,1536]{1,0:T(8,128)(2,1)} %fusion.22), channel_id=1, source_target_pairs={{0,1},{1,0},{2,3},{3,2},{4,5},{5,4},{6,7},{7,6},{8,9},{9,8},{10,11... | collective-permute-start | bytes 7077896 | tf_op jit(solution)/shard_map/ppermute | solution.py:293
  268.3 7.3 %slice-start.9 = ((s8[4718592]{0:T(1024)(128)(4,1)}), s8[4194304]{0:T(1024)(128)(4,1)S(1)}, s32[]{:S(2)}) async-start(s8[4718592]{0:T(1024)(128)(4,1)} %bitcast.204), calls=%async_computation.11 | async-start | bytes 8388608
  270.9 11.8 %collective-permute-start = (bf16[2176,384]{1,0:T(8,128)(2,1)S(1)}, bf16[2176,384]{1,0:T(8,128)(2,1)S(1)}, u32[]{:S(2)}, u32[]{:S(2)}) collective-permute-start(bf16[2176,384]{1,0:T(8,128)(2,1)S(1)} %constant_dynamic-slice_fusion.6), channel_id=1, source_target_pairs={{0,1},{1,0},{2,3},{3,2},{4,5},{5,4},{6,7},{7,6},{8,9},{9,8},{10,11... | collective-permute-start | bytes 5013512 | tf_op jit(solution)/shard_map/ppermute | solution.py:293
  272.4 7.8 %slice-start.5 = ((s8[4718592]{0:T(1024)(128)(4,1)}), s8[4194304]{0:T(1024)(128)(4,1)S(1)}, s32[]{:S(2)}) async-start(s8[4718592]{0:T(1024)(128)(4,1)} %bitcast.200), calls=%async_computation.7 | async-start | bytes 8388608
  278.5 28.8 %collective-permute-start.22 = (bf16[2,2,2,192,384]{4,3,1,0,2:T(8,128)(2,1)S(1)}, bf16[2,2,2,192,384]{4,3,1,0,2:T(8,128)(2,1)S(1)}, u32[]{:S(2)}, u32[]{:S(2)}) collective-permute-start(bf16[2,2,2,192,384]{4,3,1,0,2:T(8,128)(2,1)S(1)} %bitcast.218), channel_id=1, source_target_pairs={{0,2},{1,3},{2,0},{3,1},{4,6},{5,7},{6,4},{7,5},{8,10},{9,11},{10,... | collective-permute-start | bytes 3538952 | tf_op jit(solution)/shard_map/ppermute | solution.py:293
  283.3 21.5 %collective-permute-start.1 = (bf16[2,2,2,136,384]{4,3,2,1,0:T(8,128)(2,1)S(1)}, bf16[2,2,2,136,384]{4,3,2,1,0:T(8,128)(2,1)S(1)}, u32[]{:S(2)}, u32[]{:S(2)}) collective-permute-start(bf16[2,2,2,136,384]{4,3,2,1,0:T(8,128)(2,1)S(1)} %dynamic-slice_bitcast_fusion.1), channel_id=1, source_target_pairs={{0,4},{1,5},{2,6},{3,7},{4,0},{5,1},{6,2},{7,3},{8,12},{9,13},{10,... | collective-permute-start | bytes 2506760 | tf_op jit(solution)/shard_map/ppermute | solution.py:293
  285.0 57.9 %collective-permute-start.15 = (bf16[2,2,96,1536]{3,2,1,0:T(8,128)(2,1)S(1)}, bf16[2,2,96,1536]{3,2,1,0:T(8,128)(2,1)S(1)}, u32[]{:S(2)}, u32[]{:S(2)}) collective-permute-start(bf16[2,2,96,1536]{3,2,1,0:T(8,128)(2,1)S(1)} %dynamic-slice_bitcast_fusion), channel_id=1, source_target_pairs={{0,4},{1,5},{2,6},{3,7},{4,0},{5,1},{6,2},{7,3},{8,12},{9,13},{10,... | collective-permute-start | bytes 3538952 | tf_op jit(solution)/shard_map/ppermute | solution.py:293
  288.5 62.1 %collective-permute-start.8 = (bf16[768,768]{1,0:T(8,128)(2,1)S(1)}, bf16[768,768]{1,0:T(8,128)(2,1)S(1)}, u32[]{:S(2)}, u32[]{:S(2)}) collective-permute-start(bf16[768,768]{1,0:T(8,128)(2,1)S(1)} %constant_dynamic-slice_fusion.5), channel_id=1, source_target_pairs={{0,2},{1,3},{2,0},{3,1},{4,6},{5,7},{6,4},{7,5},{8,10},{9,11},{10,... | collective-permute-start | bytes 3538952 | tf_op jit(solution)/shard_map/ppermute | solution.py:293
  305.0 36.1 %collective-permute-start.2 = (bf16[2,2,136,384]{3,2,1,0:T(8,128)(2,1)S(1)}, bf16[2,2,136,384]{3,2,1,0:T(8,128)(2,1)S(1)}, u32[]{:S(2)}, u32[]{:S(2)}) collective-permute-start(bf16[2,2,136,384]{3,2,1,0:T(8,128)(2,1)S(1)} %dynamic-slice_bitcast_fusion.4), channel_id=1, source_target_pairs={{0,2},{1,3},{2,0},{3,1},{4,6},{5,7},{6,4},{7,5},{8,10},{9,11},{10,... | collective-permute-start | bytes 1253384 | tf_op jit(solution)/shard_map/ppermute | solution.py:293
  307.6 52.5 %collective-permute-start.23 = (bf16[2,2,192,384]{3,2,1,0:T(8,128)(2,1)S(1)}, bf16[2,2,192,384]{3,2,1,0:T(8,128)(2,1)S(1)}, u32[]{:S(2)}, u32[]{:S(2)}) collective-permute-start(bf16[2,2,192,384]{3,2,1,0:T(8,128)(2,1)S(1)} %dynamic-slice_bitcast_fusion.2), channel_id=1, source_target_pairs={{0,4},{1,5},{2,6},{3,7},{4,0},{5,1},{6,2},{7,3},{8,12},{9,13},{10,... | collective-permute-start | bytes 1769480 | tf_op jit(solution)/shard_map/ppermute | solution.py:293
  341.2 6.8 %collective-permute-start.3 = (bf16[2,136,384]{2,1,0:T(8,128)(2,1)S(1)}, bf16[2,136,384]{2,1,0:T(8,128)(2,1)S(1)}, u32[]{:S(2)}, u32[]{:S(2)}) collective-permute-start(bf16[2,136,384]{2,1,0:T(8,128)(2,1)S(1)} %dynamic-slice_bitcast_fusion.8), channel_id=1, source_target_pairs={{0,8},{1,9},{2,10},{3,11},{4,12},{5,13},{6,14},{7,15},{8,0},{9,1},... | collective-permute-start | bytes 626696 | tf_op jit(solution)/shard_map/ppermute | solution.py:293
  343.1 18.4 %collective-permute-start.16 = (bf16[2,2,96,768]{3,2,1,0:T(8,128)(2,1)S(1)}, bf16[2,2,96,768]{3,2,1,0:T(8,128)(2,1)S(1)}, u32[]{:S(2)}, u32[]{:S(2)}) collective-permute-start(bf16[2,2,96,768]{3,2,1,0:T(8,128)(2,1)S(1)} %constant_dynamic-slice_fusion.3), channel_id=1, source_target_pairs={{0,2},{1,3},{2,0},{3,1},{4,6},{5,7},{6,4},{7,5},{8,10},{9,11},{10,... | collective-permute-start | bytes 1769480 | tf_op jit(solution)/shard_map/ppermute | solution.py:293
  348.1 6.8 %collective-permute-start.4 = (bf16[136,384]{1,0:T(8,128)(2,1)S(1)}, bf16[136,384]{1,0:T(8,128)(2,1)S(1)}, u32[]{:S(2)}, u32[]{:S(2)}) collective-permute-start(bf16[136,384]{1,0:T(8,128)(2,1)S(1)} %dynamic-slice_bitcast_fusion.12), channel_id=1, source_target_pairs={{0,16},{1,17},{2,18},{3,19},{4,20},{5,21},{6,22},{7,23},{8,24},{9,... | collective-permute-start | bytes 313352 | tf_op jit(solution)/shard_map/ppermute | solution.py:293
  354.9 5.0 %collective-permute-start.5 = (bf16[136,384]{1,0:T(8,128)(2,1)S(1)}, bf16[136,384]{1,0:T(8,128)(2,1)S(1)}, u32[]{:S(2)}, u32[]{:S(2)}) collective-permute-start(bf16[136,384]{1,0:T(8,128)(2,1)S(1)} %bitcast_add_fusion.13), channel_id=1, source_target_pairs={{0,2},{1,3},{2,0},{3,1},{4,6},{5,7},{6,4},{7,5},{8,10},{9,11},{10,... | collective-permute-start | bytes 313352 | tf_op jit(solution)/shard_map/ppermute | solution.py:293
  356.4 12.5 %collective-permute-start.9 = (bf16[2,2,96,768]{3,2,1,0:T(8,128)(2,1)S(1)}, bf16[2,2,96,768]{3,2,1,0:T(8,128)(2,1)S(1)}, u32[]{:S(2)}, u32[]{:S(2)}) collective-permute-start(bf16[2,2,96,768]{3,2,1,0:T(8,128)(2,1)S(1)} %dynamic-slice_bitcast_fusion.3), channel_id=1, source_target_pairs={{0,4},{1,5},{2,6},{3,7},{4,0},{5,1},{6,2},{7,3},{8,12},{9,13},{10,... | collective-permute-start | bytes 1769480 | tf_op jit(solution)/shard_map/ppermute | solution.py:293
  360.0 10.7 %collective-permute-start.6 = (bf16[272,384]{1,0:T(8,128)(2,1)S(1)}, bf16[272,384]{1,0:T(8,128)(2,1)S(1)}, u32[]{:S(2)}, u32[]{:S(2)}) collective-permute-start(bf16[272,384]{1,0:T(8,128)(2,1)S(1)} %pad_maximum_fusion.6), channel_id=1, source_target_pairs={{0,1},{1,0},{2,3},{3,2},{4,5},{5,4},{6,7},{7,6},{8,9},{9,8},{10,11... | collective-permute-start | bytes 626696 | tf_op jit(solution)/shard_map/ppermute | solution.py:293
  360.1 8.9 %copy-start.18 = (bf16[2,2,192,384]{3,2,1,0:T(8,128)(2,1)}, bf16[2,2,192,384]{3,2,1,0:T(8,128)(2,1)S(1)}, u32[]{:S(2)}) copy-start(bf16[2,2,192,384]{3,2,1,0:T(8,128)(2,1)S(1)} %bitcast_add_fusion.3) | copy-start | bytes 1769476
  360.9 22.1 %collective-permute-start.24 = (bf16[2,192,384]{2,1,0:T(8,128)(2,1)}, bf16[2,192,384]{2,1,0:T(8,128)(2,1)}, u32[]{:S(2)}, u32[]{:S(2)}) collective-permute-start(bf16[2,192,384]{2,1,0:T(8,128)(2,1)} %dynamic-slice_bitcast_fusion.5), channel_id=1, source_target_pairs={{0,8},{1,9},{2,10},{3,11},{4,12},{5,13},{6,14},{7,15},{8,0},{9,1},... | collective-permute-start | bytes 884744 | tf_op jit(solution)/shard_map/ppermute | solution.py:293
  361.6 8.2 %copy-start.19 = (bf16[2,2,96,768]{3,2,1,0:T(8,128)(2,1)}, bf16[2,2,96,768]{3,2,1,0:T(8,128)(2,1)S(1)}, u32[]{:S(2)}) copy-start(bf16[2,2,96,768]{3,2,1,0:T(8,128)(2,1)S(1)} %dynamic-slice_add_fusion.4) | copy-start | bytes 1769476
  362.5 24.9 %collective-permute-start.17 = (bf16[2,96,768]{2,1,0:T(8,128)(2,1)}, bf16[2,96,768]{2,1,0:T(8,128)(2,1)}, u32[]{:S(2)}, u32[]{:S(2)}) collective-permute-start(bf16[2,96,768]{2,1,0:T(8,128)(2,1)} %dynamic-slice_bitcast_fusion.6), channel_id=1, source_target_pairs={{0,8},{1,9},{2,10},{3,11},{4,12},{5,13},{6,14},{7,15},{8,0},{9,1},... | collective-permute-start | bytes 884744 | tf_op jit(solution)/shard_map/ppermute | solution.py:293
  369.8 18.7 %collective-permute-start.10 = (bf16[2,96,768]{2,1,0:T(8,128)(2,1)}, bf16[2,96,768]{2,1,0:T(8,128)(2,1)}, u32[]{:S(2)}, u32[]{:S(2)}) collective-permute-start(bf16[2,96,768]{2,1,0:T(8,128)(2,1)} %dynamic-slice_bitcast_fusion.7), channel_id=1, source_target_pairs={{0,8},{1,9},{2,10},{3,11},{4,12},{5,13},{6,14},{7,15},{8,0},{9,1},... | collective-permute-start | bytes 884744 | tf_op jit(solution)/shard_map/ppermute | solution.py:293
  378.5 8.9 %copy-start.20 = (bf16[2,2,96,768]{3,2,1,0:T(8,128)(2,1)S(1)}, bf16[2,2,96,768]{3,2,1,0:T(8,128)(2,1)}, u32[]{:S(2)}) copy-start(bf16[2,2,96,768]{3,2,1,0:T(8,128)(2,1)} %copy-done.19) | copy-start | bytes 1769476
  378.5 10.0 %copy-start.22 = (bf16[2,2,96,768]{3,2,1,0:T(8,128)(2,1)S(1)}, bf16[2,2,96,768]{3,2,1,0:T(8,128)(2,1)}, u32[]{:S(2)}) copy-start(bf16[2,2,96,768]{3,2,1,0:T(8,128)(2,1)} %copy-done.21) | copy-start | bytes 1769476
  384.2 14.5 %collective-permute-start.25 = (bf16[192,384]{1,0:T(8,128)(2,1)S(1)}, bf16[192,384]{1,0:T(8,128)(2,1)S(1)}, u32[]{:S(2)}, u32[]{:S(2)}) collective-permute-start(bf16[192,384]{1,0:T(8,128)(2,1)S(1)} %dynamic-slice_bitcast_fusion.9), channel_id=1, source_target_pairs={{0,16},{1,17},{2,18},{3,19},{4,20},{5,21},{6,22},{7,23},{8,24},{9,... | collective-permute-start | bytes 442376 | tf_op jit(solution)/shard_map/ppermute | solution.py:293
  388.4 13.4 %collective-permute-start.18 = (bf16[96,768]{1,0:T(8,128)(2,1)S(1)}, bf16[96,768]{1,0:T(8,128)(2,1)S(1)}, u32[]{:S(2)}, u32[]{:S(2)}) collective-permute-start(bf16[96,768]{1,0:T(8,128)(2,1)S(1)} %dynamic-slice_bitcast_fusion.10), channel_id=1, source_target_pairs={{0,16},{1,17},{2,18},{3,19},{4,20},{5,21},{6,22},{7,23},{8,24},{9,... | collective-permute-start | bytes 442376 | tf_op jit(solution)/shard_map/ppermute | solution.py:293
  389.5 13.8 %collective-permute-start.11 = (bf16[96,768]{1,0:T(8,128)(2,1)S(1)}, bf16[96,768]{1,0:T(8,128)(2,1)S(1)}, u32[]{:S(2)}, u32[]{:S(2)}) collective-permute-start(bf16[96,768]{1,0:T(8,128)(2,1)S(1)} %dynamic-slice_bitcast_fusion.11), channel_id=1, source_target_pairs={{0,16},{1,17},{2,18},{3,19},{4,20},{5,21},{6,22},{7,23},{8,24},{9,... | collective-permute-start | bytes 442376 | tf_op jit(solution)/shard_map/ppermute | solution.py:293
  398.7 5.7 %collective-permute-start.26 = (bf16[192,384]{1,0:T(8,128)(2,1)S(1)}, bf16[192,384]{1,0:T(8,128)(2,1)S(1)}, u32[]{:S(2)}, u32[]{:S(2)}) collective-permute-start(bf16[192,384]{1,0:T(8,128)(2,1)S(1)} %bitcast_add_fusion.10), channel_id=1, source_target_pairs={{0,2},{1,3},{2,0},{3,1},{4,6},{5,7},{6,4},{7,5},{8,10},{9,11},{10,... | collective-permute-start | bytes 442376 | tf_op jit(solution)/shard_map/ppermute | solution.py:293
  401.8 7.6 %collective-permute-start.19 = (bf16[96,768]{1,0:T(8,128)(2,1)S(1)}, bf16[96,768]{1,0:T(8,128)(2,1)S(1)}, u32[]{:S(2)}, u32[]{:S(2)}) collective-permute-start(bf16[96,768]{1,0:T(8,128)(2,1)S(1)} %bitcast_add_fusion.11), channel_id=1, source_target_pairs={{0,2},{1,3},{2,0},{3,1},{4,6},{5,7},{6,4},{7,5},{8,10},{9,11},{10,... | collective-permute-start | bytes 442376 | tf_op jit(solution)/shard_map/ppermute | solution.py:293
  403.4 5.8 %collective-permute-start.12 = (bf16[96,768]{1,0:T(8,128)(2,1)S(1)}, bf16[96,768]{1,0:T(8,128)(2,1)S(1)}, u32[]{:S(2)}, u32[]{:S(2)}) collective-permute-start(bf16[96,768]{1,0:T(8,128)(2,1)S(1)} %bitcast_add_fusion.12), channel_id=1, source_target_pairs={{0,2},{1,3},{2,0},{3,1},{4,6},{5,7},{6,4},{7,5},{8,10},{9,11},{10,... | collective-permute-start | bytes 442376 | tf_op jit(solution)/shard_map/ppermute | solution.py:293
  404.5 6.6 %collective-permute-start.27 = (bf16[384,384]{1,0:T(8,128)(2,1)S(1)}, bf16[384,384]{1,0:T(8,128)(2,1)S(1)}, u32[]{:S(2)}, u32[]{:S(2)}) collective-permute-start(bf16[384,384]{1,0:T(8,128)(2,1)S(1)} %pad_maximum_fusion.5), channel_id=1, source_target_pairs={{0,1},{1,0},{2,3},{3,2},{4,5},{5,4},{6,7},{7,6},{8,9},{9,8},{10,11... | collective-permute-start | bytes 884744 | tf_op jit(solution)/shard_map/ppermute | solution.py:293
  409.3 1.6 collective-permute-start.13
  409.4 4.6 %collective-permute-start.20 = (bf16[96,1536]{1,0:T(8,128)(2,1)S(1)}, bf16[96,1536]{1,0:T(8,128)(2,1)S(1)}, u32[]{:S(2)}, u32[]{:S(2)}) collective-permute-start(bf16[96,1536]{1,0:T(8,128)(2,1)S(1)} %pad_maximum_fusion.4), channel_id=1, source_target_pairs={{0,1},{1,0},{2,3},{3,2},{4,5},{5,4},{6,7},{7,6},{8,9},{9,8},{10,11... | collective-permute-start | bytes 884744 | tf_op jit(solution)/shard_map/ppermute | solution.py:293
  (51 other events, 140.0 us)

commit v2 on v0

v2 whole, which is shorter than its diff:
```python
import jax
import jax.numpy as jnp
from jax import lax
from jax.experimental import pallas as pl
from jax.experimental.pallas import tpu as pltpu
from jax.sharding import PartitionSpec as P

HEADS = 12
HEAD = 64
epsilon = 1e-12
inv_sqrt_two = 0.7071067811865476
inv_sqrt_tau = 0.3989422804014327
f32 = jnp.float32
bf16 = jnp.bfloat16
NN = (((1,), (0,)), ((), ()))
NT = (((1,), (1,)), ((), ()))
TN = (((0,), (0,)), ((), ()))


def mm(a, b, dims=NN):
    return lax.dot_general(a, b, dims, preferred_element_type=f32)


def params(limit=56):
    return pltpu.CompilerParams(
        dimension_semantics=("arbitrary",), vmem_limit_bytes=limit << 20
    )


def whole(shape):
    return pl.BlockSpec(shape, lambda i, *s: (0,) * len(shape), pipeline_mode=pl.Buffered(1))


def shape(dims, kind=f32):
    return jax.ShapeDtypeStruct(dims, kind)


def norm_parts(values):
    centre = values - jnp.mean(values, -1, keepdims=True)
    inv_std = lax.rsqrt(jnp.mean(centre * centre, -1, keepdims=True) + epsilon)
    return centre * inv_std, inv_std


def norm_back(grad, normed, inv_std, gain):
    scaled = grad * gain
    return inv_std * (
        scaled
        - jnp.mean(scaled, -1, keepdims=True)
        - normed * jnp.mean(scaled * normed, -1, keepdims=True)
    )


def row_sum(values):
    return jnp.sum(values, 0, keepdims=True)


def one_hot(index_row, count):
    rows = lax.broadcasted_iota(jnp.int32, (count, index_row.shape[1]), 0)
    return jnp.where(rows == index_row, 1.0, 0.0).astype(bf16)


def region_forward(features, boxes, target, w_visual, w_box_t, bias, gain, shift):
    rows, feat = features.shape
    width = w_visual.shape[1]
    steps = 4
    part = feat // steps

    def kernel(f_ref, box_ref, t_ref, wv_ref, wb_ref, b_ref, g_ref, s_ref, m_ref, n_ref, i_ref, acc):
        step = pl.program_id(0)
        partial = mm(f_ref[...], wv_ref[...])

        @pl.when(step == 0)
        def _():
            acc[...] = partial + (mm(box_ref[...], wb_ref[...], TN) + b_ref[...])

        @pl.when(step > 0)
        def _():
            acc[...] += partial

        @pl.when(step == steps - 1)
        def _():
            normed, inv = norm_parts(acc[...])
            n_ref[...] = normed
            i_ref[...] = jnp.broadcast_to(inv, i_ref.shape)
            low = (normed * g_ref[...] + s_ref[...]).astype(bf16)
            m_ref[...] = mm(one_hot(t_ref[...], rows), low).astype(bf16)

    return pl.pallas_call(
        kernel,
        grid=(steps,),
        in_specs=[
            pl.BlockSpec((rows, part), lambda i: (0, i)),
            whole(boxes.shape),
            whole((1, rows)),
            pl.BlockSpec((part, width), lambda i: (i, 0)),
            whole(w_box_t.shape),
            whole((1, width)),
            whole((1, width)),
            whole((1, width)),
        ],
        out_specs=[whole((rows, width)), whole((rows, width)), whole((rows, 128))],
        out_shape=[shape((rows, width), bf16), shape((rows, width)), shape((rows, 128))],
        scratch_shapes=[pltpu.VMEM((rows, width), f32)],
        compiler_params=params(24),
        name="region_forward",
    )(features, boxes, target, w_visual, w_box_t, bias, gain, shift)


def text_qkv(text, w_qkv, qv_bias):
    rows, width = text.shape

    def kernel(t_ref, w_ref, b_ref, o_ref):
        step = pl.program_id(0)
        bias = b_ref[...] * jnp.where(step == 1, 0.0, 1.0)
        o_ref[...] = (mm(t_ref[...], w_ref[...]) + bias).astype(bf16)

    return pl.pallas_call(
        kernel,
        grid=(3,),
        in_specs=[
            whole((rows, width)),
            pl.BlockSpec((width, width), lambda i: (0, i)),
            pl.BlockSpec((1, width), lambda i: (0, i // 2)),
        ],
        out_specs=pl.BlockSpec((rows, width), lambda i: (0, i)),
        out_shape=shape((rows, 3 * width), bf16),
        compiler_params=params(24),
        name="text_qkv",
    )(text, w_qkv, qv_bias)


def forward(
    scalars, text, text_low, arrived, source, out_grad, w_qkv, qv_bias, w_out, out_bias,
    attn_gain, attn_shift, w_up, up_bias, w_down, down_bias, ffn_gain, ffn_shift, dims,
):
    captions, images = dims
    width = text.shape[1]
    text_len = text.shape[0] // captions
    slots = arrived.shape[0]
    regions = slots // images
    seq = text_len + regions
    rows = captions * seq
    ff = w_up.shape[1]
    half = width // 2
    parts = 4
    part = ff // parts
    grid = captions + 2 * parts

    def kernel(
        sc_ref, t_ref, tq_ref, a_ref, src_ref, og_ref, wq_hbm, qvb_ref, wo_hbm, ob_ref, ag_ref, as_ref,
        wu_hbm, ub_ref, wd_hbm, db_ref, fg_ref, fs_ref,
        out_ref, x_ref, qkv_ref, probs_ref, ctx_ref, an_ref, ai_ref, hid_ref, slope_ref, ds_ref, df_ref,
        sums_ref, send_ref, keep_ref,
        regs, rqkv, act_all, dffn_all, wq, wo, wu, wd, sems,
    ):
        step = pl.program_id(0)

        places = [(wq_hbm, wq), (wo_hbm, wo), (wu_hbm, wu), (wd_hbm, wd)]

        def copy(at):
            return pltpu.make_async_copy(*places[at], sems.at[at])

        @pl.when(step == 0)
        def _():
            for at in range(len(places)):
                copy(at).start()
            sums_ref[...] = jnp.zeros_like(sums_ref)
            local = mm(one_hot(src_ref[...], slots), a_ref[...], TN).astype(bf16)
            regs[...] = local
            copy(0).wait()
            for part_id in range(3):
                at = slice(part_id * width, (part_id + 1) * width)
                got = mm(local, wq[:, at])
                if part_id == 0:
                    got = got + qvb_ref[:, :width]
                if part_id == 2:
                    got = got + qvb_ref[:, width:]
                rqkv[:, at] = got.astype(bf16)

        @pl.when(step < captions)
        def _():
            image = sc_ref[step]
            length = sc_ref[captions + step]
            count = sc_ref[2 * captions + image]
            at = pl.ds(pl.multiple_of(image * regions, regions), regions)
            x_ref[:text_len, :] = t_ref[...]
            x_ref[text_len:, :] = regs[at, :]
            qkv_ref[:text_len, :] = tq_ref[...]
            qkv_ref[text_len:, :] = rqkv[at, :]
            lane = lax.broadcasted_iota(jnp.int32, (1, seq), 1)
            key_end = jnp.where(lane < text_len, length, text_len + count)
            key_bias = jnp.where(lane < key_end, 0.0, -1e30)
            place = lax.broadcasted_iota(jnp.int32, (seq, 1), 0)
            row_end = jnp.where(place < text_len, length, text_len + count)
            row_mask = jnp.where(place < row_end, 1.0, 0.0)
            pair_lane = lax.broadcasted_iota(jnp.int32, (1, 2 * HEAD), 1)
            first = pair_lane < HEAD
            scale = [
                jnp.where(first, 0.125, 0.0).astype(bf16),
                jnp.where(first, 0.0, 0.125).astype(bf16),
            ]
            for pair in range(HEADS // 2):
                lo = pair * 2 * HEAD
                q = qkv_ref[:, lo : lo + 2 * HEAD]
                k = qkv_ref[:, width + lo : width + lo + 2 * HEAD]
                v = qkv_ref[:, 2 * width + lo : 2 * width + lo + 2 * HEAD]
                outs = []
                for one in range(2):
                    scores = mm(q * scale[one], k, NT) + key_bias
                    top = jnp.max(scores, -1, keepdims=True)
                    raised = jnp.exp(scores - top)
                    total = jnp.sum(raised, -1, keepdims=True)
                    low = (raised * (1.0 / total)).astype(bf16)
                    probs_ref[2 * pair + one] = low
                    outs.append(mm(low, v))
                ctx_ref[:, lo : lo + 2 * HEAD] = jnp.where(first, outs[0], outs[1]).astype(bf16)

            @pl.when(step == 0)
            def _():
                copy(1).wait()

            x_wide = x_ref[...].astype(f32)
            attn_out = mm(ctx_ref[...], wo[...]) + ob_ref[...]
            normed, inv = norm_parts(x_wide + attn_out)
            an_ref[...] = normed
            ai_ref[...] = jnp.broadcast_to(inv, ai_ref.shape)
            hidden = normed * ag_ref[...] + as_ref[...]
            hidden_low = hidden.astype(bf16)
            hid_ref[...] = hidden_low

            @pl.when(step == 0)
            def _():
                copy(2).wait()

            here = pl.ds(pl.multiple_of(step * seq, seq), seq)
            for piece in range(parts):
                at = slice(piece * part, (piece + 1) * part)
                upper = mm(hidden_low, wu[:, at]) + ub_ref[:, at]
                phi = 0.5 * (1.0 + lax.erf(upper * inv_sqrt_two))
                act_all[here, at] = (upper * phi).astype(bf16)
                slope = phi + upper * jnp.exp(-0.5 * upper * upper) * inv_sqrt_tau
                slope_ref[:, at] = slope.astype(bf16)

            @pl.when(step == 0)
            def _():
                copy(3).wait()

            ffn_out = mm(act_all[here, :], wd[...]) + db_ref[...]
            ffn_normed, ffn_inv = norm_parts(hidden + ffn_out)
            out_ref[...] = ((ffn_normed * fg_ref[...] + fs_ref[...]) * row_mask).astype(bf16)
            cot = og_ref[...].astype(f32) * row_mask
            second = norm_back(cot, ffn_normed, ffn_inv, fg_ref[...])
            ds_ref[...] = second
            low = second.astype(bf16)
            df_ref[...] = low
            dffn_all[here, :] = low
            for at, value in enumerate(
                (
                    cot * ffn_normed,
                    cot,
                    low.astype(f32),
                    row_mask * x_wide * x_wide,
                    row_mask * attn_out * attn_out,
                    row_mask * ffn_out * ffn_out,
                    jnp.broadcast_to(row_mask, (seq, width)),
                )
            ):
                sums_ref[at : at + 1, :] += row_sum(value)

        def gradient(to_ref, piece, side):
            cols = pl.ds(pl.multiple_of(side * half, half), half)
            acts = pl.ds(pl.multiple_of(piece * part, part), part)
            to_ref[...] = mm(act_all[:, acts], dffn_all[:, cols], TN).astype(bf16)

        core = sc_ref[2 * captions + images]

        @pl.when((step >= captions) & (step < captions + parts))
        def _():
            gradient(send_ref, step - captions, 1 - core)

        @pl.when(step >= captions + parts)
        def _():
            gradient(keep_ref, step - captions - parts, core)

    def rowwise(size, cols):
        return pl.BlockSpec((size, cols), lambda i, s: (jnp.minimum(i, captions - 1), 0))

    anywhere = pl.BlockSpec(memory_space=pl.ANY)
    return pl.pallas_call(
        kernel,
        grid_spec=pltpu.PrefetchScalarGridSpec(
            num_scalar_prefetch=1,
            grid=(grid,),
            in_specs=[
                rowwise(text_len, width),
                rowwise(text_len, 3 * width),
                whole((slots, width)),
                whole((1, slots)),
                rowwise(seq, width),
                anywhere,
                whole((1, 2 * width)),
                anywhere,
                whole((1, width)),
                whole((1, width)),
                whole((1, width)),
                anywhere,
                whole((1, ff)),
                anywhere,
                whole((1, width)),
                whole((1, width)),
                whole((1, width)),
            ],
            out_specs=[
                rowwise(seq, width),
                rowwise(seq, width),
                rowwise(seq, 3 * width),
                pl.BlockSpec((HEADS, seq, seq), lambda i, s: (jnp.minimum(i, captions - 1), 0, 0)),
                rowwise(seq, width),
                rowwise(seq, width),
                rowwise(seq, 128),
                rowwise(seq, width),
                rowwise(seq, ff),
                rowwise(seq, width),
                rowwise(seq, width),
                whole((8, width)),
                pl.BlockSpec((part, half), lambda i, s: (jnp.clip(i - captions, 0, parts - 1), 0)),
                pl.BlockSpec((part, half), lambda i, s: (jnp.clip(i - captions - parts, 0, parts - 1), 0)),
            ],
            scratch_shapes=[
                pltpu.VMEM((slots, width), bf16),
                pltpu.VMEM((slots, 3 * width), bf16),
                pltpu.VMEM((rows, ff), bf16),
                pltpu.VMEM((rows, width), bf16),
                pltpu.VMEM(w_qkv.shape, bf16),
                pltpu.VMEM(w_out.shape, bf16),
                pltpu.VMEM(w_up.shape, bf16),
                pltpu.VMEM(w_down.shape, bf16),
                pltpu.SemaphoreType.DMA((4,)),
            ],
        ),
        out_shape=[
            shape((rows, width), bf16),
            shape((rows, width), bf16),
            shape((rows, 3 * width), bf16),
            shape((captions * HEADS, seq, seq), bf16),
            shape((rows, width), bf16),
            shape((rows, width)),
            shape((rows, 128)),
            shape((rows, width), bf16),
            shape((rows, ff), bf16),
            shape((rows, width)),
            shape((rows, width), bf16),
            shape((8, width)),
            shape((ff, half), bf16),
            shape((ff, half), bf16),
        ],
        compiler_params=params(60),
        name="forward",
    )(
        scalars, text, text_low, arrived, source, out_grad, w_qkv, qv_bias, w_out, out_bias,
        attn_gain, attn_shift, w_up, up_bias, w_down, down_bias, ffn_gain, ffn_shift,
    )


def ffn_backward(core, d_ffn, d_second, slope, hidden_low, attn_normed, attn_inv, w_down, w_up, attn_gain, captions):
    rows, width = d_ffn.shape
    seq = rows // captions
    ff = w_up.shape[1]
    parts = 4
    part = ff // parts
    cols = ff // (2 * parts)

    def kernel(
        c_ref, df_ref, ds_ref, sl_ref, hid_ref, an_ref, ai_ref, wd_hbm, wu_hbm, ag_ref,
        dr_ref, da_ref, sums_ref, up_ref, send_ref, keep_ref, dup, wd, wu, sems,
    ):
        step = pl.program_id(0)

        places = [(wd_hbm, wd), (wu_hbm, wu)]

        def copy(at):
            return pltpu.make_async_copy(*places[at], sems.at[at])

        @pl.when(step == 0)
        def _():
            for at in range(len(places)):
                copy(at).start()
            sums_ref[...] = jnp.zeros_like(sums_ref)
            up_ref[...] = jnp.zeros_like(up_ref)
            copy(0).wait()

        @pl.when(step < captions)
        def _():
            here = pl.ds(pl.multiple_of(step * seq, seq), seq)
            d_low = df_ref[...]
            for piece in range(parts):
                at = slice(piece * part, (piece + 1) * part)
                d_act = mm(d_low, wd[at, :], NT)
                low = (d_act * sl_ref[:, at].astype(f32)).astype(bf16)
                dup[here, at] = low
                up_ref[0:1, at] += row_sum(low.astype(f32))

            @pl.when(step == 0)
            def _():
                copy(1).wait()

            d_hidden = ds_ref[...] + mm(dup[here, :], wu[...], NT)
            normed = an_ref[...]
            resid = norm_back(d_hidden, normed, ai_ref[:, 0:1], ag_ref[...])
            dr_ref[...] = resid
            low = resid.astype(bf16)
            da_ref[...] = low
            sums_ref[0:1, :] += row_sum(d_hidden * normed)
            sums_ref[1:2, :] += row_sum(d_hidden)
            sums_ref[2:3, :] += row_sum(low.astype(f32))

        def gradient(to_ref, piece, side):
            at = pl.ds(pl.multiple_of(side * (ff // 2) + piece * cols, 128), cols)
            to_ref[...] = mm(hid_ref[...], dup[:, at], TN).astype(bf16)

        @pl.when((step >= captions) & (step < captions + parts))
        def _():
            gradient(send_ref, step - captions, 1 - c_ref[0])

        @pl.when(step >= captions + parts)
        def _():
            gradient(keep_ref, step - captions - parts, c_ref[0])

    def rowwise(cols):
        return pl.BlockSpec((seq, cols), lambda i, s: (jnp.minimum(i, captions - 1), 0))

    anywhere = pl.BlockSpec(memory_space=pl.ANY)
    return pl.pallas_call(
        kernel,
        grid_spec=pltpu.PrefetchScalarGridSpec(
            num_scalar_prefetch=1,
            grid=(captions + 2 * parts,),
            in_specs=[
                rowwise(width),
                rowwise(width),
                rowwise(ff),
                whole((rows, width)),
                rowwise(width),
                rowwise(128),
                anywhere,
                anywhere,
                whole((1, width)),
            ],
            out_specs=[
                rowwise(width),
                rowwise(width),
                whole((8, width)),
                whole((8, ff)),
                pl.BlockSpec((width, cols), lambda i, s: (0, jnp.clip(i - captions, 0, parts - 1))),
                pl.BlockSpec((width, cols), lambda i, s: (0, jnp.clip(i - captions - parts, 0, parts - 1))),
            ],
            scratch_shapes=[
                pltpu.VMEM((rows, ff), bf16),
                pltpu.VMEM(w_down.shape, bf16),
                pltpu.VMEM(w_up.shape, bf16),
                pltpu.SemaphoreType.DMA((2,)),
            ],
        ),
        out_shape=[
            shape((rows, width)),
            shape((rows, width), bf16),
            shape((8, width)),
            shape((8, ff)),
            shape((width, ff // 2), bf16),
            shape((width, ff // 2), bf16),
        ],
        compiler_params=params(56),
        name="ffn_backward",
    )(core, d_ffn, d_second, slope, hidden_low, attn_normed, attn_inv, w_down, w_up, attn_gain)


def attention_backward(scalars, d_attn, d_resid, probs, qkv, source, w_out, w_qkv, dims):
    captions, images = dims
    rows, width = d_attn.shape
    seq = rows // captions
    slots = source.shape[1]
    regions = slots // images
    text_len = seq - regions

    def kernel(
        sc_ref, da_ref, dr_ref, p_ref, qkv_ref, src_ref, wo_ref, wq_hbm,
        dqkv_ref, text_ref, back_ref, sums_ref, d_img, wq, sem,
    ):
        step = pl.program_id(0)

        def copy():
            return pltpu.make_async_copy(wq_hbm, wq, sem)

        @pl.when(step == 0)
        def _():
            copy().start()
            sums_ref[...] = jnp.zeros_like(sums_ref)
            d_img[...] = jnp.zeros_like(d_img)

        d_ctx = mm(da_ref[...], wo_ref[...], NT).astype(bf16)
        first = lax.broadcasted_iota(jnp.int32, (1, 2 * HEAD), 1) < HEAD
        masks = [jnp.where(first, 1.0, 0.0).astype(bf16), jnp.where(first, 0.0, 1.0).astype(bf16)]
        for pair in range(HEADS // 2):
            lo = pair * 2 * HEAD
            q = qkv_ref[:, lo : lo + 2 * HEAD]
            k = qkv_ref[:, width + lo : width + lo + 2 * HEAD]
            v = qkv_ref[:, 2 * width + lo : 2 * width + lo + 2 * HEAD]
            d_c = d_ctx[:, lo : lo + 2 * HEAD]
            got = []
            for one in range(2):
                low = p_ref[2 * pair + one]
                d_probs = mm(d_c * masks[one], v, NT)
                wide = low.astype(f32)
                both = wide * d_probs
                inner = jnp.sum(both, -1, keepdims=True)
                d_scores = (both - wide * inner).astype(bf16)
                got.append(
                    (mm(d_scores, k) * 0.125, mm(d_scores, q, TN) * 0.125, mm(low, d_c, TN))
                )
            for at in range(3):
                dqkv_ref[:, at * width + lo : at * width + lo + 2 * HEAD] = jnp.where(
                    first, got[0][at], got[1][at]
                ).astype(bf16)

        @pl.when(step == 0)
        def _():
            copy().wait()

        sums_ref[0:1, :] += row_sum(dqkv_ref[:, :width].astype(f32))
        sums_ref[1:2, :] += row_sum(dqkv_ref[:, 2 * width :].astype(f32))
        d_x = mm(dqkv_ref[...], wq[...], NT) + dr_ref[...]
        text_ref[...] = d_x[:text_len]
        at = pl.ds(pl.multiple_of(sc_ref[step] * regions, regions), regions)
        d_img[at, :] += d_x[text_len:]

        @pl.when(step == captions - 1)
        def _():
            back_ref[...] = mm(one_hot(src_ref[...], slots), d_img[...].astype(bf16)).astype(bf16)

    def rowwise(size, cols):
        return pl.BlockSpec((size, cols), lambda i, s: (i, 0))

    return pl.pallas_call(
        kernel,
        grid_spec=pltpu.PrefetchScalarGridSpec(
            num_scalar_prefetch=1,
            grid=(captions,),
            in_specs=[
                rowwise(seq, width),
                rowwise(seq, width),
                pl.BlockSpec((HEADS, seq, seq), lambda i, s: (i, 0, 0)),
                rowwise(seq, 3 * width),
                whole((1, slots)),
                whole(w_out.shape),
                pl.BlockSpec(memory_space=pl.ANY),
            ],
            out_specs=[
                rowwise(seq, 3 * width),
                rowwise(text_len, width),
                whole((slots, width)),
                whole((8, width)),
            ],
            scratch_shapes=[
                pltpu.VMEM((slots, width), f32),
                pltpu.VMEM(w_qkv.shape, bf16),
                pltpu.SemaphoreType.DMA,
            ],
        ),
        out_shape=[
            shape((rows, 3 * width), bf16),
            shape((captions * text_len, width)),
            shape((slots, width), bf16),
            shape((8, width)),
        ],
        compiler_params=params(48),
        name="attention_backward",
    )(scalars, d_attn, d_resid, probs, qkv, source, w_out, w_qkv)


def qkvo_gradient(core, x, d_qkv, context, d_attn):
    rows, width = x.shape
    cols = width // 2

    def kernel(c_ref, x_ref, dq_ref, ctx_ref, da_ref, send_ref, keep_ref):
        step = pl.program_id(0)
        core_bit = c_ref[0]

        def gradient(to_ref, piece, side):
            block = side * 4 + piece

            @pl.when(block < 6)
            def _():
                to_ref[...] = mm(x_ref[...], dq_ref[...], TN).astype(bf16)

            @pl.when(block >= 6)
            def _():
                to_ref[...] = mm(ctx_ref[...], da_ref[...], TN).astype(bf16)

        @pl.when(step < 4)
        def _():
            gradient(send_ref, step, 1 - core_bit)

        @pl.when(step >= 4)
        def _():
            gradient(keep_ref, step - 4, core_bit)

    def block(i, s):
        return jnp.where(i < 4, (1 - s[0]) * 4 + i, s[0] * 4 + i - 4)

    return pl.pallas_call(
        kernel,
        grid_spec=pltpu.PrefetchScalarGridSpec(
            num_scalar_prefetch=1,
            grid=(8,),
            in_specs=[
                whole((rows, width)),
                pl.BlockSpec((rows, cols), lambda i, s: (0, jnp.minimum(block(i, s), 5))),
                whole((rows, width)),
                pl.BlockSpec((rows, cols), lambda i, s: (0, jnp.maximum(block(i, s) - 6, 0))),
            ],
            out_specs=[
                pl.BlockSpec((width, cols), lambda i, s: (0, jnp.clip(i, 0, 3))),
                pl.BlockSpec((width, cols), lambda i, s: (0, jnp.clip(i - 4, 0, 3))),
            ],
        ),
        out_shape=[shape((width, 2 * width), bf16), shape((width, 2 * width), bf16)],
        compiler_params=params(40),
        name="qkvo_gradient",
    )(core, x, d_qkv, context, d_attn)


def region_backward(core, returned, target, normed, inv, gain, features, boxes, w_visual, w_box_t):
    rows, width = returned.shape
    feat = features.shape[1]
    half = width // 2
    parts = 4
    part = feat // parts
    box = boxes.shape[0]

    def kernel(
        c_ref, r_ref, t_ref, n_ref, i_ref, g_ref, f_ref, box_ref, wv_ref, wb_ref,
        send_ref, keep_ref, fg_ref, bg_ref, sums_ref, dpre,
    ):
        step = pl.program_id(0)

        @pl.when(step == 0)
        def _():
            d_region = mm(one_hot(t_ref[...], rows), r_ref[...], TN)
            normed = n_ref[...]
            low = norm_back(d_region, normed, i_ref[:, 0:1], g_ref[...]).astype(bf16)
            dpre[...] = low
            sums_ref[0:1, :] = row_sum(low.astype(f32))
            sums_ref[1:2, :] = row_sum(d_region * normed)
            sums_ref[2:3, :] = row_sum(d_region)
            sums_ref[3 : 3 + box, :] = mm(box_ref[...], low)
            bg_ref[...] = mm(wb_ref[...], low, NT)

        def gradient(to_ref, side):
            at = pl.ds(pl.multiple_of(side * half, half), half)
            to_ref[...] = mm(f_ref[...], dpre[:, at], TN).astype(bf16)

        @pl.when(step < parts)
        def _():
            gradient(send_ref, 1 - c_ref[0])

        @pl.when(step >= parts)
        def _():
            gradient(keep_ref, c_ref[0])
            fg_ref[...] = mm(dpre[...], wv_ref[...], NT)

    return pl.pallas_call(
        kernel,
        grid_spec=pltpu.PrefetchScalarGridSpec(
            num_scalar_prefetch=1,
            grid=(2 * parts,),
            in_specs=[
                whole((rows, width)),
                whole((1, rows)),
                whole((rows, width)),
                whole((rows, 128)),
                whole((1, width)),
                pl.BlockSpec((rows, part), lambda i, s: (0, lax.rem(i, parts))),
                whole(boxes.shape),
                pl.BlockSpec((part, width), lambda i, s: (jnp.maximum(i - parts, 0), 0)),
                whole(w_box_t.shape),
            ],
            out_specs=[
                pl.BlockSpec((part, half), lambda i, s: (jnp.clip(i, 0, parts - 1), 0)),
                pl.BlockSpec((part, half), lambda i, s: (jnp.clip(i - parts, 0, parts - 1), 0)),
                pl.BlockSpec((rows, part), lambda i, s: (0, jnp.maximum(i - parts, 0))),
                whole((box, rows)),
                whole((8, width)),
            ],
            scratch_shapes=[pltpu.VMEM((rows, width), bf16)],
        ),
        out_shape=[
            shape((feat, half), bf16),
            shape((feat, half), bf16),
            shape((rows, feat)),
            shape((box, rows)),
            shape((8, width)),
        ],
        compiler_params=params(24),
        name="region_backward",
    )(core, returned, target, normed, inv, gain, features, boxes, w_visual, w_box_t)


def device_bit(bit):
    me = lax.axis_index("dp") * lax.axis_size("enc") + lax.axis_index("enc")
    return lax.rem(me // bit, 2)


def swap(values, bit):
    count = lax.axis_size("dp") * lax.axis_size("enc")
    return lax.ppermute(values, ("dp", "enc"), [(i, i ^ bit) for i in range(count)])


def halve(values, bit, axis):
    mine = device_bit(bit)
    size = values.shape[axis] // 2
    sent = lax.dynamic_slice_in_dim(values, (1 - mine) * size, size, axis)
    kept = lax.dynamic_slice_in_dim(values, mine * size, size, axis)
    return kept + swap(sent, bit)


def halve_lead(values, bit, axis):
    mine = device_bit(bit)
    sent = lax.dynamic_index_in_dim(values, 1 - mine, axis, keepdims=False)
    kept = lax.dynamic_index_in_dim(values, mine, axis, keepdims=False)
    return kept + swap(sent, bit)


def double(values, bit, axis):
    mine = device_bit(bit)
    other = swap(values, bit)
    low_half = jnp.where(mine == 0, values, other)
    high_half = jnp.where(mine == 0, other, values)
    return jnp.concatenate([low_half, high_half], axis)


def reduce_tall(sent, kept, first):
    groups = lax.axis_size("dp")
    bits = groups.bit_length() - 1
    values = kept + swap(sent, 1)
    rows = values.shape[0] // groups // 2
    values = values.reshape((2,) * (bits + 1) + (rows, values.shape[1]))
    if first == 0:
        values = halve_lead(values, 2, bits)
        values = halve_lead(values, 4, bits - 1)
    else:
        values = halve_lead(values, 4, bits - 1)
        values = halve_lead(values, 2, bits - 1)
    for b in range(1, bits):
        values = halve_lead(values, 4 << b, bits - 1 - b)
    values = double(values, 2, 0)
    return double(values, 1, 1).astype(f32)


def reduce_wide(sent, kept, first):
    groups = lax.axis_size("dp")
    bits = groups.bit_length() - 1
    values = kept + swap(sent, 1)
    rows = values.shape[0] // groups

    def by_row(values, b):
        values = values.reshape((2,) * (bits - b) + (rows, values.shape[-1]))
        return halve_lead(values, 4 << b, bits - 1 - b)

    if first == 0:
        values = halve(values, 2, 1)
        values = by_row(values, 0)
    else:
        values = by_row(values, 0)
        values = halve(values, 2, values.ndim - 1)
    for b in range(1, bits):
        values = by_row(values, b)
    values = double(values, 2, 1)
    return double(values, 1, 1).astype(f32)


def all_sum(values):
    bit = 1
    while bit < lax.axis_size("dp") * lax.axis_size("enc"):
        values = values + swap(values, bit)
        bit *= 2
    return values


def on_device(
    text_embed,
    region_features,
    boxes,
    caption_image,
    caption_lengths,
    region_counts,
    region_target,
    region_source,
    w_visual,
    w_box,
    visual_bias,
    visual_gain,
    visual_shift,
    w_qkv,
    qv_bias,
    w_out,
    out_bias,
    attn_gain,
    attn_shift,
    w_up,
    up_bias,
    w_down,
    down_bias,
    ffn_gain,
    ffn_shift,
    out_grad,
):
    width = text_embed.shape[1]
    captions = caption_image.shape[0]
    images = region_counts.shape[0]
    dims = (captions, images)
    axes = ("dp", "enc")
    core = device_bit(1).astype(jnp.int32).reshape(1)
    scalars = jnp.concatenate([caption_image, caption_lengths, region_counts, core])
    w_box_t = w_box.T
    row = lambda v: v.reshape(1, -1)

    message, vis_normed, vis_inv = region_forward(
        region_features, boxes, region_target, w_visual, w_box_t,
        row(visual_bias), row(visual_gain), row(visual_shift),
    )
    arrived = lax.all_to_all(message, axes, split_axis=0, concat_axis=0, tiled=True)
    text_low = text_qkv(text_embed, w_qkv, row(qv_bias))
    (
        out_rows, x, qkv, probs, context, attn_normed, attn_inv, hidden_low, slope, d_second, d_ffn,
        sums_forward, down_sent, down_kept,
    ) = forward(
        scalars, text_embed, text_low, arrived, region_source, out_grad, w_qkv, row(qv_bias), w_out,
        row(out_bias), row(attn_gain), row(attn_shift), w_up, row(up_bias), w_down, row(down_bias),
        row(ffn_gain), row(ffn_shift), dims,
    )
    d_resid, d_attn, sums_ffn, sums_up, up_sent, up_kept = ffn_backward(
        core, d_ffn, d_second, slope, hidden_low, attn_normed, attn_inv, w_down, w_up, row(attn_gain), captions
    )
    d_qkv, text_grad, back_message, sums_attn = attention_backward(
        scalars, d_attn, d_resid, probs, qkv, region_source, w_out, w_qkv, dims
    )
    returned = lax.all_to_all(back_message, axes, split_axis=0, concat_axis=0, tiled=True)
    qkvo_sent, qkvo_kept = qkvo_gradient(core, x, d_qkv, context, d_attn)
    vis_sent, vis_kept, feature_grad, box_grad, sums_vis = region_backward(
        core, returned, region_target, vis_normed, vis_inv, row(visual_gain), region_features, boxes, w_visual, w_box_t
    )
    down = reduce_tall(down_sent, down_kept, 0)
    up = reduce_wide(up_sent, up_kept, 1)
    qkvo = reduce_wide(qkvo_sent, qkvo_kept, 0)
    share_vis = reduce_tall(vis_sent, vis_kept, 1)
    smalls = jnp.concatenate(
        [sums_forward, sums_ffn, sums_up[0].reshape(-1, width), sums_attn[:2], sums_vis], 0
    )
    smalls = all_sum(smalls)
    sums = jnp.sum(smalls[3:7], 1)
    rms_values = jnp.sqrt(sums[:3] / sums[3])
    groups = lax.axis_size("dp")
    position = lax.axis_index("dp")

    def share(values, axis=0):
        size = values.shape[axis] // groups
        return lax.dynamic_slice_in_dim(values, position * size, size, axis)

    base = 16 + w_up.shape[1] // width
    return (
        out_rows,
        text_grad,
        feature_grad,
        box_grad,
        rms_values,
        share_vis,
        share(smalls[base + 5 : base + 9], 1).T,
        share(smalls[base + 2]),
        share(smalls[base + 3]),
        share(smalls[base + 4]),
        qkvo[:, : 3 * width],
        share(smalls[base : base + 2].reshape(-1)),
        qkvo[:, 3 * width :],
        share(smalls[10]),
        share(smalls[8]),
        share(smalls[9]),
        up,
        share(smalls[16:base].reshape(-1)),
        down,
        share(smalls[2]),
        share(smalls[0]),
        share(smalls[1]),
    )


def solution(mesh):
    return jax.shard_map(
        on_device,
        mesh=mesh,
        in_specs=(
            P(("dp", "enc"), None),
            P(("dp", "enc"), None),
            P(None, ("dp", "enc")),
            P(("dp", "enc")),
            P(("dp", "enc")),
            P(("dp", "enc")),
            P(("dp", "enc"), None),
            P(("dp", "enc"), None),
            P(),
            P(),
            P(),
            P(),
            P(),
            P(),
            P(),
            P(),
            P(),
            P(),
            P(),
            P(),
            P(),
            P(),
            P(),
            P(),
            P(),
            P(("dp", "enc"), None),
        ),
        out_specs=(
            P(("dp", "enc"), None),
            P(("dp", "enc"), None),
            P(("dp", "enc"), None),
            P(None, ("dp", "enc")),
            P(),
            P("dp", None),
            P("dp", None),
            P("dp"),
            P("dp"),
            P("dp"),
            P("dp", None),
            P("dp"),
            P("dp", None),
            P("dp"),
            P("dp"),
            P("dp"),
            P("dp", None),
            P("dp"),
            P("dp", None),
            P("dp"),
            P("dp"),
            P("dp"),
        ),
        check_vma=False,
    )
```

time: 790 us -> 336 us (0.43)
  waiting for transfers between devices: 454 us -> 104 us
  matrix products: 125 us -> 0 us
  Pallas kernels: 0 us -> 117 us
  local copies, waits for them, and re-layouts: 96.6 us -> 50.5 us
  blocking collectives: 43.4 us -> 0 us
  starting transfers between devices: 11.2 us -> 41.2 us
  other arithmetic: 38.5 us -> 21.6 us
  between operations: 15.9 us -> 1.29 us
    psum x1 -> x0, waiting for transfers between devices: 447 us -> none  [on_device(): lax.psum((g_w_visual, g_w_box, g_visual_bias, g_visual_gain, g_visual_shi...]
    dot_general x26 -> x0, matrix products: 125 us -> none  [the longest x1 25.9 us: on_device(): upper = jnp.dot(hidden_low, w_up, preferred_element_type=f32) + up_bias]
    pallas_call x0 -> x7, Pallas kernels: none -> 117 us  [the longest x1 45.1 us: forward(): pl.pallas_call(kernel, grid_spec=pltpu.PrefetchScalarGridSpec(num_scalar_...]
    ppermute x0 -> x33, waiting for transfers between devices: none -> 89.9 us  [swap(): lax.ppermute(values, ('dp', 'enc'), [(i, i ^ bit) for i in range(count)])]
    psum x1 -> x0, blocking collectives: 43.4 us -> none  [on_device(): lax.psum((jnp.sum(row_mask * flat_wide * flat_wide), jnp.sum(row_mask * a...]
    reshape x9 -> x12, local copies, waits for them, and re-layouts: 39.5 us -> 10.3 us  [the longest x10 9.03 us: on_device(): row = lambda v: v.reshape(1, -1)]
    ppermute x0 -> x33, starting transfers between devices: none -> 28.8 us  [swap(): lax.ppermute(values, ('dp', 'enc'), [(i, i ^ bit) for i in range(count)])]
    reduce_sum x12 -> x0, other arithmetic: 22.5 us -> none  [the longest x3 6.42 us: col_sum(): return jnp.sum(values.astype(jnp.float32), 0)]
  transfers between devices with their start and end apart: 3 -> 35, of which waited for: 3 -> 19; matrix products, arithmetic and copies ran while one was open for 6% -> 13% of each run, Pallas kernels for 0% -> 5%
where the time goes in v2:
time: 336 us; the launch traced here: 335 us
  Pallas kernels  117 us (35%)
  waiting for transfers between devices  104 us (31%)
  local copies, waits for them, and re-layouts  50.5 us (15%)
  starting transfers between devices  41.2 us (12%)
  other arithmetic  21.6 us (6%)
    ppermute x33, waiting for transfers between devices, swap(): lax.ppermute(values, ('dp', 'enc'), [(i, i ^ bit) for i in range(count)])  89.9 us
    pallas_call x1, Pallas kernels, forward(): pl.pallas_call(kernel, grid_spec=pltpu.PrefetchScalarGridSpec(num_scalar_...  45.1 us
    ppermute x33, starting transfers between devices, swap(): lax.ppermute(values, ('dp', 'enc'), [(i, i ^ bit) for i in range(count)])  28.8 us
    pallas_call x1, Pallas kernels, ffn_backward(): pl.pallas_call(kernel, grid_spec=pltpu.PrefetchScalarGridSpec(num_scalar_...  26.7 us
    pallas_call x1, Pallas kernels, attention_backward(): pl.pallas_call(kernel, grid_spec=pltpu.PrefetchScalarGridSpec(num_scalar_...  24.6 us
    unnamed x78, local copies, waits for them, and re-layouts  24.3 us
    all_to_all x1, waiting for transfers between devices, on_device(): lax.all_to_all(back_message, axes, split_axis=0, concat_axis=0, tiled=True)  12.9 us
    reshape x10, local copies, waits for them, and re-layouts, on_device(): row = lambda v: v.reshape(1, -1)  9.03 us
  transfers between devices with their start and end apart: 35, of which 19 were waited for; matrix products, arithmetic and copies ran while one was open for 13% of the time, Pallas kernels for 5%

profile of v2, /device:TPU:0, one launch (start us, length us, event | category | flops | bytes accessed | tf_op | source)
XLA Modules:
  0.0 334.8 jit_solution(16536854741536675388)
XLA Ops:
  2.7 1.9 copy-done.1
  7.9 2.7 region_forward.1
  12.9 7.4 %all-to-all-start = ((bf16[32,8,768]{2,1,0:T(8,128)(2,1)}), bf16[32,8,768]{2,1,0:T(8,128)(2,1)}, u32[]{:S(2)}, u32[]{:S(2)}) async-start(bf16[32,8,768]{2,1,0:T(8,128)(2,1)} %bitcast.91), calls=%async_computation | async-start | bytes 786432 | tf_op jit(solution)/shard_map/all_to_all | solution.py:831
  20.9 1.3 reshape.119.ob_ref
  22.2 1.3 reshape.121.as_ref
  24.8 1.3 reshape.124.fg_ref
  26.0 1.3 reshape.125.fs_ref
  28.4 2.3 text_qkv.1.tq_ref
  33.5 45.1 %forward.1 = (bf16[768,768]{1,0:T(8,128)(2,1)}, bf16[768,768]{1,0:T(8,128)(2,1)}, bf16[768,2304]{1,0:T(8,128)(2,1)}, bf16[36,256,256]{2,1,0:T(8,128)(2,1)}, bf16...) custom-call(s32[9]{0:T(128)} %pad_add_fusion.sc_ref, ...), custom_call_target="tpu_custom_call" | custom-call | tf_op jit(solution)/shard_map/forward/pallas_call | solution.py:289
  78.6 26.7 %ffn_backward.1 = (f32[768,768]{1,0:T(8,128)}, bf16[768,768]{1,0:T(8,128)(2,1)}, f32[8,768]{1,0:T(8,128)}, f32[8,3072]{1,0:T(8,128)}, bf16[768,1536]{1,0:T(8,128)(2,1)}, /*index=5*/bf16[768,1536]{1,0:T(8,128)(2,1)}) custom-call(s32[1]{0:T(128)} %bitcast.c_ref, bf16[768,768]{1,0:T(8,128)(2,1)} %get-tuple-element.58.df_ref, ...), custom_call_target="tpu_custom_call" | custom-call | tf_op jit(solution)/shard_map/ffn_backward/pallas_call | solution.py:433
  106.6 1.7 copy-done.10
  108.2 24.6 %attention_backward.1 = (bf16[768,2304]{1,0:T(8,128)(2,1)}, f32[384,768]{1,0:T(8,128)}, bf16[256,768]{1,0:T(8,128)(2,1)S(1)}, f32[8,768]{1,0:T(8,128)S(1)}) custom-call(s32[9]{0:T(128)S(1)} %copy-done.27, bf16[768,768]{1,0:T(8,128)(2,1)S(1)} %copy-done.5, f32[768,768]{1,0:T(8,128)S(1)} %copy-done.10, bf16[36,256,256]{2,1,0:T(8,128)(2,1)} %get-tuple-element.66.p_ref, ...), custom_call_target="tpu_custom_call" | custom-call | tf_op jit(solution)/shard_map/attention_backward/pallas_call | solution.py:543
  134.2 5.0 %all-to-all-start.1 = ((bf16[32,8,768]{2,1,0:T(8,128)(2,1)}), bf16[32,8,768]{2,1,0:T(8,128)(2,1)S(1)}, u32[]{:S(2)}, u32[]{:S(2)}) async-start(bf16[32,8,768]{2,1,0:T(8,128)(2,1)} %bitcast.92), calls=%async_computation.1 | async-start | bytes 786432 | tf_op jit(solution)/shard_map/all_to_all | solution.py:847
  139.3 12.9 %all-to-all-done.1 = bf16[32,8,768]{2,1,0:T(8,128)(2,1)S(1)} async-done(((bf16[32,8,768]{2,1,0:T(8,128)(2,1)}), bf16[32,8,768]{2,1,0:T(8,128)(2,1)S(1)}, u32[]{:S(2)}, u32[]{:S(2)}) %all-to-all-start.1) | async-done | bytes 393248 | tf_op jit(solution)/shard_map/all_to_all | solution.py:847
  156.1 6.7 %region_backward.1 = (bf16[2048,384]{1,0:T(8,128)(2,1)}, bf16[2048,384]{1,0:T(8,128)(2,1)S(1)}, f32[256,2048]{1,0:T(8,128)}, f32[4,256]{1,0:T(4,128)}, f32[8,768]{1,0:T(8,128)S(1)}) custom-call(s32[1]{0:T(128)} %bitcast.c_ref, bf16[256,768]{1,0:T(8,128)(2,1)S(1)} %bitcast.90, s32[1,256]{1,0:T(1,128)S(1)} %copy-done.30, f32[256,768]{1,0:T(8,128)S(1)} %copy-done.16, ...), custom_call_target="tpu_custom_call" | custom-call | tf_op jit(solution)/shard_map/region_backward/pallas_call | solution.py:671
  166.8 2.4 concatenate.31
  169.2 2.3 collective-permute-done
  172.2 4.2 %collective-permute-done.1 = f32[30,768]{1,0:T(8,128)S(1)} collective-permute-done((f32[30,768]{1,0:T(8,128)S(1)}, f32[30,768]{1,0:T(8,128)S(1)}, u32[]{:S(2)}, u32[]{:S(2)}) %collective-permute-start.1) | collective-permute-done | bytes 92192 | tf_op jit(solution)/shard_map/ppermute | solution.py:715
  177.5 3.6 %collective-permute-done.2 = f32[30,768]{1,0:T(8,128)S(1)} collective-permute-done((f32[30,768]{1,0:T(8,128)S(1)}, f32[30,768]{1,0:T(8,128)S(1)}, u32[]{:S(2)}, u32[]{:S(2)}) %collective-permute-start.2) | collective-permute-done | bytes 92192 | tf_op jit(solution)/shard_map/ppermute | solution.py:715
  182.2 3.6 %collective-permute-done.3 = f32[30,768]{1,0:T(8,128)S(1)} collective-permute-done((f32[30,768]{1,0:T(8,128)S(1)}, f32[30,768]{1,0:T(8,128)S(1)}, u32[]{:S(2)}, u32[]{:S(2)}) %collective-permute-start.3) | collective-permute-done | bytes 92192 | tf_op jit(solution)/shard_map/ppermute | solution.py:715
  187.4 2.0 copy-done.9
  189.4 1.3 copy-done.13
  190.7 1.3 copy-done.14
  192.0 8.6 %qkvo_gradient.1 = (bf16[768,1536]{1,0:T(8,128)(2,1)}, bf16[768,1536]{1,0:T(8,128)(2,1)S(1)}) custom-call(s32[1]{0:T(128)} %bitcast.c_ref, bf16[768,768]{1,0:T(8,128)(2,1)S(1)} %copy-done.13, bf16[768,2304]{1,0:T(8,128)(2,1)S(1)} %copy-done.9, bf16[768,768]{1,0:T(8,128)(2,1)S(1)} %copy-done.14, bf16[768,768]{1,0:T(8,128)(2,1)S(1)} %copy-done.6), custom_call_target="tpu_custom_call" | custom-call | tf_op jit(solution)/shard_map/qkvo_gradient/pallas_call | solution.py:610
  202.8 2.3 add.199
  210.8 2.3 add.227
  218.1 1.3 dynamic_slice.200
  220.1 3.1 add.221
  223.1 4.3 %collective-permute-done.6 = bf16[2,2,2,128,384]{4,3,1,0,2:T(8,128)(2,1)} collective-permute-done((bf16[2,2,2,128,384]{4,3,1,0,2:T(8,128)(2,1)}, bf16[2,2,2,128,384]{4,3,1,0,2:T(8,128)(2,1)}, u32[]{:S(2)}, u32[]{:S(2)}) %collective-permute-start.6) | collective-permute-done | bytes 786464 | tf_op jit(solution)/shard_map/ppermute | solution.py:715
  230.1 2.3 add.213
  233.7 18.2 %collective-permute-done.7 = bf16[2,2,128,384]{3,2,1,0:T(8,128)(2,1)S(1)} collective-permute-done((bf16[2,2,128,384]{3,2,1,0:T(8,128)(2,1)S(1)}, bf16[2,2,128,384]{3,2,1,0:T(8,128)(2,1)S(1)}, u32[]{:S(2)}, u32[]{:S(2)}) %collective-permute-start.7) | collective-permute-done | bytes 393248 | tf_op jit(solution)/shard_map/ppermute | solution.py:715
  252.0 1.7 collective-permute-start.8
  253.7 1.4 bitcast_add_fusion
  256.3 1.7 collective-permute-done.8
  258.1 2.7 collective-permute-start.9
  260.9 3.8 %collective-permute-done.9 = bf16[128,384]{1,0:T(8,128)(2,1)S(1)} collective-permute-done((bf16[128,384]{1,0:T(8,128)(2,1)S(1)}, bf16[128,384]{1,0:T(8,128)(2,1)S(1)}, u32[]{:S(2)}, u32[]{:S(2)}) %collective-permute-start.9) | collective-permute-done | bytes 98336 | tf_op jit(solution)/shard_map/ppermute | solution.py:715
  264.9 2.1 collective-permute-start.21
  267.0 12.3 %collective-permute-done.10 = bf16[128,384]{1,0:T(8,128)(2,1)S(1)} collective-permute-done((bf16[128,384]{1,0:T(8,128)(2,1)S(1)}, bf16[128,384]{1,0:T(8,128)(2,1)S(1)}, u32[]{:S(2)}, u32[]{:S(2)}) %collective-permute-start.10) | collective-permute-done | bytes 98336 | tf_op jit(solution)/shard_map/ppermute | solution.py:715
  279.8 2.1 collective-permute-start.14
  283.8 7.7 %collective-permute-done.21 = bf16[2,2,96,768]{3,2,1,0:T(8,128)(2,1)S(1)} collective-permute-done((bf16[2,2,96,768]{3,2,1,0:T(8,128)(2,1)S(1)}, bf16[2,2,96,768]{3,2,1,0:T(8,128)(2,1)S(1)}, u32[]{:S(2)}, u32[]{:S(2)}) %collective-permute-start.21) | collective-permute-done | bytes 589856 | tf_op jit(solution)/shard_map/ppermute | solution.py:715
  291.7 1.5 collective-permute-start.22
  293.1 2.7 collective-permute-done.14
  295.9 1.5 collective-permute-start.15
  297.5 2.1 collective-permute-start.30
  299.5 6.8 %collective-permute-done.22 = bf16[2,96,768]{2,1,0:T(8,128)(2,1)S(1)} collective-permute-done((bf16[2,96,768]{2,1,0:T(8,128)(2,1)S(1)}, bf16[2,96,768]{2,1,0:T(8,128)(2,1)S(1)}, u32[]{:S(2)}, u32[]{:S(2)}) %collective-permute-start.22) | collective-permute-done | bytes 294944 | tf_op jit(solution)/shard_map/ppermute | solution.py:715
  307.5 3.9 %collective-permute-done.15 = bf16[2,96,768]{2,1,0:T(8,128)(2,1)S(1)} collective-permute-done((bf16[2,96,768]{2,1,0:T(8,128)(2,1)S(1)}, bf16[2,96,768]{2,1,0:T(8,128)(2,1)S(1)}, u32[]{:S(2)}, u32[]{:S(2)}) %collective-permute-start.15) | collective-permute-done | bytes 294944 | tf_op jit(solution)/shard_map/ppermute | solution.py:715
  312.8 8.2 %collective-permute-done.23 = bf16[96,768]{1,0:T(8,128)(2,1)S(1)} collective-permute-done((bf16[96,768]{1,0:T(8,128)(2,1)S(1)}, bf16[96,768]{1,0:T(8,128)(2,1)S(1)}, u32[]{:S(2)}, u32[]{:S(2)}) %collective-permute-start.23) | collective-permute-done | bytes 147488 | tf_op jit(solution)/shard_map/ppermute | solution.py:715
  323.9 4.8 %collective-permute-done.17 = bf16[96,768]{1,0:T(8,128)(2,1)S(1)} collective-permute-done((bf16[96,768]{1,0:T(8,128)(2,1)S(1)}, bf16[96,768]{1,0:T(8,128)(2,1)S(1)}, u32[]{:S(2)}, u32[]{:S(2)}) %collective-permute-start.17) | collective-permute-done | bytes 147488 | tf_op jit(solution)/shard_map/ppermute | solution.py:715
  (198 shorter events, 61.8 us)
Async XLA Ops:
  7.9 12.4 %copy-start.34 = (f32[1536]{0:T(1024)S(1)}, f32[1536]{0:T(1024)}, u32[]{:S(2)}) copy-start(f32[1536]{0:T(1024)} %param.40) | copy-start | bytes 18436
  7.9 12.4 %copy-start.35 = (f32[768]{0:T(1024)S(1)}, f32[768]{0:T(1024)}, u32[]{:S(2)}) copy-start(f32[768]{0:T(1024)} %param.43) | copy-start | bytes 9220
  7.9 19.4 %copy-start = (bf16[768,2304]{1,0:T(8,128)(2,1)S(1)}, bf16[768,2304]{1,0:T(8,128)(2,1)}, u32[]{:S(2)}) copy-start(bf16[768,2304]{1,0:T(8,128)(2,1)} %wq_hbm.3) | copy-start | bytes 10616836
  12.9 20.6 %all-to-all-start = ((bf16[32,8,768]{2,1,0:T(8,128)(2,1)}), bf16[32,8,768]{2,1,0:T(8,128)(2,1)}, u32[]{:S(2)}, u32[]{:S(2)}) async-start(bf16[32,8,768]{2,1,0:T(8,128)(2,1)} %bitcast.91), calls=%async_computation | async-start | bytes 786432 | tf_op jit(solution)/shard_map/all_to_all | solution.py:831
  20.3 10.3 %copy-start.21 = (f32[1,1536]{1,0:T(1,128)}, f32[1,1536]{1,0:T(1,128)S(1)}, u32[]{:S(2)}) copy-start(f32[1,1536]{1,0:T(1,128)S(1)} %reshape.115.b_ref.qvb_ref) | copy-start | bytes 18436
  78.6 26.7 %copy-start.4 = (bf16[768,768]{1,0:T(8,128)(2,1)S(1)}, bf16[768,768]{1,0:T(8,128)(2,1)}, u32[]{:S(2)}) copy-start(bf16[768,768]{1,0:T(8,128)(2,1)} %wo_ref.1) | copy-start | bytes 3538948
  78.6 26.7 %copy-start.27 = (s32[9]{0:T(128)S(1)}, s32[9]{0:T(128)}, u32[]{:S(2)}) copy-start(s32[9]{0:T(128)} %pad_add_fusion.sc_ref) | copy-start | bytes 112
  78.6 26.7 %copy-start.28 = (s32[1,256]{1,0:T(1,128)S(1)}, s32[1,256]{1,0:T(1,128)}, u32[]{:S(2)}) copy-start(s32[1,256]{1,0:T(1,128)} %src_ref.3) | copy-start | bytes 3076
  108.2 43.9 %copy-start.2 = (bf16[2048,768]{1,0:T(8,128)(2,1)S(1)}, bf16[2048,768]{1,0:T(8,128)(2,1)}, u32[]{:S(2)}) copy-start(bf16[2048,768]{1,0:T(8,128)(2,1)} %wv_ref.3) | copy-start | bytes 9437188
  108.2 43.9 %copy-start.24 = (bf16[768,4]{0,1:T(4,128)(2,1)S(1)}, bf16[768,4]{0,1:T(4,128)(2,1)}, u32[]{:S(2)}) copy-start(bf16[768,4]{0,1:T(4,128)(2,1)} %param.35) | copy-start | bytes 18436
  108.2 43.9 %copy-start.26 = (bf16[4,256]{1,0:T(4,128)(2,1)S(1)}, bf16[4,256]{1,0:T(4,128)(2,1)}, u32[]{:S(2)}) copy-start(bf16[4,256]{1,0:T(4,128)(2,1)} %box_ref.3) | copy-start | bytes 6148
  134.2 18.0 %all-to-all-start.1 = ((bf16[32,8,768]{2,1,0:T(8,128)(2,1)}), bf16[32,8,768]{2,1,0:T(8,128)(2,1)S(1)}, u32[]{:S(2)}, u32[]{:S(2)}) async-start(bf16[32,8,768]{2,1,0:T(8,128)(2,1)} %bitcast.92), calls=%async_computation.1 | async-start | bytes 786432 | tf_op jit(solution)/shard_map/all_to_all | solution.py:847
  139.2 71.6 %collective-permute-start.26 = (bf16[3072,384]{1,0:T(8,128)(2,1)}, bf16[3072,384]{1,0:T(8,128)(2,1)}, u32[]{:S(2)}, u32[]{:S(2)}) collective-permute-start(bf16[3072,384]{1,0:T(8,128)(2,1)} %get-tuple-element.89), channel_id=1, source_target_pairs={{0,1},{1,0},{2,3},{3,2},{4,5},{5,4},{6,7},{7,6},{8,9},{9,8},{10,11... | collective-permute-start | bytes 7077896 | tf_op jit(solution)/shard_map/ppermute | solution.py:715
  164.6 22.8 %copy-start.6 = (bf16[768,768]{1,0:T(8,128)(2,1)S(1)}, bf16[768,768]{1,0:T(8,128)(2,1)}, u32[]{:S(2)}) copy-start(bf16[768,768]{1,0:T(8,128)(2,1)} %get-tuple-element.64.da_ref) | copy-start | bytes 3538948
  164.6 38.2 %collective-permute-start.5 = (bf16[2048,384]{1,0:T(8,128)(2,1)}, bf16[2048,384]{1,0:T(8,128)(2,1)}, u32[]{:S(2)}, u32[]{:S(2)}) collective-permute-start(bf16[2048,384]{1,0:T(8,128)(2,1)} %get-tuple-element.80), channel_id=1, source_target_pairs={{0,1},{1,0},{2,3},{3,2},{4,5},{5,4},{6,7},{7,6},{8,9},{9,8},{10,11... | collective-permute-start | bytes 4718600 | tf_op jit(solution)/shard_map/ppermute | solution.py:715
  164.6 55.5 %collective-permute-start.19 = (bf16[768,1536]{1,0:T(8,128)(2,1)}, bf16[768,1536]{1,0:T(8,128)(2,1)}, u32[]{:S(2)}, u32[]{:S(2)}) collective-permute-start(bf16[768,1536]{1,0:T(8,128)(2,1)} %get-tuple-element.87), channel_id=1, source_target_pairs={{0,1},{1,0},{2,3},{3,2},{4,5},{5,4},{6,7},{7,6},{8,9},{9,8},{10,11... | collective-permute-start | bytes 7077896 | tf_op jit(solution)/shard_map/ppermute | solution.py:715
  169.2 2.4 collective-permute-start
  171.5 4.9 %collective-permute-start.1 = (f32[30,768]{1,0:T(8,128)S(1)}, f32[30,768]{1,0:T(8,128)S(1)}, u32[]{:S(2)}, u32[]{:S(2)}) collective-permute-start(f32[30,768]{1,0:T(8,128)S(1)} %add.194), channel_id=1, source_target_pairs={{0,2},{1,3},{2,0},{3,1},{4,6},{5,7},{6,4},{7,5},{8,10},{9,11},{10,... | collective-permute-start | bytes 276488 | tf_op jit(solution)/shard_map/ppermute | solution.py:715
  176.5 4.7 %collective-permute-start.2 = (f32[30,768]{1,0:T(8,128)S(1)}, f32[30,768]{1,0:T(8,128)S(1)}, u32[]{:S(2)}, u32[]{:S(2)}) collective-permute-start(f32[30,768]{1,0:T(8,128)S(1)} %add.195), channel_id=1, source_target_pairs={{0,4},{1,5},{2,6},{3,7},{4,0},{5,1},{6,2},{7,3},{8,12},{9,13},{10,... | collective-permute-start | bytes 276488 | tf_op jit(solution)/shard_map/ppermute | solution.py:715
  181.2 4.7 %collective-permute-start.3 = (f32[30,768]{1,0:T(8,128)S(1)}, f32[30,768]{1,0:T(8,128)S(1)}, u32[]{:S(2)}, u32[]{:S(2)}) collective-permute-start(f32[30,768]{1,0:T(8,128)S(1)} %add.196), channel_id=1, source_target_pairs={{0,8},{1,9},{2,10},{3,11},{4,12},{5,13},{6,14},{7,15},{8,0},{9,1},... | collective-permute-start | bytes 276488 | tf_op jit(solution)/shard_map/ppermute | solution.py:715
  186.5 14.0 %collective-permute-start.4 = (f32[30,768]{1,0:T(8,128)}, f32[30,768]{1,0:T(8,128)}, u32[]{:S(2)}, u32[]{:S(2)}) collective-permute-start(f32[30,768]{1,0:T(8,128)} %add.197), channel_id=1, source_target_pairs={{0,16},{1,17},{2,18},{3,19},{4,20},{5,21},{6,22},{7,23},{8,24},{9,... | collective-permute-start | bytes 276488 | tf_op jit(solution)/shard_map/ppermute | solution.py:715
  200.5 29.6 %collective-permute-start.12 = (bf16[768,1536]{1,0:T(8,128)(2,1)}, bf16[768,1536]{1,0:T(8,128)(2,1)}, u32[]{:S(2)}, u32[]{:S(2)}) collective-permute-start(bf16[768,1536]{1,0:T(8,128)(2,1)} %get-tuple-element.85), channel_id=1, source_target_pairs={{0,1},{1,0},{2,3},{3,2},{4,5},{5,4},{6,7},{7,6},{8,9},{9,8},{10,11... | collective-permute-start | bytes 7077896 | tf_op jit(solution)/shard_map/ppermute | solution.py:715
  205.1 5.7 %copy-start.33 = (bf16[3072,384]{1,0:T(8,128)(2,1)S(1)}, bf16[3072,384]{1,0:T(8,128)(2,1)}, u32[]{:S(2)}) copy-start(bf16[3072,384]{1,0:T(8,128)(2,1)} %get-tuple-element.88) | copy-start | bytes 7077892
  207.2 20.3 %collective-permute-start.6 = (bf16[2,2,2,128,384]{4,3,1,0,2:T(8,128)(2,1)}, bf16[2,2,2,128,384]{4,3,1,0,2:T(8,128)(2,1)}, u32[]{:S(2)}, u32[]{:S(2)}) collective-permute-start(bf16[2,2,2,128,384]{4,3,1,0,2:T(8,128)(2,1)} %bitcast.89), channel_id=1, source_target_pairs={{0,4},{1,5},{2,6},{3,7},{4,0},{5,1},{6,2},{7,3},{8,12},{9,13},{10,... | collective-permute-start | bytes 2359304 | tf_op jit(solution)/shard_map/ppermute | solution.py:715
  214.5 39.2 %collective-permute-start.27 = (bf16[2,2,2,192,384]{4,3,1,0,2:T(8,128)(2,1)}, bf16[2,2,2,192,384]{4,3,1,0,2:T(8,128)(2,1)}, u32[]{:S(2)}, u32[]{:S(2)}) collective-permute-start(bf16[2,2,2,192,384]{4,3,1,0,2:T(8,128)(2,1)} %bitcast.88), channel_id=1, source_target_pairs={{0,2},{1,3},{2,0},{3,1},{4,6},{5,7},{6,4},{7,5},{8,10},{9,11},{10,... | collective-permute-start | bytes 3538952 | tf_op jit(solution)/shard_map/ppermute | solution.py:715
  220.1 7.4 %copy-start.32 = (bf16[2,2,1,2,128,384]{5,4,3,2,1,0:T(8,128)(2,1)S(1)}, bf16[2,2,1,2,128,384]{5,4,3,2,1,0:T(8,128)(2,1)}, u32[]{:S(2)}) copy-start(bf16[2,2,1,2,128,384]{5,4,3,2,1,0:T(8,128)(2,1)} %get-tuple-element.92) | copy-start | bytes 2359300
  228.7 23.2 %collective-permute-start.7 = (bf16[2,2,128,384]{3,2,1,0:T(8,128)(2,1)S(1)}, bf16[2,2,128,384]{3,2,1,0:T(8,128)(2,1)S(1)}, u32[]{:S(2)}, u32[]{:S(2)}) collective-permute-start(bf16[2,2,128,384]{3,2,1,0:T(8,128)(2,1)S(1)} %dynamic-slice_bitcast_fusion.3), channel_id=1, source_target_pairs={{0,2},{1,3},{2,0},{3,1},{4,6},{5,7},{6,4},{7,5},{8,10},{9,11},{10,... | collective-permute-start | bytes 1179656 | tf_op jit(solution)/shard_map/ppermute | solution.py:715
  229.5 31.3 %collective-permute-start.20 = (bf16[2,2,96,1536]{3,2,1,0:T(8,128)(2,1)S(1)}, bf16[2,2,96,1536]{3,2,1,0:T(8,128)(2,1)S(1)}, u32[]{:S(2)}, u32[]{:S(2)}) collective-permute-start(bf16[2,2,96,1536]{3,2,1,0:T(8,128)(2,1)S(1)} %dynamic-slice_bitcast_fusion), channel_id=1, source_target_pairs={{0,4},{1,5},{2,6},{3,7},{4,0},{5,1},{6,2},{7,3},{8,12},{9,13},{10,... | collective-permute-start | bytes 3538952 | tf_op jit(solution)/shard_map/ppermute | solution.py:715
  232.5 46.9 %collective-permute-start.13 = (bf16[768,768]{1,0:T(8,128)(2,1)S(1)}, bf16[768,768]{1,0:T(8,128)(2,1)S(1)}, u32[]{:S(2)}, u32[]{:S(2)}) collective-permute-start(bf16[768,768]{1,0:T(8,128)(2,1)S(1)} %constant_dynamic-slice_fusion.9), channel_id=1, source_target_pairs={{0,2},{1,3},{2,0},{3,1},{4,6},{5,7},{6,4},{7,5},{8,10},{9,11},{10,... | collective-permute-start | bytes 3538952 | tf_op jit(solution)/shard_map/ppermute | solution.py:715
  252.0 6.1 %collective-permute-start.8 = (bf16[2,128,384]{2,1,0:T(8,128)(2,1)S(1)}, bf16[2,128,384]{2,1,0:T(8,128)(2,1)S(1)}, u32[]{:S(2)}, u32[]{:S(2)}) collective-permute-start(bf16[2,128,384]{2,1,0:T(8,128)(2,1)S(1)} %dynamic-slice_bitcast_fusion.7), channel_id=1, source_target_pairs={{0,8},{1,9},{2,10},{3,11},{4,12},{5,13},{6,14},{7,15},{8,0},{9,1},... | collective-permute-start | bytes 589832 | tf_op jit(solution)/shard_map/ppermute | solution.py:715
  255.2 27.7 %collective-permute-start.28 = (bf16[2,2,192,384]{3,2,1,0:T(8,128)(2,1)S(1)}, bf16[2,2,192,384]{3,2,1,0:T(8,128)(2,1)S(1)}, u32[]{:S(2)}, u32[]{:S(2)}) collective-permute-start(bf16[2,2,192,384]{3,2,1,0:T(8,128)(2,1)S(1)} %dynamic-slice_bitcast_fusion.1), channel_id=1, source_target_pairs={{0,4},{1,5},{2,6},{3,7},{4,0},{5,1},{6,2},{7,3},{8,12},{9,13},{10,... | collective-permute-start | bytes 1769480 | tf_op jit(solution)/shard_map/ppermute | solution.py:715
  258.1 6.6 %collective-permute-start.9 = (bf16[128,384]{1,0:T(8,128)(2,1)S(1)}, bf16[128,384]{1,0:T(8,128)(2,1)S(1)}, u32[]{:S(2)}, u32[]{:S(2)}) collective-permute-start(bf16[128,384]{1,0:T(8,128)(2,1)S(1)} %dynamic-slice_bitcast_fusion.11), channel_id=1, source_target_pairs={{0,16},{1,17},{2,18},{3,19},{4,20},{5,21},{6,22},{7,23},{8,24},{9,... | collective-permute-start | bytes 294920 | tf_op jit(solution)/shard_map/ppermute | solution.py:715
  264.8 14.5 %collective-permute-start.10 = (bf16[128,384]{1,0:T(8,128)(2,1)S(1)}, bf16[128,384]{1,0:T(8,128)(2,1)S(1)}, u32[]{:S(2)}, u32[]{:S(2)}) collective-permute-start(bf16[128,384]{1,0:T(8,128)(2,1)S(1)} %bitcast_add_fusion.13), channel_id=1, source_target_pairs={{0,2},{1,3},{2,0},{3,1},{4,6},{5,7},{6,4},{7,5},{8,10},{9,11},{10,... | collective-permute-start | bytes 294920 | tf_op jit(solution)/shard_map/ppermute | solution.py:715
  264.9 26.6 %collective-permute-start.21 = (bf16[2,2,96,768]{3,2,1,0:T(8,128)(2,1)S(1)}, bf16[2,2,96,768]{3,2,1,0:T(8,128)(2,1)S(1)}, u32[]{:S(2)}, u32[]{:S(2)}) collective-permute-start(bf16[2,2,96,768]{3,2,1,0:T(8,128)(2,1)S(1)} %constant_dynamic-slice_fusion.5), channel_id=1, source_target_pairs={{0,2},{1,3},{2,0},{3,1},{4,6},{5,7},{6,4},{7,5},{8,10},{9,11},{10,... | collective-permute-start | bytes 1769480 | tf_op jit(solution)/shard_map/ppermute | solution.py:715
  279.3 2.5 collective-permute-start.11
  279.8 16.0 %collective-permute-start.14 = (bf16[2,2,96,768]{3,2,1,0:T(8,128)(2,1)S(1)}, bf16[2,2,96,768]{3,2,1,0:T(8,128)(2,1)S(1)}, u32[]{:S(2)}, u32[]{:S(2)}) collective-permute-start(bf16[2,2,96,768]{3,2,1,0:T(8,128)(2,1)S(1)} %dynamic-slice_bitcast_fusion.2), channel_id=1, source_target_pairs={{0,4},{1,5},{2,6},{3,7},{4,0},{5,1},{6,2},{7,3},{8,12},{9,13},{10,... | collective-permute-start | bytes 1769480 | tf_op jit(solution)/shard_map/ppermute | solution.py:715
  283.0 14.4 %collective-permute-start.29 = (bf16[2,192,384]{2,1,0:T(8,128)(2,1)S(1)}, bf16[2,192,384]{2,1,0:T(8,128)(2,1)S(1)}, u32[]{:S(2)}, u32[]{:S(2)}) collective-permute-start(bf16[2,192,384]{2,1,0:T(8,128)(2,1)S(1)} %dynamic-slice_bitcast_fusion.4), channel_id=1, source_target_pairs={{0,8},{1,9},{2,10},{3,11},{4,12},{5,13},{6,14},{7,15},{8,0},{9,1},... | collective-permute-start | bytes 884744 | tf_op jit(solution)/shard_map/ppermute | solution.py:715
  291.7 14.7 %collective-permute-start.22 = (bf16[2,96,768]{2,1,0:T(8,128)(2,1)S(1)}, bf16[2,96,768]{2,1,0:T(8,128)(2,1)S(1)}, u32[]{:S(2)}, u32[]{:S(2)}) collective-permute-start(bf16[2,96,768]{2,1,0:T(8,128)(2,1)S(1)} %dynamic-slice_bitcast_fusion.5), channel_id=1, source_target_pairs={{0,8},{1,9},{2,10},{3,11},{4,12},{5,13},{6,14},{7,15},{8,0},{9,1},... | collective-permute-start | bytes 884744 | tf_op jit(solution)/shard_map/ppermute | solution.py:715
  295.9 15.5 %collective-permute-start.15 = (bf16[2,96,768]{2,1,0:T(8,128)(2,1)S(1)}, bf16[2,96,768]{2,1,0:T(8,128)(2,1)S(1)}, u32[]{:S(2)}, u32[]{:S(2)}) collective-permute-start(bf16[2,96,768]{2,1,0:T(8,128)(2,1)S(1)} %dynamic-slice_bitcast_fusion.6), channel_id=1, source_target_pairs={{0,8},{1,9},{2,10},{3,11},{4,12},{5,13},{6,14},{7,15},{8,0},{9,1},... | collective-permute-start | bytes 884744 | tf_op jit(solution)/shard_map/ppermute | solution.py:715
  297.5 14.7 %collective-permute-start.30 = (bf16[192,384]{1,0:T(8,128)(2,1)S(1)}, bf16[192,384]{1,0:T(8,128)(2,1)S(1)}, u32[]{:S(2)}, u32[]{:S(2)}) collective-permute-start(bf16[192,384]{1,0:T(8,128)(2,1)S(1)} %dynamic-slice_bitcast_fusion.8), channel_id=1, source_target_pairs={{0,16},{1,17},{2,18},{3,19},{4,20},{5,21},{6,22},{7,23},{8,24},{9,... | collective-permute-start | bytes 442376 | tf_op jit(solution)/shard_map/ppermute | solution.py:715
  306.4 14.6 %collective-permute-start.23 = (bf16[96,768]{1,0:T(8,128)(2,1)S(1)}, bf16[96,768]{1,0:T(8,128)(2,1)S(1)}, u32[]{:S(2)}, u32[]{:S(2)}) collective-permute-start(bf16[96,768]{1,0:T(8,128)(2,1)S(1)} %dynamic-slice_bitcast_fusion.9), channel_id=1, source_target_pairs={{0,16},{1,17},{2,18},{3,19},{4,20},{5,21},{6,22},{7,23},{8,24},{9,... | collective-permute-start | bytes 442376 | tf_op jit(solution)/shard_map/ppermute | solution.py:715
  311.5 11.3 %collective-permute-start.16 = (bf16[96,768]{1,0:T(8,128)(2,1)S(1)}, bf16[96,768]{1,0:T(8,128)(2,1)S(1)}, u32[]{:S(2)}, u32[]{:S(2)}) collective-permute-start(bf16[96,768]{1,0:T(8,128)(2,1)S(1)} %dynamic-slice_bitcast_fusion.10), channel_id=1, source_target_pairs={{0,16},{1,17},{2,18},{3,19},{4,20},{5,21},{6,22},{7,23},{8,24},{9,... | collective-permute-start | bytes 442376 | tf_op jit(solution)/shard_map/ppermute | solution.py:715
  312.2 11.6 %collective-permute-start.31 = (bf16[192,384]{1,0:T(8,128)(2,1)S(1)}, bf16[192,384]{1,0:T(8,128)(2,1)S(1)}, u32[]{:S(2)}, u32[]{:S(2)}) collective-permute-start(bf16[192,384]{1,0:T(8,128)(2,1)S(1)} %bitcast_add_fusion.10), channel_id=1, source_target_pairs={{0,2},{1,3},{2,0},{3,1},{4,6},{5,7},{6,4},{7,5},{8,10},{9,11},{10,... | collective-permute-start | bytes 442376 | tf_op jit(solution)/shard_map/ppermute | solution.py:715
  321.1 7.8 %collective-permute-start.24 = (bf16[96,768]{1,0:T(8,128)(2,1)S(1)}, bf16[96,768]{1,0:T(8,128)(2,1)S(1)}, u32[]{:S(2)}, u32[]{:S(2)}) collective-permute-start(bf16[96,768]{1,0:T(8,128)(2,1)S(1)} %bitcast_add_fusion.11), channel_id=1, source_target_pairs={{0,2},{1,3},{2,0},{3,1},{4,6},{5,7},{6,4},{7,5},{8,10},{9,11},{10,... | collective-permute-start | bytes 442376 | tf_op jit(solution)/shard_map/ppermute | solution.py:715
  322.7 6.0 %collective-permute-start.17 = (bf16[96,768]{1,0:T(8,128)(2,1)S(1)}, bf16[96,768]{1,0:T(8,128)(2,1)S(1)}, u32[]{:S(2)}, u32[]{:S(2)}) collective-permute-start(bf16[96,768]{1,0:T(8,128)(2,1)S(1)} %bitcast_add_fusion.12), channel_id=1, source_target_pairs={{0,2},{1,3},{2,0},{3,1},{4,6},{5,7},{6,4},{7,5},{8,10},{9,11},{10,... | collective-permute-start | bytes 442376 | tf_op jit(solution)/shard_map/ppermute | solution.py:715
  323.9 6.8 %collective-permute-start.32 = (bf16[384,384]{1,0:T(8,128)(2,1)S(1)}, bf16[384,384]{1,0:T(8,128)(2,1)S(1)}, u32[]{:S(2)}, u32[]{:S(2)}) collective-permute-start(bf16[384,384]{1,0:T(8,128)(2,1)S(1)} %pad_maximum_fusion.2), channel_id=1, source_target_pairs={{0,1},{1,0},{2,3},{3,2},{4,5},{5,4},{6,7},{7,6},{8,9},{9,8},{10,11... | collective-permute-start | bytes 884744 | tf_op jit(solution)/shard_map/ppermute | solution.py:715
  328.8 1.6 collective-permute-start.18
  329.0 4.6 %collective-permute-start.25 = (bf16[96,1536]{1,0:T(8,128)(2,1)S(1)}, bf16[96,1536]{1,0:T(8,128)(2,1)S(1)}, u32[]{:S(2)}, u32[]{:S(2)}) collective-permute-start(bf16[96,1536]{1,0:T(8,128)(2,1)S(1)} %pad_maximum_fusion.1), channel_id=1, source_target_pairs={{0,1},{1,0},{2,3},{3,2},{4,5},{5,4},{6,7},{7,6},{8,9},{9,8},{10,11... | collective-permute-start | bytes 884744 | tf_op jit(solution)/shard_map/ppermute | solution.py:715
  (26 other events, 34.9 us)

commit v3 on v2

v3 whole, which is shorter than its diff:
```python
import jax
import jax.numpy as jnp
from jax import lax
from jax.experimental import pallas as pl
from jax.experimental.pallas import tpu as pltpu
from jax.sharding import PartitionSpec as P

HEADS = 12
HEAD = 64
epsilon = 1e-12
inv_sqrt_two = 0.7071067811865476
inv_sqrt_tau = 0.3989422804014327
f32 = jnp.float32
bf16 = jnp.bfloat16
NN = (((1,), (0,)), ((), ()))
NT = (((1,), (1,)), ((), ()))
TN = (((0,), (0,)), ((), ()))


def mm(a, b, dims=NN):
    return lax.dot_general(a, b, dims, preferred_element_type=f32)


def params(limit=56):
    return pltpu.CompilerParams(
        dimension_semantics=("arbitrary",), vmem_limit_bytes=limit << 20
    )


def whole(shape):
    return pl.BlockSpec(shape, lambda i, *s: (0,) * len(shape), pipeline_mode=pl.Buffered(1))


def vec(size):
    return pl.BlockSpec((size,), lambda i, *s: (0,))


def shape(dims, kind=f32):
    return jax.ShapeDtypeStruct(dims, kind)


def norm_parts(values):
    centre = values - jnp.mean(values, -1, keepdims=True)
    inv_std = lax.rsqrt(jnp.mean(centre * centre, -1, keepdims=True) + epsilon)
    return centre * inv_std, inv_std


def norm_back(grad, normed, inv_std, gain):
    scaled = grad * gain
    return inv_std * (
        scaled
        - jnp.mean(scaled, -1, keepdims=True)
        - normed * jnp.mean(scaled * normed, -1, keepdims=True)
    )


def row_sum(values):
    return jnp.sum(values, 0, keepdims=True)


def one_hot(index_row, count):
    rows = lax.broadcasted_iota(jnp.int32, (count, index_row.shape[1]), 0)
    return jnp.where(rows == index_row, 1.0, 0.0).astype(bf16)


def region_forward(features, boxes, target, w_visual, w_box_t, bias, gain, shift):
    rows, feat = features.shape
    width = w_visual.shape[1]
    steps = 4
    part = feat // steps

    def kernel(f_ref, box_ref, t_ref, wv_ref, wb_ref, b_ref, g_ref, s_ref, m_ref, n_ref, i_ref, acc):
        step = pl.program_id(0)
        partial = mm(f_ref[...], wv_ref[...])

        @pl.when(step == 0)
        def _():
            acc[...] = partial + (mm(box_ref[...], wb_ref[...], TN) + b_ref[...])

        @pl.when(step > 0)
        def _():
            acc[...] += partial

        @pl.when(step == steps - 1)
        def _():
            normed, inv = norm_parts(acc[...])
            n_ref[...] = normed
            i_ref[...] = jnp.broadcast_to(inv, i_ref.shape)
            low = (normed * g_ref[...] + s_ref[...]).astype(bf16)
            m_ref[...] = mm(one_hot(t_ref[...], rows), low).astype(bf16)

    return pl.pallas_call(
        kernel,
        grid=(steps,),
        in_specs=[
            pl.BlockSpec((rows, part), lambda i: (0, i)),
            whole(boxes.shape),
            whole((1, rows)),
            pl.BlockSpec((part, width), lambda i: (i, 0)),
            whole(w_box_t.shape),
            vec(width),
            vec(width),
            vec(width),
        ],
        out_specs=[whole((rows, width)), whole((rows, width)), whole((rows, 128))],
        out_shape=[shape((rows, width), bf16), shape((rows, width)), shape((rows, 128))],
        scratch_shapes=[pltpu.VMEM((rows, width), f32)],
        compiler_params=params(24),
        name="region_forward",
    )(features, boxes, target, w_visual, w_box_t, bias, gain, shift)


def text_qkv(text, w_qkv, qv_bias):
    rows, width = text.shape

    def kernel(t_ref, w_ref, b_ref, o_ref):
        step = pl.program_id(0)
        bias = b_ref[...] * jnp.where(step == 1, 0.0, 1.0)
        o_ref[...] = (mm(t_ref[...], w_ref[...]) + bias).astype(bf16)

    return pl.pallas_call(
        kernel,
        grid=(3,),
        in_specs=[
            whole((rows, width)),
            pl.BlockSpec((width, width), lambda i: (0, i)),
            pl.BlockSpec((1, width), lambda i: (0, i // 2)),
        ],
        out_specs=pl.BlockSpec((rows, width), lambda i: (0, i)),
        out_shape=shape((rows, 3 * width), bf16),
        compiler_params=params(24),
        name="text_qkv",
    )(text, w_qkv, qv_bias)


def forward(
    scalars, text, text_low, arrived, source, out_grad, w_qkv, qv_bias, w_out, out_bias,
    attn_gain, attn_shift, w_up, up_bias, w_down, down_bias, ffn_gain, ffn_shift, dims,
):
    captions, images = dims
    width = text.shape[1]
    text_len = text.shape[0] // captions
    slots = arrived.shape[0]
    regions = slots // images
    seq = text_len + regions
    rows = captions * seq
    ff = w_up.shape[1]
    half = width // 2
    parts = 4
    part = ff // parts
    grid = captions + parts

    def kernel(
        sc_ref, t_ref, tq_ref, a_ref, src_ref, og_ref, wq, qvb_ref, wo, ob_ref, ag_ref, as_ref,
        wu_hbm, ub_ref, wd_hbm, db_ref, fg_ref, fs_ref,
        out_ref, x_ref, qkv_ref, probs_ref, ctx_ref, an_ref, ai_ref, hid_ref, slope_ref, ds_ref, df_ref,
        sums_ref, send_ref, keep_ref,
        regs, rqkv, act_all, dffn_all, wu, wd, sems,
    ):
        step = pl.program_id(0)

        places = [(wu_hbm, wu), (wd_hbm, wd)]

        def copy(at):
            return pltpu.make_async_copy(*places[at], sems.at[at])

        @pl.when(step == 0)
        def _():
            for at in range(len(places)):
                copy(at).start()
            sums_ref[...] = jnp.zeros_like(sums_ref)
            local = mm(one_hot(src_ref[...], slots), a_ref[...], TN).astype(bf16)
            regs[...] = local
            for part_id in range(3):
                at = slice(part_id * width, (part_id + 1) * width)
                got = mm(local, wq[:, at])
                if part_id == 0:
                    got = got + qvb_ref[:, :width]
                if part_id == 2:
                    got = got + qvb_ref[:, width:]
                rqkv[:, at] = got.astype(bf16)

        @pl.when(step < captions)
        def _():
            image = sc_ref[step]
            length = sc_ref[captions + step]
            count = sc_ref[2 * captions + image]
            at = pl.ds(pl.multiple_of(image * regions, regions), regions)
            x_ref[:text_len, :] = t_ref[...]
            x_ref[text_len:, :] = regs[at, :]
            qkv_ref[:text_len, :] = tq_ref[...]
            qkv_ref[text_len:, :] = rqkv[at, :]
            place = lax.broadcasted_iota(jnp.int32, (seq, 1), 0)
            row_end = jnp.where(place < text_len, length, text_len + count)
            row_mask = jnp.where(place < row_end, 1.0, 0.0)
            key_bias = jnp.where(place < row_end, 0.0, -1e30)
            first = lax.broadcasted_iota(jnp.int32, (1, 2 * HEAD), 1) < HEAD
            scale = [
                jnp.where(first, 0.125, 0.0).astype(bf16),
                jnp.where(first, 0.0, 0.125).astype(bf16),
            ]
            for pair in range(HEADS // 2):
                lo = pair * 2 * HEAD
                q = qkv_ref[:, lo : lo + 2 * HEAD]
                k = qkv_ref[:, width + lo : width + lo + 2 * HEAD]
                v = qkv_ref[:, 2 * width + lo : 2 * width + lo + 2 * HEAD]
                scores = mm(k, jnp.concatenate([q * scale[0], q * scale[1]], 0), NT) + key_bias
                raised = jnp.exp(scores - jnp.max(scores, 0, keepdims=True))
                low = (raised * (1.0 / jnp.sum(raised, 0, keepdims=True))).astype(bf16)
                probs_ref[pair] = low
                outs = mm(low, v, TN)
                ctx_ref[:, lo : lo + 2 * HEAD] = jnp.where(first, outs[:seq], outs[seq:]).astype(bf16)

            x_wide = x_ref[...].astype(f32)
            attn_out = mm(ctx_ref[...], wo[...]) + ob_ref[...]
            normed, inv = norm_parts(x_wide + attn_out)
            an_ref[...] = normed
            ai_ref[...] = jnp.broadcast_to(inv, ai_ref.shape)
            hidden = normed * ag_ref[...] + as_ref[...]
            hidden_low = hidden.astype(bf16)
            hid_ref[...] = hidden_low

            @pl.when(step == 0)
            def _():
                copy(0).wait()

            here = pl.ds(pl.multiple_of(step * seq, seq), seq)
            for piece in range(parts):
                at = slice(piece * part, (piece + 1) * part)
                upper = mm(hidden_low, wu[:, at]) + ub_ref[:, at]
                phi = 0.5 * (1.0 + lax.erf(upper * inv_sqrt_two))
                act_all[here, at] = (upper * phi).astype(bf16)
                slope = phi + upper * jnp.exp(-0.5 * upper * upper) * inv_sqrt_tau
                slope_ref[:, at] = slope.astype(bf16)

            @pl.when(step == 0)
            def _():
                copy(1).wait()

            ffn_out = mm(act_all[here, :], wd[...]) + db_ref[...]
            ffn_normed, ffn_inv = norm_parts(hidden + ffn_out)
            out_ref[...] = ((ffn_normed * fg_ref[...] + fs_ref[...]) * row_mask).astype(bf16)
            cot = og_ref[...].astype(f32) * row_mask
            second = norm_back(cot, ffn_normed, ffn_inv, fg_ref[...])
            ds_ref[...] = second
            low = second.astype(bf16)
            df_ref[...] = low
            dffn_all[here, :] = low
            for at, value in enumerate(
                (
                    cot * ffn_normed,
                    cot,
                    low.astype(f32),
                    row_mask * x_wide * x_wide,
                    row_mask * attn_out * attn_out,
                    row_mask * ffn_out * ffn_out,
                    jnp.broadcast_to(row_mask, (seq, width)),
                )
            ):
                sums_ref[at : at + 1, :] += row_sum(value)

        @pl.when(step >= captions)
        def _():
            acts = pl.ds(pl.multiple_of((step - captions) * part, part), part)
            got = mm(act_all[:, acts], dffn_all[...], TN)
            mine = sc_ref[2 * captions + images] == 0
            send_ref[...] = jnp.where(mine, got[:, half:], got[:, :half]).astype(bf16)
            keep_ref[...] = jnp.where(mine, got[:, :half], got[:, half:]).astype(bf16)

    def rowwise(size, cols):
        return pl.BlockSpec((size, cols), lambda i, s: (jnp.minimum(i, captions - 1), 0))

    anywhere = pl.BlockSpec(memory_space=pl.ANY)
    return pl.pallas_call(
        kernel,
        grid_spec=pltpu.PrefetchScalarGridSpec(
            num_scalar_prefetch=1,
            grid=(grid,),
            in_specs=[
                rowwise(text_len, width),
                rowwise(text_len, 3 * width),
                whole((slots, width)),
                whole((1, slots)),
                rowwise(seq, width),
                whole(w_qkv.shape),
                whole((1, 2 * width)),
                whole(w_out.shape),
                vec(width),
                vec(width),
                vec(width),
                anywhere,
                whole((1, ff)),
                anywhere,
                vec(width),
                vec(width),
                vec(width),
            ],
            out_specs=[
                rowwise(seq, width),
                rowwise(seq, width),
                rowwise(seq, 3 * width),
                pl.BlockSpec(
                    (HEADS // 2, seq, 2 * seq), lambda i, s: (jnp.minimum(i, captions - 1), 0, 0)
                ),
                rowwise(seq, width),
                rowwise(seq, width),
                rowwise(seq, 128),
                rowwise(seq, width),
                rowwise(seq, ff),
                rowwise(seq, width),
                rowwise(seq, width),
                whole((8, width)),
                pl.BlockSpec((part, half), lambda i, s: (jnp.maximum(i - captions, 0), 0)),
                pl.BlockSpec((part, half), lambda i, s: (jnp.maximum(i - captions, 0), 0)),
            ],
            scratch_shapes=[
                pltpu.VMEM((slots, width), bf16),
                pltpu.VMEM((slots, 3 * width), bf16),
                pltpu.VMEM((rows, ff), bf16),
                pltpu.VMEM((rows, width), bf16),
                pltpu.VMEM(w_up.shape, bf16),
                pltpu.VMEM(w_down.shape, bf16),
                pltpu.SemaphoreType.DMA((2,)),
            ],
        ),
        out_shape=[
            shape((rows, width), bf16),
            shape((rows, width), bf16),
            shape((rows, 3 * width), bf16),
            shape((captions * HEADS // 2, seq, 2 * seq), bf16),
            shape((rows, width), bf16),
            shape((rows, width)),
            shape((rows, 128)),
            shape((rows, width), bf16),
            shape((rows, ff), bf16),
            shape((rows, width)),
            shape((rows, width), bf16),
            shape((8, width)),
            shape((ff, half), bf16),
            shape((ff, half), bf16),
        ],
        compiler_params=params(50),
        name="forward",
    )(
        scalars, text, text_low, arrived, source, out_grad, w_qkv, qv_bias, w_out, out_bias,
        attn_gain, attn_shift, w_up, up_bias, w_down, down_bias, ffn_gain, ffn_shift,
    )


def ffn_backward(d_ffn, d_second, slope, attn_normed, attn_inv, w_down, w_up, attn_gain, captions):
    rows, width = d_ffn.shape
    seq = rows // captions
    ff = w_up.shape[1]
    parts = 4
    part = ff // parts

    def kernel(
        df_ref, ds_ref, sl_ref, an_ref, ai_ref, wd_hbm, wu_hbm, ag_ref,
        dup_ref, dr_ref, da_ref, sums_ref, up_ref, wd, wu, sems,
    ):
        step = pl.program_id(0)
        places = [(wd_hbm, wd), (wu_hbm, wu)]

        def copy(at):
            return pltpu.make_async_copy(*places[at], sems.at[at])

        @pl.when(step == 0)
        def _():
            copy(0).start()
            sums_ref[...] = jnp.zeros_like(sums_ref)
            up_ref[...] = jnp.zeros_like(up_ref)
            copy(0).wait()
            copy(1).start()

        d_low = df_ref[...]
        for piece in range(parts):
            at = slice(piece * part, (piece + 1) * part)
            d_act = mm(d_low, wd[at, :], NT)
            wide = d_act * sl_ref[:, at].astype(f32)
            low = wide.astype(bf16)
            dup_ref[:, at] = low
            up_ref[0:1, at] += row_sum(low.astype(f32))

        @pl.when(step == 0)
        def _():
            copy(1).wait()

        d_hidden = ds_ref[...] + mm(dup_ref[...], wu[...], NT)
        normed = an_ref[...]
        resid = norm_back(d_hidden, normed, ai_ref[:, 0:1], ag_ref[...])
        dr_ref[...] = resid
        low = resid.astype(bf16)
        da_ref[...] = low
        sums_ref[0:1, :] += row_sum(d_hidden * normed)
        sums_ref[1:2, :] += row_sum(d_hidden)
        sums_ref[2:3, :] += row_sum(low.astype(f32))

    def rowwise(cols):
        return pl.BlockSpec((seq, cols), lambda i: (i, 0))

    anywhere = pl.BlockSpec(memory_space=pl.ANY)
    return pl.pallas_call(
        kernel,
        grid=(captions,),
        in_specs=[
            rowwise(width),
            rowwise(width),
            rowwise(ff),
            rowwise(width),
            rowwise(128),
            anywhere,
            anywhere,
            vec(width),
        ],
        out_specs=[
            rowwise(ff),
            rowwise(width),
            rowwise(width),
            whole((8, width)),
            whole((8, ff)),
        ],
        scratch_shapes=[
            pltpu.VMEM(w_down.shape, bf16),
            pltpu.VMEM(w_up.shape, bf16),
            pltpu.SemaphoreType.DMA((2,)),
        ],
        out_shape=[
            shape((rows, ff), bf16),
            shape((rows, width)),
            shape((rows, width), bf16),
            shape((8, width)),
            shape((8, ff)),
        ],
        compiler_params=params(36),
        cost_estimate=pl.CostEstimate(flops=4 * rows * width * ff, bytes_accessed=20 << 20, transcendentals=0),
        name="ffn_backward",
    )(d_ffn, d_second, slope, attn_normed, attn_inv, w_down, w_up, attn_gain)


def up_gradient(core, hidden_low, d_upper):
    rows, width = hidden_low.shape

    def kernel(c_ref, h_ref, d_ref, send_ref, keep_ref):
        step = pl.program_id(0)
        got = mm(h_ref[...], d_ref[...], TN).astype(bf16)

        @pl.when(step < 2)
        def _():
            send_ref[...] = got

        @pl.when(step >= 2)
        def _():
            keep_ref[...] = got

    return pl.pallas_call(
        kernel,
        grid_spec=pltpu.PrefetchScalarGridSpec(
            num_scalar_prefetch=1,
            grid=(4,),
            in_specs=[
                whole((rows, width)),
                pl.BlockSpec((rows, width), lambda i, s: (0, lax.rem(i + 2 * (1 - s[0]), 4))),
            ],
            out_specs=[
                pl.BlockSpec((width, width), lambda i, s: (0, jnp.minimum(i, 1))),
                pl.BlockSpec((width, width), lambda i, s: (0, jnp.maximum(i - 2, 0))),
            ],
        ),
        out_shape=[shape((width, 2 * width), bf16), shape((width, 2 * width), bf16)],
        compiler_params=params(24),
        cost_estimate=pl.CostEstimate(flops=8 * rows * width * width, bytes_accessed=10 << 20, transcendentals=0),
        name="up_gradient",
    )(core, hidden_low, d_upper)


def attention_backward(scalars, d_attn, d_resid, probs, qkv, source, w_out, w_qkv, dims):
    captions, images = dims
    rows, width = d_attn.shape
    seq = rows // captions
    slots = source.shape[1]
    regions = slots // images
    text_len = seq - regions

    def kernel(
        sc_ref, da_ref, dr_ref, p_ref, qkv_ref, src_ref, wo_ref, wq_hbm,
        dqkv_ref, text_ref, back_ref, sums_ref, d_img, wq, sem,
    ):
        step = pl.program_id(0)

        def copy():
            return pltpu.make_async_copy(wq_hbm, wq, sem)

        @pl.when(step == 0)
        def _():
            copy().start()
            sums_ref[...] = jnp.zeros_like(sums_ref)
            d_img[...] = jnp.zeros_like(d_img)

        d_ctx = mm(da_ref[...], wo_ref[...], NT).astype(bf16)
        first = lax.broadcasted_iota(jnp.int32, (1, 2 * HEAD), 1) < HEAD
        masks = [jnp.where(first, 1.0, 0.0).astype(bf16), jnp.where(first, 0.0, 1.0).astype(bf16)]
        for pair in range(HEADS // 2):
            lo = pair * 2 * HEAD
            q = qkv_ref[:, lo : lo + 2 * HEAD]
            k = qkv_ref[:, width + lo : width + lo + 2 * HEAD]
            v = qkv_ref[:, 2 * width + lo : 2 * width + lo + 2 * HEAD]
            d_c = d_ctx[:, lo : lo + 2 * HEAD]
            both_c = jnp.concatenate([d_c * masks[0], d_c * masks[1]], 0)
            both_q = jnp.concatenate([q * masks[0], q * masks[1]], 0)
            low = p_ref[pair]
            d_probs = mm(v, both_c, NT)
            wide = low.astype(f32)
            both = wide * d_probs
            inner = jnp.sum(both, 0, keepdims=True)
            d_scores = (both - wide * inner).astype(bf16)
            d_q = mm(d_scores, k, TN) * 0.125
            dqkv_ref[:, lo : lo + 2 * HEAD] = jnp.where(first, d_q[:seq], d_q[seq:]).astype(bf16)
            dqkv_ref[:, width + lo : width + lo + 2 * HEAD] = (mm(d_scores, both_q) * 0.125).astype(bf16)
            dqkv_ref[:, 2 * width + lo : 2 * width + lo + 2 * HEAD] = mm(low, both_c).astype(bf16)

        @pl.when(step == 0)
        def _():
            copy().wait()

        sums_ref[0:1, :] += row_sum(dqkv_ref[:, :width].astype(f32))
        sums_ref[1:2, :] += row_sum(dqkv_ref[:, 2 * width :].astype(f32))
        d_x = mm(dqkv_ref[...], wq[...], NT) + dr_ref[...]
        text_ref[...] = d_x[:text_len]
        at = pl.ds(pl.multiple_of(sc_ref[step] * regions, regions), regions)
        d_img[at, :] += d_x[text_len:]

        @pl.when(step == captions - 1)
        def _():
            back_ref[...] = mm(one_hot(src_ref[...], slots), d_img[...].astype(bf16)).astype(bf16)

    def rowwise(size, cols):
        return pl.BlockSpec((size, cols), lambda i, s: (i, 0))

    return pl.pallas_call(
        kernel,
        grid_spec=pltpu.PrefetchScalarGridSpec(
            num_scalar_prefetch=1,
            grid=(captions,),
            in_specs=[
                rowwise(seq, width),
                rowwise(seq, width),
                pl.BlockSpec((HEADS // 2, seq, 2 * seq), lambda i, s: (i, 0, 0)),
                rowwise(seq, 3 * width),
                whole((1, slots)),
                whole(w_out.shape),
                pl.BlockSpec(memory_space=pl.ANY),
            ],
            out_specs=[
                rowwise(seq, 3 * width),
                rowwise(text_len, width),
                whole((slots, width)),
                whole((8, width)),
            ],
            scratch_shapes=[
                pltpu.VMEM((slots, width), f32),
                pltpu.VMEM(w_qkv.shape, bf16),
                pltpu.SemaphoreType.DMA,
            ],
        ),
        out_shape=[
            shape((rows, 3 * width), bf16),
            shape((captions * text_len, width)),
            shape((slots, width), bf16),
            shape((8, width)),
        ],
        compiler_params=params(36),
        cost_estimate=pl.CostEstimate(flops=12 << 30, bytes_accessed=20 << 20, transcendentals=0),
        name="attention_backward",
    )(scalars, d_attn, d_resid, probs, qkv, source, w_out, w_qkv)


def qkvo_gradient(core, x, d_qkv, context, d_attn):
    rows, width = x.shape

    def block(i, s):
        return lax.rem(i + 2 * (1 - s[0]), 4)

    def kernel(c_ref, x_ref, dq_ref, ctx_ref, da_ref, send_ref, keep_ref):
        step = pl.program_id(0)
        last = lax.rem(step + 2 * (1 - c_ref[0]), 4) == 3

        def gradient(to_ref):
            @pl.when(jnp.logical_not(last))
            def _():
                to_ref[...] = mm(x_ref[...], dq_ref[...], TN).astype(bf16)

            @pl.when(last)
            def _():
                to_ref[...] = mm(ctx_ref[...], da_ref[...], TN).astype(bf16)

        @pl.when(step < 2)
        def _():
            gradient(send_ref)

        @pl.when(step >= 2)
        def _():
            gradient(keep_ref)

    return pl.pallas_call(
        kernel,
        grid_spec=pltpu.PrefetchScalarGridSpec(
            num_scalar_prefetch=1,
            grid=(4,),
            in_specs=[
                whole((rows, width)),
                pl.BlockSpec((rows, width), lambda i, s: (0, jnp.minimum(block(i, s), 2))),
                whole((rows, width)),
                whole((rows, width)),
            ],
            out_specs=[
                pl.BlockSpec((width, width), lambda i, s: (0, jnp.minimum(i, 1))),
                pl.BlockSpec((width, width), lambda i, s: (0, jnp.maximum(i - 2, 0))),
            ],
        ),
        out_shape=[shape((width, 2 * width), bf16), shape((width, 2 * width), bf16)],
        compiler_params=params(24),
        cost_estimate=pl.CostEstimate(flops=8 * rows * width * width, bytes_accessed=12 << 20, transcendentals=0),
        name="qkvo_gradient",
    )(core, x, d_qkv, context, d_attn)


def region_backward(
    core, returned, target, normed, inv, gain, features, boxes, w_visual, w_box_t,
    sums_forward, sums_ffn, sums_up, sums_attn, groups,
):
    rows, width = returned.shape
    feat = features.shape[1]
    half = width // 2
    steps = 4
    part = feat // steps
    quarter = feat // groups // 4
    tall = quarter + 8
    per_step = groups // steps
    box = boxes.shape[0]
    share = width // groups
    ff_share = sums_up.shape[1] // groups

    def kernel(
        c_ref, r_ref, t_ref, n_ref, i_ref, g_ref, f_ref, box_ref, wv_ref, wb_ref, sf_ref, sn_ref, su_ref, sa_ref,
        send_ref, keep_ref, fg_ref, bg_ref, dpre, small,
    ):
        step = pl.program_id(0)

        @pl.when(step == 0)
        def _():
            d_region = mm(one_hot(t_ref[...], rows), r_ref[...], TN)
            normed = n_ref[...]
            low = norm_back(d_region, normed, i_ref[:, 0:1], g_ref[...]).astype(bf16)
            dpre[...] = low
            bg_ref[...] = mm(wb_ref[...], low, NT)
            boxes_grad = mm(box_ref[...], low)
            vectors = [
                row_sum(low.astype(f32)),
                row_sum(d_region * normed),
                row_sum(d_region),
                sf_ref[0:1, :],
                sf_ref[1:2, :],
                sf_ref[2:3, :],
                sn_ref[0:1, :],
                sn_ref[1:2, :],
                sn_ref[2:3, :],
            ] + [boxes_grad[at : at + 1] for at in range(box)]
            small[...] = jnp.zeros_like(small)
            lane = lax.broadcasted_iota(jnp.int32, (1, half), 1)
            stats = jnp.zeros((1, half), f32)
            for at in range(4):
                total = jnp.sum(sf_ref[3 + at : 4 + at, :], 1, keepdims=True)
                stats = jnp.where(lane == at, total, stats)
            for group in range(groups):
                small[group, 0:1, 0:ff_share] = su_ref[0:1, group * ff_share : (group + 1) * ff_share]
                for side in range(2):
                    first = group * 2 * share
                    flat = jnp.concatenate([sa_ref[0:1, :], sa_ref[1:2, :]], 1)
                    small[group, 1:2, 0 : 2 * share] = flat[:, first : first + 2 * share]
                for at, value in enumerate(vectors):
                    row, col = (1, 2) if at == 0 else (2 + (at - 1) // 3, (at - 1) % 3)
                    small[group, row : row + 1, 128 * col : 128 * col + share] = value[
                        :, group * share : (group + 1) * share
                    ]
                small[group, 6:7, :] = stats

        got = mm(f_ref[...], dpre[...], TN)
        mine = c_ref[0] == 0
        for to_ref, low_half in ((send_ref, jnp.logical_not(mine)), (keep_ref, mine)):
            chosen = jnp.where(low_half, got[:, :half], got[:, half:]).astype(bf16)
            for group in range(per_step):
                for bit in range(2):
                    for piece in range(2):
                        at = ((group * 2 + bit) * 2 + piece) * quarter
                        to_ref[group, bit, piece, :quarter, :] = chosen[at : at + quarter]
                        if piece == 0:
                            to_ref[group, bit, piece, quarter:, :] = small[step * per_step + group].astype(bf16)
                        else:
                            to_ref[group, bit, piece, quarter:, :] = jnp.zeros((8, half), bf16)
        fg_ref[...] = mm(dpre[...], wv_ref[...], NT)

    out = pl.BlockSpec((per_step, 2, 2, tall, half), lambda i, s: (i, 0, 0, 0, 0))
    return pl.pallas_call(
        kernel,
        grid_spec=pltpu.PrefetchScalarGridSpec(
            num_scalar_prefetch=1,
            grid=(steps,),
            in_specs=[
                whole((rows, width)),
                whole((1, rows)),
                whole((rows, width)),
                whole((rows, 128)),
                vec(width),
                pl.BlockSpec((rows, part), lambda i, s: (0, i)),
                whole(boxes.shape),
                pl.BlockSpec((part, width), lambda i, s: (i, 0)),
                whole(w_box_t.shape),
                whole(sums_forward.shape),
                whole(sums_ffn.shape),
                whole(sums_up.shape),
                whole(sums_attn.shape),
            ],
            out_specs=[out, out, pl.BlockSpec((rows, part), lambda i, s: (0, i)), whole((box, rows))],
            scratch_shapes=[pltpu.VMEM((rows, width), bf16), pltpu.VMEM((groups, 8, half), f32)],
        ),
        out_shape=[
            shape((groups, 2, 2, tall, half), bf16),
            shape((groups, 2, 2, tall, half), bf16),
            shape((rows, feat)),
            shape((box, rows)),
        ],
        compiler_params=params(24),
        cost_estimate=pl.CostEstimate(flops=5 << 30, bytes_accessed=12 << 20, transcendentals=0),
        name="region_backward",
    )(
        core, returned, target, normed, inv, gain, features, boxes, w_visual, w_box_t,
        sums_forward, sums_ffn, sums_up, sums_attn,
    )


def device_number():
    return lax.axis_index("dp") * lax.axis_size("enc") + lax.axis_index("enc")


def swap(values, bit):
    count = lax.axis_size("dp") * lax.axis_size("enc")
    return lax.ppermute(values, ("dp", "enc"), [(i, i ^ bit) for i in range(count)])


def add(a, b):
    return (a.astype(f32) + b.astype(f32)).astype(bf16)


def scalar_call(kernel, bits, ins, in_specs, outs, out_specs, grid, limit, name):
    return pl.pallas_call(
        kernel,
        grid_spec=pltpu.PrefetchScalarGridSpec(
            num_scalar_prefetch=1, grid=(grid,), in_specs=in_specs, out_specs=out_specs
        ),
        out_shape=outs,
        compiler_params=params(limit),
        cost_estimate=pl.CostEstimate(
            flops=1 << 20, bytes_accessed=2 * sum(v.size * v.dtype.itemsize for v in ins), transcendentals=0
        ),
        name=name,
    )(bits, *ins)


def first_split(bits, kept, got, groups):
    tall = kept.ndim == 5
    high = groups // 2
    if tall:
        rows, cols = kept.shape[3:]
        view = (high, 2, 2, 2, rows, cols)
        block = (1, 2, 2, 2, rows, cols)
    else:
        rows, cols = kept.shape[0] // groups, kept.shape[1] // 4
        view = (high, 2, rows, 4 * cols)
        block = (1, 2, rows, 4 * cols)

    def kernel(b_ref, k_ref, r_ref, a_send, a_keep, b_send, b_keep):
        bit2, bit4 = b_ref[1], b_ref[2]

        def total(y, x, piece):
            if tall:
                return add(k_ref[0, y, x, piece], r_ref[0, y, x, piece])
            at = pl.ds(pl.multiple_of((2 * x + piece) * cols, 128), cols)
            return add(k_ref[0, y, :, at], r_ref[0, y, :, at])

        for other in range(2):
            a_send[0, other] = total(other, 1 - bit2, 0)
            a_keep[0, other] = total(other, bit2, 0)
            b_send[0, other] = total(1 - bit4, other, 1)
            b_keep[0, other] = total(bit4, other, 1)

    spec = pl.BlockSpec(block, lambda i, s: (i,) + (0,) * (len(block) - 1))
    out = pl.BlockSpec((1, 2, rows, cols), lambda i, s: (i, 0, 0, 0))
    return scalar_call(
        kernel, bits, (kept.reshape(view), got.reshape(view)), [spec, spec],
        [shape((high, 2, rows, cols), bf16)] * 4, [out] * 4, high, 16, "first_split",
    )


def second_split(bits, a_kept, a_got, b_kept, b_got):
    high, _, rows, cols = a_kept.shape

    def kernel(b_ref, ak, ar, bk, br, a_send, a_keep, b_send, b_keep):
        bit2, bit4 = b_ref[1], b_ref[2]
        a_send[0] = add(ak[0, 1 - bit4], ar[0, 1 - bit4])
        a_keep[0] = add(ak[0, bit4], ar[0, bit4])
        b_send[0] = add(bk[0, 1 - bit2], br[0, 1 - bit2])
        b_keep[0] = add(bk[0, bit2], br[0, bit2])

    spec = pl.BlockSpec((1, 2, rows, cols), lambda i, s: (i, 0, 0, 0))
    out = pl.BlockSpec((1, rows, cols), lambda i, s: (i, 0, 0))
    return scalar_call(
        kernel, bits, (a_kept, a_got, b_kept, b_got), [spec] * 4,
        [shape((high, rows, cols), bf16)] * 4, [out] * 4, high, 16, "second_split",
    )


def join_split(bits, pairs):
    high, _, cols = pairs[0][0].shape
    sizes = [kept.shape[1] for kept, _ in pairs]

    def kernel(b_ref, *refs):
        bit = b_ref[3]
        send, keep = refs[-2:]
        at = 0
        for n, size in enumerate(sizes):
            kept, got = refs[2 * n : 2 * n + 2]
            send[0, at : at + size] = add(kept[1 - bit], got[1 - bit])
            keep[0, at : at + size] = add(kept[bit], got[bit])
            at += size

    ins = [value for pair in pairs for value in pair]
    specs = [pl.BlockSpec((2, v.shape[1], cols), lambda i, s: (i, 0, 0)) for v in ins]
    out = pl.BlockSpec((1, sum(sizes), cols), lambda i, s: (i, 0, 0))
    return scalar_call(
        kernel, bits, ins, specs, [shape((high // 2, sum(sizes), cols), bf16)] * 2, [out] * 2,
        high // 2, 16, "join_split",
    )


def late_split(bits, kept, got, which):
    high, rows, cols = kept.shape

    def kernel(b_ref, k_ref, r_ref, send, keep):
        bit = b_ref[which]
        send[0] = add(k_ref[1 - bit], r_ref[1 - bit])
        keep[0] = add(k_ref[bit], r_ref[bit])

    spec = pl.BlockSpec((2, rows, cols), lambda i, s: (i, 0, 0))
    out = pl.BlockSpec((1, rows, cols), lambda i, s: (i, 0, 0))
    return scalar_call(
        kernel, bits, (kept, got), [spec] * 2, [shape((high // 2, rows, cols), bf16)] * 2, [out] * 2,
        high // 2, 16, "late_split",
    )


def start_halving(bits, sent, kept, groups):
    got = swap(sent, 1)
    a_send, a_keep, b_send, b_keep = first_split(bits, kept, got, groups)
    return a_send, a_keep, b_send, b_keep


def next_halving(bits, halves):
    a_send, a_keep, b_send, b_keep = halves
    return second_split(bits, a_keep, swap(a_send, 2), b_keep, swap(b_send, 4))


def finish_halving(bits, chunks, groups):
    pairs = []
    for a_send, a_keep, b_send, b_keep in chunks:
        pairs += [(a_keep, swap(a_send, 4)), (b_keep, swap(b_send, 2))]
    send, keep = join_split(bits, pairs)
    bit, which = 8, 3
    while send.shape[0] > 1:
        bit, which = 2 * bit, which + 1
        send, keep = late_split(bits, keep, swap(send, bit // 2), which)
    mine = (keep + swap(send, bit))[0]
    over_core = swap(mine, 1)
    over_x = swap(mine, 2)
    return mine, over_x, over_core, swap(over_x, 1)


def pick(b_ref, pieces, core, x):
    mine, over_x, over_core, over_both = pieces
    same_x = b_ref[1] == x
    return jnp.where(
        b_ref[0] == core, jnp.where(same_x, mine, over_x), jnp.where(same_x, over_core, over_both)
    ).astype(f32)


def finish_ffn(bits, pieces):
    rows, cols = pieces[0].shape
    part = rows // 4

    def kernel(b_ref, p0, p1, p2, p3, down_ref, up_ref):
        for core in range(2):
            for x in range(2):
                got = pick(b_ref, (p0[...], p1[...], p2[...], p3[...]), core, x)
                down_ref[2 * x * part : 2 * (x + 1) * part, core * cols : (core + 1) * cols] = got[: 2 * part]
                for piece in range(2):
                    at = ((core * 2 + x) * 2 + piece) * cols
                    up_ref[:, at : at + cols] = got[(2 + piece) * part : (3 + piece) * part]

    outs = [shape((4 * part, 2 * cols)), shape((part, 8 * cols))]
    return scalar_call(
        kernel, bits, pieces, [whole((rows, cols))] * 4, outs, [whole(o.shape) for o in outs], 1, 24, "finish_ffn"
    )


def finish_rest(bits, pieces, part, tall, ff_share, share, box):
    rows, cols = pieces[0].shape
    quarter = tall - 8
    sizes = [share] * 9 + [2 * share, ff_share]

    def kernel(b_ref, p0, p1, p2, p3, qkv_ref, o_ref, vis_ref, box_ref, rms_ref, *small_refs):
        for core in range(2):
            for x in range(2):
                got = pick(b_ref, (p0[...], p1[...], p2[...], p3[...]), core, x)
                for piece in range(2):
                    block = got[piece * part : (piece + 1) * part]
                    at = ((core * 2 + x) * 2 + piece) * cols
                    if core * 2 + x < 3:
                        qkv_ref[:, at : at + cols] = block
                    else:
                        o_ref[:, piece * cols : (piece + 1) * cols] = block
                    low = 2 * part + piece * tall
                    vis_ref[(2 * x + piece) * quarter : (2 * x + piece + 1) * quarter, core * cols : (core + 1) * cols] = got[
                        low : low + quarter
                    ]
        low = 2 * part + quarter
        small = p0[low : low + 8, :].astype(f32)
        for at in range(9):
            row, col = (1, 2) if at == 0 else (2 + (at - 1) // 3, (at - 1) % 3)
            small_refs[at][...] = small[row, 128 * col : 128 * col + share]
        small_refs[9][...] = small[1, 0 : 2 * share]
        small_refs[10][...] = small[0, 0:ff_share]
        lines = []
        for at in range(9, 9 + box):
            row, col = 2 + (at - 1) // 3, (at - 1) % 3
            lines.append(small[row : row + 1, 128 * col : 128 * (col + 1)])
        lines += [jnp.zeros((1, 128), f32)] * (8 - box)
        box_ref[...] = jnp.concatenate(lines, 0).T[:share, :box]
        stats = small[6:7, 0:128]
        rms_ref[...] = jnp.sqrt(stats / stats[:, 3:4])

    outs = [
        shape((part, 6 * cols)),
        shape((part, 2 * cols)),
        shape((4 * quarter, 2 * cols)),
        shape((share, box)),
        shape((1, 128)),
    ] + [shape((size,)) for size in sizes]
    specs = [whole(o.shape) for o in outs[:5]] + [vec(size) for size in sizes]
    return scalar_call(
        kernel, bits, pieces, [whole((rows, cols))] * 4, outs, specs, 1, 24, "finish_rest"
    )


def gate(value, *others):
    return lax.optimization_barrier((value, *others))[0]


def on_device(
    text_embed,
    region_features,
    boxes,
    caption_image,
    caption_lengths,
    region_counts,
    region_target,
    region_source,
    w_visual,
    w_box,
    visual_bias,
    visual_gain,
    visual_shift,
    w_qkv,
    qv_bias,
    w_out,
    out_bias,
    attn_gain,
    attn_shift,
    w_up,
    up_bias,
    w_down,
    down_bias,
    ffn_gain,
    ffn_shift,
    out_grad,
):
    width = text_embed.shape[1]
    captions = caption_image.shape[0]
    images = region_counts.shape[0]
    dims = (captions, images)
    axes = ("dp", "enc")
    groups = lax.axis_size("dp")
    count = groups * lax.axis_size("enc")
    me = device_number().astype(jnp.int32)
    bits = jnp.stack([(me >> at) & 1 for at in range(count.bit_length() - 1)])
    core = bits[:1]
    scalars = jnp.concatenate([caption_image, caption_lengths, region_counts, core])
    w_box_t = w_box.T
    row = lambda v: v.reshape(1, -1)
    qv_row = row(qv_bias)

    message, vis_normed, vis_inv = region_forward(
        region_features, boxes, region_target, w_visual, w_box_t, visual_bias, visual_gain, visual_shift
    )
    arrived = lax.all_to_all(message, axes, split_axis=0, concat_axis=0, tiled=True)
    text_low = text_qkv(text_embed, w_qkv, qv_row)
    (
        out_rows, x, qkv, probs, context, attn_normed, attn_inv, hidden_low, slope, d_second, d_ffn,
        sums_forward, down_sent, down_kept,
    ) = forward(
        scalars, text_embed, text_low, arrived, region_source, out_grad, w_qkv, qv_row, w_out,
        out_bias, attn_gain, attn_shift, w_up, row(up_bias), w_down, down_bias, ffn_gain, ffn_shift, dims,
    )
    d_upper, d_resid, d_attn, sums_ffn, sums_up = ffn_backward(
        d_ffn, d_second, slope, attn_normed, attn_inv, w_down, w_up, attn_gain, captions
    )
    down_view = (groups, 2, 2, w_down.shape[0] // groups // 4, width // 2)
    down = start_halving(bits, down_sent.reshape(down_view), down_kept.reshape(down_view), groups)
    up_sent, up_kept = up_gradient(gate(core, *down), hidden_low, d_upper)
    d_qkv, text_grad, back_message, sums_attn = attention_backward(
        gate(scalars, up_kept), d_attn, d_resid, probs, qkv, region_source, w_out, w_qkv, dims
    )
    returned = lax.all_to_all(back_message, axes, split_axis=0, concat_axis=0, tiled=True)
    up = start_halving(bits, up_sent, up_kept, groups)
    down = next_halving(bits, down)
    qkvo_sent, qkvo_kept = qkvo_gradient(gate(core, *down, *up), x, d_qkv, context, d_attn)
    vis_sent, vis_kept, feature_grad, box_grad = region_backward(
        gate(core, qkvo_kept), returned, region_target, vis_normed, vis_inv, visual_gain, region_features, boxes,
        w_visual, w_box_t, sums_forward, sums_ffn, sums_up, sums_attn, groups,
    )
    qkvo = start_halving(bits, qkvo_sent, qkvo_kept, groups)
    vis = start_halving(bits, vis_sent, vis_kept, groups)
    up = next_halving(bits, up)
    ffn_pieces = finish_halving(bits, (down, up), groups)
    qkvo = next_halving(bits, qkvo)
    vis = next_halving(bits, vis)
    rest_pieces = finish_halving(bits, (qkvo, vis), groups)
    g_down, g_up = finish_ffn(bits, ffn_pieces)
    share = width // groups
    g_qkv, g_out, g_visual, g_box, rms, *small = finish_rest(
        bits, rest_pieces, share, w_visual.shape[0] // groups // 4 + 8, w_up.shape[1] // groups, share, boxes.shape[0]
    )
    return (
        out_rows,
        text_grad,
        feature_grad,
        box_grad,
        rms[0, :3],
        g_visual,
        g_box,
        small[0],
        small[1],
        small[2],
        g_qkv,
        small[9],
        g_out,
        small[8],
        small[6],
        small[7],
        g_up,
        small[10],
        g_down,
        small[5],
        small[3],
        small[4],
    )


def solution(mesh):
    return jax.shard_map(
        on_device,
        mesh=mesh,
        in_specs=(
            P(("dp", "enc"), None),
            P(("dp", "enc"), None),
            P(None, ("dp", "enc")),
            P(("dp", "enc")),
            P(("dp", "enc")),
            P(("dp", "enc")),
            P(("dp", "enc"), None),
            P(("dp", "enc"), None),
            P(),
            P(),
            P(),
            P(),
            P(),
            P(),
            P(),
            P(),
            P(),
            P(),
            P(),
            P(),
            P(),
            P(),
            P(),
            P(),
            P(),
            P(("dp", "enc"), None),
        ),
        out_specs=(
            P(("dp", "enc"), None),
            P(("dp", "enc"), None),
            P(("dp", "enc"), None),
            P(None, ("dp", "enc")),
            P(),
            P("dp", None),
            P("dp", None),
            P("dp"),
            P("dp"),
            P("dp"),
            P("dp", None),
            P("dp"),
            P("dp", None),
            P("dp"),
            P("dp"),
            P("dp"),
            P("dp", None),
            P("dp"),
            P("dp", None),
            P("dp"),
            P("dp"),
            P("dp"),
        ),
        check_vma=False,
    )
```

time: 336 us -> 284 us (0.85)
  waiting for transfers between devices: 104 us -> 80.3 us
  other arithmetic: 21.6 us -> 0.15 us
  local copies, waits for them, and re-layouts: 50.5 us -> 41.8 us
    pallas_call x1 -> x16, Pallas kernels: 26.7 us -> 46.5 us  [the longest x14 23.4 us: scalar_call(): pl.pallas_call(kernel, grid_spec=pltpu.PrefetchScalarGridSpec(num_scalar_...]
    ppermute x33 -> x30, waiting for transfers between devices: 89.9 us -> 71.9 us  [swap(): lax.ppermute(values, ('dp', 'enc'), [(i, i ^ bit) for i in range(count)])]
    unnamed x78 -> x165, local copies, waits for them, and re-layouts: 24.3 us -> 41.2 us
    add x25 -> x0, other arithmetic: 15.1 us -> none  [the longest x2 5.33 us: reduce_wide(): values = kept + swap(sent, 1)]
    all_to_all x1, waiting for transfers between devices: 12.9 us -> 0.01 us  [on_device(): lax.all_to_all(back_message, axes, split_axis=0, concat_axis=0, tiled=True)]
    reshape x10 -> x1, local copies, waits for them, and re-layouts: 9.03 us -> 0.01 us  [on_device(): row = lambda v: v.reshape(1, -1)]
    dynamic_slice x13 -> x0, local copies, waits for them, and re-layouts: 8.48 us -> none  [the longest x7 4.91 us: share(): return lax.dynamic_slice_in_dim(values, position * size, size, axis)]
    all_to_all x1, waiting for transfers between devices: 0.98 us -> 8.44 us  [on_device(): lax.all_to_all(message, axes, split_axis=0, concat_axis=0, tiled=True)]
  transfers between devices with their start and end apart: 35 -> 32, of which waited for: 19 -> 10; matrix products, arithmetic and copies ran while one was open for 13% -> 0% of each run, Pallas kernels for 5% -> 24%
where the time goes in v3:
time: 284 us; the launch traced here: 283 us
  Pallas kernels  120 us (42%)
  waiting for transfers between devices  80.3 us (28%)
  local copies, waits for them, and re-layouts  41.8 us (15%)
  starting transfers between devices  39.3 us (14%)
    ppermute x30, waiting for transfers between devices, swap(): lax.ppermute(values, ('dp', 'enc'), [(i, i ^ bit) for i in range(count)])  71.9 us
    unnamed x165, local copies, waits for them, and re-layouts  41.2 us
    pallas_call x1, Pallas kernels, forward(): pl.pallas_call(kernel, grid_spec=pltpu.PrefetchScalarGridSpec(num_scalar_...  38.4 us
    ppermute x30, starting transfers between devices, swap(): lax.ppermute(values, ('dp', 'enc'), [(i, i ^ bit) for i in range(count)])  28.4 us
    pallas_call x14, Pallas kernels, scalar_call(): pl.pallas_call(kernel, grid_spec=pltpu.PrefetchScalarGridSpec(num_scalar_...  23.4 us
    pallas_call x1, Pallas kernels, attention_backward(): pl.pallas_call(kernel, grid_spec=pltpu.PrefetchScalarGridSpec(num_scalar_...  18.3 us
    pallas_call x1, Pallas kernels, ffn_backward(): pl.pallas_call(kernel, grid=(captions,), in_specs=[rowwise(width), rowwis...  16.5 us
    all_to_all x1, waiting for transfers between devices, on_device(): lax.all_to_all(message, axes, split_axis=0, concat_axis=0, tiled=True)  8.44 us
  transfers between devices with their start and end apart: 32, of which 10 were waited for; matrix products, arithmetic and copies ran while one was open for 0% of the time, Pallas kernels for 24%

profile of v3, /device:TPU:0, one launch (start us, length us, event | category | flops | bytes accessed | tf_op | source)
XLA Modules:
  0.0 282.9 jit_solution(12238687603617313979)
XLA Ops:
  0.7 1.9 copy-done.3
  2.6 1.2 copy-done.11
  7.9 2.7 region_forward.1
  12.9 7.4 %all-to-all-start = ((bf16[32,8,768]{2,1,0:T(8,128)(2,1)}), bf16[32,8,768]{2,1,0:T(8,128)(2,1)}, u32[]{:S(2)}, u32[]{:S(2)}) async-start(bf16[32,8,768]{2,1,0:T(8,128)(2,1)} %bitcast.33), calls=%async_computation | async-start | bytes 786432 | tf_op jit(solution)/shard_map/all_to_all | solution.py:1013
  21.4 2.3 text_qkv.1.tq_ref
  23.7 1.2 copy-done.2
  25.0 8.4 %all-to-all-done = bf16[32,8,768]{2,1,0:T(8,128)(2,1)} async-done(((bf16[32,8,768]{2,1,0:T(8,128)(2,1)}), bf16[32,8,768]{2,1,0:T(8,128)(2,1)}, u32[]{:S(2)}, u32[]{:S(2)}) %all-to-all-start) | async-done | bytes 393248 | tf_op jit(solution)/shard_map/all_to_all | solution.py:1013
  38.7 38.4 %forward.1 = (bf16[768,768]{1,0:T(8,128)(2,1)}, bf16[768,768]{1,0:T(8,128)(2,1)S(1)}, bf16[768,2304]{1,0:T(8,128)(2,1)}, bf16[18,256,512]{2,1,0:T(8,128)(2,1)}, ...) custom-call(s32[9]{0:T(128)S(1)} %pad_add_fusion.sc_ref, ...), custom_call_target="tpu_custom_call" | custom-call | tf_op jit(solution)/shard_map/forward/pallas_call | solution.py:274
  78.1 1.1 copy-done.50
  79.9 1.7 copy-done.46
  81.6 1.7 copy-done.47
  83.3 1.3 copy-done.53
  84.6 16.5 %ffn_backward.1 = (bf16[768,3072]{1,0:T(8,128)(2,1)S(1)}, f32[768,768]{1,0:T(8,128)S(1)}, bf16[768,768]{1,0:T(8,128)(2,1)S(1)}, f32[8,768]{1,0:T(8,128)S(1)}, f32[8,3072]{1,0:T(8,128)S(1)}) custom-call(bf16[768,768]{1,0:T(8,128)(2,1)S(1)} %copy-done.53, f32[768,768]{1,0:T(8,128)S(1)} %copy-done.47, bf16[768,3072]{1,0:T(8,128)(2,1)} %get-tuple-element.130.sl_ref, ...), custom_call_target="tpu_custom_call" | custom-call | flops 7247757312 | bytes 20971520 | tf_op jit(solution)/shard_map/ffn_backward/pallas_call | solution.py:402
  102.3 2.3 first_split.4
  104.7 6.6 %up_gradient.1 = (bf16[768,1536]{1,0:T(8,128)(2,1)}, bf16[768,1536]{1,0:T(8,128)(2,1)S(1)}) custom-call(s32[1]{0:T(128)} %bitcast.c_ref, bf16[768,768]{1,0:T(8,128)(2,1)S(1)} %copy-done.52, bf16[768,3072]{1,0:T(8,128)(2,1)S(1)} %get-tuple-element.133.d_ref), custom_call_target="tpu_custom_call" | custom-call | flops 3623878656 | bytes 10485760 | tf_op jit(solution)/shard_map/up_gradient/pallas_call | solution.py:455
  112.3 1.5 collective-permute-start.2
  113.8 18.3 %attention_backward.1 = (bf16[768,2304]{1,0:T(8,128)(2,1)S(1)}, f32[384,768]{1,0:T(8,128)}, bf16[256,768]{1,0:T(8,128)(2,1)S(1)}, f32[8,768]{1,0:T(8,128)S(1)}) custom-call(s32[9]{0:T(128)S(1)} %copy-done.40, bf16[768,768]{1,0:T(8,128)(2,1)S(1)} %get-tuple-element.136.da_ref, f32[768,768]{1,0:T(8,128)S(1)} %get-tuple-element.137.dr_ref, ...), custom_call_target="tpu_custom_call" | custom-call | flops 12884901888 | bytes 20971520 | tf_op jit(solution)/shard_map/attention_backward/pallas_call | solution.py:539
  132.9 1.8 copy-done.68
  135.3 3.5 %all-to-all-start.1 = ((bf16[32,8,768]{2,1,0:T(8,128)(2,1)}), bf16[32,8,768]{2,1,0:T(8,128)(2,1)}, u32[]{:S(2)}, u32[]{:S(2)}) async-start(bf16[32,8,768]{2,1,0:T(8,128)(2,1)} %bitcast.32), calls=%async_computation.1 | async-start | bytes 786432 | tf_op jit(solution)/shard_map/all_to_all | solution.py:1031
  138.9 3.1 %second_split.4 = (bf16[4,96,384]{2,1,0:T(8,128)(2,1)S(1)}, bf16[4,96,384]{2,1,0:T(8,128)(2,1)S(1)}, bf16[4,96,384]{2,1,0:T(8,128)(2,1)S(1)}, bf16[4,96,384]{2,1,0:T(8,128)(2,1)S(1)}) custom-call(s32[5]{0:T(128)S(1)} %stack.23.b_ref, bf16[4,2,96,384]{3,2,1,0:T(8,128)(2,1)S(1)} %get-tuple-element.123.ak, bf16[4,2,96,384]{3,2,1,0:T(8,128)(2,1)} %collective-permute-done.1.ar, ...), custom_call_target="tpu_custom_call" | custom-call | flops 1048576 | bytes 4718592 | tf_op jit(solution)/shard_map/second_split/pallas_call | solution.py:755
  144.9 3.5 %first_split.5 = (bf16[4,2,96,384]{3,2,1,0:T(8,128)(2,1)S(1)}, bf16[4,2,96,384]{3,2,1,0:T(8,128)(2,1)S(1)}, bf16[4,2,96,384]{3,2,1,0:T(8,128)(2,1)S(1)}, bf16[4,2,96,384]{3,2,1,0:T(8,128)(2,1)S(1)}) custom-call(s32[5]{0:T(128)S(1)} %stack.23.b_ref, bf16[4,2,96,1536]{3,2,1,0:T(8,128)(2,1)S(1)} %bitcast.28, bf16[4,2,96,1536]{3,2,1,0:T(8,128)(2,1)} %bitcast.13.r_ref), custom_call_target="tpu_custom_call" | custom-call | flops 1048576 | bytes 9437184 | tf_op jit(solution)/shard_map/first_split/pallas_call | solution.py:755
  151.7 6.2 %qkvo_gradient.1 = (bf16[768,1536]{1,0:T(8,128)(2,1)}, bf16[768,1536]{1,0:T(8,128)(2,1)S(1)}) custom-call(s32[1]{0:T(128)} %bitcast.c_ref, bf16[768,768]{1,0:T(8,128)(2,1)S(1)} %copy-done.49, bf16[768,2304]{1,0:T(8,128)(2,1)S(1)} %copy-done.69, bf16[768,768]{1,0:T(8,128)(2,1)S(1)} %copy-done.51, bf16[768,768]{1,0:T(8,128)(2,1)S(1)} %copy-done.71), custom_call_target="tpu_custom_call" | custom-call | flops 3623878656 | bytes 12582912 | tf_op jit(solution)/shard_map/qkvo_gradient/pallas_call | solution.py:604
  158.0 1.5 copy-done.5
  159.5 1.2 copy-done.12
  160.7 1.1 copy-done.55
  163.7 5.6 %region_backward.1 = (bf16[8,2,2,72,384]{4,3,2,1,0:T(8,128)(2,1)S(1)}, bf16[8,2,2,72,384]{4,3,2,1,0:T(8,128)(2,1)S(1)}, f32[256,2048]{1,0:T(8,128)}, f32[4,256]{1,0:T(4,128)}) custom-call(s32[1]{0:T(128)} %bitcast.c_ref, bf16[256,768]{1,0:T(8,128)(2,1)} %bitcast.15.r_ref, s32[1,256]{1,0:T(1,128)S(1)} %copy-done.42, f32[256,768]{1,0:T(8,128)S(1)} %copy-done.55, ...), custom_call_target="tpu_custom_call" | custom-call | flops 5368709120 | bytes 12582912 | tf_op jit(solution)/shard_map/region_backward/pallas_call | solution.py:703
  169.8 1.4 collective-permute-start.21
  171.2 1.5 collective-permute-start.22
  173.2 11.9 %collective-permute-done.21.ar = bf16[4,2,96,384]{3,2,1,0:T(8,128)(2,1)S(1)} collective-permute-done((bf16[4,2,96,384]{3,2,1,0:T(8,128)(2,1)S(1)}, bf16[4,2,96,384]{3,2,1,0:T(8,128)(2,1)S(1)}, u32[]{:S(2)}, u32[]{:S(2)}) %collective-permute-start.21) | collective-permute-done | bytes 589856 | tf_op jit(solution)/shard_map/ppermute | solution.py:747
  185.1 1.4 collective-permute-start.20
  188.3 1.6 collective-permute-start.23
  189.9 3.2 %first_split.6 = (bf16[4,2,96,384]{3,2,1,0:T(8,128)(2,1)S(1)}, bf16[4,2,96,384]{3,2,1,0:T(8,128)(2,1)S(1)}, bf16[4,2,96,384]{3,2,1,0:T(8,128)(2,1)S(1)}, bf16[4,2,96,384]{3,2,1,0:T(8,128)(2,1)S(1)}) custom-call(s32[5]{0:T(128)S(1)} %stack.23.b_ref, bf16[4,2,96,1536]{3,2,1,0:T(8,128)(2,1)S(1)} %bitcast.26, bf16[4,2,96,1536]{3,2,1,0:T(8,128)(2,1)} %bitcast.17.r_ref), custom_call_target="tpu_custom_call" | custom-call | flops 1048576 | bytes 9437184 | tf_op jit(solution)/shard_map/first_split/pallas_call | solution.py:755
  195.4 1.4 collective-permute-start.10
  196.9 1.5 collective-permute-start.11
  198.4 1.7 collective-permute-done.23.refs_5_
  200.7 21.5 %collective-permute-done.24.refs_7_ = bf16[4,96,384]{2,1,0:T(8,128)(2,1)S(1)} collective-permute-done((bf16[4,96,384]{2,1,0:T(8,128)(2,1)S(1)}, bf16[4,96,384]{2,1,0:T(8,128)(2,1)S(1)}, u32[]{:S(2)}, u32[]{:S(2)}) %collective-permute-start.24) | collective-permute-done | bytes 294944 | tf_op jit(solution)/shard_map/ppermute | solution.py:747
  223.1 1.6 collective-permute-start.25
  225.6 1.2 collective-permute-start.7
  226.7 1.5 collective-permute-start.8
  230.6 6.5 %collective-permute-done.12.refs_5_ = bf16[4,72,384]{2,1,0:T(8,128)(2,1)S(1)} collective-permute-done((bf16[4,72,384]{2,1,0:T(8,128)(2,1)S(1)}, bf16[4,72,384]{2,1,0:T(8,128)(2,1)S(1)}, u32[]{:S(2)}, u32[]{:S(2)}) %collective-permute-start.12) | collective-permute-done | bytes 221216 | tf_op jit(solution)/shard_map/ppermute | solution.py:747
  240.1 2.7 collective-permute-start.26
  242.8 13.0 %collective-permute-done.14.r_ref = bf16[2,336,384]{2,1,0:T(8,128)(2,1)S(1)} collective-permute-done((bf16[2,336,384]{2,1,0:T(8,128)(2,1)S(1)}, bf16[2,336,384]{2,1,0:T(8,128)(2,1)S(1)}, u32[]{:S(2)}, u32[]{:S(2)}) %collective-permute-start.14) | collective-permute-done | bytes 516128 | tf_op jit(solution)/shard_map/ppermute | solution.py:747
  257.1 2.1 collective-permute-start.27
  259.2 9.6 %collective-permute-done.15 = bf16[1,336,384]{2,1,0:T(8,128)(2,1)S(1)} collective-permute-done((bf16[1,336,384]{2,1,0:T(8,128)(2,1)S(1)}, bf16[1,336,384]{2,1,0:T(8,128)(2,1)S(1)}, u32[]{:S(2)}, u32[]{:S(2)}) %collective-permute-start.15) | collective-permute-done | bytes 258080 | tf_op jit(solution)/shard_map/ppermute | solution.py:747
  268.8 2.1 collective-permute-start.16
  271.4 5.9 %collective-permute-done.16.p1 = bf16[336,384]{1,0:T(8,128)(2,1)S(1)} collective-permute-done((bf16[336,384]{1,0:T(8,128)(2,1)S(1)}, bf16[336,384]{1,0:T(8,128)(2,1)S(1)}, u32[]{:S(2)}, u32[]{:S(2)}) %collective-permute-start.16) | collective-permute-done | bytes 258080 | tf_op jit(solution)/shard_map/ppermute | solution.py:747
  277.3 2.2 finish_ffn.1
  279.5 2.2 finish_rest.1
  (209 shorter events, 42.0 us)
Async XLA Ops:
  7.9 12.4 %copy-start.78 = (f32[1536]{0:T(1024)S(1)}, f32[1536]{0:T(1024)}, u32[]{:S(2)}) copy-start(f32[1536]{0:T(1024)} %param.40) | copy-start | bytes 18436
  7.9 12.4 %copy-start = (bf16[768,2304]{1,0:T(8,128)(2,1)S(1)}, bf16[768,2304]{1,0:T(8,128)(2,1)}, u32[]{:S(2)}) copy-start(bf16[768,2304]{1,0:T(8,128)(2,1)} %wq_hbm.1) | copy-start | bytes 10616836
  12.9 20.6 %all-to-all-start = ((bf16[32,8,768]{2,1,0:T(8,128)(2,1)}), bf16[32,8,768]{2,1,0:T(8,128)(2,1)}, u32[]{:S(2)}, u32[]{:S(2)}) async-start(bf16[32,8,768]{2,1,0:T(8,128)(2,1)} %bitcast.33), calls=%async_computation | async-start | bytes 786432 | tf_op jit(solution)/shard_map/all_to_all | solution.py:1013
  21.4 12.0 %copy-start.30 = (f32[768]{0:T(1024)S(1)}, f32[768]{0:T(1024)}, u32[]{:S(2)}) copy-start(f32[768]{0:T(1024)} %ob_ref.1) | copy-start | bytes 9220
  21.4 12.0 %copy-start.31 = (f32[768]{0:T(1024)S(1)}, f32[768]{0:T(1024)}, u32[]{:S(2)}) copy-start(f32[768]{0:T(1024)} %as_ref.1) | copy-start | bytes 9220
  25.0 52.1 %copy-start.39 = (s32[9]{0:T(128)}, s32[9]{0:T(128)S(1)}, u32[]{:S(2)}) copy-start(s32[9]{0:T(128)S(1)} %pad_add_fusion.sc_ref) | copy-start | bytes 112
  38.7 41.3 %copy-start.36 = (f32[768]{0:T(1024)S(1)}, f32[768]{0:T(1024)}, u32[]{:S(2)}) copy-start(f32[768]{0:T(1024)} %ag_ref.3) | copy-start | bytes 9220
  79.9 22.5 %collective-permute-start = (bf16[8,2,2,96,384]{4,3,2,1,0:T(8,128)(2,1)}, bf16[8,2,2,96,384]{4,3,2,1,0:T(8,128)(2,1)S(1)}, u32[]{:S(2)}, u32[]{:S(2)}) collective-permute-start(bf16[8,2,2,96,384]{4,3,2,1,0:T(8,128)(2,1)} %bitcast.37), channel_id=1, source_target_pairs={{0,1},{1,0},{2,3},{3,2},{4,5},{5,4},{6,7},{7,6},{8,9},{9,8},{10,11... | collective-permute-start | bytes 7077896 | tf_op jit(solution)/shard_map/ppermute | solution.py:747
  84.5 17.8 %copy-start.7 = (bf16[3072,384]{1,0:T(8,128)(2,1)S(1)}, bf16[3072,384]{1,0:T(8,128)(2,1)}, u32[]{:S(2)}) copy-start(bf16[3072,384]{1,0:T(8,128)(2,1)} %get-tuple-element.120) | copy-start | bytes 7077892
  102.3 11.5 %copy-start.70 = (bf16[768,768]{1,0:T(8,128)(2,1)}, bf16[768,768]{1,0:T(8,128)(2,1)S(1)}, u32[]{:S(2)}) copy-start(bf16[768,768]{1,0:T(8,128)(2,1)S(1)} %get-tuple-element.136.da_ref) | copy-start | bytes 3538948
  104.6 9.2 %copy-start.10 = (bf16[768,768]{1,0:T(8,128)(2,1)S(1)}, bf16[768,768]{1,0:T(8,128)(2,1)}, u32[]{:S(2)}) copy-start(bf16[768,768]{1,0:T(8,128)(2,1)} %wo_ref.1) | copy-start | bytes 3538948
  111.3 33.6 %collective-permute-start.3 = (bf16[768,1536]{1,0:T(8,128)(2,1)}, bf16[768,1536]{1,0:T(8,128)(2,1)}, u32[]{:S(2)}, u32[]{:S(2)}) collective-permute-start(bf16[768,1536]{1,0:T(8,128)(2,1)} %get-tuple-element.145), channel_id=1, source_target_pairs={{0,1},{1,0},{2,3},{3,2},{4,5},{5,4},{6,7},{7,6},{8,9},{9,8},{10,11... | collective-permute-start | bytes 7077896 | tf_op jit(solution)/shard_map/ppermute | solution.py:747
  111.8 27.0 %collective-permute-start.1 = (bf16[4,2,96,384]{3,2,1,0:T(8,128)(2,1)}, bf16[4,2,96,384]{3,2,1,0:T(8,128)(2,1)}, u32[]{:S(2)}, u32[]{:S(2)}) collective-permute-start(bf16[4,2,96,384]{3,2,1,0:T(8,128)(2,1)} %get-tuple-element.122), channel_id=1, source_target_pairs={{0,2},{1,3},{2,0},{3,1},{4,6},{5,7},{6,4},{7,5},{8,10},{9,11},{10,... | collective-permute-start | bytes 1769480 | tf_op jit(solution)/shard_map/ppermute | solution.py:747
  112.3 26.6 %collective-permute-start.2 = (bf16[4,2,96,384]{3,2,1,0:T(8,128)(2,1)}, bf16[4,2,96,384]{3,2,1,0:T(8,128)(2,1)}, u32[]{:S(2)}, u32[]{:S(2)}) collective-permute-start(bf16[4,2,96,384]{3,2,1,0:T(8,128)(2,1)} %get-tuple-element.124), channel_id=1, source_target_pairs={{0,4},{1,5},{2,6},{3,7},{4,0},{5,1},{6,2},{7,3},{8,12},{9,13},{10,... | collective-permute-start | bytes 1769480 | tf_op jit(solution)/shard_map/ppermute | solution.py:747
  135.3 24.1 %all-to-all-start.1 = ((bf16[32,8,768]{2,1,0:T(8,128)(2,1)}), bf16[32,8,768]{2,1,0:T(8,128)(2,1)}, u32[]{:S(2)}, u32[]{:S(2)}) async-start(bf16[32,8,768]{2,1,0:T(8,128)(2,1)} %bitcast.32), calls=%async_computation.1 | async-start | bytes 786432 | tf_op jit(solution)/shard_map/all_to_all | solution.py:1031
  138.9 12.8 %copy-start.69 = (bf16[768,2304]{1,0:T(8,128)(2,1)S(1)}, bf16[768,2304]{1,0:T(8,128)(2,1)}, u32[]{:S(2)}) copy-start(bf16[768,2304]{1,0:T(8,128)(2,1)} %copy-done.68) | copy-start | bytes 10616836
  159.4 30.4 %collective-permute-start.4 = (bf16[768,1536]{1,0:T(8,128)(2,1)}, bf16[768,1536]{1,0:T(8,128)(2,1)}, u32[]{:S(2)}, u32[]{:S(2)}) collective-permute-start(bf16[768,1536]{1,0:T(8,128)(2,1)} %get-tuple-element.165), channel_id=1, source_target_pairs={{0,1},{1,0},{2,3},{3,2},{4,5},{5,4},{6,7},{7,6},{8,9},{9,8},{10,11... | collective-permute-start | bytes 7077896 | tf_op jit(solution)/shard_map/ppermute | solution.py:747
  163.7 21.4 %copy-start.61 = (bf16[4,96,384]{2,1,0:T(8,128)(2,1)S(1)}, bf16[4,96,384]{2,1,0:T(8,128)(2,1)}, u32[]{:S(2)}) copy-start(bf16[4,96,384]{2,1,0:T(8,128)(2,1)} %copy-done.60) | copy-start | bytes 884740
  163.7 23.7 %copy-start.14 = (bf16[4,2,96,384]{3,2,1,0:T(8,128)(2,1)S(1)}, bf16[4,2,96,384]{3,2,1,0:T(8,128)(2,1)}, u32[]{:S(2)}) copy-start(bf16[4,2,96,384]{3,2,1,0:T(8,128)(2,1)} %copy-done.13) | copy-start | bytes 1769476
  163.7 23.7 %copy-start.16 = (bf16[4,2,96,384]{3,2,1,0:T(8,128)(2,1)S(1)}, bf16[4,2,96,384]{3,2,1,0:T(8,128)(2,1)}, u32[]{:S(2)}) copy-start(bf16[4,2,96,384]{3,2,1,0:T(8,128)(2,1)} %copy-done.15) | copy-start | bytes 1769476
  169.3 20.6 %copy-start.6 = (bf16[768,1536]{1,0:T(8,128)(2,1)S(1)}, bf16[768,1536]{1,0:T(8,128)(2,1)}, u32[]{:S(2)}) copy-start(bf16[768,1536]{1,0:T(8,128)(2,1)} %copy-done.5) | copy-start | bytes 7077892
  169.3 24.4 %collective-permute-start.9 = (bf16[8,2,2,72,384]{4,3,2,1,0:T(8,128)(2,1)S(1)}, bf16[8,2,2,72,384]{4,3,2,1,0:T(8,128)(2,1)S(1)}, u32[]{:S(2)}, u32[]{:S(2)}) collective-permute-start(bf16[8,2,2,72,384]{4,3,2,1,0:T(8,128)(2,1)S(1)} %get-tuple-element.175), channel_id=1, source_target_pairs={{0,1},{1,0},{2,3},{3,2},{4,5},{5,4},{6,7},{7,6},{8,9},{9,8},{10,11... | collective-permute-start | bytes 5308424 | tf_op jit(solution)/shard_map/ppermute | solution.py:747
  169.8 15.3 %collective-permute-start.21 = (bf16[4,2,96,384]{3,2,1,0:T(8,128)(2,1)S(1)}, bf16[4,2,96,384]{3,2,1,0:T(8,128)(2,1)S(1)}, u32[]{:S(2)}, u32[]{:S(2)}) collective-permute-start(bf16[4,2,96,384]{3,2,1,0:T(8,128)(2,1)S(1)} %copy-done.59), channel_id=1, source_target_pairs={{0,2},{1,3},{2,0},{3,1},{4,6},{5,7},{6,4},{7,5},{8,10},{9,11},{10,... | collective-permute-start | bytes 1769480 | tf_op jit(solution)/shard_map/ppermute | solution.py:747
  171.2 16.2 %collective-permute-start.22 = (bf16[4,2,96,384]{3,2,1,0:T(8,128)(2,1)S(1)}, bf16[4,2,96,384]{3,2,1,0:T(8,128)(2,1)S(1)}, u32[]{:S(2)}, u32[]{:S(2)}) collective-permute-start(bf16[4,2,96,384]{3,2,1,0:T(8,128)(2,1)S(1)} %copy-done.57), channel_id=1, source_target_pairs={{0,4},{1,5},{2,6},{3,7},{4,0},{5,1},{6,2},{7,3},{8,12},{9,13},{10,... | collective-permute-start | bytes 1769480 | tf_op jit(solution)/shard_map/ppermute | solution.py:747
  172.7 22.8 %collective-permute-start.19 = (bf16[4,96,384]{2,1,0:T(8,128)(2,1)S(1)}, bf16[4,96,384]{2,1,0:T(8,128)(2,1)S(1)}, u32[]{:S(2)}, u32[]{:S(2)}) collective-permute-start(bf16[4,96,384]{2,1,0:T(8,128)(2,1)S(1)} %copy-done.63), channel_id=1, source_target_pairs={{0,4},{1,5},{2,6},{3,7},{4,0},{5,1},{6,2},{7,3},{8,12},{9,13},{10,... | collective-permute-start | bytes 884744 | tf_op jit(solution)/shard_map/ppermute | solution.py:747
  185.1 11.8 %collective-permute-start.20 = (bf16[4,96,384]{2,1,0:T(8,128)(2,1)S(1)}, bf16[4,96,384]{2,1,0:T(8,128)(2,1)S(1)}, u32[]{:S(2)}, u32[]{:S(2)}) collective-permute-start(bf16[4,96,384]{2,1,0:T(8,128)(2,1)S(1)} %copy-done.61), channel_id=1, source_target_pairs={{0,2},{1,3},{2,0},{3,1},{4,6},{5,7},{6,4},{7,5},{8,10},{9,11},{10,... | collective-permute-start | bytes 884744 | tf_op jit(solution)/shard_map/ppermute | solution.py:747
  188.3 11.7 %collective-permute-start.23 = (bf16[4,96,384]{2,1,0:T(8,128)(2,1)S(1)}, bf16[4,96,384]{2,1,0:T(8,128)(2,1)S(1)}, u32[]{:S(2)}, u32[]{:S(2)}) collective-permute-start(bf16[4,96,384]{2,1,0:T(8,128)(2,1)S(1)} %get-tuple-element.201), channel_id=1, source_target_pairs={{0,4},{1,5},{2,6},{3,7},{4,0},{5,1},{6,2},{7,3},{8,12},{9,13},{10,... | collective-permute-start | bytes 884744 | tf_op jit(solution)/shard_map/ppermute | solution.py:747
  193.1 29.1 %copy-start.20 = (bf16[4,96,384]{2,1,0:T(8,128)(2,1)S(1)}, bf16[4,96,384]{2,1,0:T(8,128)(2,1)}, u32[]{:S(2)}) copy-start(bf16[4,96,384]{2,1,0:T(8,128)(2,1)} %copy-done.19) | copy-start | bytes 884740
  193.1 29.1 %copy-start.22 = (bf16[4,96,384]{2,1,0:T(8,128)(2,1)S(1)}, bf16[4,96,384]{2,1,0:T(8,128)(2,1)}, u32[]{:S(2)}) copy-start(bf16[4,96,384]{2,1,0:T(8,128)(2,1)} %copy-done.21) | copy-start | bytes 884740
  193.1 31.6 %collective-permute-start.5 = (bf16[4,2,96,384]{3,2,1,0:T(8,128)(2,1)S(1)}, bf16[4,2,96,384]{3,2,1,0:T(8,128)(2,1)S(1)}, u32[]{:S(2)}, u32[]{:S(2)}) collective-permute-start(bf16[4,2,96,384]{3,2,1,0:T(8,128)(2,1)S(1)} %get-tuple-element.167), channel_id=1, source_target_pairs={{0,2},{1,3},{2,0},{3,1},{4,6},{5,7},{6,4},{7,5},{8,10},{9,11},{10,... | collective-permute-start | bytes 1769480 | tf_op jit(solution)/shard_map/ppermute | solution.py:747
  193.7 30.9 %collective-permute-start.6 = (bf16[4,2,96,384]{3,2,1,0:T(8,128)(2,1)S(1)}, bf16[4,2,96,384]{3,2,1,0:T(8,128)(2,1)S(1)}, u32[]{:S(2)}, u32[]{:S(2)}) collective-permute-start(bf16[4,2,96,384]{3,2,1,0:T(8,128)(2,1)S(1)} %get-tuple-element.169), channel_id=1, source_target_pairs={{0,4},{1,5},{2,6},{3,7},{4,0},{5,1},{6,2},{7,3},{8,12},{9,13},{10,... | collective-permute-start | bytes 1769480 | tf_op jit(solution)/shard_map/ppermute | solution.py:747
  195.4 32.8 %collective-permute-start.10 = (bf16[4,2,72,384]{3,2,1,0:T(8,128)(2,1)S(1)}, bf16[4,2,72,384]{3,2,1,0:T(8,128)(2,1)S(1)}, u32[]{:S(2)}, u32[]{:S(2)}) collective-permute-start(bf16[4,2,72,384]{3,2,1,0:T(8,128)(2,1)S(1)} %get-tuple-element.177), channel_id=1, source_target_pairs={{0,2},{1,3},{2,0},{3,1},{4,6},{5,7},{6,4},{7,5},{8,10},{9,11},{10,... | collective-permute-start | bytes 1327112 | tf_op jit(solution)/shard_map/ppermute | solution.py:747
  196.9 31.4 %collective-permute-start.11 = (bf16[4,2,72,384]{3,2,1,0:T(8,128)(2,1)S(1)}, bf16[4,2,72,384]{3,2,1,0:T(8,128)(2,1)S(1)}, u32[]{:S(2)}, u32[]{:S(2)}) collective-permute-start(bf16[4,2,72,384]{3,2,1,0:T(8,128)(2,1)S(1)} %get-tuple-element.179), channel_id=1, source_target_pairs={{0,4},{1,5},{2,6},{3,7},{4,0},{5,1},{6,2},{7,3},{8,12},{9,13},{10,... | collective-permute-start | bytes 1327112 | tf_op jit(solution)/shard_map/ppermute | solution.py:747
  200.0 22.1 %collective-permute-start.24 = (bf16[4,96,384]{2,1,0:T(8,128)(2,1)S(1)}, bf16[4,96,384]{2,1,0:T(8,128)(2,1)S(1)}, u32[]{:S(2)}, u32[]{:S(2)}) collective-permute-start(bf16[4,96,384]{2,1,0:T(8,128)(2,1)S(1)} %get-tuple-element.203), channel_id=1, source_target_pairs={{0,2},{1,3},{2,0},{3,1},{4,6},{5,7},{6,4},{7,5},{8,10},{9,11},{10,... | collective-permute-start | bytes 884744 | tf_op jit(solution)/shard_map/ppermute | solution.py:747
  223.1 16.3 %collective-permute-start.25 = (bf16[2,384,384]{2,1,0:T(8,128)(2,1)S(1)}, bf16[2,384,384]{2,1,0:T(8,128)(2,1)S(1)}, u32[]{:S(2)}, u32[]{:S(2)}) collective-permute-start(bf16[2,384,384]{2,1,0:T(8,128)(2,1)S(1)} %get-tuple-element.205), channel_id=1, source_target_pairs={{0,8},{1,9},{2,10},{3,11},{4,12},{5,13},{6,14},{7,15},{8,0},{9,1},... | collective-permute-start | bytes 1769480 | tf_op jit(solution)/shard_map/ppermute | solution.py:747
  225.6 12.5 %collective-permute-start.7 = (bf16[4,96,384]{2,1,0:T(8,128)(2,1)S(1)}, bf16[4,96,384]{2,1,0:T(8,128)(2,1)S(1)}, u32[]{:S(2)}, u32[]{:S(2)}) collective-permute-start(bf16[4,96,384]{2,1,0:T(8,128)(2,1)S(1)} %get-tuple-element.171), channel_id=1, source_target_pairs={{0,4},{1,5},{2,6},{3,7},{4,0},{5,1},{6,2},{7,3},{8,12},{9,13},{10,... | collective-permute-start | bytes 884744 | tf_op jit(solution)/shard_map/ppermute | solution.py:747
  226.7 11.4 %collective-permute-start.8 = (bf16[4,96,384]{2,1,0:T(8,128)(2,1)S(1)}, bf16[4,96,384]{2,1,0:T(8,128)(2,1)S(1)}, u32[]{:S(2)}, u32[]{:S(2)}) collective-permute-start(bf16[4,96,384]{2,1,0:T(8,128)(2,1)S(1)} %get-tuple-element.173), channel_id=1, source_target_pairs={{0,2},{1,3},{2,0},{3,1},{4,6},{5,7},{6,4},{7,5},{8,10},{9,11},{10,... | collective-permute-start | bytes 884744 | tf_op jit(solution)/shard_map/ppermute | solution.py:747
  229.1 8.0 %collective-permute-start.12 = (bf16[4,72,384]{2,1,0:T(8,128)(2,1)S(1)}, bf16[4,72,384]{2,1,0:T(8,128)(2,1)S(1)}, u32[]{:S(2)}, u32[]{:S(2)}) collective-permute-start(bf16[4,72,384]{2,1,0:T(8,128)(2,1)S(1)} %get-tuple-element.181), channel_id=1, source_target_pairs={{0,4},{1,5},{2,6},{3,7},{4,0},{5,1},{6,2},{7,3},{8,12},{9,13},{10,... | collective-permute-start | bytes 663560 | tf_op jit(solution)/shard_map/ppermute | solution.py:747
  229.7 8.4 %collective-permute-start.13 = (bf16[4,72,384]{2,1,0:T(8,128)(2,1)S(1)}, bf16[4,72,384]{2,1,0:T(8,128)(2,1)S(1)}, u32[]{:S(2)}, u32[]{:S(2)}) collective-permute-start(bf16[4,72,384]{2,1,0:T(8,128)(2,1)S(1)} %get-tuple-element.183), channel_id=1, source_target_pairs={{0,2},{1,3},{2,0},{3,1},{4,6},{5,7},{6,4},{7,5},{8,10},{9,11},{10,... | collective-permute-start | bytes 663560 | tf_op jit(solution)/shard_map/ppermute | solution.py:747
  239.0 16.8 %collective-permute-start.14 = (bf16[2,336,384]{2,1,0:T(8,128)(2,1)S(1)}, bf16[2,336,384]{2,1,0:T(8,128)(2,1)S(1)}, u32[]{:S(2)}, u32[]{:S(2)}) collective-permute-start(bf16[2,336,384]{2,1,0:T(8,128)(2,1)S(1)} %get-tuple-element.185), channel_id=1, source_target_pairs={{0,8},{1,9},{2,10},{3,11},{4,12},{5,13},{6,14},{7,15},{8,0},{9,1},... | collective-permute-start | bytes 1548296 | tf_op jit(solution)/shard_map/ppermute | solution.py:747
  240.1 16.9 %collective-permute-start.26 = (bf16[1,384,384]{2,1,0:T(8,128)(2,1)S(1)}, bf16[1,384,384]{2,1,0:T(8,128)(2,1)S(1)}, u32[]{:S(2)}, u32[]{:S(2)}) collective-permute-start(bf16[1,384,384]{2,1,0:T(8,128)(2,1)S(1)} %get-tuple-element.207), channel_id=1, source_target_pairs={{0,16},{1,17},{2,18},{3,19},{4,20},{5,21},{6,22},{7,23},{8,24},{9,... | collective-permute-start | bytes 884744 | tf_op jit(solution)/shard_map/ppermute | solution.py:747
  256.5 12.3 %collective-permute-start.15 = (bf16[1,336,384]{2,1,0:T(8,128)(2,1)S(1)}, bf16[1,336,384]{2,1,0:T(8,128)(2,1)S(1)}, u32[]{:S(2)}, u32[]{:S(2)}) collective-permute-start(bf16[1,336,384]{2,1,0:T(8,128)(2,1)S(1)} %get-tuple-element.187), channel_id=1, source_target_pairs={{0,16},{1,17},{2,18},{3,19},{4,20},{5,21},{6,22},{7,23},{8,24},{9,... | collective-permute-start | bytes 774152 | tf_op jit(solution)/shard_map/ppermute | solution.py:747
  257.1 13.8 %collective-permute-start.27 = (bf16[384,384]{1,0:T(8,128)(2,1)S(1)}, bf16[384,384]{1,0:T(8,128)(2,1)S(1)}, u32[]{:S(2)}, u32[]{:S(2)}) collective-permute-start(bf16[384,384]{1,0:T(8,128)(2,1)S(1)} %add_bitcast_fusion.p0), channel_id=1, source_target_pairs={{0,2},{1,3},{2,0},{3,1},{4,6},{5,7},{6,4},{7,5},{8,10},{9,11},{10,... | collective-permute-start | bytes 884744 | tf_op jit(solution)/shard_map/ppermute | solution.py:747
  268.8 8.5 %collective-permute-start.16 = (bf16[336,384]{1,0:T(8,128)(2,1)S(1)}, bf16[336,384]{1,0:T(8,128)(2,1)S(1)}, u32[]{:S(2)}, u32[]{:S(2)}) collective-permute-start(bf16[336,384]{1,0:T(8,128)(2,1)S(1)} %add_bitcast_fusion.1.p0), channel_id=1, source_target_pairs={{0,2},{1,3},{2,0},{3,1},{4,6},{5,7},{6,4},{7,5},{8,10},{9,11},{10,... | collective-permute-start | bytes 774152 | tf_op jit(solution)/shard_map/ppermute | solution.py:747
  270.9 6.4 %collective-permute-start.28 = (bf16[384,384]{1,0:T(8,128)(2,1)S(1)}, bf16[384,384]{1,0:T(8,128)(2,1)S(1)}, u32[]{:S(2)}, u32[]{:S(2)}) collective-permute-start(bf16[384,384]{1,0:T(8,128)(2,1)S(1)} %add_bitcast_fusion.p0), channel_id=1, source_target_pairs={{0,1},{1,0},{2,3},{3,2},{4,5},{5,4},{6,7},{7,6},{8,9},{9,8},{10,11... | collective-permute-start | bytes 884744 | tf_op jit(solution)/shard_map/ppermute | solution.py:747
  270.9 6.4 %collective-permute-start.29 = (bf16[384,384]{1,0:T(8,128)(2,1)S(1)}, bf16[384,384]{1,0:T(8,128)(2,1)S(1)}, u32[]{:S(2)}, u32[]{:S(2)}) collective-permute-start(bf16[384,384]{1,0:T(8,128)(2,1)S(1)} %collective-permute-done.27.p1), channel_id=1, source_target_pairs={{0,1},{1,0},{2,3},{3,2},{4,5},{5,4},{6,7},{7,6},{8,9},{9,8},{10,11... | collective-permute-start | bytes 884744 | tf_op jit(solution)/shard_map/ppermute | solution.py:747
  271.4 8.1 %collective-permute-start.17 = (bf16[336,384]{1,0:T(8,128)(2,1)S(1)}, bf16[336,384]{1,0:T(8,128)(2,1)S(1)}, u32[]{:S(2)}, u32[]{:S(2)}) collective-permute-start(bf16[336,384]{1,0:T(8,128)(2,1)S(1)} %add_bitcast_fusion.1.p0), channel_id=1, source_target_pairs={{0,1},{1,0},{2,3},{3,2},{4,5},{5,4},{6,7},{7,6},{8,9},{9,8},{10,11... | collective-permute-start | bytes 774152 | tf_op jit(solution)/shard_map/ppermute | solution.py:747
  277.3 2.3 collective-permute-start.18
  (66 other events, 195.0 us)

commit v4 on v3

v4 whole, which is shorter than its diff:
```python
import jax
import jax.numpy as jnp
from jax import lax
from jax.experimental import pallas as pl
from jax.experimental.pallas import tpu as pltpu
from jax.sharding import PartitionSpec as P

HEADS = 12
UNROLL = 2
HEAD = 64
epsilon = 1e-12
inv_sqrt_two = 0.7071067811865476
inv_sqrt_tau = 0.3989422804014327
f32 = jnp.float32
bf16 = jnp.bfloat16
NN = (((1,), (0,)), ((), ()))
NT = (((1,), (1,)), ((), ()))
TN = (((0,), (0,)), ((), ()))


def mm(a, b, dims=NN):
    return lax.dot_general(a, b, dims, preferred_element_type=f32)


def cost(us):
    return pl.CostEstimate(flops=int(us * 1e9), bytes_accessed=1 << 20, transcendentals=0)


def params(limit=56):
    return pltpu.CompilerParams(
        dimension_semantics=("arbitrary",), vmem_limit_bytes=limit << 20
    )


def whole(shape):
    return pl.BlockSpec(shape, lambda i, *s: (0,) * len(shape), pipeline_mode=pl.Buffered(1))


def vec(size):
    return pl.BlockSpec((size,), lambda i, *s: (0,))


VMEM = pl.BlockSpec(memory_space=pltpu.VMEM)


def far(value):
    return pltpu.with_memory_space_constraint(value, pltpu.HBM)


def apart(dims, kind=f32):
    return pltpu.HBM(dims, kind)


def near(dims, kind=f32):
    return pltpu.VMEM(dims, kind)


def shape(dims, kind=f32):
    return jax.ShapeDtypeStruct(dims, kind)


def norm_parts(values):
    centre = values - jnp.mean(values, -1, keepdims=True)
    inv_std = lax.rsqrt(jnp.mean(centre * centre, -1, keepdims=True) + epsilon)
    return centre * inv_std, inv_std


def norm_back(grad, normed, inv_std, gain):
    scaled = grad * gain
    return inv_std * (
        scaled
        - jnp.mean(scaled, -1, keepdims=True)
        - normed * jnp.mean(scaled * normed, -1, keepdims=True)
    )


def row_sum(values):
    return jnp.sum(values, 0, keepdims=True)


def one_hot(index_row, count):
    rows = lax.broadcasted_iota(jnp.int32, (count, index_row.shape[1]), 0)
    return jnp.where(rows == index_row, 1.0, 0.0).astype(bf16)


def region_forward(features, boxes, target, w_visual, w_box_t, bias, gain, shift):
    rows, feat = features.shape
    width = w_visual.shape[1]
    steps = 4
    part = feat // steps

    def kernel(f_ref, box_ref, t_ref, wv_ref, wb_ref, b_ref, g_ref, s_ref, m_ref, n_ref, i_ref, acc):
        step = pl.program_id(0)
        partial = mm(f_ref[...], wv_ref[...])

        @pl.when(step == 0)
        def _():
            acc[...] = partial + (mm(box_ref[...], wb_ref[...], TN) + b_ref[...])

        @pl.when(step > 0)
        def _():
            acc[...] += partial

        @pl.when(step == steps - 1)
        def _():
            normed, inv = norm_parts(acc[...])
            n_ref[...] = normed
            i_ref[...] = jnp.broadcast_to(inv, i_ref.shape)
            low = (normed * g_ref[...] + s_ref[...]).astype(bf16)
            m_ref[...] = mm(one_hot(t_ref[...], rows), low).astype(bf16)

    return pl.pallas_call(
        kernel,
        grid=(steps,),
        in_specs=[
            pl.BlockSpec((rows, part), lambda i: (0, i)),
            whole(boxes.shape),
            whole((1, rows)),
            pl.BlockSpec((part, width), lambda i: (i, 0)),
            whole(w_box_t.shape),
            vec(width),
            vec(width),
            vec(width),
        ],
        out_specs=[VMEM, whole((rows, width)), whole((rows, 128))],
        out_shape=[near((rows, width), bf16), apart((rows, width)), apart((rows, 128))],
        scratch_shapes=[pltpu.VMEM((rows, width), f32)],
        compiler_params=params(24),
        cost_estimate=cost(3),
        name="region_forward",
    )(far(features), far(boxes), far(target), far(w_visual), w_box_t, far(bias), far(gain), far(shift))


def text_qkv(text, w_qkv, qv_bias):
    rows, width = text.shape

    def kernel(t_ref, w_ref, b_ref, o_ref):
        step = pl.program_id(0)
        bias = b_ref[...] * jnp.where(step == 1, 0.0, 1.0)
        o_ref[...] = (mm(t_ref[...], w_ref[...]) + bias).astype(bf16)

    return pl.pallas_call(
        kernel,
        grid=(3,),
        in_specs=[
            whole((rows, width)),
            pl.BlockSpec((width, width), lambda i: (0, i)),
            pl.BlockSpec((1, width), lambda i: (0, i // 2)),
        ],
        out_specs=pl.BlockSpec((rows, width), lambda i: (0, i)),
        out_shape=apart((rows, 3 * width), bf16),
        compiler_params=params(12),
        cost_estimate=cost(3),
        name="text_qkv",
    )(far(text), far(w_qkv), qv_bias)


def forward(
    scalars, text, text_low, arrived, source, out_grad, w_qkv, qv_bias, w_out, out_bias,
    attn_gain, attn_shift, w_up, up_bias, w_down, down_bias, ffn_gain, ffn_shift, dims,
):
    captions, images = dims
    width = text.shape[1]
    text_len = text.shape[0] // captions
    slots = arrived.shape[0]
    regions = slots // images
    seq = text_len + regions
    rows = captions * seq
    ff = w_up.shape[1]
    half = width // 2
    parts = 4
    part = ff // parts
    grid = captions + parts

    def kernel(
        sc_ref, t_ref, tq_ref, a_ref, src_ref, og_ref, wq_far, qvb_ref, wo_far, ob_ref, ag_ref, as_ref,
        wu_far, ub_ref, wd_far, db_ref, fg_ref, fs_ref,
        out_ref, x_ref, qkv_ref, probs_ref, ctx_ref, an_ref, ai_ref, hid_ref, slope_ref, ds_ref, df_ref,
        sums_ref, wu, wd, send_ref, keep_ref,
        regs, rqkv, act_all, wq, wo, sems,
    ):
        step = pl.program_id(0)

        def third(at):
            cols = slice(at * width, (at + 1) * width)
            return pltpu.make_async_copy(wq_far.at[:, cols], wq.at[:, cols], sems.at[at])

        def load(at):
            source, target = ((wo_far, wo), (wu_far, wu), (wd_far, wd))[at]
            return pltpu.make_async_copy(source, target, sems.at[3 + at])

        @pl.when(step == 0)
        def _():
            for at in range(3):
                third(at).start()
            load(0).start()
            sums_ref[...] = jnp.zeros_like(sums_ref)
            local = mm(one_hot(src_ref[...], slots), a_ref[...], TN).astype(bf16)
            regs[...] = local
            for part_id in range(3):
                at = slice(part_id * width, (part_id + 1) * width)
                third(part_id).wait()
                if part_id == 2:
                    load(1).start()
                    load(2).start()
                got = mm(local, wq[:, at])
                if part_id == 0:
                    got = got + qvb_ref[:, :width]
                if part_id == 2:
                    got = got + qvb_ref[:, width:]
                rqkv[:, at] = got.astype(bf16)

        @pl.when(step < captions)
        def _():
            image = sc_ref[8 + step]
            length = sc_ref[8 + captions + step]
            count = sc_ref[8 + 2 * captions + image]
            at = pl.ds(pl.multiple_of(image * regions, regions), regions)
            here = pl.ds(pl.multiple_of(step * seq, seq), seq)
            x_ref[:text_len, :] = t_ref[...]
            x_ref[text_len:, :] = regs[at, :]
            qkv_ref[:text_len, :] = tq_ref[...]
            qkv_ref[text_len:, :] = rqkv[at, :]
            place = lax.broadcasted_iota(jnp.int32, (seq, 1), 0)
            row_end = jnp.where(place < text_len, length, text_len + count)
            row_mask = jnp.where(place < row_end, 1.0, 0.0)
            key_bias = jnp.where(place < row_end, 0.0, -1e30)
            first = lax.broadcasted_iota(jnp.int32, (1, 2 * HEAD), 1) < HEAD
            scale = [
                jnp.where(first, 0.125, 0.0).astype(bf16),
                jnp.where(first, 0.0, 0.125).astype(bf16),
            ]
            def pair_forward(pair, carry):
                def cols(base):
                    return pl.ds(pl.multiple_of(base + pair * 2 * HEAD, 2 * HEAD), 2 * HEAD)

                q = qkv_ref[:, cols(0)]
                k = qkv_ref[:, cols(width)]
                v = qkv_ref[:, cols(2 * width)]
                scores = mm(k, jnp.concatenate([q * scale[0], q * scale[1]], 0), NT) + key_bias
                raised = jnp.exp(scores - jnp.max(scores, 0, keepdims=True))
                low = (raised * (1.0 / jnp.sum(raised, 0, keepdims=True))).astype(bf16)
                probs_ref[pair] = low
                outs = mm(low, v, TN)
                ctx_ref[:, cols(0)] = jnp.where(first, outs[:seq], outs[seq:]).astype(bf16)
                return carry

            lax.fori_loop(0, HEADS // 2, pair_forward, 0, unroll=UNROLL)

            @pl.when(step == 0)
            def _():
                load(0).wait()

            x_wide = x_ref[...].astype(f32)
            attn_out = mm(ctx_ref[...], wo[...]) + ob_ref[...]
            normed, inv = norm_parts(x_wide + attn_out)
            an_ref[here, :] = normed
            ai_ref[here, :] = jnp.broadcast_to(inv, (seq, 128))
            hidden = normed * ag_ref[...] + as_ref[...]
            hidden_low = hidden.astype(bf16)
            hid_ref[here, :] = hidden_low

            @pl.when(step == 0)
            def _():
                load(1).wait()

            for piece in range(parts):
                at = slice(piece * part, (piece + 1) * part)
                upper = mm(hidden_low, wu[:, at]) + ub_ref[:, at]
                phi = 0.5 * (1.0 + lax.erf(upper * inv_sqrt_two))
                act_all[here, at] = (upper * phi).astype(bf16)
                slope = phi + upper * jnp.exp(-0.5 * upper * upper) * inv_sqrt_tau
                slope_ref[here, at] = slope.astype(bf16)

            @pl.when(step == 0)
            def _():
                load(2).wait()

            ffn_out = mm(act_all[here, :], wd[...]) + db_ref[...]
            ffn_normed, ffn_inv = norm_parts(hidden + ffn_out)
            out_ref[...] = ((ffn_normed * fg_ref[...] + fs_ref[...]) * row_mask).astype(bf16)
            cot = og_ref[...].astype(f32) * row_mask
            second = norm_back(cot, ffn_normed, ffn_inv, fg_ref[...])
            ds_ref[here, :] = second
            low = second.astype(bf16)
            df_ref[here, :] = low
            for at, value in enumerate(
                (
                    cot * ffn_normed,
                    cot,
                    low.astype(f32),
                    row_mask * x_wide * x_wide,
                    row_mask * attn_out * attn_out,
                    row_mask * ffn_out * ffn_out,
                    jnp.broadcast_to(row_mask, (seq, width)),
                )
            ):
                sums_ref[at : at + 1, :] += row_sum(value)

        @pl.when(step >= captions)
        def _():
            acts = pl.ds(pl.multiple_of((step - captions) * part, part), part)
            got = mm(act_all[:, acts], df_ref[...], TN)
            mine = sc_ref[0] == 0
            send_ref[...] = jnp.where(mine, got[:, half:], got[:, :half]).astype(bf16)
            keep_ref[...] = jnp.where(mine, got[:, :half], got[:, half:]).astype(bf16)

    def rowwise(size, cols):
        return pl.BlockSpec((size, cols), lambda i, s: (jnp.minimum(i, captions - 1), 0))

    anywhere = pl.BlockSpec(memory_space=pl.ANY)
    return pl.pallas_call(
        kernel,
        grid_spec=pltpu.PrefetchScalarGridSpec(
            num_scalar_prefetch=1,
            grid=(grid,),
            in_specs=[
                rowwise(text_len, width),
                rowwise(text_len, 3 * width),
                whole((slots, width)),
                whole((1, slots)),
                rowwise(seq, width),
                anywhere,
                whole((1, 2 * width)),
                anywhere,
                vec(width),
                vec(width),
                vec(width),
                anywhere,
                whole((1, ff)),
                anywhere,
                vec(width),
                vec(width),
                vec(width),
            ],
            out_specs=[rowwise(seq, width), rowwise(seq, width), rowwise(seq, 3 * width)]
            + [pl.BlockSpec((HEADS // 2, seq, 2 * seq), lambda i, s: (jnp.minimum(i, captions - 1), 0, 0))]
            + [rowwise(seq, width)]
            + [VMEM] * 9
            + [pl.BlockSpec((part, half), lambda i, s: (jnp.maximum(i - captions, 0), 0))] * 2,
            scratch_shapes=[
                pltpu.VMEM((slots, width), bf16),
                pltpu.VMEM((slots, 3 * width), bf16),
                pltpu.VMEM((rows, ff), bf16),
                pltpu.VMEM(w_qkv.shape, bf16),
                pltpu.VMEM(w_out.shape, bf16),
                pltpu.SemaphoreType.DMA((6,)),
            ],
        ),
        out_shape=[
            apart((rows, width), bf16),
            apart((rows, width), bf16),
            apart((rows, 3 * width), bf16),
            apart((captions * HEADS // 2, seq, 2 * seq), bf16),
            apart((rows, width), bf16),
            near((rows, width)),
            near((rows, 128)),
            near((rows, width), bf16),
            near((rows, ff), bf16),
            near((rows, width)),
            near((rows, width), bf16),
            near((8, width)),
            near(w_up.shape, bf16),
            near(w_down.shape, bf16),
            apart((ff, half), bf16),
            apart((ff, half), bf16),
        ],
        compiler_params=params(33),
        cost_estimate=cost(30),
        name="forward",
    )(
        scalars,
        *(
            far(v)
            for v in (
                text, text_low, arrived, source, out_grad, w_qkv, qv_bias, w_out, out_bias,
                attn_gain, attn_shift, w_up, up_bias, w_down, down_bias, ffn_gain, ffn_shift,
            )
        ),
    )


def ffn_backward(core, d_ffn, d_second, slope, attn_normed, attn_inv, w_down, w_up, attn_gain, seq, hold, first, size, begun):
    rows, width = d_ffn.shape
    ff = w_up.shape[1]
    parts = 4
    part = ff // parts

    def kernel(c_ref, df_ref, ds_ref, sl_ref, an_ref, ai_ref, wd, wu, ag_ref, *rest):
        dup_ref, dr_ref, da_ref, sums_ref, up_ref = rest[len(begun) + len(hold) :]
        step = pl.program_id(0)

        @pl.when(step == 0)
        def _():
            if begun:
                sums_ref[...] = rest[3][...]
                up_ref[...] = rest[4][...]
            else:
                sums_ref[...] = jnp.zeros_like(sums_ref)
                up_ref[...] = jnp.zeros_like(up_ref)

        here = pl.ds(pl.multiple_of((first + step) * seq, seq), seq)
        d_low = df_ref[here, :]
        for piece in range(parts):
            at = slice(piece * part, (piece + 1) * part)
            d_act = mm(d_low, wd[at, :], NT)
            low = (d_act * sl_ref[here, at].astype(f32)).astype(bf16)
            dup_ref[here, at] = low
            up_ref[0:1, at] += row_sum(low.astype(f32))
        d_hidden = ds_ref[here, :] + mm(dup_ref[here, :], wu[...], NT)
        normed = an_ref[here, :]
        resid = norm_back(d_hidden, normed, ai_ref[here, 0:1], ag_ref[...])
        dr_ref[here, :] = resid
        low = resid.astype(bf16)
        da_ref[here, :] = low
        sums_ref[0:1, :] += row_sum(d_hidden * normed)
        sums_ref[1:2, :] += row_sum(d_hidden)
        sums_ref[2:3, :] += row_sum(low.astype(f32))

    return pl.pallas_call(
        kernel,
        grid_spec=pltpu.PrefetchScalarGridSpec(
            num_scalar_prefetch=1,
            grid=(size,),
            in_specs=[VMEM] * 7
            + [vec(width)]
            + [VMEM] * len(begun)
            + [VMEM] * len(hold),
            out_specs=[VMEM] * 5,
        ),
        out_shape=[
            near((rows, ff), bf16),
            near((rows, width)),
            near((rows, width), bf16),
            near((8, width)),
            near((8, ff)),
        ],
        input_output_aliases={9: 0, 10: 1, 11: 2} if begun else {},
        compiler_params=params(6),
        cost_estimate=cost(4 * size),
        name="ffn_backward",
    )(core, d_ffn, d_second, slope, attn_normed, attn_inv, w_down, w_up, attn_gain, *begun, *hold)


def up_gradient(core, hidden_low, d_upper):
    rows, width = hidden_low.shape

    def kernel(c_ref, h_ref, d_ref, send_ref, keep_ref):
        step = pl.program_id(0)
        here = pl.ds(pl.multiple_of(step * width, width), width)
        for to_ref, side in ((send_ref, 1 - c_ref[0]), (keep_ref, c_ref[0])):
            cols = pl.ds(pl.multiple_of((2 * side + step) * width, width), width)
            to_ref[:, here] = mm(h_ref[...], d_ref[:, cols], TN).astype(bf16)

    return pl.pallas_call(
        kernel,
        grid_spec=pltpu.PrefetchScalarGridSpec(
            num_scalar_prefetch=1, grid=(2,), in_specs=[VMEM, VMEM], out_specs=[VMEM, VMEM]
        ),
        out_shape=[near((width, 2 * width), bf16)] * 2,
        compiler_params=params(6),
        cost_estimate=cost(0.1),
        name="up_gradient",
    )(core, hidden_low, d_upper)


def attention_backward(scalars, d_attn, d_resid, probs, qkv, source, w_out, w_qkv, dims, first_caption, size, begun):
    captions, images = dims
    rows, width = d_attn.shape
    seq = rows // captions
    slots = source.shape[1]
    regions = slots // images
    text_len = seq - regions
    last = first_caption + size == captions

    def kernel(
        sc_ref, da_ref, dr_ref, p_ref, qkv_ref, src_ref, wo_ref, wq, *rest,
    ):
        begun_refs = rest[: len(begun)]
        dqkv_ref, text_ref, back_ref, sums_ref, d_img, d_ctx_ref = rest[len(begun) :]
        step = pl.program_id(0)
        here = pl.ds(pl.multiple_of((first_caption + step) * seq, seq), seq)

        @pl.when(step == 0)
        def _():
            if begun:
                sums_ref[...] = begun_refs[3][...]
                d_img[...] = begun_refs[2][...]
            else:
                sums_ref[...] = jnp.zeros_like(sums_ref)
                d_img[...] = jnp.zeros_like(d_img)

        d_ctx_ref[...] = mm(da_ref[here, :], wo_ref[...], NT).astype(bf16)
        first = lax.broadcasted_iota(jnp.int32, (1, 2 * HEAD), 1) < HEAD
        masks = [jnp.where(first, 1.0, 0.0).astype(bf16), jnp.where(first, 0.0, 1.0).astype(bf16)]
        def pair_backward(pair, carry):
            def cols(base):
                return pl.ds(pl.multiple_of(base + pair * 2 * HEAD, 2 * HEAD), 2 * HEAD)

            q = qkv_ref[here, cols(0)]
            k = qkv_ref[here, cols(width)]
            v = qkv_ref[here, cols(2 * width)]
            d_c = d_ctx_ref[:, cols(0)]
            both_c = jnp.concatenate([d_c * masks[0], d_c * masks[1]], 0)
            both_q = jnp.concatenate([q * masks[0], q * masks[1]], 0)
            low = p_ref[(first_caption + step) * (HEADS // 2) + pair]
            d_probs = mm(v, both_c, NT)
            wide = low.astype(f32)
            both = wide * d_probs
            inner = jnp.sum(both, 0, keepdims=True)
            d_scores = (both - wide * inner).astype(bf16)
            d_q = mm(d_scores, k, TN) * 0.125
            dqkv_ref[here, cols(0)] = jnp.where(first, d_q[:seq], d_q[seq:]).astype(bf16)
            dqkv_ref[here, cols(width)] = (mm(d_scores, both_q) * 0.125).astype(bf16)
            dqkv_ref[here, cols(2 * width)] = mm(low, both_c).astype(bf16)
            return carry

        lax.fori_loop(0, HEADS // 2, pair_backward, 0, unroll=UNROLL)

        sums_ref[0:1, :] += row_sum(dqkv_ref[here, :width].astype(f32))
        sums_ref[1:2, :] += row_sum(dqkv_ref[here, 2 * width :].astype(f32))
        d_x = mm(dqkv_ref[here, :], wq[...], NT) + dr_ref[here, :]
        text_ref[...] = d_x[:text_len]
        at = pl.ds(pl.multiple_of(sc_ref[8 + first_caption + step] * regions, regions), regions)
        d_img[at, :] += d_x[text_len:]

        @pl.when(step == size - 1)
        def _():
            if last:
                back_ref[...] = mm(one_hot(src_ref[...], slots), d_img[...].astype(bf16)).astype(bf16)
            else:
                back_ref[...] = d_img[...]

    return pl.pallas_call(
        kernel,
        grid_spec=pltpu.PrefetchScalarGridSpec(
            num_scalar_prefetch=1,
            grid=(size,),
            in_specs=[VMEM] * 4
            + [whole((1, slots)), VMEM, VMEM]
            + ([VMEM, pl.BlockSpec(memory_space=pl.ANY)] + [VMEM, VMEM] if begun else []),
            out_specs=[
                VMEM,
                pl.BlockSpec((text_len, width), lambda i, s: (i + first_caption, 0)),
                VMEM,
                VMEM,
            ],
            scratch_shapes=[
                pltpu.VMEM((slots, width), f32),
                pltpu.VMEM((seq, width), bf16),
            ],
        ),
        out_shape=[
            near((rows, 3 * width), bf16),
            pltpu.HBM((captions * text_len, width), f32),
            near((slots, width), bf16 if last else f32),
            near((8, width)),
        ],
        input_output_aliases={8: 0, 9: 1} if begun else {},
        compiler_params=params(11),
        cost_estimate=cost(5 * size),
        name="attention_backward",
    )(scalars, d_attn, d_resid, probs, qkv, source, w_out, w_qkv, *begun)


def qkvo_gradient(core, x, d_qkv, context, d_attn):
    rows, width = x.shape

    def kernel(c_ref, x_ref, dq_ref, ctx_ref, da_ref, send_ref, keep_ref):
        step = pl.program_id(0)
        block = lax.rem(step + 2 * (1 - c_ref[0]), 4)
        cols = pl.ds(pl.multiple_of(jnp.minimum(block, 2) * width, width), width)

        def gradient(to_ref):
            @pl.when(block < 3)
            def _():
                to_ref[...] = mm(x_ref[...], dq_ref[:, cols], TN).astype(bf16)

            @pl.when(block == 3)
            def _():
                to_ref[...] = mm(ctx_ref[...], da_ref[...], TN).astype(bf16)

        @pl.when(step < 2)
        def _():
            gradient(send_ref)

        @pl.when(step >= 2)
        def _():
            gradient(keep_ref)

    return pl.pallas_call(
        kernel,
        grid_spec=pltpu.PrefetchScalarGridSpec(
            num_scalar_prefetch=1,
            grid=(4,),
            in_specs=[VMEM] * 4,
            out_specs=[
                pl.BlockSpec((width, width), lambda i, s: (0, jnp.minimum(i, 1))),
                pl.BlockSpec((width, width), lambda i, s: (0, jnp.maximum(i - 2, 0))),
            ],
        ),
        out_shape=[apart((width, 2 * width), bf16)] * 2,
        compiler_params=params(11),
        cost_estimate=cost(5),
        name="qkvo_gradient",
    )(core, x, d_qkv, context, d_attn)


def region_backward(
    core, returned, target, normed, inv, gain, features, boxes, w_visual, w_box_t,
    sums_forward, sums_ffn, sums_up, sums_attn, groups,
):
    rows, width = returned.shape
    feat = features.shape[1]
    half = width // 2
    steps = 4
    part = feat // steps
    quarter = feat // groups // 4
    tall = quarter + 8
    per_step = groups // steps
    box = boxes.shape[0]
    share = width // groups
    ff_share = sums_up.shape[1] // groups

    def kernel(
        c_ref, r_ref, t_ref, n_ref, i_ref, g_ref, f_ref, box_ref, wv_ref, wb_ref, sf_ref, sn_ref, su_ref, sa_ref,
        send_ref, keep_ref, fg_ref, bg_ref, dpre, small,
    ):
        step = pl.program_id(0)

        @pl.when(step == 0)
        def _():
            d_region = mm(one_hot(t_ref[...], rows), r_ref[...], TN)
            normed = n_ref[...]
            low = norm_back(d_region, normed, i_ref[:, 0:1], g_ref[...]).astype(bf16)
            dpre[...] = low
            bg_ref[...] = mm(wb_ref[...], low, NT)
            boxes_grad = mm(box_ref[...], low)
            vectors = [
                row_sum(low.astype(f32)),
                row_sum(d_region * normed),
                row_sum(d_region),
                sf_ref[0:1, :],
                sf_ref[1:2, :],
                sf_ref[2:3, :],
                sn_ref[0:1, :],
                sn_ref[1:2, :],
                sn_ref[2:3, :],
            ] + [boxes_grad[at : at + 1] for at in range(box)]
            small[...] = jnp.zeros_like(small)
            lane = lax.broadcasted_iota(jnp.int32, (1, half), 1)
            stats = jnp.zeros((1, half), f32)
            for at in range(4):
                total = jnp.sum(sf_ref[3 + at : 4 + at, :], 1, keepdims=True)
                stats = jnp.where(lane == at, total, stats)
            for group in range(groups):
                small[group, 0:1, 0:ff_share] = su_ref[0:1, group * ff_share : (group + 1) * ff_share]
                for side in range(2):
                    first = group * 2 * share
                    flat = jnp.concatenate([sa_ref[0:1, :], sa_ref[1:2, :]], 1)
                    small[group, 1:2, 0 : 2 * share] = flat[:, first : first + 2 * share]
                for at, value in enumerate(vectors):
                    row, col = (1, 2) if at == 0 else (2 + (at - 1) // 3, (at - 1) % 3)
                    small[group, row : row + 1, 128 * col : 128 * col + share] = value[
                        :, group * share : (group + 1) * share
                    ]
                small[group, 6:7, :] = stats

        got = mm(f_ref[...], dpre[...], TN)
        mine = c_ref[0] == 0
        for to_ref, low_half in ((send_ref, jnp.logical_not(mine)), (keep_ref, mine)):
            chosen = jnp.where(low_half, got[:, :half], got[:, half:]).astype(bf16)
            for group in range(per_step):
                for bit in range(2):
                    for piece in range(2):
                        at = ((group * 2 + bit) * 2 + piece) * quarter
                        to_ref[group, bit, piece, :quarter, :] = chosen[at : at + quarter]
                        if piece == 0:
                            to_ref[group, bit, piece, quarter:, :] = small[step * per_step + group].astype(bf16)
                        else:
                            to_ref[group, bit, piece, quarter:, :] = jnp.zeros((8, half), bf16)
        fg_ref[...] = mm(dpre[...], wv_ref[...], NT)

    out = pl.BlockSpec((per_step, 2, 2, tall, half), lambda i, s: (i, 0, 0, 0, 0))
    return pl.pallas_call(
        kernel,
        grid_spec=pltpu.PrefetchScalarGridSpec(
            num_scalar_prefetch=1,
            grid=(steps,),
            in_specs=[
                whole((rows, width)),
                whole((1, rows)),
                whole((rows, width)),
                whole((rows, 128)),
                vec(width),
                pl.BlockSpec((rows, part), lambda i, s: (0, i)),
                whole(boxes.shape),
                pl.BlockSpec((part, width), lambda i, s: (i, 0)),
                whole(w_box_t.shape),
                whole(sums_forward.shape),
                whole(sums_ffn.shape),
                whole(sums_up.shape),
                whole(sums_attn.shape),
            ],
            out_specs=[out, out, pl.BlockSpec((rows, part), lambda i, s: (0, i)), whole((box, rows))],
            scratch_shapes=[pltpu.VMEM((rows, width), bf16), pltpu.VMEM((groups, 8, half), f32)],
        ),
        out_shape=[
            pltpu.HBM((groups, 2, 2, tall, half), bf16),
            pltpu.HBM((groups, 2, 2, tall, half), bf16),
            pltpu.HBM((rows, feat), f32),
            shape((box, rows)),
        ],
        compiler_params=params(20),
        cost_estimate=cost(6),
        name="region_backward",
    )(
        core, returned, far(target), far(normed), far(inv), far(gain), far(features), far(boxes), far(w_visual),
        w_box_t, sums_forward, sums_ffn, sums_up, sums_attn,
    )


def device_number():
    return lax.axis_index("dp") * lax.axis_size("enc") + lax.axis_index("enc")


def swap(values, bit):
    count = lax.axis_size("dp") * lax.axis_size("enc")
    return lax.ppermute(values, ("dp", "enc"), [(i, i ^ bit) for i in range(count)])


def add(a, b):
    return (a.astype(f32) + b.astype(f32)).astype(bf16)


def scalar_call(kernel, bits, ins, in_specs, outs, out_specs, grid, limit, name, last=False, place=near):
    outs = outs if last else [place(o.shape, o.dtype) for o in outs]
    return pl.pallas_call(
        kernel,
        grid_spec=pltpu.PrefetchScalarGridSpec(
            num_scalar_prefetch=1, grid=(grid,), in_specs=in_specs, out_specs=out_specs
        ),
        out_shape=outs,
        compiler_params=params(limit),
        cost_estimate=cost(1),
        name=name,
    )(bits, *ins)


def first_split(bits, kept, got, groups, place=near):
    tall = kept.ndim == 5
    high = groups // 2
    if tall:
        rows, cols = kept.shape[3:]
        view = (high, 2, 2, 2, rows, cols)
        block = (1, 2, 2, 2, rows, cols)
    else:
        rows, cols = kept.shape[0] // groups, kept.shape[1] // 4
        view = (high, 2, rows, 4 * cols)
        block = (1, 2, rows, 4 * cols)

    def kernel(b_ref, k_ref, r_ref, a_send, a_keep, b_send, b_keep):
        bit2, bit4 = b_ref[1], b_ref[2]

        def total(y, x, piece):
            if tall:
                return add(k_ref[0, y, x, piece], r_ref[0, y, x, piece])
            at = pl.ds(pl.multiple_of((2 * x + piece) * cols, 128), cols)
            return add(k_ref[0, y, :, at], r_ref[0, y, :, at])

        for other in range(2):
            a_send[0, other] = total(other, 1 - bit2, 0)
            a_keep[0, other] = total(other, bit2, 0)
            b_send[0, other] = total(1 - bit4, other, 1)
            b_keep[0, other] = total(bit4, other, 1)

    spec = pl.BlockSpec(block, lambda i, s: (i,) + (0,) * (len(block) - 1))
    out = pl.BlockSpec((1, 2, rows, cols), lambda i, s: (i, 0, 0, 0))
    return scalar_call(
        kernel, bits, (kept.reshape(view), got.reshape(view)), [spec, spec],
        [shape((high, 2, rows, cols), bf16)] * 4, [out] * 4, high, 6, "first_split", place=place,
    )


def second_split(bits, a_kept, a_got, b_kept, b_got):
    high, _, rows, cols = a_kept.shape

    def kernel(b_ref, ak, ar, bk, br, a_send, a_keep, b_send, b_keep):
        bit2, bit4 = b_ref[1], b_ref[2]
        a_send[0] = add(ak[0, 1 - bit4], ar[0, 1 - bit4])
        a_keep[0] = add(ak[0, bit4], ar[0, bit4])
        b_send[0] = add(bk[0, 1 - bit2], br[0, 1 - bit2])
        b_keep[0] = add(bk[0, bit2], br[0, bit2])

    spec = pl.BlockSpec((1, 2, rows, cols), lambda i, s: (i, 0, 0, 0))
    out = pl.BlockSpec((1, rows, cols), lambda i, s: (i, 0, 0))
    return scalar_call(
        kernel, bits, (a_kept, a_got, b_kept, b_got), [spec] * 4,
        [shape((high, rows, cols), bf16)] * 4, [out] * 4, high, 6, "second_split",
    )


def join_split(bits, pairs, place=near):
    high, _, cols = pairs[0][0].shape
    sizes = [kept.shape[1] for kept, _ in pairs]

    def kernel(b_ref, *refs):
        bit = b_ref[3]
        send, keep = refs[-2:]
        at = 0
        for n, size in enumerate(sizes):
            kept, got = refs[2 * n : 2 * n + 2]
            send[0, at : at + size] = add(kept[1 - bit], got[1 - bit])
            keep[0, at : at + size] = add(kept[bit], got[bit])
            at += size

    ins = [value for pair in pairs for value in pair]
    specs = [pl.BlockSpec((2, v.shape[1], cols), lambda i, s: (i, 0, 0)) for v in ins]
    out = pl.BlockSpec((1, sum(sizes), cols), lambda i, s: (i, 0, 0))
    return scalar_call(
        kernel, bits, ins, specs, [shape((high // 2, sum(sizes), cols), bf16)] * 2, [out] * 2,
        high // 2, 6, "join_split", place=place,
    )


def late_split(bits, kept, got, which):
    high, rows, cols = kept.shape

    def kernel(b_ref, k_ref, r_ref, send, keep):
        bit = b_ref[which]
        send[0] = add(k_ref[1 - bit], r_ref[1 - bit])
        keep[0] = add(k_ref[bit], r_ref[bit])

    spec = pl.BlockSpec((2, rows, cols), lambda i, s: (i, 0, 0))
    out = pl.BlockSpec((1, rows, cols), lambda i, s: (i, 0, 0))
    return scalar_call(
        kernel, bits, (kept, got), [spec] * 2, [shape((high // 2, rows, cols), bf16)] * 2, [out] * 2,
        high // 2, 6, "late_split",
    )


def over_two(halves):
    return swap(halves[0], 2), halves[1], swap(halves[2], 4), halves[3]


def over_other_two(halves):
    return swap(halves[0], 4), halves[1], swap(halves[2], 2), halves[3]


def second(bits, moved):
    return second_split(bits, moved[1], moved[0], moved[3], moved[2])


def join(bits, *moved, place=near):
    pairs = []
    for one in moved:
        pairs += [(one[1], one[0]), (one[3], one[2])]
    return join_split(bits, pairs, place)


def after_all(*trees):
    leaves, tree = jax.tree.flatten(trees)
    return jax.tree.unflatten(tree, lax.optimization_barrier(leaves))


def late_first(bits, kept, got):
    if kept.shape[0] == 1:
        return (kept + got,)
    return late_split(bits, kept, got, 4)


def late_move(halves):
    return swap(halves[0], 16) if len(halves) > 1 else None


def late_rest(bits, halves, moved):
    bit, which = 16, 5
    while len(halves) > 1:
        if halves[1].shape[0] == 1:
            halves = (halves[1] + moved,)
        else:
            halves = late_split(bits, halves[1], moved, which)
            bit, which = 2 * bit, which + 1
            moved = swap(halves[0], bit)
    return halves[0][0]


def spread(mine):
    over_x = swap(mine, 2)
    return mine, over_x, swap(mine, 1), swap(over_x, 1)


def pick(b_ref, pieces, core, x):
    mine, over_x, over_core, over_both = pieces
    same_x = b_ref[1] == x
    return jnp.where(
        b_ref[0] == core, jnp.where(same_x, mine, over_x), jnp.where(same_x, over_core, over_both)
    ).astype(f32)


def finish_down(bits, pieces):
    rows, cols = pieces[0].shape

    def kernel(b_ref, p0, p1, p2, p3, down_ref):
        for core in range(2):
            for x in range(2):
                got = pick(b_ref, (p0[...], p1[...], p2[...], p3[...]), core, x)
                down_ref[x * rows : (x + 1) * rows, core * cols : (core + 1) * cols] = got

    outs = [shape((2 * rows, 2 * cols))]
    return scalar_call(
        kernel, bits, pieces, [whole((rows, cols))] * 4, outs, [whole(o.shape) for o in outs], 1, 8, "finish_down", True
    )[0]


def finish_wide(bits, pieces, sizes):
    rows, cols = pieces[0].shape
    part = rows // 2

    def kernel(b_ref, p0, p1, p2, p3, *out_refs):
        for core in range(2):
            for x in range(2):
                got = pick(b_ref, (p0[...], p1[...], p2[...], p3[...]), core, x)
                for piece in range(2):
                    at = ((core * 2 + x) * 2 + piece) * cols
                    for out_ref, size in zip(out_refs, sizes):
                        if 0 <= at < size:
                            out_ref[:, at : at + cols] = got[piece * part : (piece + 1) * part]
                        at -= size

    outs = [shape((part, size)) for size in sizes]
    return scalar_call(
        kernel, bits, pieces, [whole((rows, cols))] * 4, outs, [whole(o.shape) for o in outs], 1, 8, "finish_wide", True
    )


def finish_visual(bits, pieces, ff_share, share, box):
    rows, cols = pieces[0].shape
    tall = rows // 2
    quarter = tall - 8
    sizes = [share] * 9 + [2 * share, ff_share]

    def kernel(b_ref, p0, p1, p2, p3, vis_ref, box_ref, rms_ref, *small_refs):
        for core in range(2):
            for x in range(2):
                got = pick(b_ref, (p0[...], p1[...], p2[...], p3[...]), core, x)
                for piece in range(2):
                    low = piece * tall
                    vis_ref[(2 * x + piece) * quarter : (2 * x + piece + 1) * quarter, core * cols : (core + 1) * cols] = got[
                        low : low + quarter
                    ]
        small = p0[quarter : quarter + 8, :].astype(f32)
        for at in range(9):
            row, col = (1, 2) if at == 0 else (2 + (at - 1) // 3, (at - 1) % 3)
            small_refs[at][...] = small[row, 128 * col : 128 * col + share]
        small_refs[9][...] = small[1, 0 : 2 * share]
        small_refs[10][...] = small[0, 0:ff_share]
        for at in range(9, 9 + box):
            row, col = 2 + (at - 1) // 3, (at - 1) % 3
            box_ref[at - 9 : at - 8, :] = small[row : row + 1, 128 * col : 128 * col + share]
        stats = small[6, 0:128]
        total = jnp.sum(small[6:7, 3:4])
        rms_ref[...] = jnp.sqrt(stats / total)[:3]

    outs = [shape((4 * quarter, 2 * cols)), shape((box, share)), shape((3,))] + [shape((size,)) for size in sizes]
    specs = [whole(o.shape) for o in outs[:2]] + [vec(3)] + [vec(size) for size in sizes]
    return scalar_call(
        kernel, bits, pieces, [whole((rows, cols))] * 4, outs, specs, 1, 8, "finish_visual", True
    )


def gate(value, *others):
    return lax.optimization_barrier((value, *others))[0]


def on_device(
    text_embed,
    region_features,
    boxes,
    caption_image,
    caption_lengths,
    region_counts,
    region_target,
    region_source,
    w_visual,
    w_box,
    visual_bias,
    visual_gain,
    visual_shift,
    w_qkv,
    qv_bias,
    w_out,
    out_bias,
    attn_gain,
    attn_shift,
    w_up,
    up_bias,
    w_down,
    down_bias,
    ffn_gain,
    ffn_shift,
    out_grad,
):
    width = text_embed.shape[1]
    captions = caption_image.shape[0]
    images = region_counts.shape[0]
    dims = (captions, images)
    axes = ("dp", "enc")
    groups = lax.axis_size("dp")
    count = groups * lax.axis_size("enc")
    me = device_number().astype(jnp.int32)
    places = lax.iota(jnp.int32, 8)
    scalars = jnp.concatenate([(me >> places) & 1, caption_image, caption_lengths, region_counts])
    w_box_t = w_box.T
    row = lambda v: v.reshape(1, -1)
    qv_row = row(qv_bias)

    message, vis_normed, vis_inv = region_forward(
        region_features, boxes, region_target, w_visual, w_box_t, visual_bias, visual_gain, visual_shift
    )
    arrived = lax.all_to_all(message, axes, split_axis=0, concat_axis=0, tiled=True)
    text_low = text_qkv(text_embed, w_qkv, qv_row)
    (
        out_rows, x, qkv, probs, context, attn_normed, attn_inv, hidden_low, slope, d_second, d_ffn,
        sums_forward, w_up_near, w_down_near, down_sent, down_kept,
    ) = forward(
        scalars, text_embed, text_low, arrived, region_source, out_grad, w_qkv, qv_row, w_out,
        out_bias, attn_gain, attn_shift, w_up, row(up_bias), w_down, down_bias, ffn_gain, ffn_shift, dims,
    )
    seq = x.shape[0] // captions
    rest = captions - 1
    bits = core = scalars
    hold = ()
    ffn_ins = (d_ffn, d_second, slope, attn_normed, attn_inv, w_down_near, w_up_near, attn_gain, seq, hold)
    down_view = (groups, 2, 2, w_down.shape[0] // groups // 4, width // 2)
    down_sent, down_kept = down_sent.reshape(down_view), down_kept.reshape(down_view)

    moved = swap(down_sent, 1)
    begun = ffn_backward(core, *ffn_ins, 0, 1, ())

    moved, begun, sc = after_all(moved, begun, scalars)
    down = first_split(sc, down_kept, moved, groups)
    down, begun, sc = after_all(down, begun, sc)
    moved = over_two(down)
    d_upper, d_resid, d_attn, sums_ffn, sums_up = ffn_backward(sc, *ffn_ins, 1, rest, tuple(begun))
    up_sent, up_kept = up_gradient(sc, hidden_low, gate(d_upper, d_attn))

    moved, up_sent, up_kept, d_attn, sc = after_all(moved, up_sent, up_kept, d_attn, sc)
    down = second(sc, moved)
    down, up_sent, up_kept, sc = after_all(down, up_sent, up_kept, sc)
    moved = over_other_two(down), swap(up_sent, 1)
    att_ins = (d_attn, d_resid, probs, qkv, region_source, w_out, w_qkv, dims)
    begun = attention_backward(sc, *att_ins, 0, 1, ())

    moved, up_kept, begun, sc = after_all(moved, up_kept, begun, sc)
    up = first_split(sc, up_kept, moved[1], groups)
    down = join(sc, moved[0])
    down, up, begun, sc = after_all(down, up, begun, sc)
    moved = over_two(up), swap(down[0], 8)
    d_qkv, text_grad, back_message, sums_attn = attention_backward(sc, *att_ins, 1, rest, tuple(begun))

    moved, down, d_qkv, back_message, sc = after_all(moved, down, d_qkv, back_message, sc)
    up = second(sc, moved[0])
    down = late_first(sc, down[1], moved[1])
    up, down, sc = after_all(up, down, sc)
    moved = over_other_two(up), late_move(down)
    qkvo_sent, qkvo_kept = qkvo_gradient(sc, x, d_qkv, context, d_attn)

    moved, down, qkvo_sent, qkvo_kept, back_message, sc = after_all(
        moved, down, qkvo_sent, qkvo_kept, back_message, sc
    )
    up = join(sc, moved[0], place=apart)
    down = late_rest(sc, down, moved[1])
    up, down, qkvo_sent, qkvo_kept, back_message, sc = after_all(up, down, qkvo_sent, qkvo_kept, back_message, sc)
    returned = lax.all_to_all(back_message, axes, split_axis=0, concat_axis=0, tiled=True)
    qkvo = first_split(sc, qkvo_kept, swap(qkvo_sent, 1), groups, apart)
    up_moved = swap(up[0], 8)
    down = spread(down)

    qkvo_moved = over_two(qkvo)
    returned, sc = after_all(returned, gate(sc, *qkvo))
    vis_sent, vis_kept, feature_grad, box_grad = region_backward(
        sc, returned, region_target, vis_normed, vis_inv, visual_gain,
        region_features, boxes, w_visual, w_box_t, sums_forward, sums_ffn, sums_up, sums_attn, groups,
    )

    up_moved, qkvo_moved, vis_sent, vis_kept, sc = after_all(up_moved, qkvo_moved, vis_sent, vis_kept, sc)
    up = late_first(sc, up[1], up_moved)
    qkvo = second(sc, qkvo_moved)
    up, qkvo, vis_sent, sc = after_all(up, qkvo, vis_sent, sc)
    vis_moved = swap(vis_sent, 1)
    qkvo_moved = over_other_two(qkvo)
    up_moved = late_move(up)
    vis = first_split(sc, vis_kept, vis_moved, groups)
    vis_moved = over_two(vis)
    g_down = finish_down(gate(sc, *vis), down)
    sc = gate(sc, g_down)
    qkvo = join(sc, qkvo_moved)
    qkvo_moved = swap(qkvo[0], 8)
    up = spread(late_rest(sc, up, up_moved))
    vis = second(sc, vis_moved)
    vis_moved = over_other_two(vis)
    qkvo = late_first(sc, qkvo[1], qkvo_moved)
    qkvo_moved = late_move(qkvo)
    vis = join(sc, vis_moved)
    vis_moved = swap(vis[0], 8)
    (g_up,) = finish_wide(gate(sc, *vis), up, (4 * width,))
    sc = gate(sc, g_up)
    qkvo = spread(late_rest(sc, qkvo, qkvo_moved))
    vis = late_first(sc, vis[1], vis_moved)
    vis_moved = late_move(vis)
    g_qkv, g_out = finish_wide(gate(sc, *vis), qkvo, (3 * width, width))
    vis = late_rest(gate(sc, g_qkv), vis, vis_moved)
    vis = spread(gate(vis, g_qkv))
    g_visual, g_box_t, rms_values, *small = finish_visual(
        sc, vis, w_up.shape[1] // groups, width // groups, boxes.shape[0]
    )
    return (
        out_rows,
        text_grad,
        feature_grad,
        box_grad,
        rms_values,
        g_visual,
        g_box_t.T,
        small[0],
        small[1],
        small[2],
        g_qkv,
        small[9],
        g_out,
        small[8],
        small[6],
        small[7],
        g_up,
        small[10],
        g_down,
        small[5],
        small[3],
        small[4],
    )


def solution(mesh):
    return jax.shard_map(
        on_device,
        mesh=mesh,
        in_specs=(
            P(("dp", "enc"), None),
            P(("dp", "enc"), None),
            P(None, ("dp", "enc")),
            P(("dp", "enc")),
            P(("dp", "enc")),
            P(("dp", "enc")),
            P(("dp", "enc"), None),
            P(("dp", "enc"), None),
            P(),
            P(),
            P(),
            P(),
            P(),
            P(),
            P(),
            P(),
            P(),
            P(),
            P(),
            P(),
            P(),
            P(),
            P(),
            P(),
            P(),
            P(("dp", "enc"), None),
        ),
        out_specs=(
            P(("dp", "enc"), None),
            P(("dp", "enc"), None),
            P(("dp", "enc"), None),
            P(None, ("dp", "enc")),
            P(),
            P("dp", None),
            P("dp", None),
            P("dp"),
            P("dp"),
            P("dp"),
            P("dp", None),
            P("dp"),
            P("dp", None),
            P("dp"),
            P("dp"),
            P("dp"),
            P("dp", None),
            P("dp"),
            P("dp", None),
            P("dp"),
            P("dp"),
            P("dp"),
        ),
        check_vma=False,
    )
```

time: 284 us -> 220 us (0.77)
  local copies, waits for them, and re-layouts: 41.8 us -> 4.39 us
  waiting for transfers between devices: 80.3 us -> 45.6 us
  starting transfers between devices: 39.3 us -> 45 us
  Pallas kernels: 120 us -> 123 us
    ppermute x30 -> x40, waiting for transfers between devices: 71.9 us -> 33.8 us  [swap(): lax.ppermute(values, ('dp', 'enc'), [(i, i ^ bit) for i in range(count)])]
    unnamed x165 -> x48, local copies, waits for them, and re-layouts: 41.2 us -> 4.39 us
    pallas_call x1 -> x2, Pallas kernels: 16.5 us -> 10.8 us  [ffn_backward(): pl.pallas_call(kernel, grid_spec=pltpu.PrefetchScalarGridSpec(num_scalar_...]
    ppermute x30 -> x40, starting transfers between devices: 28.4 us -> 33.6 us  [swap(): lax.ppermute(values, ('dp', 'enc'), [(i, i ^ bit) for i in range(count)])]
    all_to_all x1, waiting for transfers between devices: 0.01 us -> 3.85 us  [on_device(): lax.all_to_all(back_message, axes, split_axis=0, concat_axis=0, tiled=True)]
    pallas_call x1, Pallas kernels: 2.68 us -> 5.76 us  [region_forward(): pl.pallas_call(kernel, grid=(steps,), in_specs=[pl.BlockSpec((rows, part)...]
    pallas_call x14 -> x20, Pallas kernels: 23.4 us -> 24.7 us  [scalar_call(): pl.pallas_call(kernel, grid_spec=pltpu.PrefetchScalarGridSpec(num_scalar_...]
    pallas_call x1 -> x2, Pallas kernels: 18.3 us -> 18.2 us  [attention_backward(): pl.pallas_call(kernel, grid_spec=pltpu.PrefetchScalarGridSpec(num_scalar_...]
  transfers between devices with their start and end apart: 32 -> 42, of which waited for: 10 -> 21; matrix products, arithmetic and copies ran while one was open for 0% -> 0% of each run, Pallas kernels for 24% -> 31%
where the time goes in v4:
time: 220 us; the launch traced here: 219 us
  Pallas kernels  123 us (56%)
  waiting for transfers between devices  45.6 us (21%)
  starting transfers between devices  45 us (20%)
  local copies, waits for them, and re-layouts  4.39 us (2%)
    pallas_call x1, Pallas kernels, forward(): pl.pallas_call(kernel, grid_spec=pltpu.PrefetchScalarGridSpec(num_scalar_...  38.8 us
    ppermute x40, waiting for transfers between devices, swap(): lax.ppermute(values, ('dp', 'enc'), [(i, i ^ bit) for i in range(count)])  33.8 us
    ppermute x40, starting transfers between devices, swap(): lax.ppermute(values, ('dp', 'enc'), [(i, i ^ bit) for i in range(count)])  33.6 us
    pallas_call x20, Pallas kernels, scalar_call(): pl.pallas_call(kernel, grid_spec=pltpu.PrefetchScalarGridSpec(num_scalar_...  24.7 us
    pallas_call x2, Pallas kernels, attention_backward(): pl.pallas_call(kernel, grid_spec=pltpu.PrefetchScalarGridSpec(num_scalar_...  18.2 us
    pallas_call x2, Pallas kernels, ffn_backward(): pl.pallas_call(kernel, grid_spec=pltpu.PrefetchScalarGridSpec(num_scalar_...  10.8 us
    all_to_all x1, waiting for transfers between devices, on_device(): lax.all_to_all(message, axes, split_axis=0, concat_axis=0, tiled=True)  7.99 us
    pallas_call x1, Pallas kernels, region_backward(): pl.pallas_call(kernel, grid_spec=pltpu.PrefetchScalarGridSpec(num_scalar_...  7.68 us
  transfers between devices with their start and end apart: 42, of which 21 were waited for; matrix products, arithmetic and copies ran while one was open for 0% of the time, Pallas kernels for 31%

profile of v4, /device:TPU:0, one launch (start us, length us, event | category | flops | bytes accessed | tf_op | source)
XLA Modules:
  0.0 219.1 jit_solution(12559939694654908273)
XLA Ops:
  1.4 5.8 %region_forward.1 = (bf16[256,768]{1,0:T(8,128)(2,1)}, f32[256,768]{1,0:T(8,128)}, f32[256,128]{1,0:T(8,128)}) custom-call(bf16[256,2048]{1,0:T(8,128)(2,1)} %f_ref.3, bf16[4,256]{1,0:T(4,128)(2,1)} %box_ref.3, s32[1,256]{1,0:T(1,128)} %t_ref.7, bf16[2048,768]{1,0:T(8,128)(2,1)} %wv_ref.3, bf16[4,768]{1,0:T(4,128)(2,1)S(1)} %bitcast.31, f32[768]{0:T(1024)} %b_ref.1, ...), custom_call_target="tpu_custom_call" | custom-call | flops 3000000000 | bytes 1048576 | tf_op jit(solution)/shard_map/region_forward/pallas_call | solution.py:112
  7.1 7.3 %all-to-all-start = ((bf16[32,8,768]{2,1,0:T(8,128)(2,1)}), bf16[32,8,768]{2,1,0:T(8,128)(2,1)S(1)}, u32[]{:S(2)}, u32[]{:S(2)}) async-start(bf16[32,8,768]{2,1,0:T(8,128)(2,1)} %bitcast.1), calls=%async_computation | async-start | bytes 786432 | tf_op jit(solution)/shard_map/all_to_all | solution.py:1021
  14.6 5.0 %text_qkv.1.tq_ref = bf16[384,2304]{1,0:T(8,128)(2,1)} custom-call(bf16[384,768]{1,0:T(8,128)(2,1)} %t_ref.6, bf16[768,2304]{1,0:T(8,128)(2,1)} %wq.3, f32[1,1536]{1,0:T(1,128)S(1)} %reshape.78.b_ref.qvb_ref), custom_call_target="tpu_custom_call" | custom-call | flops 3000000000 | bytes 1048576 | tf_op jit(solution)/shard_map/text_qkv/pallas_call | solution.py:142
  19.6 8.0 %all-to-all-done = bf16[32,8,768]{2,1,0:T(8,128)(2,1)S(1)} async-done(((bf16[32,8,768]{2,1,0:T(8,128)(2,1)}), bf16[32,8,768]{2,1,0:T(8,128)(2,1)S(1)}, u32[]{:S(2)}, u32[]{:S(2)}) %all-to-all-start) | async-done | bytes 393248 | tf_op jit(solution)/shard_map/all_to_all | solution.py:1021
  28.4 38.8 %forward.1 = (bf16[768,768]{1,0:T(8,128)(2,1)}, bf16[768,768]{1,0:T(8,128)(2,1)}, bf16[768,2304]{1,0:T(8,128)(2,1)}, bf16[18,256,512]{2,1,0:T(8,128)(2,1)}, bf16...) custom-call(s32[16]{0:T(128)S(1)} %pad_add_fusion.sc_ref.c_ref.b_ref, ...), custom_call_target="tpu_custom_call" | custom-call | flops 30000001024 | bytes 1048576 | tf_op jit(solution)/shard_map/forward/pallas_call | solution.py:312
  67.2 3.8 %ffn_backward.2 = (bf16[768,3072]{1,0:T(8,128)(2,1)S(1)}, f32[768,768]{1,0:T(8,128)S(1)}, bf16[768,768]{1,0:T(8,128)(2,1)S(1)}, f32[8,768]{1,0:T(8,128)S(1)}, f32[8,3072]{1,0:T(8,128)S(1)}) custom-call(s32[16]{0:T(128)S(1)} %pad_add_fusion.sc_ref.c_ref.b_ref, bf16[768,768]{1,0:T(8,128)(2,1)S(1)} %get-tuple-element.247.df_ref, ...), custom_call_target="tpu_custom_call" | custom-call | flops 4000000000 | bytes 1048576 | tf_op jit(solution)/shard_map/ffn_backward/pallas_call | solution.py:420
  71.9 1.4 first_split.4
  74.0 1.4 collective-permute-start.2
  75.4 7.1 %ffn_backward.3 = (bf16[768,3072]{1,0:T(8,128)(2,1)S(1)}, f32[768,768]{1,0:T(8,128)S(1)}, bf16[768,768]{1,0:T(8,128)(2,1)S(1)}, f32[8,768]{1,0:T(8,128)S(1)}, f32[8,3072]{1,0:T(8,128)S(1)}) custom-call(s32[16]{0:T(128)S(1)} %pad_add_fusion.sc_ref.c_ref.b_ref, ...), custom_call_target="tpu_custom_call", output_to_operand_aliasing={{0}: (9, {}), {1}: (10, {}), {2}: (11, {})} | custom-call | flops 8000000000 | bytes 1048576 | tf_op jit(solution)/shard_map/ffn_backward/pallas_call | solution.py:420
  82.5 4.7 %up_gradient.1 = (bf16[768,1536]{1,0:T(8,128)(2,1)S(1)}, bf16[768,1536]{1,0:T(8,128)(2,1)S(1)}) custom-call(s32[16]{0:T(128)S(1)} %pad_add_fusion.sc_ref.c_ref.b_ref, bf16[768,768]{1,0:T(8,128)(2,1)S(1)} %get-tuple-element.276.h_ref, bf16[768,3072]{1,0:T(8,128)(2,1)S(1)} %get-tuple-element.284.d_ref), custom_call_target="tpu_custom_call" | custom-call | flops 100000000 | bytes 1048576 | tf_op jit(solution)/shard_map/up_gradient/pallas_call | solution.py:455
  87.2 1.6 collective-permute-done.1.ar
  90.3 1.2 collective-permute-start.3
  92.6 2.3 %copy-done.12 = bf16[18,256,512]{2,1,0:T(8,128)(2,1)S(1)} copy-done((bf16[18,256,512]{2,1,0:T(8,128)(2,1)S(1)}, bf16[18,256,512]{2,1,0:T(8,128)(2,1)}, u32[]{:S(2)}) %copy-start.12) | copy-done | bytes 4718616
  94.9 6.4 %attention_backward.2 = (bf16[768,2304]{1,0:T(8,128)(2,1)S(1)}, f32[384,768]{1,0:T(8,128)}, f32[256,768]{1,0:T(8,128)S(1)}, f32[8,768]{1,0:T(8,128)S(1)}) custom-call(s32[16]{0:T(128)S(1)} %pad_add_fusion.sc_ref.c_ref.b_ref, bf16[768,768]{1,0:T(8,128)(2,1)S(1)} %get-tuple-element.305.da_ref, f32[768,768]{1,0:T(8,128)S(1)} %get-tuple-element.306.dr_ref, ...), custom_call_target="tpu_custom_call" | custom-call | flops 5000000000 | bytes 1048576 | tf_op jit(solution)/shard_map/attention_backward/pallas_call | solution.py:534
  101.3 1.2 first_split.5
  104.6 1.3 collective-permute-start.7
  105.9 11.8 %attention_backward.3 = (bf16[768,2304]{1,0:T(8,128)(2,1)S(1)}, f32[384,768]{1,0:T(8,128)}, bf16[256,768]{1,0:T(8,128)(2,1)}, f32[8,768]{1,0:T(8,128)S(1)}) custom-call(s32[16]{0:T(128)S(1)} %pad_add_fusion.sc_ref.c_ref.b_ref, bf16[768,768]{1,0:T(8,128)(2,1)S(1)} %get-tuple-element.305.da_ref, ...), custom_call_target="tpu_custom_call", output_to_operand_aliasing={{0}: (8, {}), {1}: (9, {})} | custom-call | flops 10000000000 | bytes 1048576 | tf_op jit(solution)/shard_map/attention_backward/pallas_call | solution.py:534
  117.7 1.1 collective-permute-done.6.ar
  120.8 1.7 collective-permute-start.11
  123.1 1.2 collective-permute-start.10
  124.2 7.1 %qkvo_gradient.1 = (bf16[768,1536]{1,0:T(8,128)(2,1)}, bf16[768,1536]{1,0:T(8,128)(2,1)}) custom-call(s32[16]{0:T(128)S(1)} %pad_add_fusion.sc_ref.c_ref.b_ref, bf16[768,768]{1,0:T(8,128)(2,1)S(1)} %copy-done.15, bf16[768,2304]{1,0:T(8,128)(2,1)S(1)} %get-tuple-element.365.dq_ref, bf16[768,768]{1,0:T(8,128)(2,1)S(1)} %copy-done.16, ...), custom_call_target="tpu_custom_call" | custom-call | flops 5000000000 | bytes 1048576 | tf_op jit(solution)/shard_map/qkvo_gradient/pallas_call | solution.py:591
  131.4 1.4 join_split.5
  132.8 4.1 %all-to-all-start.1 = ((bf16[32,8,768]{2,1,0:T(8,128)(2,1)}), bf16[32,8,768]{2,1,0:T(8,128)(2,1)S(1)}, u32[]{:S(2)}, u32[]{:S(2)}) async-start(bf16[32,8,768]{2,1,0:T(8,128)(2,1)} %bitcast.10), calls=%async_computation.1 | async-start | bytes 786432 | tf_op jit(solution)/shard_map/all_to_all | solution.py:1075
  137.7 4.5 %first_split.6 = (bf16[4,2,96,384]{3,2,1,0:T(8,128)(2,1)}, bf16[4,2,96,384]{3,2,1,0:T(8,128)(2,1)}, bf16[4,2,96,384]{3,2,1,0:T(8,128)(2,1)}, bf16[4,2,96,384]{3,2,1,0:T(8,128)(2,1)}) custom-call(s32[16]{0:T(128)S(1)} %pad_add_fusion.sc_ref.c_ref.b_ref, bf16[4,2,96,1536]{3,2,1,0:T(8,128)(2,1)S(1)} %bitcast.25, bf16[4,2,96,1536]{3,2,1,0:T(8,128)(2,1)} %bitcast.13.r_ref), custom_call_target="tpu_custom_call" | custom-call | flops 1000000000 | bytes 1048576 | tf_op jit(solution)/shard_map/first_split/pallas_call | solution.py:738
  143.1 1.5 collective-permute-start.15
  144.6 1.5 collective-permute-start.13
  146.1 3.9 %all-to-all-done.1 = bf16[32,8,768]{2,1,0:T(8,128)(2,1)S(1)} async-done(((bf16[32,8,768]{2,1,0:T(8,128)(2,1)}), bf16[32,8,768]{2,1,0:T(8,128)(2,1)S(1)}, u32[]{:S(2)}, u32[]{:S(2)}) %all-to-all-start.1) | async-done | bytes 393248 | tf_op jit(solution)/shard_map/all_to_all | solution.py:1075
  149.9 7.7 %region_backward.1 = (bf16[8,2,2,72,384]{4,3,2,1,0:T(8,128)(2,1)}, bf16[8,2,2,72,384]{4,3,2,1,0:T(8,128)(2,1)}, f32[256,2048]{1,0:T(8,128)}, f32[4,256]{1,0:T(4,128)}) custom-call(s32[16]{0:T(128)S(1)} %pad_add_fusion.sc_ref.c_ref.b_ref, bf16[256,768]{1,0:T(8,128)(2,1)S(1)} %bitcast.29, s32[1,256]{1,0:T(1,128)} %t_ref.7, ...), custom_call_target="tpu_custom_call" | custom-call | flops 6000000000 | bytes 1048576 | tf_op jit(solution)/shard_map/region_backward/pallas_call | solution.py:685
  157.6 1.2 collective-permute-done.14.ar
  163.6 1.4 collective-permute-start.31
  165.0 3.4 %collective-permute-done.17.p1 = bf16[192,384]{1,0:T(8,128)(2,1)S(1)} collective-permute-done((bf16[192,384]{1,0:T(8,128)(2,1)S(1)}, bf16[192,384]{1,0:T(8,128)(2,1)S(1)}, u32[]{:S(2)}, u32[]{:S(2)}) %collective-permute-start.17) | collective-permute-done | bytes 147488 | tf_op jit(solution)/shard_map/ppermute | solution.py:729
  168.4 2.2 %collective-permute-start.24 = (bf16[1,192,384]{2,1,0:T(8,128)(2,1)S(1)}, bf16[1,192,384]{2,1,0:T(8,128)(2,1)S(1)}, u32[]{:S(2)}, u32[]{:S(2)}) collective-permute-start(bf16[1,192,384]{2,1,0:T(8,128)(2,1)S(1)} %get-tuple-element.436), channel_id=1, source_target_pairs={{0,16},{1,17},{2,18},{3,19},{4,20},{5,21},{6,22},{7,23},{8,24},{9,... | collective-permute-start | bytes 442376 | tf_op jit(solution)/shard_map/ppermute | solution.py:729
  170.7 1.1 first_split.7
  173.4 1.7 finish_down.1
  176.0 1.5 collective-permute-start.32
  177.5 1.3 collective-permute-done.24
  179.7 5.3 %collective-permute-done.32.r_ref = bf16[2,192,384]{2,1,0:T(8,128)(2,1)S(1)} collective-permute-done((bf16[2,192,384]{2,1,0:T(8,128)(2,1)S(1)}, bf16[2,192,384]{2,1,0:T(8,128)(2,1)S(1)}, u32[]{:S(2)}, u32[]{:S(2)}) %collective-permute-start.32) | collective-permute-done | bytes 294944 | tf_op jit(solution)/shard_map/ppermute | solution.py:729
  188.2 1.1 collective-permute-start.22
  190.0 4.8 %collective-permute-done.33 = bf16[1,192,384]{2,1,0:T(8,128)(2,1)S(1)} collective-permute-done((bf16[1,192,384]{2,1,0:T(8,128)(2,1)S(1)}, bf16[1,192,384]{2,1,0:T(8,128)(2,1)S(1)}, u32[]{:S(2)}, u32[]{:S(2)}) %collective-permute-start.33) | collective-permute-done | bytes 147488 | tf_op jit(solution)/shard_map/ppermute | solution.py:729
  197.5 3.4 %collective-permute-start.28 = (bf16[2,144,384]{2,1,0:T(8,128)(2,1)S(1)}, bf16[2,144,384]{2,1,0:T(8,128)(2,1)S(1)}, u32[]{:S(2)}, u32[]{:S(2)}) collective-permute-start(bf16[2,144,384]{2,1,0:T(8,128)(2,1)S(1)} %get-tuple-element.432), channel_id=1, source_target_pairs={{0,8},{1,9},{2,10},{3,11},{4,12},{5,13},{6,14},{7,15},{8,0},{9,1},... | collective-permute-start | bytes 663560 | tf_op jit(solution)/shard_map/ppermute | solution.py:729
  201.5 1.7 finish_wide.2
  203.2 1.7 collective-permute-done.28.r_ref
  205.5 1.6 collective-permute-start.29
  207.0 1.7 finish_wide.3
  208.7 2.4 %collective-permute-done.29 = bf16[1,144,384]{2,1,0:T(8,128)(2,1)S(1)} collective-permute-done((bf16[1,144,384]{2,1,0:T(8,128)(2,1)S(1)}, bf16[1,144,384]{2,1,0:T(8,128)(2,1)S(1)}, u32[]{:S(2)}, u32[]{:S(2)}) %collective-permute-start.29) | collective-permute-done | bytes 110624 | tf_op jit(solution)/shard_map/ppermute | solution.py:729
  211.9 4.1 %collective-permute-done.37.p1 = bf16[144,384]{1,0:T(8,128)(2,1)S(1)} collective-permute-done((bf16[144,384]{1,0:T(8,128)(2,1)S(1)}, bf16[144,384]{1,0:T(8,128)(2,1)S(1)}, u32[]{:S(2)}, u32[]{:S(2)}) %collective-permute-start.37) | collective-permute-done | bytes 110624 | tf_op jit(solution)/shard_map/ppermute | solution.py:729
  216.0 1.3 collective-permute-done.39.p3
  217.3 1.6 finish_visual.1
  (121 shorter events, 28.8 us)
Async XLA Ops:
  1.4 13.1 %copy-start.18 = (f32[1536]{0:T(1024)S(1)}, f32[1536]{0:T(1024)}, u32[]{:S(2)}) copy-start(f32[1536]{0:T(1024)} %param.40) | copy-start | bytes 18436
  1.4 13.1 %copy-start.19 = (s32[2]{0:T(128)S(1)}, s32[2]{0:T(128)}, u32[]{:S(2)}) copy-start(s32[2]{0:T(128)} %param.31) | copy-start | bytes 28
  1.4 13.2 %copy-start.20 = (s32[3]{0:T(128)S(1)}, s32[3]{0:T(128)}, u32[]{:S(2)}) copy-start(s32[3]{0:T(128)} %param.30) | copy-start | bytes 40
  1.4 13.2 %copy-start.21 = (s32[3]{0:T(128)S(1)}, s32[3]{0:T(128)}, u32[]{:S(2)}) copy-start(s32[3]{0:T(128)} %param.29) | copy-start | bytes 40
  7.1 20.5 %all-to-all-start = ((bf16[32,8,768]{2,1,0:T(8,128)(2,1)}), bf16[32,8,768]{2,1,0:T(8,128)(2,1)S(1)}, u32[]{:S(2)}, u32[]{:S(2)}) async-start(bf16[32,8,768]{2,1,0:T(8,128)(2,1)} %bitcast.1), calls=%async_computation | async-start | bytes 786432 | tf_op jit(solution)/shard_map/all_to_all | solution.py:1021
  28.4 38.8 %copy-start.3 = (f32[768]{0:T(1024)S(1)}, f32[768]{0:T(1024)}, u32[]{:S(2)}) copy-start(f32[768]{0:T(1024)} %ag_ref.5) | copy-start | bytes 9220
  67.1 4.8 %collective-permute-start = (bf16[8,2,2,96,384]{4,3,2,1,0:T(8,128)(2,1)}, bf16[8,2,2,96,384]{4,3,2,1,0:T(8,128)(2,1)S(1)}, u32[]{:S(2)}, u32[]{:S(2)}) collective-permute-start(bf16[8,2,2,96,384]{4,3,2,1,0:T(8,128)(2,1)} %bitcast.35), channel_id=1, source_target_pairs={{0,1},{1,0},{2,3},{3,2},{4,5},{5,4},{6,7},{7,6},{8,9},{9,8},{10,11... | collective-permute-start | bytes 7077896 | tf_op jit(solution)/shard_map/ppermute | solution.py:729
  73.3 15.4 %collective-permute-start.1 = (bf16[4,2,96,384]{3,2,1,0:T(8,128)(2,1)S(1)}, bf16[4,2,96,384]{3,2,1,0:T(8,128)(2,1)S(1)}, u32[]{:S(2)}, u32[]{:S(2)}) collective-permute-start(bf16[4,2,96,384]{3,2,1,0:T(8,128)(2,1)S(1)} %get-tuple-element.271), channel_id=1, source_target_pairs={{0,2},{1,3},{2,0},{3,1},{4,6},{5,7},{6,4},{7,5},{8,10},{9,11},{10,... | collective-permute-start | bytes 1769480 | tf_op jit(solution)/shard_map/ppermute | solution.py:729
  74.0 15.3 %collective-permute-start.2 = (bf16[4,2,96,384]{3,2,1,0:T(8,128)(2,1)S(1)}, bf16[4,2,96,384]{3,2,1,0:T(8,128)(2,1)S(1)}, u32[]{:S(2)}, u32[]{:S(2)}) collective-permute-start(bf16[4,2,96,384]{3,2,1,0:T(8,128)(2,1)S(1)} %get-tuple-element.273), channel_id=1, source_target_pairs={{0,4},{1,5},{2,6},{3,7},{4,0},{5,1},{6,2},{7,3},{8,12},{9,13},{10,... | collective-permute-start | bytes 1769480 | tf_op jit(solution)/shard_map/ppermute | solution.py:729
  90.2 11.0 %collective-permute-start.5 = (bf16[768,1536]{1,0:T(8,128)(2,1)S(1)}, bf16[768,1536]{1,0:T(8,128)(2,1)S(1)}, u32[]{:S(2)}, u32[]{:S(2)}) collective-permute-start(bf16[768,1536]{1,0:T(8,128)(2,1)S(1)} %get-tuple-element.302), channel_id=1, source_target_pairs={{0,1},{1,0},{2,3},{3,2},{4,5},{5,4},{6,7},{7,6},{8,9},{9,8},{10,11... | collective-permute-start | bytes 7077896 | tf_op jit(solution)/shard_map/ppermute | solution.py:729
  90.3 11.0 %collective-permute-start.3 = (bf16[4,96,384]{2,1,0:T(8,128)(2,1)S(1)}, bf16[4,96,384]{2,1,0:T(8,128)(2,1)S(1)}, u32[]{:S(2)}, u32[]{:S(2)}) collective-permute-start(bf16[4,96,384]{2,1,0:T(8,128)(2,1)S(1)} %get-tuple-element.298), channel_id=1, source_target_pairs={{0,4},{1,5},{2,6},{3,7},{4,0},{5,1},{6,2},{7,3},{8,12},{9,13},{10,... | collective-permute-start | bytes 884744 | tf_op jit(solution)/shard_map/ppermute | solution.py:729
  91.5 9.7 %collective-permute-start.4 = (bf16[4,96,384]{2,1,0:T(8,128)(2,1)S(1)}, bf16[4,96,384]{2,1,0:T(8,128)(2,1)S(1)}, u32[]{:S(2)}, u32[]{:S(2)}) collective-permute-start(bf16[4,96,384]{2,1,0:T(8,128)(2,1)S(1)} %get-tuple-element.300), channel_id=1, source_target_pairs={{0,2},{1,3},{2,0},{3,1},{4,6},{5,7},{6,4},{7,5},{8,10},{9,11},{10,... | collective-permute-start | bytes 884744 | tf_op jit(solution)/shard_map/ppermute | solution.py:729
  103.2 14.5 %collective-permute-start.8 = (bf16[2,192,384]{2,1,0:T(8,128)(2,1)S(1)}, bf16[2,192,384]{2,1,0:T(8,128)(2,1)S(1)}, u32[]{:S(2)}, u32[]{:S(2)}) collective-permute-start(bf16[2,192,384]{2,1,0:T(8,128)(2,1)S(1)} %get-tuple-element.340), channel_id=1, source_target_pairs={{0,8},{1,9},{2,10},{3,11},{4,12},{5,13},{6,14},{7,15},{8,0},{9,1},... | collective-permute-start | bytes 884744 | tf_op jit(solution)/shard_map/ppermute | solution.py:729
  104.0 14.8 %collective-permute-start.6 = (bf16[4,2,96,384]{3,2,1,0:T(8,128)(2,1)S(1)}, bf16[4,2,96,384]{3,2,1,0:T(8,128)(2,1)S(1)}, u32[]{:S(2)}, u32[]{:S(2)}) collective-permute-start(bf16[4,2,96,384]{3,2,1,0:T(8,128)(2,1)S(1)} %get-tuple-element.336), channel_id=1, source_target_pairs={{0,2},{1,3},{2,0},{3,1},{4,6},{5,7},{6,4},{7,5},{8,10},{9,11},{10,... | collective-permute-start | bytes 1769480 | tf_op jit(solution)/shard_map/ppermute | solution.py:729
  104.6 14.6 %collective-permute-start.7 = (bf16[4,2,96,384]{3,2,1,0:T(8,128)(2,1)S(1)}, bf16[4,2,96,384]{3,2,1,0:T(8,128)(2,1)S(1)}, u32[]{:S(2)}, u32[]{:S(2)}) collective-permute-start(bf16[4,2,96,384]{3,2,1,0:T(8,128)(2,1)S(1)} %get-tuple-element.338), channel_id=1, source_target_pairs={{0,4},{1,5},{2,6},{3,7},{4,0},{5,1},{6,2},{7,3},{8,12},{9,13},{10,... | collective-permute-start | bytes 1769480 | tf_op jit(solution)/shard_map/ppermute | solution.py:729
  120.8 10.5 %collective-permute-start.11 = (bf16[1,192,384]{2,1,0:T(8,128)(2,1)S(1)}, bf16[1,192,384]{2,1,0:T(8,128)(2,1)S(1)}, u32[]{:S(2)}, u32[]{:S(2)}) collective-permute-start(bf16[1,192,384]{2,1,0:T(8,128)(2,1)S(1)} %get-tuple-element.361), channel_id=1, source_target_pairs={{0,16},{1,17},{2,18},{3,19},{4,20},{5,21},{6,22},{7,23},{8,24},{9,... | collective-permute-start | bytes 442376 | tf_op jit(solution)/shard_map/ppermute | solution.py:729
  122.5 8.8 %collective-permute-start.9 = (bf16[4,96,384]{2,1,0:T(8,128)(2,1)S(1)}, bf16[4,96,384]{2,1,0:T(8,128)(2,1)S(1)}, u32[]{:S(2)}, u32[]{:S(2)}) collective-permute-start(bf16[4,96,384]{2,1,0:T(8,128)(2,1)S(1)} %get-tuple-element.357), channel_id=1, source_target_pairs={{0,4},{1,5},{2,6},{3,7},{4,0},{5,1},{6,2},{7,3},{8,12},{9,13},{10,... | collective-permute-start | bytes 884744 | tf_op jit(solution)/shard_map/ppermute | solution.py:729
  123.1 8.3 %collective-permute-start.10 = (bf16[4,96,384]{2,1,0:T(8,128)(2,1)S(1)}, bf16[4,96,384]{2,1,0:T(8,128)(2,1)S(1)}, u32[]{:S(2)}, u32[]{:S(2)}) collective-permute-start(bf16[4,96,384]{2,1,0:T(8,128)(2,1)S(1)} %get-tuple-element.359), channel_id=1, source_target_pairs={{0,2},{1,3},{2,0},{3,1},{4,6},{5,7},{6,4},{7,5},{8,10},{9,11},{10,... | collective-permute-start | bytes 884744 | tf_op jit(solution)/shard_map/ppermute | solution.py:729
  132.8 4.9 %collective-permute-start.12 = (bf16[768,1536]{1,0:T(8,128)(2,1)}, bf16[768,1536]{1,0:T(8,128)(2,1)}, u32[]{:S(2)}, u32[]{:S(2)}) collective-permute-start(bf16[768,1536]{1,0:T(8,128)(2,1)} %get-tuple-element.385), channel_id=1, source_target_pairs={{0,1},{1,0},{2,3},{3,2},{4,5},{5,4},{6,7},{7,6},{8,9},{9,8},{10,11... | collective-permute-start | bytes 7077896 | tf_op jit(solution)/shard_map/ppermute | solution.py:729
  132.8 17.1 %all-to-all-start.1 = ((bf16[32,8,768]{2,1,0:T(8,128)(2,1)}), bf16[32,8,768]{2,1,0:T(8,128)(2,1)S(1)}, u32[]{:S(2)}, u32[]{:S(2)}) async-start(bf16[32,8,768]{2,1,0:T(8,128)(2,1)} %bitcast.10), calls=%async_computation.1 | async-start | bytes 786432 | tf_op jit(solution)/shard_map/all_to_all | solution.py:1075
  137.7 12.3 %copy-start.9 = (bf16[768,4]{0,1:T(4,128)(2,1)S(1)}, bf16[768,4]{0,1:T(4,128)(2,1)}, u32[]{:S(2)}) copy-start(bf16[768,4]{0,1:T(4,128)(2,1)} %param.35) | copy-start | bytes 18436
  142.1 16.6 %collective-permute-start.14 = (bf16[4,2,96,384]{3,2,1,0:T(8,128)(2,1)}, bf16[4,2,96,384]{3,2,1,0:T(8,128)(2,1)S(1)}, u32[]{:S(2)}, u32[]{:S(2)}) collective-permute-start(bf16[4,2,96,384]{3,2,1,0:T(8,128)(2,1)} %get-tuple-element.386), channel_id=1, source_target_pairs={{0,2},{1,3},{2,0},{3,1},{4,6},{5,7},{6,4},{7,5},{8,10},{9,11},{10,... | collective-permute-start | bytes 1769480 | tf_op jit(solution)/shard_map/ppermute | solution.py:729
  143.1 16.5 %collective-permute-start.15 = (bf16[4,2,96,384]{3,2,1,0:T(8,128)(2,1)}, bf16[4,2,96,384]{3,2,1,0:T(8,128)(2,1)S(1)}, u32[]{:S(2)}, u32[]{:S(2)}) collective-permute-start(bf16[4,2,96,384]{3,2,1,0:T(8,128)(2,1)} %get-tuple-element.388), channel_id=1, source_target_pairs={{0,4},{1,5},{2,6},{3,7},{4,0},{5,1},{6,2},{7,3},{8,12},{9,13},{10,... | collective-permute-start | bytes 1769480 | tf_op jit(solution)/shard_map/ppermute | solution.py:729
  144.6 13.0 %collective-permute-start.13 = (bf16[2,192,384]{2,1,0:T(8,128)(2,1)S(1)}, bf16[2,192,384]{2,1,0:T(8,128)(2,1)S(1)}, u32[]{:S(2)}, u32[]{:S(2)}) collective-permute-start(bf16[2,192,384]{2,1,0:T(8,128)(2,1)S(1)} %copy-done.23), channel_id=1, source_target_pairs={{0,8},{1,9},{2,10},{3,11},{4,12},{5,13},{6,14},{7,15},{8,0},{9,1},... | collective-permute-start | bytes 884744 | tf_op jit(solution)/shard_map/ppermute | solution.py:729
  161.8 6.7 %collective-permute-start.16 = (bf16[8,2,2,72,384]{4,3,2,1,0:T(8,128)(2,1)S(1)}, bf16[8,2,2,72,384]{4,3,2,1,0:T(8,128)(2,1)S(1)}, u32[]{:S(2)}, u32[]{:S(2)}) collective-permute-start(bf16[8,2,2,72,384]{4,3,2,1,0:T(8,128)(2,1)S(1)} %copy-done.22), channel_id=1, source_target_pairs={{0,1},{1,0},{2,3},{3,2},{4,5},{5,4},{6,7},{7,6},{8,9},{9,8},{10,11... | collective-permute-start | bytes 5308424 | tf_op jit(solution)/shard_map/ppermute | solution.py:729
  161.8 6.6 %collective-permute-start.17 = (bf16[192,384]{1,0:T(8,128)(2,1)S(1)}, bf16[192,384]{1,0:T(8,128)(2,1)S(1)}, u32[]{:S(2)}, u32[]{:S(2)}) collective-permute-start(bf16[192,384]{1,0:T(8,128)(2,1)S(1)} %add_bitcast_fusion.2.p0), channel_id=1, source_target_pairs={{0,2},{1,3},{2,0},{3,1},{4,6},{5,7},{6,4},{7,5},{8,10},{9,11},{10,... | collective-permute-start | bytes 442376 | tf_op jit(solution)/shard_map/ppermute | solution.py:729
  162.7 12.5 %collective-permute-start.30 = (bf16[4,96,384]{2,1,0:T(8,128)(2,1)S(1)}, bf16[4,96,384]{2,1,0:T(8,128)(2,1)S(1)}, u32[]{:S(2)}, u32[]{:S(2)}) collective-permute-start(bf16[4,96,384]{2,1,0:T(8,128)(2,1)S(1)} %get-tuple-element.442), channel_id=1, source_target_pairs={{0,4},{1,5},{2,6},{3,7},{4,0},{5,1},{6,2},{7,3},{8,12},{9,13},{10,... | collective-permute-start | bytes 884744 | tf_op jit(solution)/shard_map/ppermute | solution.py:729
  163.6 11.6 %collective-permute-start.31 = (bf16[4,96,384]{2,1,0:T(8,128)(2,1)S(1)}, bf16[4,96,384]{2,1,0:T(8,128)(2,1)S(1)}, u32[]{:S(2)}, u32[]{:S(2)}) collective-permute-start(bf16[4,96,384]{2,1,0:T(8,128)(2,1)S(1)} %get-tuple-element.444), channel_id=1, source_target_pairs={{0,2},{1,3},{2,0},{3,1},{4,6},{5,7},{6,4},{7,5},{8,10},{9,11},{10,... | collective-permute-start | bytes 884744 | tf_op jit(solution)/shard_map/ppermute | solution.py:729
  165.0 6.8 %collective-permute-start.18 = (bf16[192,384]{1,0:T(8,128)(2,1)S(1)}, bf16[192,384]{1,0:T(8,128)(2,1)S(1)}, u32[]{:S(2)}, u32[]{:S(2)}) collective-permute-start(bf16[192,384]{1,0:T(8,128)(2,1)S(1)} %add_bitcast_fusion.2.p0), channel_id=1, source_target_pairs={{0,1},{1,0},{2,3},{3,2},{4,5},{5,4},{6,7},{7,6},{8,9},{9,8},{10,11... | collective-permute-start | bytes 442376 | tf_op jit(solution)/shard_map/ppermute | solution.py:729
  168.4 4.3 %collective-permute-start.19 = (bf16[192,384]{1,0:T(8,128)(2,1)S(1)}, bf16[192,384]{1,0:T(8,128)(2,1)S(1)}, u32[]{:S(2)}, u32[]{:S(2)}) collective-permute-start(bf16[192,384]{1,0:T(8,128)(2,1)S(1)} %collective-permute-done.17.p1), channel_id=1, source_target_pairs={{0,1},{1,0},{2,3},{3,2},{4,5},{5,4},{6,7},{7,6},{8,9},{9,8},{10,11... | collective-permute-start | bytes 442376 | tf_op jit(solution)/shard_map/ppermute | solution.py:729
  168.4 10.4 %collective-permute-start.24 = (bf16[1,192,384]{2,1,0:T(8,128)(2,1)S(1)}, bf16[1,192,384]{2,1,0:T(8,128)(2,1)S(1)}, u32[]{:S(2)}, u32[]{:S(2)}) collective-permute-start(bf16[1,192,384]{2,1,0:T(8,128)(2,1)S(1)} %get-tuple-element.436), channel_id=1, source_target_pairs={{0,16},{1,17},{2,18},{3,19},{4,20},{5,21},{6,22},{7,23},{8,24},{9,... | collective-permute-start | bytes 442376 | tf_op jit(solution)/shard_map/ppermute | solution.py:729
  171.8 15.5 %collective-permute-start.20 = (bf16[4,2,72,384]{3,2,1,0:T(8,128)(2,1)S(1)}, bf16[4,2,72,384]{3,2,1,0:T(8,128)(2,1)S(1)}, u32[]{:S(2)}, u32[]{:S(2)}) collective-permute-start(bf16[4,2,72,384]{3,2,1,0:T(8,128)(2,1)S(1)} %get-tuple-element.421), channel_id=1, source_target_pairs={{0,2},{1,3},{2,0},{3,1},{4,6},{5,7},{6,4},{7,5},{8,10},{9,11},{10,... | collective-permute-start | bytes 1327112 | tf_op jit(solution)/shard_map/ppermute | solution.py:729
  172.7 14.6 %collective-permute-start.21 = (bf16[4,2,72,384]{3,2,1,0:T(8,128)(2,1)S(1)}, bf16[4,2,72,384]{3,2,1,0:T(8,128)(2,1)S(1)}, u32[]{:S(2)}, u32[]{:S(2)}) collective-permute-start(bf16[4,2,72,384]{3,2,1,0:T(8,128)(2,1)S(1)} %get-tuple-element.423), channel_id=1, source_target_pairs={{0,4},{1,5},{2,6},{3,7},{4,0},{5,1},{6,2},{7,3},{8,12},{9,13},{10,... | collective-permute-start | bytes 1327112 | tf_op jit(solution)/shard_map/ppermute | solution.py:729
  176.0 9.1 %collective-permute-start.32 = (bf16[2,192,384]{2,1,0:T(8,128)(2,1)S(1)}, bf16[2,192,384]{2,1,0:T(8,128)(2,1)S(1)}, u32[]{:S(2)}, u32[]{:S(2)}) collective-permute-start(bf16[2,192,384]{2,1,0:T(8,128)(2,1)S(1)} %get-tuple-element.446), channel_id=1, source_target_pairs={{0,8},{1,9},{2,10},{3,11},{4,12},{5,13},{6,14},{7,15},{8,0},{9,1},... | collective-permute-start | bytes 884744 | tf_op jit(solution)/shard_map/ppermute | solution.py:729
  178.8 8.5 %collective-permute-start.25 = (bf16[192,384]{1,0:T(8,128)(2,1)S(1)}, bf16[192,384]{1,0:T(8,128)(2,1)S(1)}, u32[]{:S(2)}, u32[]{:S(2)}) collective-permute-start(bf16[192,384]{1,0:T(8,128)(2,1)S(1)} %add_bitcast_fusion.1.p0), channel_id=1, source_target_pairs={{0,2},{1,3},{2,0},{3,1},{4,6},{5,7},{6,4},{7,5},{8,10},{9,11},{10,... | collective-permute-start | bytes 442376 | tf_op jit(solution)/shard_map/ppermute | solution.py:729
  185.7 9.1 %collective-permute-start.33 = (bf16[1,192,384]{2,1,0:T(8,128)(2,1)S(1)}, bf16[1,192,384]{2,1,0:T(8,128)(2,1)S(1)}, u32[]{:S(2)}, u32[]{:S(2)}) collective-permute-start(bf16[1,192,384]{2,1,0:T(8,128)(2,1)S(1)} %get-tuple-element.448), channel_id=1, source_target_pairs={{0,16},{1,17},{2,18},{3,19},{4,20},{5,21},{6,22},{7,23},{8,24},{9,... | collective-permute-start | bytes 442376 | tf_op jit(solution)/shard_map/ppermute | solution.py:729
  186.7 14.7 %collective-permute-start.26 = (bf16[192,384]{1,0:T(8,128)(2,1)S(1)}, bf16[192,384]{1,0:T(8,128)(2,1)S(1)}, u32[]{:S(2)}, u32[]{:S(2)}) collective-permute-start(bf16[192,384]{1,0:T(8,128)(2,1)S(1)} %add_bitcast_fusion.1.p0), channel_id=1, source_target_pairs={{0,1},{1,0},{2,3},{3,2},{4,5},{5,4},{6,7},{7,6},{8,9},{9,8},{10,11... | collective-permute-start | bytes 442376 | tf_op jit(solution)/shard_map/ppermute | solution.py:729
  187.3 14.1 %collective-permute-start.27 = (bf16[192,384]{1,0:T(8,128)(2,1)S(1)}, bf16[192,384]{1,0:T(8,128)(2,1)S(1)}, u32[]{:S(2)}, u32[]{:S(2)}) collective-permute-start(bf16[192,384]{1,0:T(8,128)(2,1)S(1)} %collective-permute-done.25.p1), channel_id=1, source_target_pairs={{0,1},{1,0},{2,3},{3,2},{4,5},{5,4},{6,7},{7,6},{8,9},{9,8},{10,11... | collective-permute-start | bytes 442376 | tf_op jit(solution)/shard_map/ppermute | solution.py:729
  188.2 7.9 %collective-permute-start.22 = (bf16[4,72,384]{2,1,0:T(8,128)(2,1)S(1)}, bf16[4,72,384]{2,1,0:T(8,128)(2,1)S(1)}, u32[]{:S(2)}, u32[]{:S(2)}) collective-permute-start(bf16[4,72,384]{2,1,0:T(8,128)(2,1)S(1)} %get-tuple-element.429), channel_id=1, source_target_pairs={{0,4},{1,5},{2,6},{3,7},{4,0},{5,1},{6,2},{7,3},{8,12},{9,13},{10,... | collective-permute-start | bytes 663560 | tf_op jit(solution)/shard_map/ppermute | solution.py:729
  189.3 7.5 %collective-permute-start.23 = (bf16[4,72,384]{2,1,0:T(8,128)(2,1)S(1)}, bf16[4,72,384]{2,1,0:T(8,128)(2,1)S(1)}, u32[]{:S(2)}, u32[]{:S(2)}) collective-permute-start(bf16[4,72,384]{2,1,0:T(8,128)(2,1)S(1)} %get-tuple-element.431), channel_id=1, source_target_pairs={{0,2},{1,3},{2,0},{3,1},{4,6},{5,7},{6,4},{7,5},{8,10},{9,11},{10,... | collective-permute-start | bytes 663560 | tf_op jit(solution)/shard_map/ppermute | solution.py:729
  194.8 6.1 %collective-permute-start.34 = (bf16[192,384]{1,0:T(8,128)(2,1)S(1)}, bf16[192,384]{1,0:T(8,128)(2,1)S(1)}, u32[]{:S(2)}, u32[]{:S(2)}) collective-permute-start(bf16[192,384]{1,0:T(8,128)(2,1)S(1)} %add_bitcast_fusion.p0), channel_id=1, source_target_pairs={{0,2},{1,3},{2,0},{3,1},{4,6},{5,7},{6,4},{7,5},{8,10},{9,11},{10,... | collective-permute-start | bytes 442376 | tf_op jit(solution)/shard_map/ppermute | solution.py:729
  197.5 7.3 %collective-permute-start.28 = (bf16[2,144,384]{2,1,0:T(8,128)(2,1)S(1)}, bf16[2,144,384]{2,1,0:T(8,128)(2,1)S(1)}, u32[]{:S(2)}, u32[]{:S(2)}) collective-permute-start(bf16[2,144,384]{2,1,0:T(8,128)(2,1)S(1)} %get-tuple-element.432), channel_id=1, source_target_pairs={{0,8},{1,9},{2,10},{3,11},{4,12},{5,13},{6,14},{7,15},{8,0},{9,1},... | collective-permute-start | bytes 663560 | tf_op jit(solution)/shard_map/ppermute | solution.py:729
  200.9 6.1 %collective-permute-start.35 = (bf16[192,384]{1,0:T(8,128)(2,1)S(1)}, bf16[192,384]{1,0:T(8,128)(2,1)S(1)}, u32[]{:S(2)}, u32[]{:S(2)}) collective-permute-start(bf16[192,384]{1,0:T(8,128)(2,1)S(1)} %add_bitcast_fusion.p0), channel_id=1, source_target_pairs={{0,1},{1,0},{2,3},{3,2},{4,5},{5,4},{6,7},{7,6},{8,9},{9,8},{10,11... | collective-permute-start | bytes 442376 | tf_op jit(solution)/shard_map/ppermute | solution.py:729
  200.9 6.1 %collective-permute-start.36 = (bf16[192,384]{1,0:T(8,128)(2,1)S(1)}, bf16[192,384]{1,0:T(8,128)(2,1)S(1)}, u32[]{:S(2)}, u32[]{:S(2)}) collective-permute-start(bf16[192,384]{1,0:T(8,128)(2,1)S(1)} %collective-permute-done.34.p1), channel_id=1, source_target_pairs={{0,1},{1,0},{2,3},{3,2},{4,5},{5,4},{6,7},{7,6},{8,9},{9,8},{10,11... | collective-permute-start | bytes 442376 | tf_op jit(solution)/shard_map/ppermute | solution.py:729
  205.5 5.7 %collective-permute-start.29 = (bf16[1,144,384]{2,1,0:T(8,128)(2,1)S(1)}, bf16[1,144,384]{2,1,0:T(8,128)(2,1)S(1)}, u32[]{:S(2)}, u32[]{:S(2)}) collective-permute-start(bf16[1,144,384]{2,1,0:T(8,128)(2,1)S(1)} %get-tuple-element.439), channel_id=1, source_target_pairs={{0,16},{1,17},{2,18},{3,19},{4,20},{5,21},{6,22},{7,23},{8,24},{9,... | collective-permute-start | bytes 331784 | tf_op jit(solution)/shard_map/ppermute | solution.py:729
  211.2 4.8 %collective-permute-start.37 = (bf16[144,384]{1,0:T(8,128)(2,1)S(1)}, bf16[144,384]{1,0:T(8,128)(2,1)S(1)}, u32[]{:S(2)}, u32[]{:S(2)}) collective-permute-start(bf16[144,384]{1,0:T(8,128)(2,1)S(1)} %add_bitcast_fusion.3.p0), channel_id=1, source_target_pairs={{0,2},{1,3},{2,0},{3,1},{4,6},{5,7},{6,4},{7,5},{8,10},{9,11},{10,... | collective-permute-start | bytes 331784 | tf_op jit(solution)/shard_map/ppermute | solution.py:729
  211.9 4.1 %collective-permute-start.38 = (bf16[144,384]{1,0:T(8,128)(2,1)S(1)}, bf16[144,384]{1,0:T(8,128)(2,1)S(1)}, u32[]{:S(2)}, u32[]{:S(2)}) collective-permute-start(bf16[144,384]{1,0:T(8,128)(2,1)S(1)} %add_bitcast_fusion.3.p0), channel_id=1, source_target_pairs={{0,1},{1,0},{2,3},{3,2},{4,5},{5,4},{6,7},{7,6},{8,9},{9,8},{10,11... | collective-permute-start | bytes 331784 | tf_op jit(solution)/shard_map/ppermute | solution.py:729
  216.0 1.3 collective-permute-start.39
  (18 other events, 93.7 us)

commit v5 on v4

--- a/solution.py
+++ b/solution.py
@@ -245,7 +245,7 @@
                 ctx_ref[:, cols(0)] = jnp.where(first, outs[:seq], outs[seq:]).astype(bf16)
                 return carry
 
-            lax.fori_loop(0, HEADS // 2, pair_forward, 0, unroll=UNROLL)
+            lax.fori_loop(0, HEADS // 2, pair_forward, 0, unroll=3)
 
             @pl.when(step == 0)
             def _():
@@ -606,118 +606,173 @@
     )(core, x, d_qkv, context, d_attn)
 
 
-def region_backward(
-    core, returned, target, normed, inv, gain, features, boxes, w_visual, w_box_t,
-    sums_forward, sums_ffn, sums_up, sums_attn, groups,
+def region_norm_backward(
+    core, returned, target, normed, inv, gain, boxes, w_box_t, sums_forward, sums_ffn, sums_up, sums_attn, groups
 ):
     rows, width = returned.shape
-    feat = features.shape[1]
     half = width // 2
+    box = boxes.shape[0]
+    share = width // groups
+    ff_share = sums_up.shape[1] // groups
+
+    def kernel(
+        c_ref, r_ref, t_ref, n_ref, i_ref, g_ref, box_ref, wb_ref, sf_ref, sn_ref, su_ref, sa_ref,
+        all_ref, send_ref, keep_ref, small_ref, bg_ref, small,
+    ):
+        d_region = mm(one_hot(t_ref[...], rows), r_ref[...], TN)
+        normed = n_ref[...]
+        low = norm_back(d_region, normed, i_ref[:, 0:1], g_ref[...]).astype(bf16)
+        all_ref[...] = low
+        mine = c_ref[0] == 0
+        send_ref[:rows, :] = jnp.where(mine, low[:, half:], low[:, :half])
+        keep_ref[...] = jnp.where(mine, low[:, :half], low[:, half:])
+        bg_ref[...] = mm(wb_ref[...], low, NT)
+        boxes_grad = mm(box_ref[...], low)
+        vectors = [
+            row_sum(low.astype(f32)),
+            row_sum(d_region * normed),
+            row_sum(d_region),
+            sf_ref[0:1, :],
+            sf_ref[1:2, :],
+            sf_ref[2:3, :],
+            sn_ref[0:1, :],
+            sn_ref[1:2, :],
+            sn_ref[2:3, :],
+        ] + [boxes_grad[at : at + 1] for at in range(box)]
+        small[...] = jnp.zeros_like(small)
+        lane = lax.broadcasted_iota(jnp.int32, (1, half), 1)
+        stats = jnp.zeros((1, half), f32)
+        for at in range(4):
+            total = jnp.sum(sf_ref[3 + at : 4 + at, :], 1, keepdims=True)
+            stats = jnp.where(lane == at, total, stats)
+        flat = jnp.concatenate([sa_ref[0:1, :], sa_ref[1:2, :]], 1)
+        for group in range(groups):
+            small[group, 0:1, 0:ff_share] = su_ref[0:1, group * ff_share : (group + 1) * ff_share]
+            small[group, 1:2, 0 : 2 * share] = flat[:, group * 2 * share : (group + 1) * 2 * share]
+            for at, value in enumerate(vectors):
+                row, col = (1, 2) if at == 0 else (2 + (at - 1) // 3, (at - 1) % 3)
+                small[group, row : row + 1, 128 * col : 128 * col + share] = value[
+                    :, group * share : (group + 1) * share
+                ]
+            small[group, 6:7, :] = stats
+        small_ref[...] = small[...].astype(bf16)
+        for group in range(groups):
+            send_ref[rows + 8 * group : rows + 8 * (group + 1), :] = small_ref[group]
+
+    sizes = (sums_forward, sums_ffn, sums_up, sums_attn)
+    return pl.pallas_call(
+        kernel,
+        grid_spec=pltpu.PrefetchScalarGridSpec(
+            num_scalar_prefetch=1,
+            grid=(1,),
+            in_specs=[
+                whole((rows, width)),
+                whole((1, rows)),
+                whole((rows, width)),
+                whole((rows, 128)),
+                vec(width),
+                whole(boxes.shape),
+                whole(w_box_t.shape),
+            ]
+            + [whole(v.shape) for v in sizes],
+            out_specs=[VMEM] * 4 + [whole((box, rows))],
+            scratch_shapes=[pltpu.VMEM((groups, 8, half), f32)],
+        ),
+        out_shape=[
+            near((rows, width), bf16),
+            near((rows + 8 * groups, half), bf16),
+            near((rows, half), bf16),
+            near((groups, 8, half), bf16),
+            shape((box, rows)),
+        ],
+        compiler_params=params(14),
+        cost_estimate=cost(0.1),
+        name="region_norm_backward",
+    )(core, returned, far(target), far(normed), far(inv), far(gain), far(boxes), w_box_t, *sizes)
+
+
+def visual_gradient(bits, features, other_features, d_pre, other_d_pre, small, groups):
+    rows, feat = features.shape
+    half = d_pre.shape[1]
     steps = 4
     part = feat // steps
     quarter = feat // groups // 4
     tall = quarter + 8
     per_step = groups // steps
-    box = boxes.shape[0]
-    share = width // groups
-    ff_share = sums_up.shape[1] // groups
-
-    def kernel(
-        c_ref, r_ref, t_ref, n_ref, i_ref, g_ref, f_ref, box_ref, wv_ref, wb_ref, sf_ref, sn_ref, su_ref, sa_ref,
-        send_ref, keep_ref, fg_ref, bg_ref, dpre, small,
-    ):
+    high = groups // 2
+
+    def kernel(b_ref, f_ref, o_ref, d_ref, p_ref, s_ref, a_send, a_keep, b_send, b_keep, got):
         step = pl.program_id(0)
-
-        @pl.when(step == 0)
-        def _():
-            d_region = mm(one_hot(t_ref[...], rows), r_ref[...], TN)
-            normed = n_ref[...]
-            low = norm_back(d_region, normed, i_ref[:, 0:1], g_ref[...]).astype(bf16)
-            dpre[...] = low
-            bg_ref[...] = mm(wb_ref[...], low, NT)
-            boxes_grad = mm(box_ref[...], low)
-            vectors = [
-                row_sum(low.astype(f32)),
-                row_sum(d_region * normed),
-                row_sum(d_region),
-                sf_ref[0:1, :],
-                sf_ref[1:2, :],
-                sf_ref[2:3, :],
-                sn_ref[0:1, :],
-                sn_ref[1:2, :],
-                sn_ref[2:3, :],
-            ] + [boxes_grad[at : at + 1] for at in range(box)]
-            small[...] = jnp.zeros_like(small)
-            lane = lax.broadcasted_iota(jnp.int32, (1, half), 1)
-            stats = jnp.zeros((1, half), f32)
-            for at in range(4):
-                total = jnp.sum(sf_ref[3 + at : 4 + at, :], 1, keepdims=True)
-                stats = jnp.where(lane == at, total, stats)
-            for group in range(groups):
-                small[group, 0:1, 0:ff_share] = su_ref[0:1, group * ff_share : (group + 1) * ff_share]
-                for side in range(2):
-                    first = group * 2 * share
-                    flat = jnp.concatenate([sa_ref[0:1, :], sa_ref[1:2, :]], 1)
-                    small[group, 1:2, 0 : 2 * share] = flat[:, first : first + 2 * share]
-                for at, value in enumerate(vectors):
-                    row, col = (1, 2) if at == 0 else (2 + (at - 1) // 3, (at - 1) % 3)
-                    small[group, row : row + 1, 128 * col : 128 * col + share] = value[
-                        :, group * share : (group + 1) * share
-                    ]
-                small[group, 6:7, :] = stats
-
-        got = mm(f_ref[...], dpre[...], TN)
-        mine = c_ref[0] == 0
-        for to_ref, low_half in ((send_ref, jnp.logical_not(mine)), (keep_ref, mine)):
-            chosen = jnp.where(low_half, got[:, :half], got[:, half:]).astype(bf16)
-            for group in range(per_step):
-                for bit in range(2):
-                    for piece in range(2):
-                        at = ((group * 2 + bit) * 2 + piece) * quarter
-                        to_ref[group, bit, piece, :quarter, :] = chosen[at : at + quarter]
-                        if piece == 0:
-                            to_ref[group, bit, piece, quarter:, :] = small[step * per_step + group].astype(bf16)
-                        else:
-                            to_ref[group, bit, piece, quarter:, :] = jnp.zeros((8, half), bf16)
-        fg_ref[...] = mm(dpre[...], wv_ref[...], NT)
-
-    out = pl.BlockSpec((per_step, 2, 2, tall, half), lambda i, s: (i, 0, 0, 0, 0))
+        bit2, bit4 = b_ref[1], b_ref[2]
+        got[...] = mm(f_ref[...], d_ref[...], TN) + mm(o_ref[...], p_ref[:rows, :], TN)
+
+        def fill(to_ref, at, which, group, x, piece):
+            here = pl.ds(pl.multiple_of(((group * 2 + x) * 2 + piece) * quarter, 8), quarter)
+            to_ref[at, which, :quarter, :] = got[here, :].astype(bf16)
+            number = step * per_step + group
+            other = p_ref[pl.ds(pl.multiple_of(rows + 8 * number, 8), 8), :]
+            to_ref[at, which, quarter:, :] = add(s_ref[number], other)
+
+        for group in range(per_step):
+            y = group % 2
+            at = step * (per_step // 2) + group // 2
+            fill(a_send, at, y, group, 1 - bit2, 0)
+            fill(a_keep, at, y, group, bit2, 0)
+
+            @pl.when(bit4 == y)
+            def _():
+                for x in range(2):
+                    fill(b_keep, at, x, group, x, 1)
+
+            @pl.when(bit4 != y)
+            def _():
+                for x in range(2):
+                    fill(b_send, at, x, group, x, 1)
+
     return pl.pallas_call(
         kernel,
         grid_spec=pltpu.PrefetchScalarGridSpec(
             num_scalar_prefetch=1,
             grid=(steps,),
             in_specs=[
-                whole((rows, width)),
-                whole((1, rows)),
-                whole((rows, width)),
-                whole((rows, 128)),
-                vec(width),
                 pl.BlockSpec((rows, part), lambda i, s: (0, i)),
-                whole(boxes.shape),
-                pl.BlockSpec((part, width), lambda i, s: (i, 0)),
-                whole(w_box_t.shape),
-                whole(sums_forward.shape),
-                whole(sums_ffn.shape),
-                whole(sums_up.shape),
-                whole(sums_attn.shape),
+                pl.BlockSpec((rows, part), lambda i, s: (0, i)),
+                VMEM,
+                VMEM,
+                VMEM,
             ],
-            out_specs=[out, out, pl.BlockSpec((rows, part), lambda i, s: (0, i)), whole((box, rows))],
-            scratch_shapes=[pltpu.VMEM((rows, width), bf16), pltpu.VMEM((groups, 8, half), f32)],
+            out_specs=[VMEM] * 4,
+            scratch_shapes=[pltpu.VMEM((part, half), f32)],
         ),
-        out_shape=[
-            pltpu.HBM((groups, 2, 2, tall, half), bf16),
-            pltpu.HBM((groups, 2, 2, tall, half), bf16),
-            pltpu.HBM((rows, feat), f32),
-            shape((box, rows)),
-        ],
-        compiler_params=params(20),
-        cost_estimate=cost(6),
-        name="region_backward",
-    )(
-        core, returned, far(target), far(normed), far(inv), far(gain), far(features), far(boxes), far(w_visual),
-        w_box_t, sums_forward, sums_ffn, sums_up, sums_attn,
-    )
+        out_shape=[near((high, 2, tall, half), bf16)] * 4,
+        compiler_params=params(10),
+        cost_estimate=cost(0.1),
+        name="visual_gradient",
+    )(bits, far(features), far(other_features), d_pre, other_d_pre, small)
+
+
+def feature_gradient(bits, d_pre, w_visual):
+    rows, width = d_pre.shape
+    feat = w_visual.shape[0]
+    steps = 4
+    part = feat // steps
+
+    def kernel(b_ref, d_ref, w_ref, o_ref):
+        o_ref[...] = mm(d_ref[...], w_ref[...], NT)
+
+    return pl.pallas_call(
+        kernel,
+        grid_spec=pltpu.PrefetchScalarGridSpec(
+            num_scalar_prefetch=1,
+            grid=(steps,),
+            in_specs=[VMEM, pl.BlockSpec((part, width), lambda i, s: (i, 0))],
+            out_specs=pl.BlockSpec((rows, part), lambda i, s: (0, i)),
+        ),
+        out_shape=shape((rows, feat)),
+        compiler_params=params(8),
+        cost_estimate=cost(10),
+        name="feature_gradient",
+    )(bits, d_pre, far(w_visual))
 
 
 def device_number():
@@ -885,9 +940,10 @@
     return halves[0][0]
 
 
-def spread(mine):
+def spread(mine, *late):
     over_x = swap(mine, 2)
-    return mine, over_x, swap(mine, 1), swap(over_x, 1)
+    over_core = swap(mine, 1)
+    return mine, over_x, over_core, swap(gate(over_x, *late), 1)
 
 
 def pick(b_ref, pieces, core, x):
@@ -898,19 +954,24 @@
     ).astype(f32)
 
 
-def finish_down(bits, pieces):
+def finish_ffn(bits, pieces):
     rows, cols = pieces[0].shape
-
-    def kernel(b_ref, p0, p1, p2, p3, down_ref):
+    half = rows // 2
+    part = rows // 4
+
+    def kernel(b_ref, p0, p1, p2, p3, down_ref, up_ref):
         for core in range(2):
             for x in range(2):
                 got = pick(b_ref, (p0[...], p1[...], p2[...], p3[...]), core, x)
-                down_ref[x * rows : (x + 1) * rows, core * cols : (core + 1) * cols] = got
-
-    outs = [shape((2 * rows, 2 * cols))]
+                down_ref[x * half : (x + 1) * half, core * cols : (core + 1) * cols] = got[:half]
+                for piece in range(2):
+                    at = ((core * 2 + x) * 2 + piece) * cols
+                    up_ref[:, at : at + cols] = got[half + piece * part : half + (piece + 1) * part]
+
+    outs = [shape((rows, 2 * cols)), shape((part, 8 * cols))]
     return scalar_call(
-        kernel, bits, pieces, [whole((rows, cols))] * 4, outs, [whole(o.shape) for o in outs], 1, 8, "finish_down", True
-    )[0]
+        kernel, bits, pieces, [whole((rows, cols))] * 4, outs, [whole(o.shape) for o in outs], 1, 12, "finish_ffn", True
+    )
 
 
 def finish_wide(bits, pieces, sizes):
@@ -1053,65 +1114,69 @@
     begun = attention_backward(sc, *att_ins, 0, 1, ())
 
     moved, up_kept, begun, sc = after_all(moved, up_kept, begun, sc)
+    down = moved[0]
     up = first_split(sc, up_kept, moved[1], groups)
-    down = join(sc, moved[0])
     down, up, begun, sc = after_all(down, up, begun, sc)
-    moved = over_two(up), swap(down[0], 8)
+    moved = over_two(up)
     d_qkv, text_grad, back_message, sums_attn = attention_backward(sc, *att_ins, 1, rest, tuple(begun))
 
     moved, down, d_qkv, back_message, sc = after_all(moved, down, d_qkv, back_message, sc)
-    up = second(sc, moved[0])
-    down = late_first(sc, down[1], moved[1])
+    up = second(sc, moved)
     up, down, sc = after_all(up, down, sc)
-    moved = over_other_two(up), late_move(down)
+    moved = over_other_two(up)
     qkvo_sent, qkvo_kept = qkvo_gradient(sc, x, d_qkv, context, d_attn)
 
     moved, down, qkvo_sent, qkvo_kept, back_message, sc = after_all(
         moved, down, qkvo_sent, qkvo_kept, back_message, sc
     )
-    up = join(sc, moved[0], place=apart)
-    down = late_rest(sc, down, moved[1])
-    up, down, qkvo_sent, qkvo_kept, back_message, sc = after_all(up, down, qkvo_sent, qkvo_kept, back_message, sc)
+    ffn = join(sc, down, moved, place=apart)
+    ffn, qkvo_sent, qkvo_kept, back_message, sc = after_all(ffn, qkvo_sent, qkvo_kept, back_message, sc)
     returned = lax.all_to_all(back_message, axes, split_axis=0, concat_axis=0, tiled=True)
+    other_features = swap(gate(region_features, qkvo_kept), 1)
     qkvo = first_split(sc, qkvo_kept, swap(qkvo_sent, 1), groups, apart)
-    up_moved = swap(up[0], 8)
-    down = spread(down)
-
     qkvo_moved = over_two(qkvo)
+    ffn_moved = swap(gate(ffn[0], *qkvo), 8)
     returned, sc = after_all(returned, gate(sc, *qkvo))
-    vis_sent, vis_kept, feature_grad, box_grad = region_backward(
-        sc, returned, region_target, vis_normed, vis_inv, visual_gain,
-        region_features, boxes, w_visual, w_box_t, sums_forward, sums_ffn, sums_up, sums_attn, groups,
-    )
-
-    up_moved, qkvo_moved, vis_sent, vis_kept, sc = after_all(up_moved, qkvo_moved, vis_sent, vis_kept, sc)
-    up = late_first(sc, up[1], up_moved)
+    d_pre, d_pre_sent, d_pre_kept, small, box_grad = region_norm_backward(
+        sc, returned, region_target, vis_normed, vis_inv, visual_gain, boxes, w_box_t,
+        sums_forward, sums_ffn, sums_up, sums_attn, groups,
+    )
+    vis = visual_gradient(
+        sc, region_features, other_features, d_pre_kept, swap(d_pre_sent, 1), small, groups
+    )
+    vis_moved = over_two(vis)
+    sc = gate(sc, *vis)
     qkvo = second(sc, qkvo_moved)
-    up, qkvo, vis_sent, sc = after_all(up, qkvo, vis_sent, sc)
-    vis_moved = swap(vis_sent, 1)
     qkvo_moved = over_other_two(qkvo)
-    up_moved = late_move(up)
-    vis = first_split(sc, vis_kept, vis_moved, groups)
-    vis_moved = over_two(vis)
-    g_down = finish_down(gate(sc, *vis), down)
-    sc = gate(sc, g_down)
+    ffn = late_first(gate(sc, *qkvo), ffn[1], ffn_moved)
+    ffn_moved = late_move(ffn)
+    feature_grad = feature_gradient(gate(sc, *ffn), d_pre, w_visual)
+
+    sc = gate(sc, feature_grad)
+    vis = second(sc, vis_moved)
+    vis_moved = over_other_two(vis)
+    sc = gate(sc, *vis)
     qkvo = join(sc, qkvo_moved)
     qkvo_moved = swap(qkvo[0], 8)
-    up = spread(late_rest(sc, up, up_moved))
-    vis = second(sc, vis_moved)
-    vis_moved = over_other_two(vis)
+    ffn = late_rest(sc, ffn, gate(ffn_moved, *qkvo))
+
+    vis = join(gate(sc, *qkvo, ffn), vis_moved)
+    vis_moved = swap(vis[0], 8)
+    sc = gate(sc, *vis)
     qkvo = late_first(sc, qkvo[1], qkvo_moved)
     qkvo_moved = late_move(qkvo)
-    vis = join(sc, vis_moved)
-    vis_moved = swap(vis[0], 8)
-    (g_up,) = finish_wide(gate(sc, *vis), up, (4 * width,))
-    sc = gate(sc, g_up)
-    qkvo = spread(late_rest(sc, qkvo, qkvo_moved))
-    vis = late_first(sc, vis[1], vis_moved)
+
+    vis = late_first(gate(sc, *qkvo), vis[1], vis_moved)
     vis_moved = late_move(vis)
-    g_qkv, g_out = finish_wide(gate(sc, *vis), qkvo, (3 * width, width))
-    vis = late_rest(gate(sc, g_qkv), vis, vis_moved)
-    vis = spread(gate(vis, g_qkv))
+    ffn = spread(ffn, *vis)
+    sc = gate(sc, *vis)
+    g_down, g_up = finish_ffn(sc, ffn)
+    qkvo = late_rest(sc, qkvo, gate(qkvo_moved, *vis))
+
+    vis = late_rest(sc, vis, gate(vis_moved, g_up, qkvo))
+    qkvo = spread(qkvo, vis)
+    g_qkv, g_out = finish_wide(gate(sc, vis), qkvo, (3 * width, width))
+    vis = spread(vis, g_qkv)
     g_visual, g_box_t, rms_values, *small = finish_visual(
         sc, vis, w_up.shape[1] // groups, width // groups, boxes.shape[0]
     )

time: 220 us -> 208 us (0.945)
  starting transfers between devices: 45 us -> 36.3 us
  waiting for transfers between devices: 45.6 us -> 42.6 us
    ppermute x40 -> x36, starting transfers between devices: 33.6 us -> 26.3 us  [swap(): lax.ppermute(values, ('dp', 'enc'), [(i, i ^ bit) for i in range(count)])]
    pallas_call x1 -> x3, Pallas kernels: 7.68 us -> 12.8 us  [the longest x1 5.26 us: feature_gradient(): pl.pallas_call(kernel, grid_spec=pltpu.PrefetchScalarGridSpec(num_scalar_...]
    pallas_call x20 -> x16, Pallas kernels: 24.7 us -> 21.4 us  [scalar_call(): pl.pallas_call(kernel, grid_spec=pltpu.PrefetchScalarGridSpec(num_scalar_...]
    ppermute x40 -> x36, waiting for transfers between devices: 33.8 us -> 30.8 us  [swap(): lax.ppermute(values, ('dp', 'enc'), [(i, i ^ bit) for i in range(count)])]
  transfers between devices with their start and end apart: 42 -> 38, of which waited for: 21 -> 21; matrix products, arithmetic and copies ran while one was open for 0% -> 0% of each run, Pallas kernels for 31% -> 35%
where the time goes in v5:
time: 208 us; the launch traced here: 207 us
  Pallas kernels  123 us (59%)
  waiting for transfers between devices  42.6 us (20%)
  starting transfers between devices  36.3 us (17%)
  local copies, waits for them, and re-layouts  3.85 us (2%)
    pallas_call x1, Pallas kernels, forward(): pl.pallas_call(kernel, grid_spec=pltpu.PrefetchScalarGridSpec(num_scalar_...  37.6 us
    ppermute x36, waiting for transfers between devices, swap(): lax.ppermute(values, ('dp', 'enc'), [(i, i ^ bit) for i in range(count)])  30.8 us
    ppermute x36, starting transfers between devices, swap(): lax.ppermute(values, ('dp', 'enc'), [(i, i ^ bit) for i in range(count)])  26.3 us
    pallas_call x16, Pallas kernels, scalar_call(): pl.pallas_call(kernel, grid_spec=pltpu.PrefetchScalarGridSpec(num_scalar_...  21.4 us
    pallas_call x2, Pallas kernels, attention_backward(): pl.pallas_call(kernel, grid_spec=pltpu.PrefetchScalarGridSpec(num_scalar_...  18.2 us
    pallas_call x2, Pallas kernels, ffn_backward(): pl.pallas_call(kernel, grid_spec=pltpu.PrefetchScalarGridSpec(num_scalar_...  10.8 us
    all_to_all x1, waiting for transfers between devices, on_device(): lax.all_to_all(message, axes, split_axis=0, concat_axis=0, tiled=True)  8 us
    all_to_all x1, starting transfers between devices, on_device(): lax.all_to_all(message, axes, split_axis=0, concat_axis=0, tiled=True)  7.3 us
  transfers between devices with their start and end apart: 38, of which 21 were waited for; matrix products, arithmetic and copies ran while one was open for 0% of the time, Pallas kernels for 35%

profile of v5, /device:TPU:0, one launch (start us, length us, event | category | flops | bytes accessed | tf_op | source)
XLA Modules:
  0.0 207.4 jit_solution(5541786138776309161)
XLA Ops:
  1.4 5.8 %region_forward.1 = (bf16[256,768]{1,0:T(8,128)(2,1)}, f32[256,768]{1,0:T(8,128)}, f32[256,128]{1,0:T(8,128)}) custom-call(bf16[256,2048]{1,0:T(8,128)(2,1)} %f_ref.3, bf16[4,256]{1,0:T(4,128)(2,1)} %box_ref.3, s32[1,256]{1,0:T(1,128)} %t_ref.7, bf16[2048,768]{1,0:T(8,128)(2,1)} %w_ref.3, bf16[4,768]{1,0:T(4,128)(2,1)S(1)} %bitcast.26, f32[768]{0:T(1024)} %b_ref.1, ...), custom_call_target="tpu_custom_call" | custom-call | flops 3000000000 | bytes 1048576 | tf_op jit(solution)/shard_map/region_forward/pallas_call | solution.py:112
  7.1 7.3 %all-to-all-start = ((bf16[32,8,768]{2,1,0:T(8,128)(2,1)}), bf16[32,8,768]{2,1,0:T(8,128)(2,1)S(1)}, u32[]{:S(2)}, u32[]{:S(2)}) async-start(bf16[32,8,768]{2,1,0:T(8,128)(2,1)} %bitcast.1), calls=%async_computation | async-start | bytes 786432 | tf_op jit(solution)/shard_map/all_to_all | solution.py:1082
  14.6 5.0 %text_qkv.1.tq_ref = bf16[384,2304]{1,0:T(8,128)(2,1)} custom-call(bf16[384,768]{1,0:T(8,128)(2,1)} %t_ref.6, bf16[768,2304]{1,0:T(8,128)(2,1)} %wq.3, f32[1,1536]{1,0:T(1,128)S(1)} %reshape.72.b_ref.qvb_ref), custom_call_target="tpu_custom_call" | custom-call | flops 3000000000 | bytes 1048576 | tf_op jit(solution)/shard_map/text_qkv/pallas_call | solution.py:142
  19.6 8.0 %all-to-all-done = bf16[32,8,768]{2,1,0:T(8,128)(2,1)S(1)} async-done(((bf16[32,8,768]{2,1,0:T(8,128)(2,1)}), bf16[32,8,768]{2,1,0:T(8,128)(2,1)S(1)}, u32[]{:S(2)}, u32[]{:S(2)}) %all-to-all-start) | async-done | bytes 393248 | tf_op jit(solution)/shard_map/all_to_all | solution.py:1082
  28.4 37.6 %forward.1 = (bf16[768,768]{1,0:T(8,128)(2,1)}, bf16[768,768]{1,0:T(8,128)(2,1)}, bf16[768,2304]{1,0:T(8,128)(2,1)}, bf16[18,256,512]{2,1,0:T(8,128)(2,1)}, bf16...) custom-call(s32[16]{0:T(128)S(1)} %pad_add_fusion.sc_ref.c_ref.b_ref, ...), custom_call_target="tpu_custom_call" | custom-call | flops 30000001024 | bytes 1048576 | tf_op jit(solution)/shard_map/forward/pallas_call | solution.py:312
  66.1 3.8 %ffn_backward.2 = (bf16[768,3072]{1,0:T(8,128)(2,1)S(1)}, f32[768,768]{1,0:T(8,128)S(1)}, bf16[768,768]{1,0:T(8,128)(2,1)S(1)}, f32[8,768]{1,0:T(8,128)S(1)}, f32[8,3072]{1,0:T(8,128)S(1)}) custom-call(s32[16]{0:T(128)S(1)} %pad_add_fusion.sc_ref.c_ref.b_ref, bf16[768,768]{1,0:T(8,128)(2,1)S(1)} %get-tuple-element.249.df_ref, ...), custom_call_target="tpu_custom_call" | custom-call | flops 4000000000 | bytes 1048576 | tf_op jit(solution)/shard_map/ffn_backward/pallas_call | solution.py:420
  70.8 1.4 first_split.3
  72.9 1.4 collective-permute-start.2
  74.2 7.1 %ffn_backward.3 = (bf16[768,3072]{1,0:T(8,128)(2,1)S(1)}, f32[768,768]{1,0:T(8,128)S(1)}, bf16[768,768]{1,0:T(8,128)(2,1)S(1)}, f32[8,768]{1,0:T(8,128)S(1)}, f32[8,3072]{1,0:T(8,128)S(1)}) custom-call(s32[16]{0:T(128)S(1)} %pad_add_fusion.sc_ref.c_ref.b_ref, ...), custom_call_target="tpu_custom_call", output_to_operand_aliasing={{0}: (9, {}), {1}: (10, {}), {2}: (11, {})} | custom-call | flops 8000000000 | bytes 1048576 | tf_op jit(solution)/shard_map/ffn_backward/pallas_call | solution.py:420
  81.3 4.7 %up_gradient.1 = (bf16[768,1536]{1,0:T(8,128)(2,1)S(1)}, bf16[768,1536]{1,0:T(8,128)(2,1)S(1)}) custom-call(s32[16]{0:T(128)S(1)} %pad_add_fusion.sc_ref.c_ref.b_ref, bf16[768,768]{1,0:T(8,128)(2,1)S(1)} %get-tuple-element.278.h_ref, bf16[768,3072]{1,0:T(8,128)(2,1)S(1)} %get-tuple-element.286.d_ref), custom_call_target="tpu_custom_call" | custom-call | flops 100000000 | bytes 1048576 | tf_op jit(solution)/shard_map/up_gradient/pallas_call | solution.py:455
  86.0 1.6 collective-permute-done.1.ar
  89.2 1.2 collective-permute-start.3
  90.4 1.0 collective-permute-start.4
  91.4 2.3 %copy-done.11 = bf16[18,256,512]{2,1,0:T(8,128)(2,1)S(1)} copy-done((bf16[18,256,512]{2,1,0:T(8,128)(2,1)S(1)}, bf16[18,256,512]{2,1,0:T(8,128)(2,1)}, u32[]{:S(2)}) %copy-start.11) | copy-done | bytes 4718616
  93.8 6.3 %attention_backward.2 = (bf16[768,2304]{1,0:T(8,128)(2,1)S(1)}, f32[384,768]{1,0:T(8,128)}, f32[256,768]{1,0:T(8,128)S(1)}, f32[8,768]{1,0:T(8,128)S(1)}) custom-call(s32[16]{0:T(128)S(1)} %pad_add_fusion.sc_ref.c_ref.b_ref, bf16[768,768]{1,0:T(8,128)(2,1)S(1)} %get-tuple-element.307.da_ref, f32[768,768]{1,0:T(8,128)S(1)} %get-tuple-element.308.dr_ref, ...), custom_call_target="tpu_custom_call" | custom-call | flops 5000000000 | bytes 1048576 | tf_op jit(solution)/shard_map/attention_backward/pallas_call | solution.py:534
  100.1 1.2 first_split.4
  101.3 1.1 collective-permute-start.6
  103.3 11.9 %attention_backward.3 = (bf16[768,2304]{1,0:T(8,128)(2,1)S(1)}, f32[384,768]{1,0:T(8,128)}, bf16[256,768]{1,0:T(8,128)(2,1)}, f32[8,768]{1,0:T(8,128)S(1)}) custom-call(s32[16]{0:T(128)S(1)} %pad_add_fusion.sc_ref.c_ref.b_ref, bf16[768,768]{1,0:T(8,128)(2,1)S(1)} %get-tuple-element.307.da_ref, ...), custom_call_target="tpu_custom_call", output_to_operand_aliasing={{0}: (8, {}), {1}: (9, {})} | custom-call | flops 10000000000 | bytes 1048576 | tf_op jit(solution)/shard_map/attention_backward/pallas_call | solution.py:534
  115.2 1.3 collective-permute-done.6.ar
  119.1 1.2 collective-permute-start.9
  120.3 7.0 %qkvo_gradient.1 = (bf16[768,1536]{1,0:T(8,128)(2,1)}, bf16[768,1536]{1,0:T(8,128)(2,1)}) custom-call(s32[16]{0:T(128)S(1)} %pad_add_fusion.sc_ref.c_ref.b_ref, bf16[768,768]{1,0:T(8,128)(2,1)S(1)} %copy-done.14, bf16[768,2304]{1,0:T(8,128)(2,1)S(1)} %get-tuple-element.369.dq_ref, bf16[768,768]{1,0:T(8,128)(2,1)S(1)} %copy-done.15, ...), custom_call_target="tpu_custom_call" | custom-call | flops 5000000000 | bytes 1048576 | tf_op jit(solution)/shard_map/qkvo_gradient/pallas_call | solution.py:591
  127.3 1.8 join_split.3
  129.5 2.6 %all-to-all-start.1 = ((bf16[32,8,768]{2,1,0:T(8,128)(2,1)}), bf16[32,8,768]{2,1,0:T(8,128)(2,1)S(1)}, u32[]{:S(2)}, u32[]{:S(2)}) async-start(bf16[32,8,768]{2,1,0:T(8,128)(2,1)} %bitcast.9), calls=%async_computation.1 | async-start | bytes 786432 | tf_op jit(solution)/shard_map/all_to_all | solution.py:1134
  132.2 1.7 collective-permute-done.10
  133.9 4.5 %first_split.5 = (bf16[4,2,96,384]{3,2,1,0:T(8,128)(2,1)}, bf16[4,2,96,384]{3,2,1,0:T(8,128)(2,1)}, bf16[4,2,96,384]{3,2,1,0:T(8,128)(2,1)}, bf16[4,2,96,384]{3,2,1,0:T(8,128)(2,1)}) custom-call(s32[16]{0:T(128)S(1)} %pad_add_fusion.sc_ref.c_ref.b_ref, bf16[4,2,96,1536]{3,2,1,0:T(8,128)(2,1)S(1)} %bitcast.21, bf16[4,2,96,1536]{3,2,1,0:T(8,128)(2,1)} %bitcast.12.r_ref), custom_call_target="tpu_custom_call" | custom-call | flops 1000000000 | bytes 1048576 | tf_op jit(solution)/shard_map/first_split/pallas_call | solution.py:793
  139.2 1.1 collective-permute-start.14
  141.4 3.8 %all-to-all-done.1 = bf16[32,8,768]{2,1,0:T(8,128)(2,1)S(1)} async-done(((bf16[32,8,768]{2,1,0:T(8,128)(2,1)}), bf16[32,8,768]{2,1,0:T(8,128)(2,1)S(1)}, u32[]{:S(2)}, u32[]{:S(2)}) %all-to-all-start.1) | async-done | bytes 393248 | tf_op jit(solution)/shard_map/all_to_all | solution.py:1134
  145.3 3.2 %region_norm_backward.1 = (bf16[256,768]{1,0:T(8,128)(2,1)S(1)}, bf16[320,384]{1,0:T(8,128)(2,1)S(1)}, bf16[256,384]{1,0:T(8,128)(2,1)S(1)}, bf16[8,8,384]{2,1,0:T(8,128)(2,1)S(1)}, f32[4,256]{1,0:T(4,128)}) custom-call(s32[16]{0:T(128)S(1)} %pad_add_fusion.sc_ref.c_ref.b_ref, bf16[256,768]{1,0:T(8,128)(2,1)S(1)} %bitcast.25, s32[1,256]{1,0:T(1,128)} %t_ref.7, ...), custom_call_target="tpu_custom_call" | custom-call | flops 100000000 | bytes 1048576 | tf_op jit(solution)/shard_map/region_norm_backward/pallas_call | solution.py:663
  148.5 1.5 collective-permute-done.12.p_ref
  150.0 4.3 %visual_gradient.1 = (bf16[4,2,72,384]{3,2,1,0:T(8,128)(2,1)S(1)}, bf16[4,2,72,384]{3,2,1,0:T(8,128)(2,1)S(1)}, bf16[4,2,72,384]{3,2,1,0:T(8,128)(2,1)S(1)}, bf16[4,2,72,384]{3,2,1,0:T(8,128)(2,1)S(1)}) custom-call(s32[16]{0:T(128)S(1)} %pad_add_fusion.sc_ref.c_ref.b_ref, bf16[256,2048]{1,0:T(8,128)(2,1)} %f_ref.3, ...), custom_call_target="tpu_custom_call" | custom-call | flops 100000000 | bytes 1048576 | tf_op jit(solution)/shard_map/visual_gradient/pallas_call | solution.py:732
  155.2 1.3 collective-permute-start.17
  158.2 1.2 collective-permute-start.19
  161.1 5.3 %feature_gradient.1 = f32[256,2048]{1,0:T(8,128)} custom-call(s32[16]{0:T(128)S(1)} %pad_add_fusion.sc_ref.c_ref.b_ref, bf16[256,768]{1,0:T(8,128)(2,1)S(1)} %get-tuple-element.425.d_ref, bf16[2048,768]{1,0:T(8,128)(2,1)} %w_ref.3), custom_call_target="tpu_custom_call" | custom-call | flops 10000000000 | bytes 1048576 | tf_op jit(solution)/shard_map/feature_gradient/pallas_call | solution.py:763
  169.0 1.4 collective-permute-start.21
  170.4 1.2 collective-permute-start.22
  171.6 2.9 %collective-permute-done.18.refs_1_ = bf16[4,96,384]{2,1,0:T(8,128)(2,1)S(1)} collective-permute-done((bf16[4,96,384]{2,1,0:T(8,128)(2,1)S(1)}, bf16[4,96,384]{2,1,0:T(8,128)(2,1)S(1)}, u32[]{:S(2)}, u32[]{:S(2)}) %collective-permute-start.18) | collective-permute-done | bytes 294944 | tf_op jit(solution)/shard_map/ppermute | solution.py:784
  176.0 2.3 %collective-permute-done.21.refs_1_ = bf16[4,72,384]{2,1,0:T(8,128)(2,1)S(1)} collective-permute-done((bf16[4,72,384]{2,1,0:T(8,128)(2,1)S(1)}, bf16[4,72,384]{2,1,0:T(8,128)(2,1)S(1)}, u32[]{:S(2)}, u32[]{:S(2)}) %collective-permute-start.21) | collective-permute-done | bytes 221216 | tf_op jit(solution)/shard_map/ppermute | solution.py:784
  179.8 1.6 collective-permute-start.26
  181.4 2.8 %collective-permute-done.23.r_ref = bf16[2,192,384]{2,1,0:T(8,128)(2,1)S(1)} collective-permute-done((bf16[2,192,384]{2,1,0:T(8,128)(2,1)S(1)}, bf16[2,192,384]{2,1,0:T(8,128)(2,1)S(1)}, u32[]{:S(2)}, u32[]{:S(2)}) %collective-permute-start.23) | collective-permute-done | bytes 294944 | tf_op jit(solution)/shard_map/ppermute | solution.py:784
  185.5 3.3 %collective-permute-done.24.r_ref = bf16[2,144,384]{2,1,0:T(8,128)(2,1)S(1)} collective-permute-done((bf16[2,144,384]{2,1,0:T(8,128)(2,1)S(1)}, bf16[2,144,384]{2,1,0:T(8,128)(2,1)S(1)}, u32[]{:S(2)}, u32[]{:S(2)}) %collective-permute-start.24) | collective-permute-done | bytes 221216 | tf_op jit(solution)/shard_map/ppermute | solution.py:784
  189.9 2.6 %collective-permute-done.29 = bf16[1,192,384]{2,1,0:T(8,128)(2,1)S(1)} collective-permute-done((bf16[1,192,384]{2,1,0:T(8,128)(2,1)S(1)}, bf16[1,192,384]{2,1,0:T(8,128)(2,1)S(1)}, u32[]{:S(2)}, u32[]{:S(2)}) %collective-permute-start.29) | collective-permute-done | bytes 147488 | tf_op jit(solution)/shard_map/ppermute | solution.py:784
  192.5 1.1 collective-permute-start.32
  193.6 2.4 %finish_ffn.1 = (f32[384,768]{1,0:T(8,128)}, f32[96,3072]{1,0:T(8,128)}) custom-call(s32[16]{0:T(128)S(1)} %pad_add_fusion.sc_ref.c_ref.b_ref, bf16[384,384]{1,0:T(8,128)(2,1)S(1)} %add_bitcast_fusion.p0, bf16[384,384]{1,0:T(8,128)(2,1)S(1)} %collective-permute-done.26.p1, bf16[384,384]{1,0:T(8,128)(2,1)S(1)} %collective-permute-done.27.p2, ...), custom_call_target="tpu_custom_call" | custom-call | flops 1000000000 | bytes 1048576 | tf_op jit(solution)/shard_map/finish_ffn/pallas_call | solution.py:793
  196.0 2.3 %collective-permute-done.25 = bf16[1,144,384]{2,1,0:T(8,128)(2,1)S(1)} collective-permute-done((bf16[1,144,384]{2,1,0:T(8,128)(2,1)S(1)}, bf16[1,144,384]{2,1,0:T(8,128)(2,1)S(1)}, u32[]{:S(2)}, u32[]{:S(2)}) %collective-permute-start.25) | collective-permute-done | bytes 110624 | tf_op jit(solution)/shard_map/ppermute | solution.py:784
  200.2 1.7 finish_wide.1
  201.9 2.4 %collective-permute-done.30.p1 = bf16[144,384]{1,0:T(8,128)(2,1)S(1)} collective-permute-done((bf16[144,384]{1,0:T(8,128)(2,1)S(1)}, bf16[144,384]{1,0:T(8,128)(2,1)S(1)}, u32[]{:S(2)}, u32[]{:S(2)}) %collective-permute-start.30) | collective-permute-done | bytes 110624 | tf_op jit(solution)/shard_map/ppermute | solution.py:784
  204.3 1.3 collective-permute-done.35.p3
  205.6 1.6 finish_visual.1
  (104 shorter events, 24.9 us)
Async XLA Ops:
  1.4 13.1 %copy-start.17 = (f32[1536]{0:T(1024)S(1)}, f32[1536]{0:T(1024)}, u32[]{:S(2)}) copy-start(f32[1536]{0:T(1024)} %param.40) | copy-start | bytes 18436
  1.4 13.1 %copy-start.18 = (s32[2]{0:T(128)S(1)}, s32[2]{0:T(128)}, u32[]{:S(2)}) copy-start(s32[2]{0:T(128)} %param.31) | copy-start | bytes 28
  1.4 13.1 %copy-start.19 = (s32[3]{0:T(128)S(1)}, s32[3]{0:T(128)}, u32[]{:S(2)}) copy-start(s32[3]{0:T(128)} %param.30) | copy-start | bytes 40
  1.4 13.2 %copy-start.20 = (s32[3]{0:T(128)S(1)}, s32[3]{0:T(128)}, u32[]{:S(2)}) copy-start(s32[3]{0:T(128)} %param.29) | copy-start | bytes 40
  7.1 20.5 %all-to-all-start = ((bf16[32,8,768]{2,1,0:T(8,128)(2,1)}), bf16[32,8,768]{2,1,0:T(8,128)(2,1)S(1)}, u32[]{:S(2)}, u32[]{:S(2)}) async-start(bf16[32,8,768]{2,1,0:T(8,128)(2,1)} %bitcast.1), calls=%async_computation | async-start | bytes 786432 | tf_op jit(solution)/shard_map/all_to_all | solution.py:1082
  28.4 37.7 %copy-start.5 = (f32[768]{0:T(1024)S(1)}, f32[768]{0:T(1024)}, u32[]{:S(2)}) copy-start(f32[768]{0:T(1024)} %ag_ref.5) | copy-start | bytes 9220
  66.0 4.8 %collective-permute-start = (bf16[8,2,2,96,384]{4,3,2,1,0:T(8,128)(2,1)}, bf16[8,2,2,96,384]{4,3,2,1,0:T(8,128)(2,1)S(1)}, u32[]{:S(2)}, u32[]{:S(2)}) collective-permute-start(bf16[8,2,2,96,384]{4,3,2,1,0:T(8,128)(2,1)} %bitcast.29), channel_id=1, source_target_pairs={{0,1},{1,0},{2,3},{3,2},{4,5},{5,4},{6,7},{7,6},{8,9},{9,8},{10,11... | collective-permute-start | bytes 7077896 | tf_op jit(solution)/shard_map/ppermute | solution.py:784
  72.2 15.4 %collective-permute-start.1 = (bf16[4,2,96,384]{3,2,1,0:T(8,128)(2,1)S(1)}, bf16[4,2,96,384]{3,2,1,0:T(8,128)(2,1)S(1)}, u32[]{:S(2)}, u32[]{:S(2)}) collective-permute-start(bf16[4,2,96,384]{3,2,1,0:T(8,128)(2,1)S(1)} %get-tuple-element.273), channel_id=1, source_target_pairs={{0,2},{1,3},{2,0},{3,1},{4,6},{5,7},{6,4},{7,5},{8,10},{9,11},{10,... | collective-permute-start | bytes 1769480 | tf_op jit(solution)/shard_map/ppermute | solution.py:784
  72.9 15.3 %collective-permute-start.2 = (bf16[4,2,96,384]{3,2,1,0:T(8,128)(2,1)S(1)}, bf16[4,2,96,384]{3,2,1,0:T(8,128)(2,1)S(1)}, u32[]{:S(2)}, u32[]{:S(2)}) collective-permute-start(bf16[4,2,96,384]{3,2,1,0:T(8,128)(2,1)S(1)} %get-tuple-element.275), channel_id=1, source_target_pairs={{0,4},{1,5},{2,6},{3,7},{4,0},{5,1},{6,2},{7,3},{8,12},{9,13},{10,... | collective-permute-start | bytes 1769480 | tf_op jit(solution)/shard_map/ppermute | solution.py:784
  81.3 10.1 %copy-start.7 = (bf16[768,768]{1,0:T(8,128)(2,1)S(1)}, bf16[768,768]{1,0:T(8,128)(2,1)}, u32[]{:S(2)}) copy-start(bf16[768,768]{1,0:T(8,128)(2,1)} %wo_ref.3) | copy-start | bytes 3538948
  81.3 10.1 %copy-start.12 = (bf16[768,2304]{1,0:T(8,128)(2,1)S(1)}, bf16[768,2304]{1,0:T(8,128)(2,1)}, u32[]{:S(2)}) copy-start(bf16[768,2304]{1,0:T(8,128)(2,1)} %get-tuple-element.310.qkv_ref) | copy-start | bytes 10616836
  89.1 11.0 %collective-permute-start.5 = (bf16[768,1536]{1,0:T(8,128)(2,1)S(1)}, bf16[768,1536]{1,0:T(8,128)(2,1)S(1)}, u32[]{:S(2)}, u32[]{:S(2)}) collective-permute-start(bf16[768,1536]{1,0:T(8,128)(2,1)S(1)} %get-tuple-element.304), channel_id=1, source_target_pairs={{0,1},{1,0},{2,3},{3,2},{4,5},{5,4},{6,7},{7,6},{8,9},{9,8},{10,11... | collective-permute-start | bytes 7077896 | tf_op jit(solution)/shard_map/ppermute | solution.py:784
  89.2 10.9 %collective-permute-start.3 = (bf16[4,96,384]{2,1,0:T(8,128)(2,1)S(1)}, bf16[4,96,384]{2,1,0:T(8,128)(2,1)S(1)}, u32[]{:S(2)}, u32[]{:S(2)}) collective-permute-start(bf16[4,96,384]{2,1,0:T(8,128)(2,1)S(1)} %get-tuple-element.300), channel_id=1, source_target_pairs={{0,4},{1,5},{2,6},{3,7},{4,0},{5,1},{6,2},{7,3},{8,12},{9,13},{10,... | collective-permute-start | bytes 884744 | tf_op jit(solution)/shard_map/ppermute | solution.py:784
  90.4 9.7 %collective-permute-start.4 = (bf16[4,96,384]{2,1,0:T(8,128)(2,1)S(1)}, bf16[4,96,384]{2,1,0:T(8,128)(2,1)S(1)}, u32[]{:S(2)}, u32[]{:S(2)}) collective-permute-start(bf16[4,96,384]{2,1,0:T(8,128)(2,1)S(1)} %get-tuple-element.302), channel_id=1, source_target_pairs={{0,2},{1,3},{2,0},{3,1},{4,6},{5,7},{6,4},{7,5},{8,10},{9,11},{10,... | collective-permute-start | bytes 884744 | tf_op jit(solution)/shard_map/ppermute | solution.py:784
  101.3 15.2 %collective-permute-start.6 = (bf16[4,2,96,384]{3,2,1,0:T(8,128)(2,1)S(1)}, bf16[4,2,96,384]{3,2,1,0:T(8,128)(2,1)S(1)}, u32[]{:S(2)}, u32[]{:S(2)}) collective-permute-start(bf16[4,2,96,384]{3,2,1,0:T(8,128)(2,1)S(1)} %get-tuple-element.336), channel_id=1, source_target_pairs={{0,2},{1,3},{2,0},{3,1},{4,6},{5,7},{6,4},{7,5},{8,10},{9,11},{10,... | collective-permute-start | bytes 1769480 | tf_op jit(solution)/shard_map/ppermute | solution.py:784
  102.4 14.8 %collective-permute-start.7 = (bf16[4,2,96,384]{3,2,1,0:T(8,128)(2,1)S(1)}, bf16[4,2,96,384]{3,2,1,0:T(8,128)(2,1)S(1)}, u32[]{:S(2)}, u32[]{:S(2)}) collective-permute-start(bf16[4,2,96,384]{3,2,1,0:T(8,128)(2,1)S(1)} %get-tuple-element.338), channel_id=1, source_target_pairs={{0,4},{1,5},{2,6},{3,7},{4,0},{5,1},{6,2},{7,3},{8,12},{9,13},{10,... | collective-permute-start | bytes 1769480 | tf_op jit(solution)/shard_map/ppermute | solution.py:784
  118.1 9.1 %collective-permute-start.8 = (bf16[4,96,384]{2,1,0:T(8,128)(2,1)S(1)}, bf16[4,96,384]{2,1,0:T(8,128)(2,1)S(1)}, u32[]{:S(2)}, u32[]{:S(2)}) collective-permute-start(bf16[4,96,384]{2,1,0:T(8,128)(2,1)S(1)} %get-tuple-element.359), channel_id=1, source_target_pairs={{0,4},{1,5},{2,6},{3,7},{4,0},{5,1},{6,2},{7,3},{8,12},{9,13},{10,... | collective-permute-start | bytes 884744 | tf_op jit(solution)/shard_map/ppermute | solution.py:784
  119.1 8.2 %collective-permute-start.9 = (bf16[4,96,384]{2,1,0:T(8,128)(2,1)S(1)}, bf16[4,96,384]{2,1,0:T(8,128)(2,1)S(1)}, u32[]{:S(2)}, u32[]{:S(2)}) collective-permute-start(bf16[4,96,384]{2,1,0:T(8,128)(2,1)S(1)} %get-tuple-element.361), channel_id=1, source_target_pairs={{0,2},{1,3},{2,0},{3,1},{4,6},{5,7},{6,4},{7,5},{8,10},{9,11},{10,... | collective-permute-start | bytes 884744 | tf_op jit(solution)/shard_map/ppermute | solution.py:784
  129.0 4.9 %collective-permute-start.10 = (bf16[768,1536]{1,0:T(8,128)(2,1)}, bf16[768,1536]{1,0:T(8,128)(2,1)}, u32[]{:S(2)}, u32[]{:S(2)}) collective-permute-start(bf16[768,1536]{1,0:T(8,128)(2,1)} %get-tuple-element.391), channel_id=1, source_target_pairs={{0,1},{1,0},{2,3},{3,2},{4,5},{5,4},{6,7},{7,6},{8,9},{9,8},{10,11... | collective-permute-start | bytes 7077896 | tf_op jit(solution)/shard_map/ppermute | solution.py:784
  129.0 19.4 %collective-permute-start.11 = (bf16[256,2048]{1,0:T(8,128)(2,1)}, bf16[256,2048]{1,0:T(8,128)(2,1)}, u32[]{:S(2)}, u32[]{:S(2)}) collective-permute-start(bf16[256,2048]{1,0:T(8,128)(2,1)} %f_ref.3), channel_id=1, source_target_pairs={{0,1},{1,0},{2,3},{3,2},{4,5},{5,4},{6,7},{7,6},{8,9},{9,8},{10,11... | collective-permute-start | bytes 3145736 | tf_op jit(solution)/shard_map/ppermute | solution.py:784
  129.5 15.7 %all-to-all-start.1 = ((bf16[32,8,768]{2,1,0:T(8,128)(2,1)}), bf16[32,8,768]{2,1,0:T(8,128)(2,1)S(1)}, u32[]{:S(2)}, u32[]{:S(2)}) async-start(bf16[32,8,768]{2,1,0:T(8,128)(2,1)} %bitcast.9), calls=%async_computation.1 | async-start | bytes 786432 | tf_op jit(solution)/shard_map/all_to_all | solution.py:1134
  133.9 11.3 %copy-start.3 = (bf16[768,4]{0,1:T(4,128)(2,1)S(1)}, bf16[768,4]{0,1:T(4,128)(2,1)}, u32[]{:S(2)}) copy-start(bf16[768,4]{0,1:T(4,128)(2,1)} %param.35) | copy-start | bytes 18436
  138.4 18.1 %copy-start.8 = (bf16[4,2,96,384]{3,2,1,0:T(8,128)(2,1)S(1)}, bf16[4,2,96,384]{3,2,1,0:T(8,128)(2,1)}, u32[]{:S(2)}) copy-start(bf16[4,2,96,384]{3,2,1,0:T(8,128)(2,1)} %get-tuple-element.393.ak) | copy-start | bytes 1769476
  138.4 18.1 %copy-start.9 = (bf16[4,2,96,384]{3,2,1,0:T(8,128)(2,1)S(1)}, bf16[4,2,96,384]{3,2,1,0:T(8,128)(2,1)}, u32[]{:S(2)}) copy-start(bf16[4,2,96,384]{3,2,1,0:T(8,128)(2,1)} %get-tuple-element.395.bk) | copy-start | bytes 1769476
  138.4 18.1 %collective-permute-start.13 = (bf16[4,2,96,384]{3,2,1,0:T(8,128)(2,1)}, bf16[4,2,96,384]{3,2,1,0:T(8,128)(2,1)S(1)}, u32[]{:S(2)}, u32[]{:S(2)}) collective-permute-start(bf16[4,2,96,384]{3,2,1,0:T(8,128)(2,1)} %get-tuple-element.392), channel_id=1, source_target_pairs={{0,2},{1,3},{2,0},{3,1},{4,6},{5,7},{6,4},{7,5},{8,10},{9,11},{10,... | collective-permute-start | bytes 1769480 | tf_op jit(solution)/shard_map/ppermute | solution.py:784
  139.2 17.2 %collective-permute-start.14 = (bf16[4,2,96,384]{3,2,1,0:T(8,128)(2,1)}, bf16[4,2,96,384]{3,2,1,0:T(8,128)(2,1)S(1)}, u32[]{:S(2)}, u32[]{:S(2)}) collective-permute-start(bf16[4,2,96,384]{3,2,1,0:T(8,128)(2,1)} %get-tuple-element.394), channel_id=1, source_target_pairs={{0,4},{1,5},{2,6},{3,7},{4,0},{5,1},{6,2},{7,3},{8,12},{9,13},{10,... | collective-permute-start | bytes 1769480 | tf_op jit(solution)/shard_map/ppermute | solution.py:784
  140.4 19.0 %collective-permute-start.15 = (bf16[2,384,384]{2,1,0:T(8,128)(2,1)}, bf16[2,384,384]{2,1,0:T(8,128)(2,1)S(1)}, u32[]{:S(2)}, u32[]{:S(2)}) collective-permute-start(bf16[2,384,384]{2,1,0:T(8,128)(2,1)} %get-tuple-element.421), channel_id=1, source_target_pairs={{0,8},{1,9},{2,10},{3,11},{4,12},{5,13},{6,14},{7,15},{8,0},{9,1},... | collective-permute-start | bytes 1769480 | tf_op jit(solution)/shard_map/ppermute | solution.py:784
  148.5 1.5 collective-permute-start.12
  154.3 13.1 %collective-permute-start.16 = (bf16[4,2,72,384]{3,2,1,0:T(8,128)(2,1)S(1)}, bf16[4,2,72,384]{3,2,1,0:T(8,128)(2,1)S(1)}, u32[]{:S(2)}, u32[]{:S(2)}) collective-permute-start(bf16[4,2,72,384]{3,2,1,0:T(8,128)(2,1)S(1)} %get-tuple-element.409), channel_id=1, source_target_pairs={{0,2},{1,3},{2,0},{3,1},{4,6},{5,7},{6,4},{7,5},{8,10},{9,11},{10,... | collective-permute-start | bytes 1327112 | tf_op jit(solution)/shard_map/ppermute | solution.py:784
  155.2 13.0 %collective-permute-start.17 = (bf16[4,2,72,384]{3,2,1,0:T(8,128)(2,1)S(1)}, bf16[4,2,72,384]{3,2,1,0:T(8,128)(2,1)S(1)}, u32[]{:S(2)}, u32[]{:S(2)}) collective-permute-start(bf16[4,2,72,384]{3,2,1,0:T(8,128)(2,1)S(1)} %get-tuple-element.411), channel_id=1, source_target_pairs={{0,4},{1,5},{2,6},{3,7},{4,0},{5,1},{6,2},{7,3},{8,12},{9,13},{10,... | collective-permute-start | bytes 1327112 | tf_op jit(solution)/shard_map/ppermute | solution.py:784
  157.4 17.1 %collective-permute-start.18 = (bf16[4,96,384]{2,1,0:T(8,128)(2,1)S(1)}, bf16[4,96,384]{2,1,0:T(8,128)(2,1)S(1)}, u32[]{:S(2)}, u32[]{:S(2)}) collective-permute-start(bf16[4,96,384]{2,1,0:T(8,128)(2,1)S(1)} %get-tuple-element.414), channel_id=1, source_target_pairs={{0,4},{1,5},{2,6},{3,7},{4,0},{5,1},{6,2},{7,3},{8,12},{9,13},{10,... | collective-permute-start | bytes 884744 | tf_op jit(solution)/shard_map/ppermute | solution.py:784
  158.2 16.3 %collective-permute-start.19 = (bf16[4,96,384]{2,1,0:T(8,128)(2,1)S(1)}, bf16[4,96,384]{2,1,0:T(8,128)(2,1)S(1)}, u32[]{:S(2)}, u32[]{:S(2)}) collective-permute-start(bf16[4,96,384]{2,1,0:T(8,128)(2,1)S(1)} %get-tuple-element.416), channel_id=1, source_target_pairs={{0,2},{1,3},{2,0},{3,1},{4,6},{5,7},{6,4},{7,5},{8,10},{9,11},{10,... | collective-permute-start | bytes 884744 | tf_op jit(solution)/shard_map/ppermute | solution.py:784
  160.1 15.9 %collective-permute-start.20 = (bf16[1,384,384]{2,1,0:T(8,128)(2,1)S(1)}, bf16[1,384,384]{2,1,0:T(8,128)(2,1)S(1)}, u32[]{:S(2)}, u32[]{:S(2)}) collective-permute-start(bf16[1,384,384]{2,1,0:T(8,128)(2,1)S(1)} %get-tuple-element.422), channel_id=1, source_target_pairs={{0,16},{1,17},{2,18},{3,19},{4,20},{5,21},{6,22},{7,23},{8,24},{9,... | collective-permute-start | bytes 884744 | tf_op jit(solution)/shard_map/ppermute | solution.py:784
  169.0 9.3 %collective-permute-start.21 = (bf16[4,72,384]{2,1,0:T(8,128)(2,1)S(1)}, bf16[4,72,384]{2,1,0:T(8,128)(2,1)S(1)}, u32[]{:S(2)}, u32[]{:S(2)}) collective-permute-start(bf16[4,72,384]{2,1,0:T(8,128)(2,1)S(1)} %get-tuple-element.428), channel_id=1, source_target_pairs={{0,4},{1,5},{2,6},{3,7},{4,0},{5,1},{6,2},{7,3},{8,12},{9,13},{10,... | collective-permute-start | bytes 663560 | tf_op jit(solution)/shard_map/ppermute | solution.py:784
  170.4 8.0 %collective-permute-start.22 = (bf16[4,72,384]{2,1,0:T(8,128)(2,1)S(1)}, bf16[4,72,384]{2,1,0:T(8,128)(2,1)S(1)}, u32[]{:S(2)}, u32[]{:S(2)}) collective-permute-start(bf16[4,72,384]{2,1,0:T(8,128)(2,1)S(1)} %get-tuple-element.430), channel_id=1, source_target_pairs={{0,2},{1,3},{2,0},{3,1},{4,6},{5,7},{6,4},{7,5},{8,10},{9,11},{10,... | collective-permute-start | bytes 663560 | tf_op jit(solution)/shard_map/ppermute | solution.py:784
  175.3 8.9 %collective-permute-start.23 = (bf16[2,192,384]{2,1,0:T(8,128)(2,1)S(1)}, bf16[2,192,384]{2,1,0:T(8,128)(2,1)S(1)}, u32[]{:S(2)}, u32[]{:S(2)}) collective-permute-start(bf16[2,192,384]{2,1,0:T(8,128)(2,1)S(1)} %get-tuple-element.433), channel_id=1, source_target_pairs={{0,8},{1,9},{2,10},{3,11},{4,12},{5,13},{6,14},{7,15},{8,0},{9,1},... | collective-permute-start | bytes 884744 | tf_op jit(solution)/shard_map/ppermute | solution.py:784
  179.1 9.8 %collective-permute-start.24 = (bf16[2,144,384]{2,1,0:T(8,128)(2,1)S(1)}, bf16[2,144,384]{2,1,0:T(8,128)(2,1)S(1)}, u32[]{:S(2)}, u32[]{:S(2)}) collective-permute-start(bf16[2,144,384]{2,1,0:T(8,128)(2,1)S(1)} %get-tuple-element.437), channel_id=1, source_target_pairs={{0,8},{1,9},{2,10},{3,11},{4,12},{5,13},{6,14},{7,15},{8,0},{9,1},... | collective-permute-start | bytes 663560 | tf_op jit(solution)/shard_map/ppermute | solution.py:784
  179.8 9.7 %collective-permute-start.26 = (bf16[384,384]{1,0:T(8,128)(2,1)S(1)}, bf16[384,384]{1,0:T(8,128)(2,1)S(1)}, u32[]{:S(2)}, u32[]{:S(2)}) collective-permute-start(bf16[384,384]{1,0:T(8,128)(2,1)S(1)} %add_bitcast_fusion.p0), channel_id=1, source_target_pairs={{0,2},{1,3},{2,0},{3,1},{4,6},{5,7},{6,4},{7,5},{8,10},{9,11},{10,... | collective-permute-start | bytes 884744 | tf_op jit(solution)/shard_map/ppermute | solution.py:784
  181.4 12.3 %collective-permute-start.27 = (bf16[384,384]{1,0:T(8,128)(2,1)S(1)}, bf16[384,384]{1,0:T(8,128)(2,1)S(1)}, u32[]{:S(2)}, u32[]{:S(2)}) collective-permute-start(bf16[384,384]{1,0:T(8,128)(2,1)S(1)} %add_bitcast_fusion.p0), channel_id=1, source_target_pairs={{0,1},{1,0},{2,3},{3,2},{4,5},{5,4},{6,7},{7,6},{8,9},{9,8},{10,11... | collective-permute-start | bytes 884744 | tf_op jit(solution)/shard_map/ppermute | solution.py:784
  184.8 7.7 %collective-permute-start.29 = (bf16[1,192,384]{2,1,0:T(8,128)(2,1)S(1)}, bf16[1,192,384]{2,1,0:T(8,128)(2,1)S(1)}, u32[]{:S(2)}, u32[]{:S(2)}) collective-permute-start(bf16[1,192,384]{2,1,0:T(8,128)(2,1)S(1)} %get-tuple-element.440), channel_id=1, source_target_pairs={{0,16},{1,17},{2,18},{3,19},{4,20},{5,21},{6,22},{7,23},{8,24},{9,... | collective-permute-start | bytes 442376 | tf_op jit(solution)/shard_map/ppermute | solution.py:784
  189.5 4.2 %collective-permute-start.28 = (bf16[384,384]{1,0:T(8,128)(2,1)S(1)}, bf16[384,384]{1,0:T(8,128)(2,1)S(1)}, u32[]{:S(2)}, u32[]{:S(2)}) collective-permute-start(bf16[384,384]{1,0:T(8,128)(2,1)S(1)} %collective-permute-done.26.p1), channel_id=1, source_target_pairs={{0,1},{1,0},{2,3},{3,2},{4,5},{5,4},{6,7},{7,6},{8,9},{9,8},{10,11... | collective-permute-start | bytes 884744 | tf_op jit(solution)/shard_map/ppermute | solution.py:784
  189.5 8.7 %collective-permute-start.25 = (bf16[1,144,384]{2,1,0:T(8,128)(2,1)S(1)}, bf16[1,144,384]{2,1,0:T(8,128)(2,1)S(1)}, u32[]{:S(2)}, u32[]{:S(2)}) collective-permute-start(bf16[1,144,384]{2,1,0:T(8,128)(2,1)S(1)} %get-tuple-element.443), channel_id=1, source_target_pairs={{0,16},{1,17},{2,18},{3,19},{4,20},{5,21},{6,22},{7,23},{8,24},{9,... | collective-permute-start | bytes 331784 | tf_op jit(solution)/shard_map/ppermute | solution.py:784
  192.5 7.6 %collective-permute-start.33 = (bf16[192,384]{1,0:T(8,128)(2,1)S(1)}, bf16[192,384]{1,0:T(8,128)(2,1)S(1)}, u32[]{:S(2)}, u32[]{:S(2)}) collective-permute-start(bf16[192,384]{1,0:T(8,128)(2,1)S(1)} %add_bitcast_fusion.1.p0), channel_id=1, source_target_pairs={{0,1},{1,0},{2,3},{3,2},{4,5},{5,4},{6,7},{7,6},{8,9},{9,8},{10,11... | collective-permute-start | bytes 442376 | tf_op jit(solution)/shard_map/ppermute | solution.py:784
  192.5 6.3 %collective-permute-start.32 = (bf16[192,384]{1,0:T(8,128)(2,1)S(1)}, bf16[192,384]{1,0:T(8,128)(2,1)S(1)}, u32[]{:S(2)}, u32[]{:S(2)}) collective-permute-start(bf16[192,384]{1,0:T(8,128)(2,1)S(1)} %add_bitcast_fusion.1.p0), channel_id=1, source_target_pairs={{0,2},{1,3},{2,0},{3,1},{4,6},{5,7},{6,4},{7,5},{8,10},{9,11},{10,... | collective-permute-start | bytes 442376 | tf_op jit(solution)/shard_map/ppermute | solution.py:784
  198.8 1.4 collective-permute-start.34
  198.8 5.5 %collective-permute-start.30 = (bf16[144,384]{1,0:T(8,128)(2,1)S(1)}, bf16[144,384]{1,0:T(8,128)(2,1)S(1)}, u32[]{:S(2)}, u32[]{:S(2)}) collective-permute-start(bf16[144,384]{1,0:T(8,128)(2,1)S(1)} %add_bitcast_fusion.2.p0), channel_id=1, source_target_pairs={{0,2},{1,3},{2,0},{3,1},{4,6},{5,7},{6,4},{7,5},{8,10},{9,11},{10,... | collective-permute-start | bytes 331784 | tf_op jit(solution)/shard_map/ppermute | solution.py:784
  199.8 4.5 %collective-permute-start.31 = (bf16[144,384]{1,0:T(8,128)(2,1)S(1)}, bf16[144,384]{1,0:T(8,128)(2,1)S(1)}, u32[]{:S(2)}, u32[]{:S(2)}) collective-permute-start(bf16[144,384]{1,0:T(8,128)(2,1)S(1)} %add_bitcast_fusion.2.p0), channel_id=1, source_target_pairs={{0,1},{1,0},{2,3},{3,2},{4,5},{5,4},{6,7},{7,6},{8,9},{9,8},{10,11... | collective-permute-start | bytes 331784 | tf_op jit(solution)/shard_map/ppermute | solution.py:784
  204.3 1.3 collective-permute-start.35
  (11 other events, 46.6 us)

commit v6 on v5

--- a/solution.py
+++ b/solution.py
@@ -86,7 +86,7 @@
 def region_forward(features, boxes, target, w_visual, w_box_t, bias, gain, shift):
     rows, feat = features.shape
     width = w_visual.shape[1]
-    steps = 4
+    steps = 2
     part = feat // steps
 
     def kernel(f_ref, box_ref, t_ref, wv_ref, wb_ref, b_ref, g_ref, s_ref, m_ref, n_ref, i_ref, acc):
@@ -128,7 +128,7 @@
         compiler_params=params(24),
         cost_estimate=cost(3),
         name="region_forward",
-    )(far(features), far(boxes), far(target), far(w_visual), w_box_t, far(bias), far(gain), far(shift))
+    )(far(features), far(boxes), far(target), far(w_visual), far(w_box_t), far(bias), far(gain), far(shift))
 
 
 def text_qkv(text, w_qkv, qv_bias):
@@ -271,12 +271,16 @@
                 act_all[here, at] = (upper * phi).astype(bf16)
                 slope = phi + upper * jnp.exp(-0.5 * upper * upper) * inv_sqrt_tau
                 slope_ref[here, at] = slope.astype(bf16)
-
-            @pl.when(step == 0)
-            def _():
-                load(2).wait()
-
-            ffn_out = mm(act_all[here, :], wd[...]) + db_ref[...]
+                if piece == 0:
+
+                    @pl.when(step == 0)
+                    def _():
+                        load(2).wait()
+
+                term = mm(act_all[here, at], wd[at, :])
+                ffn_sum = term if piece == 0 else ffn_sum + term
+
+            ffn_out = ffn_sum + db_ref[...]
             ffn_normed, ffn_inv = norm_parts(hidden + ffn_out)
             out_ref[...] = ((ffn_normed * fg_ref[...] + fs_ref[...]) * row_mask).astype(bf16)
             cot = og_ref[...].astype(f32) * row_mask
@@ -317,7 +321,7 @@
             in_specs=[
                 rowwise(text_len, width),
                 rowwise(text_len, 3 * width),
-                whole((slots, width)),
+                VMEM,
                 whole((1, slots)),
                 rowwise(seq, width),
                 anywhere,
@@ -370,10 +374,13 @@
         name="forward",
     )(
         scalars,
+        far(text),
+        far(text_low),
+        arrived,
         *(
             far(v)
             for v in (
-                text, text_low, arrived, source, out_grad, w_qkv, qv_bias, w_out, out_bias,
+                source, out_grad, w_qkv, qv_bias, w_out, out_bias,
                 attn_gain, attn_shift, w_up, up_bias, w_down, down_bias, ffn_gain, ffn_shift,
             )
         ),
@@ -503,7 +510,7 @@
             d_c = d_ctx_ref[:, cols(0)]
             both_c = jnp.concatenate([d_c * masks[0], d_c * masks[1]], 0)
             both_q = jnp.concatenate([q * masks[0], q * masks[1]], 0)
-            low = p_ref[(first_caption + step) * (HEADS // 2) + pair]
+            low = p_ref[pair]
             d_probs = mm(v, both_c, NT)
             wide = low.astype(f32)
             both = wide * d_probs
@@ -515,7 +522,7 @@
             dqkv_ref[here, cols(2 * width)] = mm(low, both_c).astype(bf16)
             return carry
 
-        lax.fori_loop(0, HEADS // 2, pair_backward, 0, unroll=UNROLL)
+        lax.fori_loop(0, HEADS // 2, pair_backward, 0, unroll=3)
 
         sums_ref[0:1, :] += row_sum(dqkv_ref[here, :width].astype(f32))
         sums_ref[1:2, :] += row_sum(dqkv_ref[here, 2 * width :].astype(f32))
@@ -536,7 +543,8 @@
         grid_spec=pltpu.PrefetchScalarGridSpec(
             num_scalar_prefetch=1,
             grid=(size,),
-            in_specs=[VMEM] * 4
+            in_specs=[VMEM] * 2
+            + [pl.BlockSpec((HEADS // 2, seq, 2 * seq), lambda i, s: (i + first_caption, 0, 0)), VMEM]
             + [whole((1, slots)), VMEM, VMEM]
             + ([VMEM, pl.BlockSpec(memory_space=pl.ANY)] + [VMEM, VMEM] if begun else []),
             out_specs=[
@@ -560,7 +568,7 @@
         compiler_params=params(11),
         cost_estimate=cost(5 * size),
         name="attention_backward",
-    )(scalars, d_attn, d_resid, probs, qkv, source, w_out, w_qkv, *begun)
+    )(scalars, d_attn, d_resid, far(probs), qkv, source, w_out, w_qkv, *begun)
 
 
 def qkvo_gradient(core, x, d_qkv, context, d_attn):
@@ -568,39 +576,36 @@
 
     def kernel(c_ref, x_ref, dq_ref, ctx_ref, da_ref, send_ref, keep_ref):
         step = pl.program_id(0)
-        block = lax.rem(step + 2 * (1 - c_ref[0]), 4)
-        cols = pl.ds(pl.multiple_of(jnp.minimum(block, 2) * width, width), width)
-
-        def gradient(to_ref):
-            @pl.when(block < 3)
+
+        def store(low_block, high_block):
+            low, high = low_block.astype(bf16), high_block.astype(bf16)
+
+            @pl.when(c_ref[0] == 0)
             def _():
-                to_ref[...] = mm(x_ref[...], dq_ref[:, cols], TN).astype(bf16)
-
-            @pl.when(block == 3)
+                keep_ref[...] = low
+                send_ref[...] = high
+
+            @pl.when(c_ref[0] != 0)
             def _():
-                to_ref[...] = mm(ctx_ref[...], da_ref[...], TN).astype(bf16)
-
-        @pl.when(step < 2)
+                send_ref[...] = low
+                keep_ref[...] = high
+
+        @pl.when(step == 0)
         def _():
-            gradient(send_ref)
-
-        @pl.when(step >= 2)
+            store(mm(x_ref[...], dq_ref[:, :width], TN), mm(x_ref[...], dq_ref[:, 2 * width :], TN))
+
+        @pl.when(step == 1)
         def _():
-            gradient(keep_ref)
-
+            store(mm(x_ref[...], dq_ref[:, width : 2 * width], TN), mm(ctx_ref[...], da_ref[...], TN))
+
+    out = pl.BlockSpec((width, width), lambda i, s: (0, i))
     return pl.pallas_call(
         kernel,
         grid_spec=pltpu.PrefetchScalarGridSpec(
-            num_scalar_prefetch=1,
-            grid=(4,),
-            in_specs=[VMEM] * 4,
-            out_specs=[
-                pl.BlockSpec((width, width), lambda i, s: (0, jnp.minimum(i, 1))),
-                pl.BlockSpec((width, width), lambda i, s: (0, jnp.maximum(i - 2, 0))),
-            ],
+            num_scalar_prefetch=1, grid=(2,), in_specs=[VMEM] * 4, out_specs=[out, out]
         ),
         out_shape=[apart((width, 2 * width), bf16)] * 2,
-        compiler_params=params(11),
+        compiler_params=params(14),
         cost_estimate=cost(5),
         name="qkvo_gradient",
     )(core, x, d_qkv, context, d_attn)
@@ -688,7 +693,7 @@
         compiler_params=params(14),
         cost_estimate=cost(0.1),
         name="region_norm_backward",
-    )(core, returned, far(target), far(normed), far(inv), far(gain), far(boxes), w_box_t, *sizes)
+    )(core, returned, far(target), far(normed), far(inv), far(gain), far(boxes), far(w_box_t), *sizes)
 
 
 def visual_gradient(bits, features, other_features, d_pre, other_d_pre, small, groups):

time: 208 us -> 204 us (0.981)
  local copies, waits for them, and re-layouts: 3.85 us -> 0.83 us
    unnamed x42 -> x36, local copies, waits for them, and re-layouts: 3.84 us -> 0.82 us
    pallas_call x2, Pallas kernels: 18.2 us -> 20.5 us  [attention_backward(): pl.pallas_call(kernel, grid_spec=pltpu.PrefetchScalarGridSpec(num_scalar_...]
  transfers between devices with their start and end apart: 38 -> 38, of which waited for: 21 -> 21; matrix products, arithmetic and copies ran while one was open for 0% -> 0% of each run, Pallas kernels for 35% -> 37%
where the time goes in v6:
time: 204 us; the launch traced here: 203 us
  Pallas kernels  123 us (60%)
  waiting for transfers between devices  41.4 us (20%)
  starting transfers between devices  36.4 us (18%)
    pallas_call x1, Pallas kernels, forward(): pl.pallas_call(kernel, grid_spec=pltpu.PrefetchScalarGridSpec(num_scalar_...  36.2 us
    ppermute x36, waiting for transfers between devices, swap(): lax.ppermute(values, ('dp', 'enc'), [(i, i ^ bit) for i in range(count)])  29.6 us
    ppermute x36, starting transfers between devices, swap(): lax.ppermute(values, ('dp', 'enc'), [(i, i ^ bit) for i in range(count)])  26.5 us
    pallas_call x16, Pallas kernels, scalar_call(): pl.pallas_call(kernel, grid_spec=pltpu.PrefetchScalarGridSpec(num_scalar_...  21.4 us
    pallas_call x2, Pallas kernels, attention_backward(): pl.pallas_call(kernel, grid_spec=pltpu.PrefetchScalarGridSpec(num_scalar_...  20.5 us
    pallas_call x2, Pallas kernels, ffn_backward(): pl.pallas_call(kernel, grid_spec=pltpu.PrefetchScalarGridSpec(num_scalar_...  10.8 us
    all_to_all x1, waiting for transfers between devices, on_device(): lax.all_to_all(message, axes, split_axis=0, concat_axis=0, tiled=True)  8 us
    all_to_all x1, starting transfers between devices, on_device(): lax.all_to_all(message, axes, split_axis=0, concat_axis=0, tiled=True)  7.3 us
  transfers between devices with their start and end apart: 38, of which 21 were waited for; matrix products, arithmetic and copies ran while one was open for 0% of the time, Pallas kernels for 37%

profile of v6, /device:TPU:0, one launch (start us, length us, event | category | flops | bytes accessed | tf_op | source)
XLA Modules:
  0.0 203.0 jit_solution(15538193640898331371)
XLA Ops:
  0.7 4.8 %region_forward.1 = (bf16[256,768]{1,0:T(8,128)(2,1)}, f32[256,768]{1,0:T(8,128)}, f32[256,128]{1,0:T(8,128)}) custom-call(bf16[256,2048]{1,0:T(8,128)(2,1)} %f_ref.3, bf16[4,256]{1,0:T(4,128)(2,1)} %box_ref.3, s32[1,256]{1,0:T(1,128)} %t_ref.7, bf16[2048,768]{1,0:T(8,128)(2,1)} %w_ref.3, bf16[4,768]{1,0:T(4,128)(2,1)} %bitcast.27, f32[768]{0:T(1024)} %b_ref.1, ...), custom_call_target="tpu_custom_call" | custom-call | flops 3000000000 | bytes 1048576 | tf_op jit(solution)/shard_map/region_forward/pallas_call | solution.py:112
  5.5 7.3 %all-to-all-start = ((bf16[32,8,768]{2,1,0:T(8,128)(2,1)}), bf16[32,8,768]{2,1,0:T(8,128)(2,1)S(1)}, u32[]{:S(2)}, u32[]{:S(2)}) async-start(bf16[32,8,768]{2,1,0:T(8,128)(2,1)} %bitcast.1), calls=%async_computation | async-start | bytes 786432 | tf_op jit(solution)/shard_map/all_to_all | solution.py:1087
  12.9 5.0 %text_qkv.1.tq_ref = bf16[384,2304]{1,0:T(8,128)(2,1)} custom-call(bf16[384,768]{1,0:T(8,128)(2,1)} %t_ref.6, bf16[768,2304]{1,0:T(8,128)(2,1)} %wq.3, f32[1,1536]{1,0:T(1,128)S(1)} %reshape.72.b_ref.qvb_ref), custom_call_target="tpu_custom_call" | custom-call | flops 3000000000 | bytes 1048576 | tf_op jit(solution)/shard_map/text_qkv/pallas_call | solution.py:142
  17.9 8.0 %all-to-all-done = bf16[32,8,768]{2,1,0:T(8,128)(2,1)S(1)} async-done(((bf16[32,8,768]{2,1,0:T(8,128)(2,1)}), bf16[32,8,768]{2,1,0:T(8,128)(2,1)S(1)}, u32[]{:S(2)}, u32[]{:S(2)}) %all-to-all-start) | async-done | bytes 393248 | tf_op jit(solution)/shard_map/all_to_all | solution.py:1087
  26.7 36.2 %forward.1 = (bf16[768,768]{1,0:T(8,128)(2,1)}, bf16[768,768]{1,0:T(8,128)(2,1)}, bf16[768,2304]{1,0:T(8,128)(2,1)}, bf16[18,256,512]{2,1,0:T(8,128)(2,1)}, bf16...) custom-call(s32[16]{0:T(128)S(1)} %pad_add_fusion.sc_ref.c_ref.b_ref, ...), custom_call_target="tpu_custom_call" | custom-call | flops 30000001024 | bytes 1048576 | tf_op jit(solution)/shard_map/forward/pallas_call | solution.py:316
  63.0 3.8 %ffn_backward.2 = (bf16[768,3072]{1,0:T(8,128)(2,1)S(1)}, f32[768,768]{1,0:T(8,128)S(1)}, bf16[768,768]{1,0:T(8,128)(2,1)S(1)}, f32[8,768]{1,0:T(8,128)S(1)}, f32[8,3072]{1,0:T(8,128)S(1)}) custom-call(s32[16]{0:T(128)S(1)} %pad_add_fusion.sc_ref.c_ref.b_ref, bf16[768,768]{1,0:T(8,128)(2,1)S(1)} %get-tuple-element.249.df_ref, ...), custom_call_target="tpu_custom_call" | custom-call | flops 4000000000 | bytes 1048576 | tf_op jit(solution)/shard_map/ffn_backward/pallas_call | solution.py:427
  67.7 1.4 first_split.3
  69.8 1.4 collective-permute-start.2
  71.1 7.1 %ffn_backward.3 = (bf16[768,3072]{1,0:T(8,128)(2,1)S(1)}, f32[768,768]{1,0:T(8,128)S(1)}, bf16[768,768]{1,0:T(8,128)(2,1)S(1)}, f32[8,768]{1,0:T(8,128)S(1)}, f32[8,3072]{1,0:T(8,128)S(1)}) custom-call(s32[16]{0:T(128)S(1)} %pad_add_fusion.sc_ref.c_ref.b_ref, ...), custom_call_target="tpu_custom_call", output_to_operand_aliasing={{0}: (9, {}), {1}: (10, {}), {2}: (11, {})} | custom-call | flops 8000000000 | bytes 1048576 | tf_op jit(solution)/shard_map/ffn_backward/pallas_call | solution.py:427
  78.2 4.7 %up_gradient.1 = (bf16[768,1536]{1,0:T(8,128)(2,1)S(1)}, bf16[768,1536]{1,0:T(8,128)(2,1)S(1)}) custom-call(s32[16]{0:T(128)S(1)} %pad_add_fusion.sc_ref.c_ref.b_ref, bf16[768,768]{1,0:T(8,128)(2,1)S(1)} %get-tuple-element.278.h_ref, bf16[768,3072]{1,0:T(8,128)(2,1)S(1)} %get-tuple-element.286.d_ref), custom_call_target="tpu_custom_call" | custom-call | flops 100000000 | bytes 1048576 | tf_op jit(solution)/shard_map/up_gradient/pallas_call | solution.py:462
  82.9 1.6 collective-permute-done.1.ar
  86.1 1.2 collective-permute-start.3
  87.3 1.0 collective-permute-start.4
  88.3 7.6 %attention_backward.2 = (bf16[768,2304]{1,0:T(8,128)(2,1)S(1)}, f32[384,768]{1,0:T(8,128)}, f32[256,768]{1,0:T(8,128)S(1)}, f32[8,768]{1,0:T(8,128)S(1)}) custom-call(s32[16]{0:T(128)S(1)} %pad_add_fusion.sc_ref.c_ref.b_ref, bf16[768,768]{1,0:T(8,128)(2,1)S(1)} %get-tuple-element.307.da_ref, f32[768,768]{1,0:T(8,128)S(1)} %get-tuple-element.308.dr_ref, ...), custom_call_target="tpu_custom_call" | custom-call | flops 5000000000 | bytes 1048576 | tf_op jit(solution)/shard_map/attention_backward/pallas_call | solution.py:541
  96.4 1.2 first_split.4
  97.6 1.1 collective-permute-start.6
  98.7 1.0 collective-permute-start.7
  99.7 12.9 %attention_backward.3 = (bf16[768,2304]{1,0:T(8,128)(2,1)S(1)}, f32[384,768]{1,0:T(8,128)}, bf16[256,768]{1,0:T(8,128)(2,1)}, f32[8,768]{1,0:T(8,128)S(1)}) custom-call(s32[16]{0:T(128)S(1)} %pad_add_fusion.sc_ref.c_ref.b_ref, bf16[768,768]{1,0:T(8,128)(2,1)S(1)} %get-tuple-element.307.da_ref, ...), custom_call_target="tpu_custom_call", output_to_operand_aliasing={{0}: (8, {}), {1}: (9, {})} | custom-call | flops 10000000000 | bytes 1048576 | tf_op jit(solution)/shard_map/attention_backward/pallas_call | solution.py:541
  113.9 1.0 collective-permute-start.8
  115.0 1.1 collective-permute-start.9
  116.1 6.8 %qkvo_gradient.1 = (bf16[768,1536]{1,0:T(8,128)(2,1)}, bf16[768,1536]{1,0:T(8,128)(2,1)}) custom-call(s32[16]{0:T(128)S(1)} %pad_add_fusion.sc_ref.c_ref.b_ref, bf16[768,768]{1,0:T(8,128)(2,1)S(1)} %copy-done.11, bf16[768,2304]{1,0:T(8,128)(2,1)S(1)} %get-tuple-element.369.dq_ref, bf16[768,768]{1,0:T(8,128)(2,1)S(1)} %copy-done.12, ...), custom_call_target="tpu_custom_call" | custom-call | flops 5000000000 | bytes 1048576 | tf_op jit(solution)/shard_map/qkvo_gradient/pallas_call | solution.py:602
  122.9 1.7 join_split.3
  125.1 2.6 %all-to-all-start.1 = ((bf16[32,8,768]{2,1,0:T(8,128)(2,1)}), bf16[32,8,768]{2,1,0:T(8,128)(2,1)S(1)}, u32[]{:S(2)}, u32[]{:S(2)}) async-start(bf16[32,8,768]{2,1,0:T(8,128)(2,1)} %bitcast.9), calls=%async_computation.1 | async-start | bytes 786432 | tf_op jit(solution)/shard_map/all_to_all | solution.py:1139
  127.8 1.7 collective-permute-done.10
  129.5 4.5 %first_split.5 = (bf16[4,2,96,384]{3,2,1,0:T(8,128)(2,1)}, bf16[4,2,96,384]{3,2,1,0:T(8,128)(2,1)}, bf16[4,2,96,384]{3,2,1,0:T(8,128)(2,1)}, bf16[4,2,96,384]{3,2,1,0:T(8,128)(2,1)}) custom-call(s32[16]{0:T(128)S(1)} %pad_add_fusion.sc_ref.c_ref.b_ref, bf16[4,2,96,1536]{3,2,1,0:T(8,128)(2,1)S(1)} %bitcast.21, bf16[4,2,96,1536]{3,2,1,0:T(8,128)(2,1)} %bitcast.12.r_ref), custom_call_target="tpu_custom_call" | custom-call | flops 1000000000 | bytes 1048576 | tf_op jit(solution)/shard_map/first_split/pallas_call | solution.py:798
  134.9 1.1 collective-permute-start.14
  137.0 3.8 %all-to-all-done.1 = bf16[32,8,768]{2,1,0:T(8,128)(2,1)S(1)} async-done(((bf16[32,8,768]{2,1,0:T(8,128)(2,1)}), bf16[32,8,768]{2,1,0:T(8,128)(2,1)S(1)}, u32[]{:S(2)}, u32[]{:S(2)}) %all-to-all-start.1) | async-done | bytes 393248 | tf_op jit(solution)/shard_map/all_to_all | solution.py:1139
  140.8 3.2 %region_norm_backward.1 = (bf16[256,768]{1,0:T(8,128)(2,1)S(1)}, bf16[320,384]{1,0:T(8,128)(2,1)S(1)}, bf16[256,384]{1,0:T(8,128)(2,1)S(1)}, bf16[8,8,384]{2,1,0:T(8,128)(2,1)S(1)}, f32[4,256]{1,0:T(4,128)}) custom-call(s32[16]{0:T(128)S(1)} %pad_add_fusion.sc_ref.c_ref.b_ref, bf16[256,768]{1,0:T(8,128)(2,1)S(1)} %bitcast.25, s32[1,256]{1,0:T(1,128)} %t_ref.7, ...), custom_call_target="tpu_custom_call" | custom-call | flops 100000000 | bytes 1048576 | tf_op jit(solution)/shard_map/region_norm_backward/pallas_call | solution.py:668
  144.0 1.5 collective-permute-done.12.p_ref
  145.5 4.3 %visual_gradient.1 = (bf16[4,2,72,384]{3,2,1,0:T(8,128)(2,1)S(1)}, bf16[4,2,72,384]{3,2,1,0:T(8,128)(2,1)S(1)}, bf16[4,2,72,384]{3,2,1,0:T(8,128)(2,1)S(1)}, bf16[4,2,72,384]{3,2,1,0:T(8,128)(2,1)S(1)}) custom-call(s32[16]{0:T(128)S(1)} %pad_add_fusion.sc_ref.c_ref.b_ref, bf16[256,2048]{1,0:T(8,128)(2,1)} %f_ref.3, ...), custom_call_target="tpu_custom_call" | custom-call | flops 100000000 | bytes 1048576 | tf_op jit(solution)/shard_map/visual_gradient/pallas_call | solution.py:737
  150.7 1.3 collective-permute-start.17
  153.8 1.2 collective-permute-start.19
  156.7 5.3 %feature_gradient.1 = f32[256,2048]{1,0:T(8,128)} custom-call(s32[16]{0:T(128)S(1)} %pad_add_fusion.sc_ref.c_ref.b_ref, bf16[256,768]{1,0:T(8,128)(2,1)S(1)} %get-tuple-element.425.d_ref, bf16[2048,768]{1,0:T(8,128)(2,1)} %w_ref.3), custom_call_target="tpu_custom_call" | custom-call | flops 10000000000 | bytes 1048576 | tf_op jit(solution)/shard_map/feature_gradient/pallas_call | solution.py:768
  164.6 1.4 collective-permute-start.21
  166.0 1.2 collective-permute-start.22
  167.1 3.0 %collective-permute-done.18.refs_1_ = bf16[4,96,384]{2,1,0:T(8,128)(2,1)S(1)} collective-permute-done((bf16[4,96,384]{2,1,0:T(8,128)(2,1)S(1)}, bf16[4,96,384]{2,1,0:T(8,128)(2,1)S(1)}, u32[]{:S(2)}, u32[]{:S(2)}) %collective-permute-start.18) | collective-permute-done | bytes 294944 | tf_op jit(solution)/shard_map/ppermute | solution.py:789
  171.6 2.3 %collective-permute-done.21.refs_1_ = bf16[4,72,384]{2,1,0:T(8,128)(2,1)S(1)} collective-permute-done((bf16[4,72,384]{2,1,0:T(8,128)(2,1)S(1)}, bf16[4,72,384]{2,1,0:T(8,128)(2,1)S(1)}, u32[]{:S(2)}, u32[]{:S(2)}) %collective-permute-start.21) | collective-permute-done | bytes 221216 | tf_op jit(solution)/shard_map/ppermute | solution.py:789
  175.3 1.6 collective-permute-start.26
  177.0 2.8 %collective-permute-done.23.r_ref = bf16[2,192,384]{2,1,0:T(8,128)(2,1)S(1)} collective-permute-done((bf16[2,192,384]{2,1,0:T(8,128)(2,1)S(1)}, bf16[2,192,384]{2,1,0:T(8,128)(2,1)S(1)}, u32[]{:S(2)}, u32[]{:S(2)}) %collective-permute-start.23) | collective-permute-done | bytes 294944 | tf_op jit(solution)/shard_map/ppermute | solution.py:789
  181.1 3.3 %collective-permute-done.24.r_ref = bf16[2,144,384]{2,1,0:T(8,128)(2,1)S(1)} collective-permute-done((bf16[2,144,384]{2,1,0:T(8,128)(2,1)S(1)}, bf16[2,144,384]{2,1,0:T(8,128)(2,1)S(1)}, u32[]{:S(2)}, u32[]{:S(2)}) %collective-permute-start.24) | collective-permute-done | bytes 221216 | tf_op jit(solution)/shard_map/ppermute | solution.py:789
  185.5 2.6 %collective-permute-done.29 = bf16[1,192,384]{2,1,0:T(8,128)(2,1)S(1)} collective-permute-done((bf16[1,192,384]{2,1,0:T(8,128)(2,1)S(1)}, bf16[1,192,384]{2,1,0:T(8,128)(2,1)S(1)}, u32[]{:S(2)}, u32[]{:S(2)}) %collective-permute-start.29) | collective-permute-done | bytes 147488 | tf_op jit(solution)/shard_map/ppermute | solution.py:789
  188.1 1.1 collective-permute-start.32
  189.2 2.4 %finish_ffn.1 = (f32[384,768]{1,0:T(8,128)}, f32[96,3072]{1,0:T(8,128)}) custom-call(s32[16]{0:T(128)S(1)} %pad_add_fusion.sc_ref.c_ref.b_ref, bf16[384,384]{1,0:T(8,128)(2,1)S(1)} %add_bitcast_fusion.p0, bf16[384,384]{1,0:T(8,128)(2,1)S(1)} %collective-permute-done.26.p1, bf16[384,384]{1,0:T(8,128)(2,1)S(1)} %collective-permute-done.27.p2, ...), custom_call_target="tpu_custom_call" | custom-call | flops 1000000000 | bytes 1048576 | tf_op jit(solution)/shard_map/finish_ffn/pallas_call | solution.py:798
  191.6 2.3 %collective-permute-done.25 = bf16[1,144,384]{2,1,0:T(8,128)(2,1)S(1)} collective-permute-done((bf16[1,144,384]{2,1,0:T(8,128)(2,1)S(1)}, bf16[1,144,384]{2,1,0:T(8,128)(2,1)S(1)}, u32[]{:S(2)}, u32[]{:S(2)}) %collective-permute-start.25) | collective-permute-done | bytes 110624 | tf_op jit(solution)/shard_map/ppermute | solution.py:789
  195.8 1.7 finish_wide.1
  197.5 2.4 %collective-permute-done.30.p1 = bf16[144,384]{1,0:T(8,128)(2,1)S(1)} collective-permute-done((bf16[144,384]{1,0:T(8,128)(2,1)S(1)}, bf16[144,384]{1,0:T(8,128)(2,1)S(1)}, u32[]{:S(2)}, u32[]{:S(2)}) %collective-permute-start.30) | collective-permute-done | bytes 110624 | tf_op jit(solution)/shard_map/ppermute | solution.py:789
  199.9 1.3 collective-permute-done.35.p3
  201.2 1.6 finish_visual.1
  (98 shorter events, 22.6 us)
Async XLA Ops:
  0.7 12.1 %copy-start.14 = (f32[1536]{0:T(1024)S(1)}, f32[1536]{0:T(1024)}, u32[]{:S(2)}) copy-start(f32[1536]{0:T(1024)} %param.40) | copy-start | bytes 18436
  0.7 12.2 %copy-start.15 = (s32[2]{0:T(128)S(1)}, s32[2]{0:T(128)}, u32[]{:S(2)}) copy-start(s32[2]{0:T(128)} %param.31) | copy-start | bytes 28
  0.7 12.2 %copy-start.16 = (s32[3]{0:T(128)S(1)}, s32[3]{0:T(128)}, u32[]{:S(2)}) copy-start(s32[3]{0:T(128)} %param.30) | copy-start | bytes 40
  0.7 12.2 %copy-start.17 = (s32[3]{0:T(128)S(1)}, s32[3]{0:T(128)}, u32[]{:S(2)}) copy-start(s32[3]{0:T(128)} %param.29) | copy-start | bytes 40
  5.5 20.5 %all-to-all-start = ((bf16[32,8,768]{2,1,0:T(8,128)(2,1)}), bf16[32,8,768]{2,1,0:T(8,128)(2,1)S(1)}, u32[]{:S(2)}, u32[]{:S(2)}) async-start(bf16[32,8,768]{2,1,0:T(8,128)(2,1)} %bitcast.1), calls=%async_computation | async-start | bytes 786432 | tf_op jit(solution)/shard_map/all_to_all | solution.py:1087
  26.7 36.3 %copy-start.3 = (f32[768]{0:T(1024)S(1)}, f32[768]{0:T(1024)}, u32[]{:S(2)}) copy-start(f32[768]{0:T(1024)} %ag_ref.5) | copy-start | bytes 9220
  62.9 4.8 %collective-permute-start = (bf16[8,2,2,96,384]{4,3,2,1,0:T(8,128)(2,1)}, bf16[8,2,2,96,384]{4,3,2,1,0:T(8,128)(2,1)S(1)}, u32[]{:S(2)}, u32[]{:S(2)}) collective-permute-start(bf16[8,2,2,96,384]{4,3,2,1,0:T(8,128)(2,1)} %bitcast.29), channel_id=1, source_target_pairs={{0,1},{1,0},{2,3},{3,2},{4,5},{5,4},{6,7},{7,6},{8,9},{9,8},{10,11... | collective-permute-start | bytes 7077896 | tf_op jit(solution)/shard_map/ppermute | solution.py:789
  69.1 15.4 %collective-permute-start.1 = (bf16[4,2,96,384]{3,2,1,0:T(8,128)(2,1)S(1)}, bf16[4,2,96,384]{3,2,1,0:T(8,128)(2,1)S(1)}, u32[]{:S(2)}, u32[]{:S(2)}) collective-permute-start(bf16[4,2,96,384]{3,2,1,0:T(8,128)(2,1)S(1)} %get-tuple-element.273), channel_id=1, source_target_pairs={{0,2},{1,3},{2,0},{3,1},{4,6},{5,7},{6,4},{7,5},{8,10},{9,11},{10,... | collective-permute-start | bytes 1769480 | tf_op jit(solution)/shard_map/ppermute | solution.py:789
  69.8 15.3 %collective-permute-start.2 = (bf16[4,2,96,384]{3,2,1,0:T(8,128)(2,1)S(1)}, bf16[4,2,96,384]{3,2,1,0:T(8,128)(2,1)S(1)}, u32[]{:S(2)}, u32[]{:S(2)}) collective-permute-start(bf16[4,2,96,384]{3,2,1,0:T(8,128)(2,1)S(1)} %get-tuple-element.275), channel_id=1, source_target_pairs={{0,4},{1,5},{2,6},{3,7},{4,0},{5,1},{6,2},{7,3},{8,12},{9,13},{10,... | collective-permute-start | bytes 1769480 | tf_op jit(solution)/shard_map/ppermute | solution.py:789
  78.2 10.1 %copy-start.5 = (bf16[768,768]{1,0:T(8,128)(2,1)S(1)}, bf16[768,768]{1,0:T(8,128)(2,1)}, u32[]{:S(2)}) copy-start(bf16[768,768]{1,0:T(8,128)(2,1)} %wo_ref.3) | copy-start | bytes 3538948
  78.2 10.1 %copy-start.9 = (bf16[768,2304]{1,0:T(8,128)(2,1)S(1)}, bf16[768,2304]{1,0:T(8,128)(2,1)}, u32[]{:S(2)}) copy-start(bf16[768,2304]{1,0:T(8,128)(2,1)} %get-tuple-element.310.qkv_ref) | copy-start | bytes 10616836
  86.0 10.4 %collective-permute-start.5 = (bf16[768,1536]{1,0:T(8,128)(2,1)S(1)}, bf16[768,1536]{1,0:T(8,128)(2,1)S(1)}, u32[]{:S(2)}, u32[]{:S(2)}) collective-permute-start(bf16[768,1536]{1,0:T(8,128)(2,1)S(1)} %get-tuple-element.304), channel_id=1, source_target_pairs={{0,1},{1,0},{2,3},{3,2},{4,5},{5,4},{6,7},{7,6},{8,9},{9,8},{10,11... | collective-permute-start | bytes 7077896 | tf_op jit(solution)/shard_map/ppermute | solution.py:789
  86.1 9.9 %collective-permute-start.3 = (bf16[4,96,384]{2,1,0:T(8,128)(2,1)S(1)}, bf16[4,96,384]{2,1,0:T(8,128)(2,1)S(1)}, u32[]{:S(2)}, u32[]{:S(2)}) collective-permute-start(bf16[4,96,384]{2,1,0:T(8,128)(2,1)S(1)} %get-tuple-element.300), channel_id=1, source_target_pairs={{0,4},{1,5},{2,6},{3,7},{4,0},{5,1},{6,2},{7,3},{8,12},{9,13},{10,... | collective-permute-start | bytes 884744 | tf_op jit(solution)/shard_map/ppermute | solution.py:789
  87.3 9.1 %collective-permute-start.4 = (bf16[4,96,384]{2,1,0:T(8,128)(2,1)S(1)}, bf16[4,96,384]{2,1,0:T(8,128)(2,1)S(1)}, u32[]{:S(2)}, u32[]{:S(2)}) collective-permute-start(bf16[4,96,384]{2,1,0:T(8,128)(2,1)S(1)} %get-tuple-element.302), channel_id=1, source_target_pairs={{0,2},{1,3},{2,0},{3,1},{4,6},{5,7},{6,4},{7,5},{8,10},{9,11},{10,... | collective-permute-start | bytes 884744 | tf_op jit(solution)/shard_map/ppermute | solution.py:789
  97.6 15.1 %collective-permute-start.6 = (bf16[4,2,96,384]{3,2,1,0:T(8,128)(2,1)S(1)}, bf16[4,2,96,384]{3,2,1,0:T(8,128)(2,1)S(1)}, u32[]{:S(2)}, u32[]{:S(2)}) collective-permute-start(bf16[4,2,96,384]{3,2,1,0:T(8,128)(2,1)S(1)} %get-tuple-element.336), channel_id=1, source_target_pairs={{0,2},{1,3},{2,0},{3,1},{4,6},{5,7},{6,4},{7,5},{8,10},{9,11},{10,... | collective-permute-start | bytes 1769480 | tf_op jit(solution)/shard_map/ppermute | solution.py:789
  98.7 14.4 %collective-permute-start.7 = (bf16[4,2,96,384]{3,2,1,0:T(8,128)(2,1)S(1)}, bf16[4,2,96,384]{3,2,1,0:T(8,128)(2,1)S(1)}, u32[]{:S(2)}, u32[]{:S(2)}) collective-permute-start(bf16[4,2,96,384]{3,2,1,0:T(8,128)(2,1)S(1)} %get-tuple-element.338), channel_id=1, source_target_pairs={{0,4},{1,5},{2,6},{3,7},{4,0},{5,1},{6,2},{7,3},{8,12},{9,13},{10,... | collective-permute-start | bytes 1769480 | tf_op jit(solution)/shard_map/ppermute | solution.py:789
  113.9 9.0 %collective-permute-start.8 = (bf16[4,96,384]{2,1,0:T(8,128)(2,1)S(1)}, bf16[4,96,384]{2,1,0:T(8,128)(2,1)S(1)}, u32[]{:S(2)}, u32[]{:S(2)}) collective-permute-start(bf16[4,96,384]{2,1,0:T(8,128)(2,1)S(1)} %get-tuple-element.359), channel_id=1, source_target_pairs={{0,4},{1,5},{2,6},{3,7},{4,0},{5,1},{6,2},{7,3},{8,12},{9,13},{10,... | collective-permute-start | bytes 884744 | tf_op jit(solution)/shard_map/ppermute | solution.py:789
  115.0 7.9 %collective-permute-start.9 = (bf16[4,96,384]{2,1,0:T(8,128)(2,1)S(1)}, bf16[4,96,384]{2,1,0:T(8,128)(2,1)S(1)}, u32[]{:S(2)}, u32[]{:S(2)}) collective-permute-start(bf16[4,96,384]{2,1,0:T(8,128)(2,1)S(1)} %get-tuple-element.361), channel_id=1, source_target_pairs={{0,2},{1,3},{2,0},{3,1},{4,6},{5,7},{6,4},{7,5},{8,10},{9,11},{10,... | collective-permute-start | bytes 884744 | tf_op jit(solution)/shard_map/ppermute | solution.py:789
  122.9 6.6 %copy-start = (bf16[768,1536]{1,0:T(8,128)(2,1)S(1)}, bf16[768,1536]{1,0:T(8,128)(2,1)}, u32[]{:S(2)}) copy-start(bf16[768,1536]{1,0:T(8,128)(2,1)} %get-tuple-element.390) | copy-start | bytes 7077892
  124.6 4.9 %collective-permute-start.10 = (bf16[768,1536]{1,0:T(8,128)(2,1)}, bf16[768,1536]{1,0:T(8,128)(2,1)}, u32[]{:S(2)}, u32[]{:S(2)}) collective-permute-start(bf16[768,1536]{1,0:T(8,128)(2,1)} %get-tuple-element.391), channel_id=1, source_target_pairs={{0,1},{1,0},{2,3},{3,2},{4,5},{5,4},{6,7},{7,6},{8,9},{9,8},{10,11... | collective-permute-start | bytes 7077896 | tf_op jit(solution)/shard_map/ppermute | solution.py:789
  124.6 19.4 %collective-permute-start.11 = (bf16[256,2048]{1,0:T(8,128)(2,1)}, bf16[256,2048]{1,0:T(8,128)(2,1)}, u32[]{:S(2)}, u32[]{:S(2)}) collective-permute-start(bf16[256,2048]{1,0:T(8,128)(2,1)} %f_ref.3), channel_id=1, source_target_pairs={{0,1},{1,0},{2,3},{3,2},{4,5},{5,4},{6,7},{7,6},{8,9},{9,8},{10,11... | collective-permute-start | bytes 3145736 | tf_op jit(solution)/shard_map/ppermute | solution.py:789
  125.1 15.7 %all-to-all-start.1 = ((bf16[32,8,768]{2,1,0:T(8,128)(2,1)}), bf16[32,8,768]{2,1,0:T(8,128)(2,1)S(1)}, u32[]{:S(2)}, u32[]{:S(2)}) async-start(bf16[32,8,768]{2,1,0:T(8,128)(2,1)} %bitcast.9), calls=%async_computation.1 | async-start | bytes 786432 | tf_op jit(solution)/shard_map/all_to_all | solution.py:1139
  133.9 18.1 %copy-start.6 = (bf16[4,2,96,384]{3,2,1,0:T(8,128)(2,1)S(1)}, bf16[4,2,96,384]{3,2,1,0:T(8,128)(2,1)}, u32[]{:S(2)}) copy-start(bf16[4,2,96,384]{3,2,1,0:T(8,128)(2,1)} %get-tuple-element.393.ak) | copy-start | bytes 1769476
  133.9 18.1 %copy-start.7 = (bf16[4,2,96,384]{3,2,1,0:T(8,128)(2,1)S(1)}, bf16[4,2,96,384]{3,2,1,0:T(8,128)(2,1)}, u32[]{:S(2)}) copy-start(bf16[4,2,96,384]{3,2,1,0:T(8,128)(2,1)} %get-tuple-element.395.bk) | copy-start | bytes 1769476
  133.9 18.1 %collective-permute-start.13 = (bf16[4,2,96,384]{3,2,1,0:T(8,128)(2,1)}, bf16[4,2,96,384]{3,2,1,0:T(8,128)(2,1)S(1)}, u32[]{:S(2)}, u32[]{:S(2)}) collective-permute-start(bf16[4,2,96,384]{3,2,1,0:T(8,128)(2,1)} %get-tuple-element.392), channel_id=1, source_target_pairs={{0,2},{1,3},{2,0},{3,1},{4,6},{5,7},{6,4},{7,5},{8,10},{9,11},{10,... | collective-permute-start | bytes 1769480 | tf_op jit(solution)/shard_map/ppermute | solution.py:789
  134.9 17.1 %collective-permute-start.14 = (bf16[4,2,96,384]{3,2,1,0:T(8,128)(2,1)}, bf16[4,2,96,384]{3,2,1,0:T(8,128)(2,1)S(1)}, u32[]{:S(2)}, u32[]{:S(2)}) collective-permute-start(bf16[4,2,96,384]{3,2,1,0:T(8,128)(2,1)} %get-tuple-element.394), channel_id=1, source_target_pairs={{0,4},{1,5},{2,6},{3,7},{4,0},{5,1},{6,2},{7,3},{8,12},{9,13},{10,... | collective-permute-start | bytes 1769480 | tf_op jit(solution)/shard_map/ppermute | solution.py:789
  136.0 19.0 %collective-permute-start.15 = (bf16[2,384,384]{2,1,0:T(8,128)(2,1)}, bf16[2,384,384]{2,1,0:T(8,128)(2,1)S(1)}, u32[]{:S(2)}, u32[]{:S(2)}) collective-permute-start(bf16[2,384,384]{2,1,0:T(8,128)(2,1)} %get-tuple-element.421), channel_id=1, source_target_pairs={{0,8},{1,9},{2,10},{3,11},{4,12},{5,13},{6,14},{7,15},{8,0},{9,1},... | collective-permute-start | bytes 1769480 | tf_op jit(solution)/shard_map/ppermute | solution.py:789
  144.0 1.5 collective-permute-start.12
  149.9 13.1 %collective-permute-start.16 = (bf16[4,2,72,384]{3,2,1,0:T(8,128)(2,1)S(1)}, bf16[4,2,72,384]{3,2,1,0:T(8,128)(2,1)S(1)}, u32[]{:S(2)}, u32[]{:S(2)}) collective-permute-start(bf16[4,2,72,384]{3,2,1,0:T(8,128)(2,1)S(1)} %get-tuple-element.409), channel_id=1, source_target_pairs={{0,2},{1,3},{2,0},{3,1},{4,6},{5,7},{6,4},{7,5},{8,10},{9,11},{10,... | collective-permute-start | bytes 1327112 | tf_op jit(solution)/shard_map/ppermute | solution.py:789
  150.7 13.0 %collective-permute-start.17 = (bf16[4,2,72,384]{3,2,1,0:T(8,128)(2,1)S(1)}, bf16[4,2,72,384]{3,2,1,0:T(8,128)(2,1)S(1)}, u32[]{:S(2)}, u32[]{:S(2)}) collective-permute-start(bf16[4,2,72,384]{3,2,1,0:T(8,128)(2,1)S(1)} %get-tuple-element.411), channel_id=1, source_target_pairs={{0,4},{1,5},{2,6},{3,7},{4,0},{5,1},{6,2},{7,3},{8,12},{9,13},{10,... | collective-permute-start | bytes 1327112 | tf_op jit(solution)/shard_map/ppermute | solution.py:789
  153.0 17.1 %collective-permute-start.18 = (bf16[4,96,384]{2,1,0:T(8,128)(2,1)S(1)}, bf16[4,96,384]{2,1,0:T(8,128)(2,1)S(1)}, u32[]{:S(2)}, u32[]{:S(2)}) collective-permute-start(bf16[4,96,384]{2,1,0:T(8,128)(2,1)S(1)} %get-tuple-element.414), channel_id=1, source_target_pairs={{0,4},{1,5},{2,6},{3,7},{4,0},{5,1},{6,2},{7,3},{8,12},{9,13},{10,... | collective-permute-start | bytes 884744 | tf_op jit(solution)/shard_map/ppermute | solution.py:789
  153.8 16.3 %collective-permute-start.19 = (bf16[4,96,384]{2,1,0:T(8,128)(2,1)S(1)}, bf16[4,96,384]{2,1,0:T(8,128)(2,1)S(1)}, u32[]{:S(2)}, u32[]{:S(2)}) collective-permute-start(bf16[4,96,384]{2,1,0:T(8,128)(2,1)S(1)} %get-tuple-element.416), channel_id=1, source_target_pairs={{0,2},{1,3},{2,0},{3,1},{4,6},{5,7},{6,4},{7,5},{8,10},{9,11},{10,... | collective-permute-start | bytes 884744 | tf_op jit(solution)/shard_map/ppermute | solution.py:789
  155.7 15.9 %collective-permute-start.20 = (bf16[1,384,384]{2,1,0:T(8,128)(2,1)S(1)}, bf16[1,384,384]{2,1,0:T(8,128)(2,1)S(1)}, u32[]{:S(2)}, u32[]{:S(2)}) collective-permute-start(bf16[1,384,384]{2,1,0:T(8,128)(2,1)S(1)} %get-tuple-element.422), channel_id=1, source_target_pairs={{0,16},{1,17},{2,18},{3,19},{4,20},{5,21},{6,22},{7,23},{8,24},{9,... | collective-permute-start | bytes 884744 | tf_op jit(solution)/shard_map/ppermute | solution.py:789
  164.6 9.3 %collective-permute-start.21 = (bf16[4,72,384]{2,1,0:T(8,128)(2,1)S(1)}, bf16[4,72,384]{2,1,0:T(8,128)(2,1)S(1)}, u32[]{:S(2)}, u32[]{:S(2)}) collective-permute-start(bf16[4,72,384]{2,1,0:T(8,128)(2,1)S(1)} %get-tuple-element.428), channel_id=1, source_target_pairs={{0,4},{1,5},{2,6},{3,7},{4,0},{5,1},{6,2},{7,3},{8,12},{9,13},{10,... | collective-permute-start | bytes 663560 | tf_op jit(solution)/shard_map/ppermute | solution.py:789
  166.0 8.0 %collective-permute-start.22 = (bf16[4,72,384]{2,1,0:T(8,128)(2,1)S(1)}, bf16[4,72,384]{2,1,0:T(8,128)(2,1)S(1)}, u32[]{:S(2)}, u32[]{:S(2)}) collective-permute-start(bf16[4,72,384]{2,1,0:T(8,128)(2,1)S(1)} %get-tuple-element.430), channel_id=1, source_target_pairs={{0,2},{1,3},{2,0},{3,1},{4,6},{5,7},{6,4},{7,5},{8,10},{9,11},{10,... | collective-permute-start | bytes 663560 | tf_op jit(solution)/shard_map/ppermute | solution.py:789
  170.8 8.9 %collective-permute-start.23 = (bf16[2,192,384]{2,1,0:T(8,128)(2,1)S(1)}, bf16[2,192,384]{2,1,0:T(8,128)(2,1)S(1)}, u32[]{:S(2)}, u32[]{:S(2)}) collective-permute-start(bf16[2,192,384]{2,1,0:T(8,128)(2,1)S(1)} %get-tuple-element.433), channel_id=1, source_target_pairs={{0,8},{1,9},{2,10},{3,11},{4,12},{5,13},{6,14},{7,15},{8,0},{9,1},... | collective-permute-start | bytes 884744 | tf_op jit(solution)/shard_map/ppermute | solution.py:789
  174.7 9.8 %collective-permute-start.24 = (bf16[2,144,384]{2,1,0:T(8,128)(2,1)S(1)}, bf16[2,144,384]{2,1,0:T(8,128)(2,1)S(1)}, u32[]{:S(2)}, u32[]{:S(2)}) collective-permute-start(bf16[2,144,384]{2,1,0:T(8,128)(2,1)S(1)} %get-tuple-element.437), channel_id=1, source_target_pairs={{0,8},{1,9},{2,10},{3,11},{4,12},{5,13},{6,14},{7,15},{8,0},{9,1},... | collective-permute-start | bytes 663560 | tf_op jit(solution)/shard_map/ppermute | solution.py:789
  175.3 9.7 %collective-permute-start.26 = (bf16[384,384]{1,0:T(8,128)(2,1)S(1)}, bf16[384,384]{1,0:T(8,128)(2,1)S(1)}, u32[]{:S(2)}, u32[]{:S(2)}) collective-permute-start(bf16[384,384]{1,0:T(8,128)(2,1)S(1)} %add_bitcast_fusion.p0), channel_id=1, source_target_pairs={{0,2},{1,3},{2,0},{3,1},{4,6},{5,7},{6,4},{7,5},{8,10},{9,11},{10,... | collective-permute-start | bytes 884744 | tf_op jit(solution)/shard_map/ppermute | solution.py:789
  176.9 12.2 %collective-permute-start.27 = (bf16[384,384]{1,0:T(8,128)(2,1)S(1)}, bf16[384,384]{1,0:T(8,128)(2,1)S(1)}, u32[]{:S(2)}, u32[]{:S(2)}) collective-permute-start(bf16[384,384]{1,0:T(8,128)(2,1)S(1)} %add_bitcast_fusion.p0), channel_id=1, source_target_pairs={{0,1},{1,0},{2,3},{3,2},{4,5},{5,4},{6,7},{7,6},{8,9},{9,8},{10,11... | collective-permute-start | bytes 884744 | tf_op jit(solution)/shard_map/ppermute | solution.py:789
  180.4 7.7 %collective-permute-start.29 = (bf16[1,192,384]{2,1,0:T(8,128)(2,1)S(1)}, bf16[1,192,384]{2,1,0:T(8,128)(2,1)S(1)}, u32[]{:S(2)}, u32[]{:S(2)}) collective-permute-start(bf16[1,192,384]{2,1,0:T(8,128)(2,1)S(1)} %get-tuple-element.440), channel_id=1, source_target_pairs={{0,16},{1,17},{2,18},{3,19},{4,20},{5,21},{6,22},{7,23},{8,24},{9,... | collective-permute-start | bytes 442376 | tf_op jit(solution)/shard_map/ppermute | solution.py:789
  185.0 4.2 %collective-permute-start.28 = (bf16[384,384]{1,0:T(8,128)(2,1)S(1)}, bf16[384,384]{1,0:T(8,128)(2,1)S(1)}, u32[]{:S(2)}, u32[]{:S(2)}) collective-permute-start(bf16[384,384]{1,0:T(8,128)(2,1)S(1)} %collective-permute-done.26.p1), channel_id=1, source_target_pairs={{0,1},{1,0},{2,3},{3,2},{4,5},{5,4},{6,7},{7,6},{8,9},{9,8},{10,11... | collective-permute-start | bytes 884744 | tf_op jit(solution)/shard_map/ppermute | solution.py:789
  185.1 8.7 %collective-permute-start.25 = (bf16[1,144,384]{2,1,0:T(8,128)(2,1)S(1)}, bf16[1,144,384]{2,1,0:T(8,128)(2,1)S(1)}, u32[]{:S(2)}, u32[]{:S(2)}) collective-permute-start(bf16[1,144,384]{2,1,0:T(8,128)(2,1)S(1)} %get-tuple-element.443), channel_id=1, source_target_pairs={{0,16},{1,17},{2,18},{3,19},{4,20},{5,21},{6,22},{7,23},{8,24},{9,... | collective-permute-start | bytes 331784 | tf_op jit(solution)/shard_map/ppermute | solution.py:789
  188.0 7.6 %collective-permute-start.33 = (bf16[192,384]{1,0:T(8,128)(2,1)S(1)}, bf16[192,384]{1,0:T(8,128)(2,1)S(1)}, u32[]{:S(2)}, u32[]{:S(2)}) collective-permute-start(bf16[192,384]{1,0:T(8,128)(2,1)S(1)} %add_bitcast_fusion.1.p0), channel_id=1, source_target_pairs={{0,1},{1,0},{2,3},{3,2},{4,5},{5,4},{6,7},{7,6},{8,9},{9,8},{10,11... | collective-permute-start | bytes 442376 | tf_op jit(solution)/shard_map/ppermute | solution.py:789
  188.1 6.3 %collective-permute-start.32 = (bf16[192,384]{1,0:T(8,128)(2,1)S(1)}, bf16[192,384]{1,0:T(8,128)(2,1)S(1)}, u32[]{:S(2)}, u32[]{:S(2)}) collective-permute-start(bf16[192,384]{1,0:T(8,128)(2,1)S(1)} %add_bitcast_fusion.1.p0), channel_id=1, source_target_pairs={{0,2},{1,3},{2,0},{3,1},{4,6},{5,7},{6,4},{7,5},{8,10},{9,11},{10,... | collective-permute-start | bytes 442376 | tf_op jit(solution)/shard_map/ppermute | solution.py:789
  194.4 1.4 collective-permute-start.34
  194.4 5.5 %collective-permute-start.30 = (bf16[144,384]{1,0:T(8,128)(2,1)S(1)}, bf16[144,384]{1,0:T(8,128)(2,1)S(1)}, u32[]{:S(2)}, u32[]{:S(2)}) collective-permute-start(bf16[144,384]{1,0:T(8,128)(2,1)S(1)} %add_bitcast_fusion.2.p0), channel_id=1, source_target_pairs={{0,2},{1,3},{2,0},{3,1},{4,6},{5,7},{6,4},{7,5},{8,10},{9,11},{10,... | collective-permute-start | bytes 331784 | tf_op jit(solution)/shard_map/ppermute | solution.py:789
  195.4 4.5 %collective-permute-start.31 = (bf16[144,384]{1,0:T(8,128)(2,1)S(1)}, bf16[144,384]{1,0:T(8,128)(2,1)S(1)}, u32[]{:S(2)}, u32[]{:S(2)}) collective-permute-start(bf16[144,384]{1,0:T(8,128)(2,1)S(1)} %add_bitcast_fusion.2.p0), channel_id=1, source_target_pairs={{0,1},{1,0},{2,3},{3,2},{4,5},{5,4},{6,7},{7,6},{8,9},{9,8},{10,11... | collective-permute-start | bytes 331784 | tf_op jit(solution)/shard_map/ppermute | solution.py:789
  199.9 1.3 collective-permute-start.35
  (8 other events, 33.5 us)

commit v7 on v6

--- a/solution.py
+++ b/solution.py
@@ -296,10 +296,12 @@
                     row_mask * x_wide * x_wide,
                     row_mask * attn_out * attn_out,
                     row_mask * ffn_out * ffn_out,
-                    jnp.broadcast_to(row_mask, (seq, width)),
                 )
             ):
                 sums_ref[at : at + 1, :] += row_sum(value)
+            lane = lax.broadcasted_iota(jnp.int32, (1, width), 1)
+            slots_here = ((length + count) * width).astype(f32)
+            sums_ref[6:7, :] += jnp.where(lane == 0, slots_here, 0.0)
 
         @pl.when(step >= captions)
         def _():
@@ -565,7 +567,7 @@
             near((8, width)),
         ],
         input_output_aliases={8: 0, 9: 1} if begun else {},
-        compiler_params=params(11),
+        compiler_params=params(15),
         cost_estimate=cost(5 * size),
         name="attention_backward",
     )(scalars, d_attn, d_resid, far(probs), qkv, source, w_out, w_qkv, *begun)
@@ -699,7 +701,7 @@
 def visual_gradient(bits, features, other_features, d_pre, other_d_pre, small, groups):
     rows, feat = features.shape
     half = d_pre.shape[1]
-    steps = 4
+    steps = 2
     part = feat // steps
     quarter = feat // groups // 4
     tall = quarter + 8
@@ -750,7 +752,7 @@
             scratch_shapes=[pltpu.VMEM((part, half), f32)],
         ),
         out_shape=[near((high, 2, tall, half), bf16)] * 4,
-        compiler_params=params(10),
+        compiler_params=params(14),
         cost_estimate=cost(0.1),
         name="visual_gradient",
     )(bits, far(features), far(other_features), d_pre, other_d_pre, small)

time: 204 us -> 203 us (level)
  transfers between devices with their start and end apart: 38 -> 38, of which waited for: 21 -> 21; matrix products, arithmetic and copies ran while one was open for 0% -> 0% of each run, Pallas kernels for 37% -> 36%
where the time goes in v7:
time: 203 us; the launch traced here: 202 us
  Pallas kernels  122 us (60%)
  waiting for transfers between devices  41 us (20%)
  starting transfers between devices  36.8 us (18%)
    pallas_call x1, Pallas kernels, forward(): pl.pallas_call(kernel, grid_spec=pltpu.PrefetchScalarGridSpec(num_scalar_...  36.2 us
    ppermute x36, waiting for transfers between devices, swap(): lax.ppermute(values, ('dp', 'enc'), [(i, i ^ bit) for i in range(count)])  29.2 us
    ppermute x36, starting transfers between devices, swap(): lax.ppermute(values, ('dp', 'enc'), [(i, i ^ bit) for i in range(count)])  26.9 us
    pallas_call x16, Pallas kernels, scalar_call(): pl.pallas_call(kernel, grid_spec=pltpu.PrefetchScalarGridSpec(num_scalar_...  21.4 us
    pallas_call x2, Pallas kernels, attention_backward(): pl.pallas_call(kernel, grid_spec=pltpu.PrefetchScalarGridSpec(num_scalar_...  20.5 us
    pallas_call x2, Pallas kernels, ffn_backward(): pl.pallas_call(kernel, grid_spec=pltpu.PrefetchScalarGridSpec(num_scalar_...  10.8 us
    all_to_all x1, waiting for transfers between devices, on_device(): lax.all_to_all(message, axes, split_axis=0, concat_axis=0, tiled=True)  8 us
    all_to_all x1, starting transfers between devices, on_device(): lax.all_to_all(message, axes, split_axis=0, concat_axis=0, tiled=True)  7.3 us
  transfers between devices with their start and end apart: 38, of which 21 were waited for; matrix products, arithmetic and copies ran while one was open for 0% of the time, Pallas kernels for 36%

profile of v7, /device:TPU:0, one launch (start us, length us, event | category | flops | bytes accessed | tf_op | source)
XLA Modules:
  0.0 202.3 jit_solution(10200366395331384245)
XLA Ops:
  0.7 4.8 %region_forward.1 = (bf16[256,768]{1,0:T(8,128)(2,1)}, f32[256,768]{1,0:T(8,128)}, f32[256,128]{1,0:T(8,128)}) custom-call(bf16[256,2048]{1,0:T(8,128)(2,1)} %f_ref.3, bf16[4,256]{1,0:T(4,128)(2,1)} %box_ref.3, s32[1,256]{1,0:T(1,128)} %t_ref.7, bf16[2048,768]{1,0:T(8,128)(2,1)} %w_ref.3, bf16[4,768]{1,0:T(4,128)(2,1)} %bitcast.27, f32[768]{0:T(1024)} %b_ref.1, ...), custom_call_target="tpu_custom_call" | custom-call | flops 3000000000 | bytes 1048576 | tf_op jit(solution)/shard_map/region_forward/pallas_call | solution.py:112
  5.5 7.3 %all-to-all-start = ((bf16[32,8,768]{2,1,0:T(8,128)(2,1)}), bf16[32,8,768]{2,1,0:T(8,128)(2,1)S(1)}, u32[]{:S(2)}, u32[]{:S(2)}) async-start(bf16[32,8,768]{2,1,0:T(8,128)(2,1)} %bitcast.1), calls=%async_computation | async-start | bytes 786432 | tf_op jit(solution)/shard_map/all_to_all | solution.py:1089
  12.9 5.0 %text_qkv.1.tq_ref = bf16[384,2304]{1,0:T(8,128)(2,1)} custom-call(bf16[384,768]{1,0:T(8,128)(2,1)} %t_ref.6, bf16[768,2304]{1,0:T(8,128)(2,1)} %wq.3, f32[1,1536]{1,0:T(1,128)S(1)} %reshape.72.b_ref.qvb_ref), custom_call_target="tpu_custom_call" | custom-call | flops 3000000000 | bytes 1048576 | tf_op jit(solution)/shard_map/text_qkv/pallas_call | solution.py:142
  17.9 8.0 %all-to-all-done = bf16[32,8,768]{2,1,0:T(8,128)(2,1)S(1)} async-done(((bf16[32,8,768]{2,1,0:T(8,128)(2,1)}), bf16[32,8,768]{2,1,0:T(8,128)(2,1)S(1)}, u32[]{:S(2)}, u32[]{:S(2)}) %all-to-all-start) | async-done | bytes 393248 | tf_op jit(solution)/shard_map/all_to_all | solution.py:1089
  26.7 36.2 %forward.1 = (bf16[768,768]{1,0:T(8,128)(2,1)}, bf16[768,768]{1,0:T(8,128)(2,1)}, bf16[768,2304]{1,0:T(8,128)(2,1)}, bf16[18,256,512]{2,1,0:T(8,128)(2,1)}, bf16...) custom-call(s32[16]{0:T(128)S(1)} %pad_add_fusion.sc_ref.c_ref.b_ref, ...), custom_call_target="tpu_custom_call" | custom-call | flops 30000001024 | bytes 1048576 | tf_op jit(solution)/shard_map/forward/pallas_call | solution.py:318
  63.0 3.8 %ffn_backward.2 = (bf16[768,3072]{1,0:T(8,128)(2,1)S(1)}, f32[768,768]{1,0:T(8,128)S(1)}, bf16[768,768]{1,0:T(8,128)(2,1)S(1)}, f32[8,768]{1,0:T(8,128)S(1)}, f32[8,3072]{1,0:T(8,128)S(1)}) custom-call(s32[16]{0:T(128)S(1)} %pad_add_fusion.sc_ref.c_ref.b_ref, bf16[768,768]{1,0:T(8,128)(2,1)S(1)} %get-tuple-element.249.df_ref, ...), custom_call_target="tpu_custom_call" | custom-call | flops 4000000000 | bytes 1048576 | tf_op jit(solution)/shard_map/ffn_backward/pallas_call | solution.py:429
  67.7 1.4 first_split.3
  69.8 1.4 collective-permute-start.2
  71.2 7.1 %ffn_backward.3 = (bf16[768,3072]{1,0:T(8,128)(2,1)S(1)}, f32[768,768]{1,0:T(8,128)S(1)}, bf16[768,768]{1,0:T(8,128)(2,1)S(1)}, f32[8,768]{1,0:T(8,128)S(1)}, f32[8,3072]{1,0:T(8,128)S(1)}) custom-call(s32[16]{0:T(128)S(1)} %pad_add_fusion.sc_ref.c_ref.b_ref, ...), custom_call_target="tpu_custom_call", output_to_operand_aliasing={{0}: (9, {}), {1}: (10, {}), {2}: (11, {})} | custom-call | flops 8000000000 | bytes 1048576 | tf_op jit(solution)/shard_map/ffn_backward/pallas_call | solution.py:429
  78.3 4.7 %up_gradient.1 = (bf16[768,1536]{1,0:T(8,128)(2,1)S(1)}, bf16[768,1536]{1,0:T(8,128)(2,1)S(1)}) custom-call(s32[16]{0:T(128)S(1)} %pad_add_fusion.sc_ref.c_ref.b_ref, bf16[768,768]{1,0:T(8,128)(2,1)S(1)} %get-tuple-element.278.h_ref, bf16[768,3072]{1,0:T(8,128)(2,1)S(1)} %get-tuple-element.286.d_ref), custom_call_target="tpu_custom_call" | custom-call | flops 100000000 | bytes 1048576 | tf_op jit(solution)/shard_map/up_gradient/pallas_call | solution.py:464
  83.0 1.6 collective-permute-done.1.ar
  86.1 1.2 collective-permute-start.3
  88.4 7.6 %attention_backward.2 = (bf16[768,2304]{1,0:T(8,128)(2,1)S(1)}, f32[384,768]{1,0:T(8,128)}, f32[256,768]{1,0:T(8,128)S(1)}, f32[8,768]{1,0:T(8,128)S(1)}) custom-call(s32[16]{0:T(128)S(1)} %pad_add_fusion.sc_ref.c_ref.b_ref, bf16[768,768]{1,0:T(8,128)(2,1)S(1)} %get-tuple-element.307.da_ref, f32[768,768]{1,0:T(8,128)S(1)} %get-tuple-element.308.dr_ref, ...), custom_call_target="tpu_custom_call" | custom-call | flops 5000000000 | bytes 1048576 | tf_op jit(solution)/shard_map/attention_backward/pallas_call | solution.py:543
  96.4 1.2 first_split.4
  97.6 1.1 collective-permute-start.6
  98.7 1.0 collective-permute-start.7
  99.7 13.0 %attention_backward.3 = (bf16[768,2304]{1,0:T(8,128)(2,1)S(1)}, f32[384,768]{1,0:T(8,128)}, bf16[256,768]{1,0:T(8,128)(2,1)}, f32[8,768]{1,0:T(8,128)S(1)}) custom-call(s32[16]{0:T(128)S(1)} %pad_add_fusion.sc_ref.c_ref.b_ref, bf16[768,768]{1,0:T(8,128)(2,1)S(1)} %get-tuple-element.307.da_ref, ...), custom_call_target="tpu_custom_call", output_to_operand_aliasing={{0}: (8, {}), {1}: (9, {})} | custom-call | flops 10000000000 | bytes 1048576 | tf_op jit(solution)/shard_map/attention_backward/pallas_call | solution.py:543
  114.0 1.0 collective-permute-start.8
  115.0 1.1 collective-permute-start.9
  116.1 6.8 %qkvo_gradient.1 = (bf16[768,1536]{1,0:T(8,128)(2,1)}, bf16[768,1536]{1,0:T(8,128)(2,1)}) custom-call(s32[16]{0:T(128)S(1)} %pad_add_fusion.sc_ref.c_ref.b_ref, bf16[768,768]{1,0:T(8,128)(2,1)S(1)} %copy-done.11, bf16[768,2304]{1,0:T(8,128)(2,1)S(1)} %get-tuple-element.369.dq_ref, bf16[768,768]{1,0:T(8,128)(2,1)S(1)} %copy-done.12, ...), custom_call_target="tpu_custom_call" | custom-call | flops 5000000000 | bytes 1048576 | tf_op jit(solution)/shard_map/qkvo_gradient/pallas_call | solution.py:604
  122.9 1.7 join_split.3
  125.2 2.6 %all-to-all-start.1 = ((bf16[32,8,768]{2,1,0:T(8,128)(2,1)}), bf16[32,8,768]{2,1,0:T(8,128)(2,1)S(1)}, u32[]{:S(2)}, u32[]{:S(2)}) async-start(bf16[32,8,768]{2,1,0:T(8,128)(2,1)} %bitcast.9), calls=%async_computation.1 | async-start | bytes 786432 | tf_op jit(solution)/shard_map/all_to_all | solution.py:1141
  127.8 1.7 collective-permute-done.10
  129.5 4.5 %first_split.5 = (bf16[4,2,96,384]{3,2,1,0:T(8,128)(2,1)}, bf16[4,2,96,384]{3,2,1,0:T(8,128)(2,1)}, bf16[4,2,96,384]{3,2,1,0:T(8,128)(2,1)}, bf16[4,2,96,384]{3,2,1,0:T(8,128)(2,1)}) custom-call(s32[16]{0:T(128)S(1)} %pad_add_fusion.sc_ref.c_ref.b_ref, bf16[4,2,96,1536]{3,2,1,0:T(8,128)(2,1)S(1)} %bitcast.21, bf16[4,2,96,1536]{3,2,1,0:T(8,128)(2,1)} %bitcast.12.r_ref), custom_call_target="tpu_custom_call" | custom-call | flops 1000000000 | bytes 1048576 | tf_op jit(solution)/shard_map/first_split/pallas_call | solution.py:800
  135.0 1.1 collective-permute-start.14
  137.0 3.8 %all-to-all-done.1 = bf16[32,8,768]{2,1,0:T(8,128)(2,1)S(1)} async-done(((bf16[32,8,768]{2,1,0:T(8,128)(2,1)}), bf16[32,8,768]{2,1,0:T(8,128)(2,1)S(1)}, u32[]{:S(2)}, u32[]{:S(2)}) %all-to-all-start.1) | async-done | bytes 393248 | tf_op jit(solution)/shard_map/all_to_all | solution.py:1141
  140.9 3.2 %region_norm_backward.1 = (bf16[256,768]{1,0:T(8,128)(2,1)S(1)}, bf16[320,384]{1,0:T(8,128)(2,1)S(1)}, bf16[256,384]{1,0:T(8,128)(2,1)S(1)}, bf16[8,8,384]{2,1,0:T(8,128)(2,1)S(1)}, f32[4,256]{1,0:T(4,128)}) custom-call(s32[16]{0:T(128)S(1)} %pad_add_fusion.sc_ref.c_ref.b_ref, bf16[256,768]{1,0:T(8,128)(2,1)S(1)} %bitcast.25, s32[1,256]{1,0:T(1,128)} %t_ref.7, ...), custom_call_target="tpu_custom_call" | custom-call | flops 100000000 | bytes 1048576 | tf_op jit(solution)/shard_map/region_norm_backward/pallas_call | solution.py:670
  144.1 1.5 collective-permute-done.12.p_ref
  145.6 3.5 %visual_gradient.1 = (bf16[4,2,72,384]{3,2,1,0:T(8,128)(2,1)S(1)}, bf16[4,2,72,384]{3,2,1,0:T(8,128)(2,1)S(1)}, bf16[4,2,72,384]{3,2,1,0:T(8,128)(2,1)S(1)}, bf16[4,2,72,384]{3,2,1,0:T(8,128)(2,1)S(1)}) custom-call(s32[16]{0:T(128)S(1)} %pad_add_fusion.sc_ref.c_ref.b_ref, bf16[256,2048]{1,0:T(8,128)(2,1)} %f_ref.3, ...), custom_call_target="tpu_custom_call" | custom-call | flops 100000000 | bytes 1048576 | tf_op jit(solution)/shard_map/visual_gradient/pallas_call | solution.py:739
  150.0 1.3 collective-permute-start.17
  153.1 1.2 collective-permute-start.19
  155.0 1.3 collective-permute-start.20
  156.3 5.3 %feature_gradient.1 = f32[256,2048]{1,0:T(8,128)} custom-call(s32[16]{0:T(128)S(1)} %pad_add_fusion.sc_ref.c_ref.b_ref, bf16[256,768]{1,0:T(8,128)(2,1)S(1)} %get-tuple-element.425.d_ref, bf16[2048,768]{1,0:T(8,128)(2,1)} %w_ref.3), custom_call_target="tpu_custom_call" | custom-call | flops 10000000000 | bytes 1048576 | tf_op jit(solution)/shard_map/feature_gradient/pallas_call | solution.py:770
  163.9 1.4 collective-permute-start.21
  165.3 1.1 collective-permute-start.22
  166.4 3.0 %collective-permute-done.18.refs_1_ = bf16[4,96,384]{2,1,0:T(8,128)(2,1)S(1)} collective-permute-done((bf16[4,96,384]{2,1,0:T(8,128)(2,1)S(1)}, bf16[4,96,384]{2,1,0:T(8,128)(2,1)S(1)}, u32[]{:S(2)}, u32[]{:S(2)}) %collective-permute-start.18) | collective-permute-done | bytes 294944 | tf_op jit(solution)/shard_map/ppermute | solution.py:791
  170.9 2.3 %collective-permute-done.21.refs_1_ = bf16[4,72,384]{2,1,0:T(8,128)(2,1)S(1)} collective-permute-done((bf16[4,72,384]{2,1,0:T(8,128)(2,1)S(1)}, bf16[4,72,384]{2,1,0:T(8,128)(2,1)S(1)}, u32[]{:S(2)}, u32[]{:S(2)}) %collective-permute-start.21) | collective-permute-done | bytes 221216 | tf_op jit(solution)/shard_map/ppermute | solution.py:791
  174.6 1.6 collective-permute-start.26
  176.2 2.8 %collective-permute-done.23.r_ref = bf16[2,192,384]{2,1,0:T(8,128)(2,1)S(1)} collective-permute-done((bf16[2,192,384]{2,1,0:T(8,128)(2,1)S(1)}, bf16[2,192,384]{2,1,0:T(8,128)(2,1)S(1)}, u32[]{:S(2)}, u32[]{:S(2)}) %collective-permute-start.23) | collective-permute-done | bytes 294944 | tf_op jit(solution)/shard_map/ppermute | solution.py:791
  180.4 3.3 %collective-permute-done.24.r_ref = bf16[2,144,384]{2,1,0:T(8,128)(2,1)S(1)} collective-permute-done((bf16[2,144,384]{2,1,0:T(8,128)(2,1)S(1)}, bf16[2,144,384]{2,1,0:T(8,128)(2,1)S(1)}, u32[]{:S(2)}, u32[]{:S(2)}) %collective-permute-start.24) | collective-permute-done | bytes 221216 | tf_op jit(solution)/shard_map/ppermute | solution.py:791
  184.8 2.5 %collective-permute-done.29 = bf16[1,192,384]{2,1,0:T(8,128)(2,1)S(1)} collective-permute-done((bf16[1,192,384]{2,1,0:T(8,128)(2,1)S(1)}, bf16[1,192,384]{2,1,0:T(8,128)(2,1)S(1)}, u32[]{:S(2)}, u32[]{:S(2)}) %collective-permute-start.29) | collective-permute-done | bytes 147488 | tf_op jit(solution)/shard_map/ppermute | solution.py:791
  187.4 1.1 collective-permute-start.32
  188.5 2.4 %finish_ffn.1 = (f32[384,768]{1,0:T(8,128)}, f32[96,3072]{1,0:T(8,128)}) custom-call(s32[16]{0:T(128)S(1)} %pad_add_fusion.sc_ref.c_ref.b_ref, bf16[384,384]{1,0:T(8,128)(2,1)S(1)} %add_bitcast_fusion.p0, bf16[384,384]{1,0:T(8,128)(2,1)S(1)} %collective-permute-done.26.p1, bf16[384,384]{1,0:T(8,128)(2,1)S(1)} %collective-permute-done.27.p2, ...), custom_call_target="tpu_custom_call" | custom-call | flops 1000000000 | bytes 1048576 | tf_op jit(solution)/shard_map/finish_ffn/pallas_call | solution.py:800
  190.9 2.3 %collective-permute-done.25 = bf16[1,144,384]{2,1,0:T(8,128)(2,1)S(1)} collective-permute-done((bf16[1,144,384]{2,1,0:T(8,128)(2,1)S(1)}, bf16[1,144,384]{2,1,0:T(8,128)(2,1)S(1)}, u32[]{:S(2)}, u32[]{:S(2)}) %collective-permute-start.25) | collective-permute-done | bytes 110624 | tf_op jit(solution)/shard_map/ppermute | solution.py:791
  195.0 1.7 finish_wide.1
  196.7 2.4 %collective-permute-done.30.p1 = bf16[144,384]{1,0:T(8,128)(2,1)S(1)} collective-permute-done((bf16[144,384]{1,0:T(8,128)(2,1)S(1)}, bf16[144,384]{1,0:T(8,128)(2,1)S(1)}, u32[]{:S(2)}, u32[]{:S(2)}) %collective-permute-start.30) | collective-permute-done | bytes 110624 | tf_op jit(solution)/shard_map/ppermute | solution.py:791
  199.1 1.3 collective-permute-done.35.p3
  200.5 1.6 finish_visual.1
  (98 shorter events, 22.4 us)
Async XLA Ops:
  0.7 12.1 %copy-start.14 = (f32[1536]{0:T(1024)S(1)}, f32[1536]{0:T(1024)}, u32[]{:S(2)}) copy-start(f32[1536]{0:T(1024)} %param.40) | copy-start | bytes 18436
  0.7 12.2 %copy-start.15 = (s32[2]{0:T(128)S(1)}, s32[2]{0:T(128)}, u32[]{:S(2)}) copy-start(s32[2]{0:T(128)} %param.31) | copy-start | bytes 28
  0.7 12.2 %copy-start.16 = (s32[3]{0:T(128)S(1)}, s32[3]{0:T(128)}, u32[]{:S(2)}) copy-start(s32[3]{0:T(128)} %param.30) | copy-start | bytes 40
  0.7 12.2 %copy-start.17 = (s32[3]{0:T(128)S(1)}, s32[3]{0:T(128)}, u32[]{:S(2)}) copy-start(s32[3]{0:T(128)} %param.29) | copy-start | bytes 40
  5.5 20.5 %all-to-all-start = ((bf16[32,8,768]{2,1,0:T(8,128)(2,1)}), bf16[32,8,768]{2,1,0:T(8,128)(2,1)S(1)}, u32[]{:S(2)}, u32[]{:S(2)}) async-start(bf16[32,8,768]{2,1,0:T(8,128)(2,1)} %bitcast.1), calls=%async_computation | async-start | bytes 786432 | tf_op jit(solution)/shard_map/all_to_all | solution.py:1089
  26.7 36.3 %copy-start.3 = (f32[768]{0:T(1024)S(1)}, f32[768]{0:T(1024)}, u32[]{:S(2)}) copy-start(f32[768]{0:T(1024)} %ag_ref.5) | copy-start | bytes 9220
  62.9 4.8 %collective-permute-start = (bf16[8,2,2,96,384]{4,3,2,1,0:T(8,128)(2,1)}, bf16[8,2,2,96,384]{4,3,2,1,0:T(8,128)(2,1)S(1)}, u32[]{:S(2)}, u32[]{:S(2)}) collective-permute-start(bf16[8,2,2,96,384]{4,3,2,1,0:T(8,128)(2,1)} %bitcast.29), channel_id=1, source_target_pairs={{0,1},{1,0},{2,3},{3,2},{4,5},{5,4},{6,7},{7,6},{8,9},{9,8},{10,11... | collective-permute-start | bytes 7077896 | tf_op jit(solution)/shard_map/ppermute | solution.py:791
  69.1 15.4 %collective-permute-start.1 = (bf16[4,2,96,384]{3,2,1,0:T(8,128)(2,1)S(1)}, bf16[4,2,96,384]{3,2,1,0:T(8,128)(2,1)S(1)}, u32[]{:S(2)}, u32[]{:S(2)}) collective-permute-start(bf16[4,2,96,384]{3,2,1,0:T(8,128)(2,1)S(1)} %get-tuple-element.273), channel_id=1, source_target_pairs={{0,2},{1,3},{2,0},{3,1},{4,6},{5,7},{6,4},{7,5},{8,10},{9,11},{10,... | collective-permute-start | bytes 1769480 | tf_op jit(solution)/shard_map/ppermute | solution.py:791
  69.8 15.3 %collective-permute-start.2 = (bf16[4,2,96,384]{3,2,1,0:T(8,128)(2,1)S(1)}, bf16[4,2,96,384]{3,2,1,0:T(8,128)(2,1)S(1)}, u32[]{:S(2)}, u32[]{:S(2)}) collective-permute-start(bf16[4,2,96,384]{3,2,1,0:T(8,128)(2,1)S(1)} %get-tuple-element.275), channel_id=1, source_target_pairs={{0,4},{1,5},{2,6},{3,7},{4,0},{5,1},{6,2},{7,3},{8,12},{9,13},{10,... | collective-permute-start | bytes 1769480 | tf_op jit(solution)/shard_map/ppermute | solution.py:791
  78.2 10.1 %copy-start.5 = (bf16[768,768]{1,0:T(8,128)(2,1)S(1)}, bf16[768,768]{1,0:T(8,128)(2,1)}, u32[]{:S(2)}) copy-start(bf16[768,768]{1,0:T(8,128)(2,1)} %wo_ref.3) | copy-start | bytes 3538948
  78.3 10.1 %copy-start.9 = (bf16[768,2304]{1,0:T(8,128)(2,1)S(1)}, bf16[768,2304]{1,0:T(8,128)(2,1)}, u32[]{:S(2)}) copy-start(bf16[768,2304]{1,0:T(8,128)(2,1)} %get-tuple-element.310.qkv_ref) | copy-start | bytes 10616836
  86.0 10.4 %collective-permute-start.5 = (bf16[768,1536]{1,0:T(8,128)(2,1)S(1)}, bf16[768,1536]{1,0:T(8,128)(2,1)S(1)}, u32[]{:S(2)}, u32[]{:S(2)}) collective-permute-start(bf16[768,1536]{1,0:T(8,128)(2,1)S(1)} %get-tuple-element.304), channel_id=1, source_target_pairs={{0,1},{1,0},{2,3},{3,2},{4,5},{5,4},{6,7},{7,6},{8,9},{9,8},{10,11... | collective-permute-start | bytes 7077896 | tf_op jit(solution)/shard_map/ppermute | solution.py:791
  86.1 9.8 %collective-permute-start.3 = (bf16[4,96,384]{2,1,0:T(8,128)(2,1)S(1)}, bf16[4,96,384]{2,1,0:T(8,128)(2,1)S(1)}, u32[]{:S(2)}, u32[]{:S(2)}) collective-permute-start(bf16[4,96,384]{2,1,0:T(8,128)(2,1)S(1)} %get-tuple-element.300), channel_id=1, source_target_pairs={{0,4},{1,5},{2,6},{3,7},{4,0},{5,1},{6,2},{7,3},{8,12},{9,13},{10,... | collective-permute-start | bytes 884744 | tf_op jit(solution)/shard_map/ppermute | solution.py:791
  87.3 9.1 %collective-permute-start.4 = (bf16[4,96,384]{2,1,0:T(8,128)(2,1)S(1)}, bf16[4,96,384]{2,1,0:T(8,128)(2,1)S(1)}, u32[]{:S(2)}, u32[]{:S(2)}) collective-permute-start(bf16[4,96,384]{2,1,0:T(8,128)(2,1)S(1)} %get-tuple-element.302), channel_id=1, source_target_pairs={{0,2},{1,3},{2,0},{3,1},{4,6},{5,7},{6,4},{7,5},{8,10},{9,11},{10,... | collective-permute-start | bytes 884744 | tf_op jit(solution)/shard_map/ppermute | solution.py:791
  97.6 15.1 %collective-permute-start.6 = (bf16[4,2,96,384]{3,2,1,0:T(8,128)(2,1)S(1)}, bf16[4,2,96,384]{3,2,1,0:T(8,128)(2,1)S(1)}, u32[]{:S(2)}, u32[]{:S(2)}) collective-permute-start(bf16[4,2,96,384]{3,2,1,0:T(8,128)(2,1)S(1)} %get-tuple-element.336), channel_id=1, source_target_pairs={{0,2},{1,3},{2,0},{3,1},{4,6},{5,7},{6,4},{7,5},{8,10},{9,11},{10,... | collective-permute-start | bytes 1769480 | tf_op jit(solution)/shard_map/ppermute | solution.py:791
  98.7 14.4 %collective-permute-start.7 = (bf16[4,2,96,384]{3,2,1,0:T(8,128)(2,1)S(1)}, bf16[4,2,96,384]{3,2,1,0:T(8,128)(2,1)S(1)}, u32[]{:S(2)}, u32[]{:S(2)}) collective-permute-start(bf16[4,2,96,384]{3,2,1,0:T(8,128)(2,1)S(1)} %get-tuple-element.338), channel_id=1, source_target_pairs={{0,4},{1,5},{2,6},{3,7},{4,0},{5,1},{6,2},{7,3},{8,12},{9,13},{10,... | collective-permute-start | bytes 1769480 | tf_op jit(solution)/shard_map/ppermute | solution.py:791
  114.0 9.0 %collective-permute-start.8 = (bf16[4,96,384]{2,1,0:T(8,128)(2,1)S(1)}, bf16[4,96,384]{2,1,0:T(8,128)(2,1)S(1)}, u32[]{:S(2)}, u32[]{:S(2)}) collective-permute-start(bf16[4,96,384]{2,1,0:T(8,128)(2,1)S(1)} %get-tuple-element.359), channel_id=1, source_target_pairs={{0,4},{1,5},{2,6},{3,7},{4,0},{5,1},{6,2},{7,3},{8,12},{9,13},{10,... | collective-permute-start | bytes 884744 | tf_op jit(solution)/shard_map/ppermute | solution.py:791
  115.0 7.9 %collective-permute-start.9 = (bf16[4,96,384]{2,1,0:T(8,128)(2,1)S(1)}, bf16[4,96,384]{2,1,0:T(8,128)(2,1)S(1)}, u32[]{:S(2)}, u32[]{:S(2)}) collective-permute-start(bf16[4,96,384]{2,1,0:T(8,128)(2,1)S(1)} %get-tuple-element.361), channel_id=1, source_target_pairs={{0,2},{1,3},{2,0},{3,1},{4,6},{5,7},{6,4},{7,5},{8,10},{9,11},{10,... | collective-permute-start | bytes 884744 | tf_op jit(solution)/shard_map/ppermute | solution.py:791
  122.9 6.6 %copy-start = (bf16[768,1536]{1,0:T(8,128)(2,1)S(1)}, bf16[768,1536]{1,0:T(8,128)(2,1)}, u32[]{:S(2)}) copy-start(bf16[768,1536]{1,0:T(8,128)(2,1)} %get-tuple-element.390) | copy-start | bytes 7077892
  124.7 4.9 %collective-permute-start.10 = (bf16[768,1536]{1,0:T(8,128)(2,1)}, bf16[768,1536]{1,0:T(8,128)(2,1)}, u32[]{:S(2)}, u32[]{:S(2)}) collective-permute-start(bf16[768,1536]{1,0:T(8,128)(2,1)} %get-tuple-element.391), channel_id=1, source_target_pairs={{0,1},{1,0},{2,3},{3,2},{4,5},{5,4},{6,7},{7,6},{8,9},{9,8},{10,11... | collective-permute-start | bytes 7077896 | tf_op jit(solution)/shard_map/ppermute | solution.py:791
  124.7 19.4 %collective-permute-start.11 = (bf16[256,2048]{1,0:T(8,128)(2,1)}, bf16[256,2048]{1,0:T(8,128)(2,1)}, u32[]{:S(2)}, u32[]{:S(2)}) collective-permute-start(bf16[256,2048]{1,0:T(8,128)(2,1)} %f_ref.3), channel_id=1, source_target_pairs={{0,1},{1,0},{2,3},{3,2},{4,5},{5,4},{6,7},{7,6},{8,9},{9,8},{10,11... | collective-permute-start | bytes 3145736 | tf_op jit(solution)/shard_map/ppermute | solution.py:791
  125.2 15.7 %all-to-all-start.1 = ((bf16[32,8,768]{2,1,0:T(8,128)(2,1)}), bf16[32,8,768]{2,1,0:T(8,128)(2,1)S(1)}, u32[]{:S(2)}, u32[]{:S(2)}) async-start(bf16[32,8,768]{2,1,0:T(8,128)(2,1)} %bitcast.9), calls=%async_computation.1 | async-start | bytes 786432 | tf_op jit(solution)/shard_map/all_to_all | solution.py:1141
  134.0 17.3 %copy-start.6 = (bf16[4,2,96,384]{3,2,1,0:T(8,128)(2,1)S(1)}, bf16[4,2,96,384]{3,2,1,0:T(8,128)(2,1)}, u32[]{:S(2)}) copy-start(bf16[4,2,96,384]{3,2,1,0:T(8,128)(2,1)} %get-tuple-element.393.ak) | copy-start | bytes 1769476
  134.0 17.3 %copy-start.7 = (bf16[4,2,96,384]{3,2,1,0:T(8,128)(2,1)S(1)}, bf16[4,2,96,384]{3,2,1,0:T(8,128)(2,1)}, u32[]{:S(2)}) copy-start(bf16[4,2,96,384]{3,2,1,0:T(8,128)(2,1)} %get-tuple-element.395.bk) | copy-start | bytes 1769476
  134.0 17.3 %collective-permute-start.13 = (bf16[4,2,96,384]{3,2,1,0:T(8,128)(2,1)}, bf16[4,2,96,384]{3,2,1,0:T(8,128)(2,1)S(1)}, u32[]{:S(2)}, u32[]{:S(2)}) collective-permute-start(bf16[4,2,96,384]{3,2,1,0:T(8,128)(2,1)} %get-tuple-element.392), channel_id=1, source_target_pairs={{0,2},{1,3},{2,0},{3,1},{4,6},{5,7},{6,4},{7,5},{8,10},{9,11},{10,... | collective-permute-start | bytes 1769480 | tf_op jit(solution)/shard_map/ppermute | solution.py:791
  135.0 16.3 %collective-permute-start.14 = (bf16[4,2,96,384]{3,2,1,0:T(8,128)(2,1)}, bf16[4,2,96,384]{3,2,1,0:T(8,128)(2,1)S(1)}, u32[]{:S(2)}, u32[]{:S(2)}) collective-permute-start(bf16[4,2,96,384]{3,2,1,0:T(8,128)(2,1)} %get-tuple-element.394), channel_id=1, source_target_pairs={{0,4},{1,5},{2,6},{3,7},{4,0},{5,1},{6,2},{7,3},{8,12},{9,13},{10,... | collective-permute-start | bytes 1769480 | tf_op jit(solution)/shard_map/ppermute | solution.py:791
  136.0 18.3 %collective-permute-start.15 = (bf16[2,384,384]{2,1,0:T(8,128)(2,1)}, bf16[2,384,384]{2,1,0:T(8,128)(2,1)S(1)}, u32[]{:S(2)}, u32[]{:S(2)}) collective-permute-start(bf16[2,384,384]{2,1,0:T(8,128)(2,1)} %get-tuple-element.421), channel_id=1, source_target_pairs={{0,8},{1,9},{2,10},{3,11},{4,12},{5,13},{6,14},{7,15},{8,0},{9,1},... | collective-permute-start | bytes 1769480 | tf_op jit(solution)/shard_map/ppermute | solution.py:791
  144.1 1.5 collective-permute-start.12
  149.2 13.1 %collective-permute-start.16 = (bf16[4,2,72,384]{3,2,1,0:T(8,128)(2,1)S(1)}, bf16[4,2,72,384]{3,2,1,0:T(8,128)(2,1)S(1)}, u32[]{:S(2)}, u32[]{:S(2)}) collective-permute-start(bf16[4,2,72,384]{3,2,1,0:T(8,128)(2,1)S(1)} %get-tuple-element.409), channel_id=1, source_target_pairs={{0,2},{1,3},{2,0},{3,1},{4,6},{5,7},{6,4},{7,5},{8,10},{9,11},{10,... | collective-permute-start | bytes 1327112 | tf_op jit(solution)/shard_map/ppermute | solution.py:791
  150.0 13.0 %collective-permute-start.17 = (bf16[4,2,72,384]{3,2,1,0:T(8,128)(2,1)S(1)}, bf16[4,2,72,384]{3,2,1,0:T(8,128)(2,1)S(1)}, u32[]{:S(2)}, u32[]{:S(2)}) collective-permute-start(bf16[4,2,72,384]{3,2,1,0:T(8,128)(2,1)S(1)} %get-tuple-element.411), channel_id=1, source_target_pairs={{0,4},{1,5},{2,6},{3,7},{4,0},{5,1},{6,2},{7,3},{8,12},{9,13},{10,... | collective-permute-start | bytes 1327112 | tf_op jit(solution)/shard_map/ppermute | solution.py:791
  152.2 17.1 %collective-permute-start.18 = (bf16[4,96,384]{2,1,0:T(8,128)(2,1)S(1)}, bf16[4,96,384]{2,1,0:T(8,128)(2,1)S(1)}, u32[]{:S(2)}, u32[]{:S(2)}) collective-permute-start(bf16[4,96,384]{2,1,0:T(8,128)(2,1)S(1)} %get-tuple-element.414), channel_id=1, source_target_pairs={{0,4},{1,5},{2,6},{3,7},{4,0},{5,1},{6,2},{7,3},{8,12},{9,13},{10,... | collective-permute-start | bytes 884744 | tf_op jit(solution)/shard_map/ppermute | solution.py:791
  153.1 16.3 %collective-permute-start.19 = (bf16[4,96,384]{2,1,0:T(8,128)(2,1)S(1)}, bf16[4,96,384]{2,1,0:T(8,128)(2,1)S(1)}, u32[]{:S(2)}, u32[]{:S(2)}) collective-permute-start(bf16[4,96,384]{2,1,0:T(8,128)(2,1)S(1)} %get-tuple-element.416), channel_id=1, source_target_pairs={{0,2},{1,3},{2,0},{3,1},{4,6},{5,7},{6,4},{7,5},{8,10},{9,11},{10,... | collective-permute-start | bytes 884744 | tf_op jit(solution)/shard_map/ppermute | solution.py:791
  155.0 15.9 %collective-permute-start.20 = (bf16[1,384,384]{2,1,0:T(8,128)(2,1)S(1)}, bf16[1,384,384]{2,1,0:T(8,128)(2,1)S(1)}, u32[]{:S(2)}, u32[]{:S(2)}) collective-permute-start(bf16[1,384,384]{2,1,0:T(8,128)(2,1)S(1)} %get-tuple-element.422), channel_id=1, source_target_pairs={{0,16},{1,17},{2,18},{3,19},{4,20},{5,21},{6,22},{7,23},{8,24},{9,... | collective-permute-start | bytes 884744 | tf_op jit(solution)/shard_map/ppermute | solution.py:791
  163.9 9.3 %collective-permute-start.21 = (bf16[4,72,384]{2,1,0:T(8,128)(2,1)S(1)}, bf16[4,72,384]{2,1,0:T(8,128)(2,1)S(1)}, u32[]{:S(2)}, u32[]{:S(2)}) collective-permute-start(bf16[4,72,384]{2,1,0:T(8,128)(2,1)S(1)} %get-tuple-element.428), channel_id=1, source_target_pairs={{0,4},{1,5},{2,6},{3,7},{4,0},{5,1},{6,2},{7,3},{8,12},{9,13},{10,... | collective-permute-start | bytes 663560 | tf_op jit(solution)/shard_map/ppermute | solution.py:791
  165.3 8.0 %collective-permute-start.22 = (bf16[4,72,384]{2,1,0:T(8,128)(2,1)S(1)}, bf16[4,72,384]{2,1,0:T(8,128)(2,1)S(1)}, u32[]{:S(2)}, u32[]{:S(2)}) collective-permute-start(bf16[4,72,384]{2,1,0:T(8,128)(2,1)S(1)} %get-tuple-element.430), channel_id=1, source_target_pairs={{0,2},{1,3},{2,0},{3,1},{4,6},{5,7},{6,4},{7,5},{8,10},{9,11},{10,... | collective-permute-start | bytes 663560 | tf_op jit(solution)/shard_map/ppermute | solution.py:791
  170.1 8.9 %collective-permute-start.23 = (bf16[2,192,384]{2,1,0:T(8,128)(2,1)S(1)}, bf16[2,192,384]{2,1,0:T(8,128)(2,1)S(1)}, u32[]{:S(2)}, u32[]{:S(2)}) collective-permute-start(bf16[2,192,384]{2,1,0:T(8,128)(2,1)S(1)} %get-tuple-element.433), channel_id=1, source_target_pairs={{0,8},{1,9},{2,10},{3,11},{4,12},{5,13},{6,14},{7,15},{8,0},{9,1},... | collective-permute-start | bytes 884744 | tf_op jit(solution)/shard_map/ppermute | solution.py:791
  174.0 9.7 %collective-permute-start.24 = (bf16[2,144,384]{2,1,0:T(8,128)(2,1)S(1)}, bf16[2,144,384]{2,1,0:T(8,128)(2,1)S(1)}, u32[]{:S(2)}, u32[]{:S(2)}) collective-permute-start(bf16[2,144,384]{2,1,0:T(8,128)(2,1)S(1)} %get-tuple-element.437), channel_id=1, source_target_pairs={{0,8},{1,9},{2,10},{3,11},{4,12},{5,13},{6,14},{7,15},{8,0},{9,1},... | collective-permute-start | bytes 663560 | tf_op jit(solution)/shard_map/ppermute | solution.py:791
  174.6 9.7 %collective-permute-start.26 = (bf16[384,384]{1,0:T(8,128)(2,1)S(1)}, bf16[384,384]{1,0:T(8,128)(2,1)S(1)}, u32[]{:S(2)}, u32[]{:S(2)}) collective-permute-start(bf16[384,384]{1,0:T(8,128)(2,1)S(1)} %add_bitcast_fusion.p0), channel_id=1, source_target_pairs={{0,2},{1,3},{2,0},{3,1},{4,6},{5,7},{6,4},{7,5},{8,10},{9,11},{10,... | collective-permute-start | bytes 884744 | tf_op jit(solution)/shard_map/ppermute | solution.py:791
  176.2 12.2 %collective-permute-start.27 = (bf16[384,384]{1,0:T(8,128)(2,1)S(1)}, bf16[384,384]{1,0:T(8,128)(2,1)S(1)}, u32[]{:S(2)}, u32[]{:S(2)}) collective-permute-start(bf16[384,384]{1,0:T(8,128)(2,1)S(1)} %add_bitcast_fusion.p0), channel_id=1, source_target_pairs={{0,1},{1,0},{2,3},{3,2},{4,5},{5,4},{6,7},{7,6},{8,9},{9,8},{10,11... | collective-permute-start | bytes 884744 | tf_op jit(solution)/shard_map/ppermute | solution.py:791
  179.6 7.7 %collective-permute-start.29 = (bf16[1,192,384]{2,1,0:T(8,128)(2,1)S(1)}, bf16[1,192,384]{2,1,0:T(8,128)(2,1)S(1)}, u32[]{:S(2)}, u32[]{:S(2)}) collective-permute-start(bf16[1,192,384]{2,1,0:T(8,128)(2,1)S(1)} %get-tuple-element.440), channel_id=1, source_target_pairs={{0,16},{1,17},{2,18},{3,19},{4,20},{5,21},{6,22},{7,23},{8,24},{9,... | collective-permute-start | bytes 442376 | tf_op jit(solution)/shard_map/ppermute | solution.py:791
  184.3 4.2 %collective-permute-start.28 = (bf16[384,384]{1,0:T(8,128)(2,1)S(1)}, bf16[384,384]{1,0:T(8,128)(2,1)S(1)}, u32[]{:S(2)}, u32[]{:S(2)}) collective-permute-start(bf16[384,384]{1,0:T(8,128)(2,1)S(1)} %collective-permute-done.26.p1), channel_id=1, source_target_pairs={{0,1},{1,0},{2,3},{3,2},{4,5},{5,4},{6,7},{7,6},{8,9},{9,8},{10,11... | collective-permute-start | bytes 884744 | tf_op jit(solution)/shard_map/ppermute | solution.py:791
  184.4 8.7 %collective-permute-start.25 = (bf16[1,144,384]{2,1,0:T(8,128)(2,1)S(1)}, bf16[1,144,384]{2,1,0:T(8,128)(2,1)S(1)}, u32[]{:S(2)}, u32[]{:S(2)}) collective-permute-start(bf16[1,144,384]{2,1,0:T(8,128)(2,1)S(1)} %get-tuple-element.443), channel_id=1, source_target_pairs={{0,16},{1,17},{2,18},{3,19},{4,20},{5,21},{6,22},{7,23},{8,24},{9,... | collective-permute-start | bytes 331784 | tf_op jit(solution)/shard_map/ppermute | solution.py:791
  187.3 7.6 %collective-permute-start.33 = (bf16[192,384]{1,0:T(8,128)(2,1)S(1)}, bf16[192,384]{1,0:T(8,128)(2,1)S(1)}, u32[]{:S(2)}, u32[]{:S(2)}) collective-permute-start(bf16[192,384]{1,0:T(8,128)(2,1)S(1)} %add_bitcast_fusion.1.p0), channel_id=1, source_target_pairs={{0,1},{1,0},{2,3},{3,2},{4,5},{5,4},{6,7},{7,6},{8,9},{9,8},{10,11... | collective-permute-start | bytes 442376 | tf_op jit(solution)/shard_map/ppermute | solution.py:791
  187.4 6.3 %collective-permute-start.32 = (bf16[192,384]{1,0:T(8,128)(2,1)S(1)}, bf16[192,384]{1,0:T(8,128)(2,1)S(1)}, u32[]{:S(2)}, u32[]{:S(2)}) collective-permute-start(bf16[192,384]{1,0:T(8,128)(2,1)S(1)} %add_bitcast_fusion.1.p0), channel_id=1, source_target_pairs={{0,2},{1,3},{2,0},{3,1},{4,6},{5,7},{6,4},{7,5},{8,10},{9,11},{10,... | collective-permute-start | bytes 442376 | tf_op jit(solution)/shard_map/ppermute | solution.py:791
  193.7 1.4 collective-permute-start.34
  193.7 5.5 %collective-permute-start.30 = (bf16[144,384]{1,0:T(8,128)(2,1)S(1)}, bf16[144,384]{1,0:T(8,128)(2,1)S(1)}, u32[]{:S(2)}, u32[]{:S(2)}) collective-permute-start(bf16[144,384]{1,0:T(8,128)(2,1)S(1)} %add_bitcast_fusion.2.p0), channel_id=1, source_target_pairs={{0,2},{1,3},{2,0},{3,1},{4,6},{5,7},{6,4},{7,5},{8,10},{9,11},{10,... | collective-permute-start | bytes 331784 | tf_op jit(solution)/shard_map/ppermute | solution.py:791
  194.7 4.5 %collective-permute-start.31 = (bf16[144,384]{1,0:T(8,128)(2,1)S(1)}, bf16[144,384]{1,0:T(8,128)(2,1)S(1)}, u32[]{:S(2)}, u32[]{:S(2)}) collective-permute-start(bf16[144,384]{1,0:T(8,128)(2,1)S(1)} %add_bitcast_fusion.2.p0), channel_id=1, source_target_pairs={{0,1},{1,0},{2,3},{3,2},{4,5},{5,4},{6,7},{7,6},{8,9},{9,8},{10,11... | collective-permute-start | bytes 331784 | tf_op jit(solution)/shard_map/ppermute | solution.py:791
  199.1 1.3 collective-permute-start.35
  (8 other events, 33.5 us)

commit v8 on v7

--- a/solution.py
+++ b/solution.py
@@ -224,7 +224,7 @@
             place = lax.broadcasted_iota(jnp.int32, (seq, 1), 0)
             row_end = jnp.where(place < text_len, length, text_len + count)
             row_mask = jnp.where(place < row_end, 1.0, 0.0)
-            key_bias = jnp.where(place < row_end, 0.0, -1e30)
+            key_mask = jnp.broadcast_to(row_mask, (seq, 2 * seq)) > 0.5
             first = lax.broadcasted_iota(jnp.int32, (1, 2 * HEAD), 1) < HEAD
             scale = [
                 jnp.where(first, 0.125, 0.0).astype(bf16),
@@ -237,7 +237,8 @@
                 q = qkv_ref[:, cols(0)]
                 k = qkv_ref[:, cols(width)]
                 v = qkv_ref[:, cols(2 * width)]
-                scores = mm(k, jnp.concatenate([q * scale[0], q * scale[1]], 0), NT) + key_bias
+                scores = mm(k, jnp.concatenate([q * scale[0], q * scale[1]], 0), NT)
+                scores = jnp.where(key_mask, scores, -1e30)
                 raised = jnp.exp(scores - jnp.max(scores, 0, keepdims=True))
                 low = (raised * (1.0 / jnp.sum(raised, 0, keepdims=True))).astype(bf16)
                 probs_ref[pair] = low

time: 203 us -> 203 us (level)
  no operation moved by 1% of the time
where the time goes in v8:
time: 203 us; the launch traced here: 202 us
  Pallas kernels  122 us (60%)
  waiting for transfers between devices  41 us (20%)
  starting transfers between devices  36.8 us (18%)
    pallas_call x1, Pallas kernels, forward(): pl.pallas_call(kernel, grid_spec=pltpu.PrefetchScalarGridSpec(num_scalar_...  36.2 us
    ppermute x36, waiting for transfers between devices, swap(): lax.ppermute(values, ('dp', 'enc'), [(i, i ^ bit) for i in range(count)])  29.2 us
    ppermute x36, starting transfers between devices, swap(): lax.ppermute(values, ('dp', 'enc'), [(i, i ^ bit) for i in range(count)])  26.9 us
    pallas_call x16, Pallas kernels, scalar_call(): pl.pallas_call(kernel, grid_spec=pltpu.PrefetchScalarGridSpec(num_scalar_...  21.4 us
    pallas_call x2, Pallas kernels, attention_backward(): pl.pallas_call(kernel, grid_spec=pltpu.PrefetchScalarGridSpec(num_scalar_...  20.5 us
    pallas_call x2, Pallas kernels, ffn_backward(): pl.pallas_call(kernel, grid_spec=pltpu.PrefetchScalarGridSpec(num_scalar_...  10.8 us
    all_to_all x1, waiting for transfers between devices, on_device(): lax.all_to_all(message, axes, split_axis=0, concat_axis=0, tiled=True)  8 us
    all_to_all x1, starting transfers between devices, on_device(): lax.all_to_all(message, axes, split_axis=0, concat_axis=0, tiled=True)  7.3 us
  transfers between devices with their start and end apart: 38, of which 21 were waited for; matrix products, arithmetic and copies ran while one was open for 0% of the time, Pallas kernels for 36%

profile of v8, /device:TPU:0, one launch (start us, length us, event | category | flops | bytes accessed | tf_op | source)
XLA Modules:
  0.0 202.2 jit_solution(12889788406159602547)
XLA Ops:
  0.7 4.8 %region_forward.1 = (bf16[256,768]{1,0:T(8,128)(2,1)}, f32[256,768]{1,0:T(8,128)}, f32[256,128]{1,0:T(8,128)}) custom-call(bf16[256,2048]{1,0:T(8,128)(2,1)} %f_ref.3, bf16[4,256]{1,0:T(4,128)(2,1)} %box_ref.3, s32[1,256]{1,0:T(1,128)} %t_ref.7, bf16[2048,768]{1,0:T(8,128)(2,1)} %w_ref.3, bf16[4,768]{1,0:T(4,128)(2,1)} %bitcast.27, f32[768]{0:T(1024)} %b_ref.1, ...), custom_call_target="tpu_custom_call" | custom-call | flops 3000000000 | bytes 1048576 | tf_op jit(solution)/shard_map/region_forward/pallas_call | solution.py:112
  5.5 7.3 %all-to-all-start = ((bf16[32,8,768]{2,1,0:T(8,128)(2,1)}), bf16[32,8,768]{2,1,0:T(8,128)(2,1)S(1)}, u32[]{:S(2)}, u32[]{:S(2)}) async-start(bf16[32,8,768]{2,1,0:T(8,128)(2,1)} %bitcast.1), calls=%async_computation | async-start | bytes 786432 | tf_op jit(solution)/shard_map/all_to_all | solution.py:1090
  12.9 5.0 %text_qkv.1.tq_ref = bf16[384,2304]{1,0:T(8,128)(2,1)} custom-call(bf16[384,768]{1,0:T(8,128)(2,1)} %t_ref.6, bf16[768,2304]{1,0:T(8,128)(2,1)} %wq.3, f32[1,1536]{1,0:T(1,128)S(1)} %reshape.72.b_ref.qvb_ref), custom_call_target="tpu_custom_call" | custom-call | flops 3000000000 | bytes 1048576 | tf_op jit(solution)/shard_map/text_qkv/pallas_call | solution.py:142
  17.9 8.0 %all-to-all-done = bf16[32,8,768]{2,1,0:T(8,128)(2,1)S(1)} async-done(((bf16[32,8,768]{2,1,0:T(8,128)(2,1)}), bf16[32,8,768]{2,1,0:T(8,128)(2,1)S(1)}, u32[]{:S(2)}, u32[]{:S(2)}) %all-to-all-start) | async-done | bytes 393248 | tf_op jit(solution)/shard_map/all_to_all | solution.py:1090
  26.7 36.2 %forward.1 = (bf16[768,768]{1,0:T(8,128)(2,1)}, bf16[768,768]{1,0:T(8,128)(2,1)}, bf16[768,2304]{1,0:T(8,128)(2,1)}, bf16[18,256,512]{2,1,0:T(8,128)(2,1)}, bf16...) custom-call(s32[16]{0:T(128)S(1)} %pad_add_fusion.sc_ref.c_ref.b_ref, ...), custom_call_target="tpu_custom_call" | custom-call | flops 30000001024 | bytes 1048576 | tf_op jit(solution)/shard_map/forward/pallas_call | solution.py:319
  63.0 3.8 %ffn_backward.2 = (bf16[768,3072]{1,0:T(8,128)(2,1)S(1)}, f32[768,768]{1,0:T(8,128)S(1)}, bf16[768,768]{1,0:T(8,128)(2,1)S(1)}, f32[8,768]{1,0:T(8,128)S(1)}, f32[8,3072]{1,0:T(8,128)S(1)}) custom-call(s32[16]{0:T(128)S(1)} %pad_add_fusion.sc_ref.c_ref.b_ref, bf16[768,768]{1,0:T(8,128)(2,1)S(1)} %get-tuple-element.249.df_ref, ...), custom_call_target="tpu_custom_call" | custom-call | flops 4000000000 | bytes 1048576 | tf_op jit(solution)/shard_map/ffn_backward/pallas_call | solution.py:430
  67.7 1.4 first_split.3
  69.8 1.4 collective-permute-start.2
  71.1 7.1 %ffn_backward.3 = (bf16[768,3072]{1,0:T(8,128)(2,1)S(1)}, f32[768,768]{1,0:T(8,128)S(1)}, bf16[768,768]{1,0:T(8,128)(2,1)S(1)}, f32[8,768]{1,0:T(8,128)S(1)}, f32[8,3072]{1,0:T(8,128)S(1)}) custom-call(s32[16]{0:T(128)S(1)} %pad_add_fusion.sc_ref.c_ref.b_ref, ...), custom_call_target="tpu_custom_call", output_to_operand_aliasing={{0}: (9, {}), {1}: (10, {}), {2}: (11, {})} | custom-call | flops 8000000000 | bytes 1048576 | tf_op jit(solution)/shard_map/ffn_backward/pallas_call | solution.py:430
  78.2 4.7 %up_gradient.1 = (bf16[768,1536]{1,0:T(8,128)(2,1)S(1)}, bf16[768,1536]{1,0:T(8,128)(2,1)S(1)}) custom-call(s32[16]{0:T(128)S(1)} %pad_add_fusion.sc_ref.c_ref.b_ref, bf16[768,768]{1,0:T(8,128)(2,1)S(1)} %get-tuple-element.278.h_ref, bf16[768,3072]{1,0:T(8,128)(2,1)S(1)} %get-tuple-element.286.d_ref), custom_call_target="tpu_custom_call" | custom-call | flops 100000000 | bytes 1048576 | tf_op jit(solution)/shard_map/up_gradient/pallas_call | solution.py:465
  82.9 1.6 collective-permute-done.1.ar
  86.1 1.2 collective-permute-start.3
  87.3 1.0 collective-permute-start.4
  88.3 7.6 %attention_backward.2 = (bf16[768,2304]{1,0:T(8,128)(2,1)S(1)}, f32[384,768]{1,0:T(8,128)}, f32[256,768]{1,0:T(8,128)S(1)}, f32[8,768]{1,0:T(8,128)S(1)}) custom-call(s32[16]{0:T(128)S(1)} %pad_add_fusion.sc_ref.c_ref.b_ref, bf16[768,768]{1,0:T(8,128)(2,1)S(1)} %get-tuple-element.307.da_ref, f32[768,768]{1,0:T(8,128)S(1)} %get-tuple-element.308.dr_ref, ...), custom_call_target="tpu_custom_call" | custom-call | flops 5000000000 | bytes 1048576 | tf_op jit(solution)/shard_map/attention_backward/pallas_call | solution.py:544
  96.4 1.2 first_split.4
  97.6 1.1 collective-permute-start.6
  98.7 1.0 collective-permute-start.7
  99.7 13.0 %attention_backward.3 = (bf16[768,2304]{1,0:T(8,128)(2,1)S(1)}, f32[384,768]{1,0:T(8,128)}, bf16[256,768]{1,0:T(8,128)(2,1)}, f32[8,768]{1,0:T(8,128)S(1)}) custom-call(s32[16]{0:T(128)S(1)} %pad_add_fusion.sc_ref.c_ref.b_ref, bf16[768,768]{1,0:T(8,128)(2,1)S(1)} %get-tuple-element.307.da_ref, ...), custom_call_target="tpu_custom_call", output_to_operand_aliasing={{0}: (8, {}), {1}: (9, {})} | custom-call | flops 10000000000 | bytes 1048576 | tf_op jit(solution)/shard_map/attention_backward/pallas_call | solution.py:544
  115.0 1.1 collective-permute-start.9
  116.1 6.8 %qkvo_gradient.1 = (bf16[768,1536]{1,0:T(8,128)(2,1)}, bf16[768,1536]{1,0:T(8,128)(2,1)}) custom-call(s32[16]{0:T(128)S(1)} %pad_add_fusion.sc_ref.c_ref.b_ref, bf16[768,768]{1,0:T(8,128)(2,1)S(1)} %copy-done.11, bf16[768,2304]{1,0:T(8,128)(2,1)S(1)} %get-tuple-element.369.dq_ref, bf16[768,768]{1,0:T(8,128)(2,1)S(1)} %copy-done.12, ...), custom_call_target="tpu_custom_call" | custom-call | flops 5000000000 | bytes 1048576 | tf_op jit(solution)/shard_map/qkvo_gradient/pallas_call | solution.py:605
  122.9 1.7 join_split.3
  125.1 2.6 %all-to-all-start.1 = ((bf16[32,8,768]{2,1,0:T(8,128)(2,1)}), bf16[32,8,768]{2,1,0:T(8,128)(2,1)S(1)}, u32[]{:S(2)}, u32[]{:S(2)}) async-start(bf16[32,8,768]{2,1,0:T(8,128)(2,1)} %bitcast.9), calls=%async_computation.1 | async-start | bytes 786432 | tf_op jit(solution)/shard_map/all_to_all | solution.py:1142
  127.8 1.7 collective-permute-done.10
  129.5 4.5 %first_split.5 = (bf16[4,2,96,384]{3,2,1,0:T(8,128)(2,1)}, bf16[4,2,96,384]{3,2,1,0:T(8,128)(2,1)}, bf16[4,2,96,384]{3,2,1,0:T(8,128)(2,1)}, bf16[4,2,96,384]{3,2,1,0:T(8,128)(2,1)}) custom-call(s32[16]{0:T(128)S(1)} %pad_add_fusion.sc_ref.c_ref.b_ref, bf16[4,2,96,1536]{3,2,1,0:T(8,128)(2,1)S(1)} %bitcast.21, bf16[4,2,96,1536]{3,2,1,0:T(8,128)(2,1)} %bitcast.12.r_ref), custom_call_target="tpu_custom_call" | custom-call | flops 1000000000 | bytes 1048576 | tf_op jit(solution)/shard_map/first_split/pallas_call | solution.py:801
  134.9 1.1 collective-permute-start.14
  137.0 3.8 %all-to-all-done.1 = bf16[32,8,768]{2,1,0:T(8,128)(2,1)S(1)} async-done(((bf16[32,8,768]{2,1,0:T(8,128)(2,1)}), bf16[32,8,768]{2,1,0:T(8,128)(2,1)S(1)}, u32[]{:S(2)}, u32[]{:S(2)}) %all-to-all-start.1) | async-done | bytes 393248 | tf_op jit(solution)/shard_map/all_to_all | solution.py:1142
  140.9 3.2 %region_norm_backward.1 = (bf16[256,768]{1,0:T(8,128)(2,1)S(1)}, bf16[320,384]{1,0:T(8,128)(2,1)S(1)}, bf16[256,384]{1,0:T(8,128)(2,1)S(1)}, bf16[8,8,384]{2,1,0:T(8,128)(2,1)S(1)}, f32[4,256]{1,0:T(4,128)}) custom-call(s32[16]{0:T(128)S(1)} %pad_add_fusion.sc_ref.c_ref.b_ref, bf16[256,768]{1,0:T(8,128)(2,1)S(1)} %bitcast.25, s32[1,256]{1,0:T(1,128)} %t_ref.7, ...), custom_call_target="tpu_custom_call" | custom-call | flops 100000000 | bytes 1048576 | tf_op jit(solution)/shard_map/region_norm_backward/pallas_call | solution.py:671
  144.1 1.5 collective-permute-done.12.p_ref
  145.6 3.5 %visual_gradient.1 = (bf16[4,2,72,384]{3,2,1,0:T(8,128)(2,1)S(1)}, bf16[4,2,72,384]{3,2,1,0:T(8,128)(2,1)S(1)}, bf16[4,2,72,384]{3,2,1,0:T(8,128)(2,1)S(1)}, bf16[4,2,72,384]{3,2,1,0:T(8,128)(2,1)S(1)}) custom-call(s32[16]{0:T(128)S(1)} %pad_add_fusion.sc_ref.c_ref.b_ref, bf16[256,2048]{1,0:T(8,128)(2,1)} %f_ref.3, ...), custom_call_target="tpu_custom_call" | custom-call | flops 100000000 | bytes 1048576 | tf_op jit(solution)/shard_map/visual_gradient/pallas_call | solution.py:740
  150.0 1.3 collective-permute-start.17
  153.1 1.2 collective-permute-start.19
  155.0 1.3 collective-permute-start.20
  156.3 5.3 %feature_gradient.1 = f32[256,2048]{1,0:T(8,128)} custom-call(s32[16]{0:T(128)S(1)} %pad_add_fusion.sc_ref.c_ref.b_ref, bf16[256,768]{1,0:T(8,128)(2,1)S(1)} %get-tuple-element.425.d_ref, bf16[2048,768]{1,0:T(8,128)(2,1)} %w_ref.3), custom_call_target="tpu_custom_call" | custom-call | flops 10000000000 | bytes 1048576 | tf_op jit(solution)/shard_map/feature_gradient/pallas_call | solution.py:771
  163.9 1.4 collective-permute-start.21
  165.2 1.1 collective-permute-start.22
  166.4 3.0 %collective-permute-done.18.refs_1_ = bf16[4,96,384]{2,1,0:T(8,128)(2,1)S(1)} collective-permute-done((bf16[4,96,384]{2,1,0:T(8,128)(2,1)S(1)}, bf16[4,96,384]{2,1,0:T(8,128)(2,1)S(1)}, u32[]{:S(2)}, u32[]{:S(2)}) %collective-permute-start.18) | collective-permute-done | bytes 294944 | tf_op jit(solution)/shard_map/ppermute | solution.py:792
  170.9 2.3 %collective-permute-done.21.refs_1_ = bf16[4,72,384]{2,1,0:T(8,128)(2,1)S(1)} collective-permute-done((bf16[4,72,384]{2,1,0:T(8,128)(2,1)S(1)}, bf16[4,72,384]{2,1,0:T(8,128)(2,1)S(1)}, u32[]{:S(2)}, u32[]{:S(2)}) %collective-permute-start.21) | collective-permute-done | bytes 221216 | tf_op jit(solution)/shard_map/ppermute | solution.py:792
  174.6 1.6 collective-permute-start.26
  176.2 2.8 %collective-permute-done.23.r_ref = bf16[2,192,384]{2,1,0:T(8,128)(2,1)S(1)} collective-permute-done((bf16[2,192,384]{2,1,0:T(8,128)(2,1)S(1)}, bf16[2,192,384]{2,1,0:T(8,128)(2,1)S(1)}, u32[]{:S(2)}, u32[]{:S(2)}) %collective-permute-start.23) | collective-permute-done | bytes 294944 | tf_op jit(solution)/shard_map/ppermute | solution.py:792
  180.4 3.3 %collective-permute-done.24.r_ref = bf16[2,144,384]{2,1,0:T(8,128)(2,1)S(1)} collective-permute-done((bf16[2,144,384]{2,1,0:T(8,128)(2,1)S(1)}, bf16[2,144,384]{2,1,0:T(8,128)(2,1)S(1)}, u32[]{:S(2)}, u32[]{:S(2)}) %collective-permute-start.24) | collective-permute-done | bytes 221216 | tf_op jit(solution)/shard_map/ppermute | solution.py:792
  184.7 2.5 %collective-permute-done.29 = bf16[1,192,384]{2,1,0:T(8,128)(2,1)S(1)} collective-permute-done((bf16[1,192,384]{2,1,0:T(8,128)(2,1)S(1)}, bf16[1,192,384]{2,1,0:T(8,128)(2,1)S(1)}, u32[]{:S(2)}, u32[]{:S(2)}) %collective-permute-start.29) | collective-permute-done | bytes 147488 | tf_op jit(solution)/shard_map/ppermute | solution.py:792
  187.4 1.1 collective-permute-start.32
  188.5 2.4 %finish_ffn.1 = (f32[384,768]{1,0:T(8,128)}, f32[96,3072]{1,0:T(8,128)}) custom-call(s32[16]{0:T(128)S(1)} %pad_add_fusion.sc_ref.c_ref.b_ref, bf16[384,384]{1,0:T(8,128)(2,1)S(1)} %add_bitcast_fusion.p0, bf16[384,384]{1,0:T(8,128)(2,1)S(1)} %collective-permute-done.26.p1, bf16[384,384]{1,0:T(8,128)(2,1)S(1)} %collective-permute-done.27.p2, ...), custom_call_target="tpu_custom_call" | custom-call | flops 1000000000 | bytes 1048576 | tf_op jit(solution)/shard_map/finish_ffn/pallas_call | solution.py:801
  190.8 2.3 %collective-permute-done.25 = bf16[1,144,384]{2,1,0:T(8,128)(2,1)S(1)} collective-permute-done((bf16[1,144,384]{2,1,0:T(8,128)(2,1)S(1)}, bf16[1,144,384]{2,1,0:T(8,128)(2,1)S(1)}, u32[]{:S(2)}, u32[]{:S(2)}) %collective-permute-start.25) | collective-permute-done | bytes 110624 | tf_op jit(solution)/shard_map/ppermute | solution.py:792
  195.0 1.7 finish_wide.1
  196.7 2.4 %collective-permute-done.30.p1 = bf16[144,384]{1,0:T(8,128)(2,1)S(1)} collective-permute-done((bf16[144,384]{1,0:T(8,128)(2,1)S(1)}, bf16[144,384]{1,0:T(8,128)(2,1)S(1)}, u32[]{:S(2)}, u32[]{:S(2)}) %collective-permute-start.30) | collective-permute-done | bytes 110624 | tf_op jit(solution)/shard_map/ppermute | solution.py:792
  199.1 1.3 collective-permute-done.35.p3
  200.4 1.6 finish_visual.1
  (98 shorter events, 22.4 us)
Async XLA Ops:
  0.7 12.1 %copy-start.14 = (f32[1536]{0:T(1024)S(1)}, f32[1536]{0:T(1024)}, u32[]{:S(2)}) copy-start(f32[1536]{0:T(1024)} %param.40) | copy-start | bytes 18436
  0.7 12.2 %copy-start.15 = (s32[2]{0:T(128)S(1)}, s32[2]{0:T(128)}, u32[]{:S(2)}) copy-start(s32[2]{0:T(128)} %param.31) | copy-start | bytes 28
  0.7 12.2 %copy-start.16 = (s32[3]{0:T(128)S(1)}, s32[3]{0:T(128)}, u32[]{:S(2)}) copy-start(s32[3]{0:T(128)} %param.30) | copy-start | bytes 40
  0.7 12.2 %copy-start.17 = (s32[3]{0:T(128)S(1)}, s32[3]{0:T(128)}, u32[]{:S(2)}) copy-start(s32[3]{0:T(128)} %param.29) | copy-start | bytes 40
  5.5 20.5 %all-to-all-start = ((bf16[32,8,768]{2,1,0:T(8,128)(2,1)}), bf16[32,8,768]{2,1,0:T(8,128)(2,1)S(1)}, u32[]{:S(2)}, u32[]{:S(2)}) async-start(bf16[32,8,768]{2,1,0:T(8,128)(2,1)} %bitcast.1), calls=%async_computation | async-start | bytes 786432 | tf_op jit(solution)/shard_map/all_to_all | solution.py:1090
  26.7 36.3 %copy-start.3 = (f32[768]{0:T(1024)S(1)}, f32[768]{0:T(1024)}, u32[]{:S(2)}) copy-start(f32[768]{0:T(1024)} %ag_ref.5) | copy-start | bytes 9220
  62.9 4.8 %collective-permute-start = (bf16[8,2,2,96,384]{4,3,2,1,0:T(8,128)(2,1)}, bf16[8,2,2,96,384]{4,3,2,1,0:T(8,128)(2,1)S(1)}, u32[]{:S(2)}, u32[]{:S(2)}) collective-permute-start(bf16[8,2,2,96,384]{4,3,2,1,0:T(8,128)(2,1)} %bitcast.29), channel_id=1, source_target_pairs={{0,1},{1,0},{2,3},{3,2},{4,5},{5,4},{6,7},{7,6},{8,9},{9,8},{10,11... | collective-permute-start | bytes 7077896 | tf_op jit(solution)/shard_map/ppermute | solution.py:792
  69.1 15.4 %collective-permute-start.1 = (bf16[4,2,96,384]{3,2,1,0:T(8,128)(2,1)S(1)}, bf16[4,2,96,384]{3,2,1,0:T(8,128)(2,1)S(1)}, u32[]{:S(2)}, u32[]{:S(2)}) collective-permute-start(bf16[4,2,96,384]{3,2,1,0:T(8,128)(2,1)S(1)} %get-tuple-element.273), channel_id=1, source_target_pairs={{0,2},{1,3},{2,0},{3,1},{4,6},{5,7},{6,4},{7,5},{8,10},{9,11},{10,... | collective-permute-start | bytes 1769480 | tf_op jit(solution)/shard_map/ppermute | solution.py:792
  69.8 15.3 %collective-permute-start.2 = (bf16[4,2,96,384]{3,2,1,0:T(8,128)(2,1)S(1)}, bf16[4,2,96,384]{3,2,1,0:T(8,128)(2,1)S(1)}, u32[]{:S(2)}, u32[]{:S(2)}) collective-permute-start(bf16[4,2,96,384]{3,2,1,0:T(8,128)(2,1)S(1)} %get-tuple-element.275), channel_id=1, source_target_pairs={{0,4},{1,5},{2,6},{3,7},{4,0},{5,1},{6,2},{7,3},{8,12},{9,13},{10,... | collective-permute-start | bytes 1769480 | tf_op jit(solution)/shard_map/ppermute | solution.py:792
  78.2 10.1 %copy-start.5 = (bf16[768,768]{1,0:T(8,128)(2,1)S(1)}, bf16[768,768]{1,0:T(8,128)(2,1)}, u32[]{:S(2)}) copy-start(bf16[768,768]{1,0:T(8,128)(2,1)} %wo_ref.3) | copy-start | bytes 3538948
  78.2 10.1 %copy-start.9 = (bf16[768,2304]{1,0:T(8,128)(2,1)S(1)}, bf16[768,2304]{1,0:T(8,128)(2,1)}, u32[]{:S(2)}) copy-start(bf16[768,2304]{1,0:T(8,128)(2,1)} %get-tuple-element.310.qkv_ref) | copy-start | bytes 10616836
  86.0 10.4 %collective-permute-start.5 = (bf16[768,1536]{1,0:T(8,128)(2,1)S(1)}, bf16[768,1536]{1,0:T(8,128)(2,1)S(1)}, u32[]{:S(2)}, u32[]{:S(2)}) collective-permute-start(bf16[768,1536]{1,0:T(8,128)(2,1)S(1)} %get-tuple-element.304), channel_id=1, source_target_pairs={{0,1},{1,0},{2,3},{3,2},{4,5},{5,4},{6,7},{7,6},{8,9},{9,8},{10,11... | collective-permute-start | bytes 7077896 | tf_op jit(solution)/shard_map/ppermute | solution.py:792
  86.1 9.8 %collective-permute-start.3 = (bf16[4,96,384]{2,1,0:T(8,128)(2,1)S(1)}, bf16[4,96,384]{2,1,0:T(8,128)(2,1)S(1)}, u32[]{:S(2)}, u32[]{:S(2)}) collective-permute-start(bf16[4,96,384]{2,1,0:T(8,128)(2,1)S(1)} %get-tuple-element.300), channel_id=1, source_target_pairs={{0,4},{1,5},{2,6},{3,7},{4,0},{5,1},{6,2},{7,3},{8,12},{9,13},{10,... | collective-permute-start | bytes 884744 | tf_op jit(solution)/shard_map/ppermute | solution.py:792
  87.3 9.1 %collective-permute-start.4 = (bf16[4,96,384]{2,1,0:T(8,128)(2,1)S(1)}, bf16[4,96,384]{2,1,0:T(8,128)(2,1)S(1)}, u32[]{:S(2)}, u32[]{:S(2)}) collective-permute-start(bf16[4,96,384]{2,1,0:T(8,128)(2,1)S(1)} %get-tuple-element.302), channel_id=1, source_target_pairs={{0,2},{1,3},{2,0},{3,1},{4,6},{5,7},{6,4},{7,5},{8,10},{9,11},{10,... | collective-permute-start | bytes 884744 | tf_op jit(solution)/shard_map/ppermute | solution.py:792
  97.6 15.1 %collective-permute-start.6 = (bf16[4,2,96,384]{3,2,1,0:T(8,128)(2,1)S(1)}, bf16[4,2,96,384]{3,2,1,0:T(8,128)(2,1)S(1)}, u32[]{:S(2)}, u32[]{:S(2)}) collective-permute-start(bf16[4,2,96,384]{3,2,1,0:T(8,128)(2,1)S(1)} %get-tuple-element.336), channel_id=1, source_target_pairs={{0,2},{1,3},{2,0},{3,1},{4,6},{5,7},{6,4},{7,5},{8,10},{9,11},{10,... | collective-permute-start | bytes 1769480 | tf_op jit(solution)/shard_map/ppermute | solution.py:792
  98.7 14.4 %collective-permute-start.7 = (bf16[4,2,96,384]{3,2,1,0:T(8,128)(2,1)S(1)}, bf16[4,2,96,384]{3,2,1,0:T(8,128)(2,1)S(1)}, u32[]{:S(2)}, u32[]{:S(2)}) collective-permute-start(bf16[4,2,96,384]{3,2,1,0:T(8,128)(2,1)S(1)} %get-tuple-element.338), channel_id=1, source_target_pairs={{0,4},{1,5},{2,6},{3,7},{4,0},{5,1},{6,2},{7,3},{8,12},{9,13},{10,... | collective-permute-start | bytes 1769480 | tf_op jit(solution)/shard_map/ppermute | solution.py:792
  113.9 9.0 %collective-permute-start.8 = (bf16[4,96,384]{2,1,0:T(8,128)(2,1)S(1)}, bf16[4,96,384]{2,1,0:T(8,128)(2,1)S(1)}, u32[]{:S(2)}, u32[]{:S(2)}) collective-permute-start(bf16[4,96,384]{2,1,0:T(8,128)(2,1)S(1)} %get-tuple-element.359), channel_id=1, source_target_pairs={{0,4},{1,5},{2,6},{3,7},{4,0},{5,1},{6,2},{7,3},{8,12},{9,13},{10,... | collective-permute-start | bytes 884744 | tf_op jit(solution)/shard_map/ppermute | solution.py:792
  115.0 7.9 %collective-permute-start.9 = (bf16[4,96,384]{2,1,0:T(8,128)(2,1)S(1)}, bf16[4,96,384]{2,1,0:T(8,128)(2,1)S(1)}, u32[]{:S(2)}, u32[]{:S(2)}) collective-permute-start(bf16[4,96,384]{2,1,0:T(8,128)(2,1)S(1)} %get-tuple-element.361), channel_id=1, source_target_pairs={{0,2},{1,3},{2,0},{3,1},{4,6},{5,7},{6,4},{7,5},{8,10},{9,11},{10,... | collective-permute-start | bytes 884744 | tf_op jit(solution)/shard_map/ppermute | solution.py:792
  122.9 6.6 %copy-start = (bf16[768,1536]{1,0:T(8,128)(2,1)S(1)}, bf16[768,1536]{1,0:T(8,128)(2,1)}, u32[]{:S(2)}) copy-start(bf16[768,1536]{1,0:T(8,128)(2,1)} %get-tuple-element.390) | copy-start | bytes 7077892
  124.6 4.9 %collective-permute-start.10 = (bf16[768,1536]{1,0:T(8,128)(2,1)}, bf16[768,1536]{1,0:T(8,128)(2,1)}, u32[]{:S(2)}, u32[]{:S(2)}) collective-permute-start(bf16[768,1536]{1,0:T(8,128)(2,1)} %get-tuple-element.391), channel_id=1, source_target_pairs={{0,1},{1,0},{2,3},{3,2},{4,5},{5,4},{6,7},{7,6},{8,9},{9,8},{10,11... | collective-permute-start | bytes 7077896 | tf_op jit(solution)/shard_map/ppermute | solution.py:792
  124.6 19.4 %collective-permute-start.11 = (bf16[256,2048]{1,0:T(8,128)(2,1)}, bf16[256,2048]{1,0:T(8,128)(2,1)}, u32[]{:S(2)}, u32[]{:S(2)}) collective-permute-start(bf16[256,2048]{1,0:T(8,128)(2,1)} %f_ref.3), channel_id=1, source_target_pairs={{0,1},{1,0},{2,3},{3,2},{4,5},{5,4},{6,7},{7,6},{8,9},{9,8},{10,11... | collective-permute-start | bytes 3145736 | tf_op jit(solution)/shard_map/ppermute | solution.py:792
  125.1 15.7 %all-to-all-start.1 = ((bf16[32,8,768]{2,1,0:T(8,128)(2,1)}), bf16[32,8,768]{2,1,0:T(8,128)(2,1)S(1)}, u32[]{:S(2)}, u32[]{:S(2)}) async-start(bf16[32,8,768]{2,1,0:T(8,128)(2,1)} %bitcast.9), calls=%async_computation.1 | async-start | bytes 786432 | tf_op jit(solution)/shard_map/all_to_all | solution.py:1142
  134.0 17.3 %copy-start.6 = (bf16[4,2,96,384]{3,2,1,0:T(8,128)(2,1)S(1)}, bf16[4,2,96,384]{3,2,1,0:T(8,128)(2,1)}, u32[]{:S(2)}) copy-start(bf16[4,2,96,384]{3,2,1,0:T(8,128)(2,1)} %get-tuple-element.393.ak) | copy-start | bytes 1769476
  134.0 17.3 %copy-start.7 = (bf16[4,2,96,384]{3,2,1,0:T(8,128)(2,1)S(1)}, bf16[4,2,96,384]{3,2,1,0:T(8,128)(2,1)}, u32[]{:S(2)}) copy-start(bf16[4,2,96,384]{3,2,1,0:T(8,128)(2,1)} %get-tuple-element.395.bk) | copy-start | bytes 1769476
  134.0 17.3 %collective-permute-start.13 = (bf16[4,2,96,384]{3,2,1,0:T(8,128)(2,1)}, bf16[4,2,96,384]{3,2,1,0:T(8,128)(2,1)S(1)}, u32[]{:S(2)}, u32[]{:S(2)}) collective-permute-start(bf16[4,2,96,384]{3,2,1,0:T(8,128)(2,1)} %get-tuple-element.392), channel_id=1, source_target_pairs={{0,2},{1,3},{2,0},{3,1},{4,6},{5,7},{6,4},{7,5},{8,10},{9,11},{10,... | collective-permute-start | bytes 1769480 | tf_op jit(solution)/shard_map/ppermute | solution.py:792
  134.9 16.3 %collective-permute-start.14 = (bf16[4,2,96,384]{3,2,1,0:T(8,128)(2,1)}, bf16[4,2,96,384]{3,2,1,0:T(8,128)(2,1)S(1)}, u32[]{:S(2)}, u32[]{:S(2)}) collective-permute-start(bf16[4,2,96,384]{3,2,1,0:T(8,128)(2,1)} %get-tuple-element.394), channel_id=1, source_target_pairs={{0,4},{1,5},{2,6},{3,7},{4,0},{5,1},{6,2},{7,3},{8,12},{9,13},{10,... | collective-permute-start | bytes 1769480 | tf_op jit(solution)/shard_map/ppermute | solution.py:792
  136.0 18.3 %collective-permute-start.15 = (bf16[2,384,384]{2,1,0:T(8,128)(2,1)}, bf16[2,384,384]{2,1,0:T(8,128)(2,1)S(1)}, u32[]{:S(2)}, u32[]{:S(2)}) collective-permute-start(bf16[2,384,384]{2,1,0:T(8,128)(2,1)} %get-tuple-element.421), channel_id=1, source_target_pairs={{0,8},{1,9},{2,10},{3,11},{4,12},{5,13},{6,14},{7,15},{8,0},{9,1},... | collective-permute-start | bytes 1769480 | tf_op jit(solution)/shard_map/ppermute | solution.py:792
  144.1 1.5 collective-permute-start.12
  149.1 13.1 %collective-permute-start.16 = (bf16[4,2,72,384]{3,2,1,0:T(8,128)(2,1)S(1)}, bf16[4,2,72,384]{3,2,1,0:T(8,128)(2,1)S(1)}, u32[]{:S(2)}, u32[]{:S(2)}) collective-permute-start(bf16[4,2,72,384]{3,2,1,0:T(8,128)(2,1)S(1)} %get-tuple-element.409), channel_id=1, source_target_pairs={{0,2},{1,3},{2,0},{3,1},{4,6},{5,7},{6,4},{7,5},{8,10},{9,11},{10,... | collective-permute-start | bytes 1327112 | tf_op jit(solution)/shard_map/ppermute | solution.py:792
  150.0 13.0 %collective-permute-start.17 = (bf16[4,2,72,384]{3,2,1,0:T(8,128)(2,1)S(1)}, bf16[4,2,72,384]{3,2,1,0:T(8,128)(2,1)S(1)}, u32[]{:S(2)}, u32[]{:S(2)}) collective-permute-start(bf16[4,2,72,384]{3,2,1,0:T(8,128)(2,1)S(1)} %get-tuple-element.411), channel_id=1, source_target_pairs={{0,4},{1,5},{2,6},{3,7},{4,0},{5,1},{6,2},{7,3},{8,12},{9,13},{10,... | collective-permute-start | bytes 1327112 | tf_op jit(solution)/shard_map/ppermute | solution.py:792
  152.2 17.1 %collective-permute-start.18 = (bf16[4,96,384]{2,1,0:T(8,128)(2,1)S(1)}, bf16[4,96,384]{2,1,0:T(8,128)(2,1)S(1)}, u32[]{:S(2)}, u32[]{:S(2)}) collective-permute-start(bf16[4,96,384]{2,1,0:T(8,128)(2,1)S(1)} %get-tuple-element.414), channel_id=1, source_target_pairs={{0,4},{1,5},{2,6},{3,7},{4,0},{5,1},{6,2},{7,3},{8,12},{9,13},{10,... | collective-permute-start | bytes 884744 | tf_op jit(solution)/shard_map/ppermute | solution.py:792
  153.1 16.3 %collective-permute-start.19 = (bf16[4,96,384]{2,1,0:T(8,128)(2,1)S(1)}, bf16[4,96,384]{2,1,0:T(8,128)(2,1)S(1)}, u32[]{:S(2)}, u32[]{:S(2)}) collective-permute-start(bf16[4,96,384]{2,1,0:T(8,128)(2,1)S(1)} %get-tuple-element.416), channel_id=1, source_target_pairs={{0,2},{1,3},{2,0},{3,1},{4,6},{5,7},{6,4},{7,5},{8,10},{9,11},{10,... | collective-permute-start | bytes 884744 | tf_op jit(solution)/shard_map/ppermute | solution.py:792
  155.0 15.9 %collective-permute-start.20 = (bf16[1,384,384]{2,1,0:T(8,128)(2,1)S(1)}, bf16[1,384,384]{2,1,0:T(8,128)(2,1)S(1)}, u32[]{:S(2)}, u32[]{:S(2)}) collective-permute-start(bf16[1,384,384]{2,1,0:T(8,128)(2,1)S(1)} %get-tuple-element.422), channel_id=1, source_target_pairs={{0,16},{1,17},{2,18},{3,19},{4,20},{5,21},{6,22},{7,23},{8,24},{9,... | collective-permute-start | bytes 884744 | tf_op jit(solution)/shard_map/ppermute | solution.py:792
  163.9 9.3 %collective-permute-start.21 = (bf16[4,72,384]{2,1,0:T(8,128)(2,1)S(1)}, bf16[4,72,384]{2,1,0:T(8,128)(2,1)S(1)}, u32[]{:S(2)}, u32[]{:S(2)}) collective-permute-start(bf16[4,72,384]{2,1,0:T(8,128)(2,1)S(1)} %get-tuple-element.428), channel_id=1, source_target_pairs={{0,4},{1,5},{2,6},{3,7},{4,0},{5,1},{6,2},{7,3},{8,12},{9,13},{10,... | collective-permute-start | bytes 663560 | tf_op jit(solution)/shard_map/ppermute | solution.py:792
  165.2 8.0 %collective-permute-start.22 = (bf16[4,72,384]{2,1,0:T(8,128)(2,1)S(1)}, bf16[4,72,384]{2,1,0:T(8,128)(2,1)S(1)}, u32[]{:S(2)}, u32[]{:S(2)}) collective-permute-start(bf16[4,72,384]{2,1,0:T(8,128)(2,1)S(1)} %get-tuple-element.430), channel_id=1, source_target_pairs={{0,2},{1,3},{2,0},{3,1},{4,6},{5,7},{6,4},{7,5},{8,10},{9,11},{10,... | collective-permute-start | bytes 663560 | tf_op jit(solution)/shard_map/ppermute | solution.py:792
  170.1 8.9 %collective-permute-start.23 = (bf16[2,192,384]{2,1,0:T(8,128)(2,1)S(1)}, bf16[2,192,384]{2,1,0:T(8,128)(2,1)S(1)}, u32[]{:S(2)}, u32[]{:S(2)}) collective-permute-start(bf16[2,192,384]{2,1,0:T(8,128)(2,1)S(1)} %get-tuple-element.433), channel_id=1, source_target_pairs={{0,8},{1,9},{2,10},{3,11},{4,12},{5,13},{6,14},{7,15},{8,0},{9,1},... | collective-permute-start | bytes 884744 | tf_op jit(solution)/shard_map/ppermute | solution.py:792
  173.9 9.7 %collective-permute-start.24 = (bf16[2,144,384]{2,1,0:T(8,128)(2,1)S(1)}, bf16[2,144,384]{2,1,0:T(8,128)(2,1)S(1)}, u32[]{:S(2)}, u32[]{:S(2)}) collective-permute-start(bf16[2,144,384]{2,1,0:T(8,128)(2,1)S(1)} %get-tuple-element.437), channel_id=1, source_target_pairs={{0,8},{1,9},{2,10},{3,11},{4,12},{5,13},{6,14},{7,15},{8,0},{9,1},... | collective-permute-start | bytes 663560 | tf_op jit(solution)/shard_map/ppermute | solution.py:792
  174.6 9.7 %collective-permute-start.26 = (bf16[384,384]{1,0:T(8,128)(2,1)S(1)}, bf16[384,384]{1,0:T(8,128)(2,1)S(1)}, u32[]{:S(2)}, u32[]{:S(2)}) collective-permute-start(bf16[384,384]{1,0:T(8,128)(2,1)S(1)} %add_bitcast_fusion.p0), channel_id=1, source_target_pairs={{0,2},{1,3},{2,0},{3,1},{4,6},{5,7},{6,4},{7,5},{8,10},{9,11},{10,... | collective-permute-start | bytes 884744 | tf_op jit(solution)/shard_map/ppermute | solution.py:792
  176.2 12.2 %collective-permute-start.27 = (bf16[384,384]{1,0:T(8,128)(2,1)S(1)}, bf16[384,384]{1,0:T(8,128)(2,1)S(1)}, u32[]{:S(2)}, u32[]{:S(2)}) collective-permute-start(bf16[384,384]{1,0:T(8,128)(2,1)S(1)} %add_bitcast_fusion.p0), channel_id=1, source_target_pairs={{0,1},{1,0},{2,3},{3,2},{4,5},{5,4},{6,7},{7,6},{8,9},{9,8},{10,11... | collective-permute-start | bytes 884744 | tf_op jit(solution)/shard_map/ppermute | solution.py:792
  179.6 7.7 %collective-permute-start.29 = (bf16[1,192,384]{2,1,0:T(8,128)(2,1)S(1)}, bf16[1,192,384]{2,1,0:T(8,128)(2,1)S(1)}, u32[]{:S(2)}, u32[]{:S(2)}) collective-permute-start(bf16[1,192,384]{2,1,0:T(8,128)(2,1)S(1)} %get-tuple-element.440), channel_id=1, source_target_pairs={{0,16},{1,17},{2,18},{3,19},{4,20},{5,21},{6,22},{7,23},{8,24},{9,... | collective-permute-start | bytes 442376 | tf_op jit(solution)/shard_map/ppermute | solution.py:792
  184.3 4.2 %collective-permute-start.28 = (bf16[384,384]{1,0:T(8,128)(2,1)S(1)}, bf16[384,384]{1,0:T(8,128)(2,1)S(1)}, u32[]{:S(2)}, u32[]{:S(2)}) collective-permute-start(bf16[384,384]{1,0:T(8,128)(2,1)S(1)} %collective-permute-done.26.p1), channel_id=1, source_target_pairs={{0,1},{1,0},{2,3},{3,2},{4,5},{5,4},{6,7},{7,6},{8,9},{9,8},{10,11... | collective-permute-start | bytes 884744 | tf_op jit(solution)/shard_map/ppermute | solution.py:792
  184.4 8.7 %collective-permute-start.25 = (bf16[1,144,384]{2,1,0:T(8,128)(2,1)S(1)}, bf16[1,144,384]{2,1,0:T(8,128)(2,1)S(1)}, u32[]{:S(2)}, u32[]{:S(2)}) collective-permute-start(bf16[1,144,384]{2,1,0:T(8,128)(2,1)S(1)} %get-tuple-element.443), channel_id=1, source_target_pairs={{0,16},{1,17},{2,18},{3,19},{4,20},{5,21},{6,22},{7,23},{8,24},{9,... | collective-permute-start | bytes 331784 | tf_op jit(solution)/shard_map/ppermute | solution.py:792
  187.3 7.6 %collective-permute-start.33 = (bf16[192,384]{1,0:T(8,128)(2,1)S(1)}, bf16[192,384]{1,0:T(8,128)(2,1)S(1)}, u32[]{:S(2)}, u32[]{:S(2)}) collective-permute-start(bf16[192,384]{1,0:T(8,128)(2,1)S(1)} %add_bitcast_fusion.1.p0), channel_id=1, source_target_pairs={{0,1},{1,0},{2,3},{3,2},{4,5},{5,4},{6,7},{7,6},{8,9},{9,8},{10,11... | collective-permute-start | bytes 442376 | tf_op jit(solution)/shard_map/ppermute | solution.py:792
  187.4 6.3 %collective-permute-start.32 = (bf16[192,384]{1,0:T(8,128)(2,1)S(1)}, bf16[192,384]{1,0:T(8,128)(2,1)S(1)}, u32[]{:S(2)}, u32[]{:S(2)}) collective-permute-start(bf16[192,384]{1,0:T(8,128)(2,1)S(1)} %add_bitcast_fusion.1.p0), channel_id=1, source_target_pairs={{0,2},{1,3},{2,0},{3,1},{4,6},{5,7},{6,4},{7,5},{8,10},{9,11},{10,... | collective-permute-start | bytes 442376 | tf_op jit(solution)/shard_map/ppermute | solution.py:792
  193.6 1.4 collective-permute-start.34
  193.6 5.5 %collective-permute-start.30 = (bf16[144,384]{1,0:T(8,128)(2,1)S(1)}, bf16[144,384]{1,0:T(8,128)(2,1)S(1)}, u32[]{:S(2)}, u32[]{:S(2)}) collective-permute-start(bf16[144,384]{1,0:T(8,128)(2,1)S(1)} %add_bitcast_fusion.2.p0), channel_id=1, source_target_pairs={{0,2},{1,3},{2,0},{3,1},{4,6},{5,7},{6,4},{7,5},{8,10},{9,11},{10,... | collective-permute-start | bytes 331784 | tf_op jit(solution)/shard_map/ppermute | solution.py:792
  194.6 4.5 %collective-permute-start.31 = (bf16[144,384]{1,0:T(8,128)(2,1)S(1)}, bf16[144,384]{1,0:T(8,128)(2,1)S(1)}, u32[]{:S(2)}, u32[]{:S(2)}) collective-permute-start(bf16[144,384]{1,0:T(8,128)(2,1)S(1)} %add_bitcast_fusion.2.p0), channel_id=1, source_target_pairs={{0,1},{1,0},{2,3},{3,2},{4,5},{5,4},{6,7},{7,6},{8,9},{9,8},{10,11... | collective-permute-start | bytes 331784 | tf_op jit(solution)/shard_map/ppermute | solution.py:792
  199.1 1.3 collective-permute-start.35
  (8 other events, 33.5 us)

commit v9 on v8

--- a/solution.py
+++ b/solution.py
@@ -417,7 +417,9 @@
             low = (d_act * sl_ref[here, at].astype(f32)).astype(bf16)
             dup_ref[here, at] = low
             up_ref[0:1, at] += row_sum(low.astype(f32))
-        d_hidden = ds_ref[here, :] + mm(dup_ref[here, :], wu[...], NT)
+            term = mm(low, wu[:, at], NT)
+            through = term if piece == 0 else through + term
+        d_hidden = ds_ref[here, :] + through
         normed = an_ref[here, :]
         resid = norm_back(d_hidden, normed, ai_ref[here, 0:1], ag_ref[...])
         dr_ref[here, :] = resid

time: 203 us -> 202 us (level)
  transfers between devices with their start and end apart: 38 -> 38, of which waited for: 21 -> 21; matrix products, arithmetic and copies ran while one was open for 0% -> 0% of each run, Pallas kernels for 36% -> 37%
where the time goes in v9:
time: 202 us
  Pallas kernels  122 us (60%)
  waiting for transfers between devices  40.2 us (20%)
  starting transfers between devices  37.1 us (18%)
    pallas_call x1, Pallas kernels, forward(): pl.pallas_call(kernel, grid_spec=pltpu.PrefetchScalarGridSpec(num_scalar_...  36.2 us
    ppermute x36, waiting for transfers between devices, swap(): lax.ppermute(values, ('dp', 'enc'), [(i, i ^ bit) for i in range(count)])  28.4 us
    ppermute x36, starting transfers between devices, swap(): lax.ppermute(values, ('dp', 'enc'), [(i, i ^ bit) for i in range(count)])  26.9 us
    pallas_call x16, Pallas kernels, scalar_call(): pl.pallas_call(kernel, grid_spec=pltpu.PrefetchScalarGridSpec(num_scalar_...  21.2 us
    pallas_call x2, Pallas kernels, attention_backward(): pl.pallas_call(kernel, grid_spec=pltpu.PrefetchScalarGridSpec(num_scalar_...  20.8 us
    pallas_call x2, Pallas kernels, ffn_backward(): pl.pallas_call(kernel, grid_spec=pltpu.PrefetchScalarGridSpec(num_scalar_...  11.1 us
    all_to_all x1, waiting for transfers between devices, on_device(): lax.all_to_all(message, axes, split_axis=0, concat_axis=0, tiled=True)  8 us
    all_to_all x1, starting transfers between devices, on_device(): lax.all_to_all(message, axes, split_axis=0, concat_axis=0, tiled=True)  7.3 us
  transfers between devices with their start and end apart: 38, of which 21 were waited for; matrix products, arithmetic and copies ran while one was open for 0% of the time, Pallas kernels for 37%

profile of v9, /device:TPU:0, one launch (start us, length us, event | category | flops | bytes accessed | tf_op | source)
XLA Modules:
  0.0 201.9 jit_solution(13207898744992254743)
XLA Ops:
  0.7 4.8 %region_forward.1 = (bf16[256,768]{1,0:T(8,128)(2,1)}, f32[256,768]{1,0:T(8,128)}, f32[256,128]{1,0:T(8,128)}) custom-call(bf16[256,2048]{1,0:T(8,128)(2,1)} %f_ref.3, bf16[4,256]{1,0:T(4,128)(2,1)} %box_ref.3, s32[1,256]{1,0:T(1,128)} %t_ref.7, bf16[2048,768]{1,0:T(8,128)(2,1)} %w_ref.3, bf16[4,768]{1,0:T(4,128)(2,1)} %bitcast.27, f32[768]{0:T(1024)} %b_ref.1, ...), custom_call_target="tpu_custom_call" | custom-call | flops 3000000000 | bytes 1048576 | tf_op jit(solution)/shard_map/region_forward/pallas_call | solution.py:112
  5.5 7.3 %all-to-all-start = ((bf16[32,8,768]{2,1,0:T(8,128)(2,1)}), bf16[32,8,768]{2,1,0:T(8,128)(2,1)S(1)}, u32[]{:S(2)}, u32[]{:S(2)}) async-start(bf16[32,8,768]{2,1,0:T(8,128)(2,1)} %bitcast.1), calls=%async_computation | async-start | bytes 786432 | tf_op jit(solution)/shard_map/all_to_all | solution.py:1092
  12.9 5.0 %text_qkv.1.tq_ref = bf16[384,2304]{1,0:T(8,128)(2,1)} custom-call(bf16[384,768]{1,0:T(8,128)(2,1)} %t_ref.6, bf16[768,2304]{1,0:T(8,128)(2,1)} %wq.3, f32[1,1536]{1,0:T(1,128)S(1)} %reshape.72.b_ref.qvb_ref), custom_call_target="tpu_custom_call" | custom-call | flops 3000000000 | bytes 1048576 | tf_op jit(solution)/shard_map/text_qkv/pallas_call | solution.py:142
  17.9 8.0 %all-to-all-done = bf16[32,8,768]{2,1,0:T(8,128)(2,1)S(1)} async-done(((bf16[32,8,768]{2,1,0:T(8,128)(2,1)}), bf16[32,8,768]{2,1,0:T(8,128)(2,1)S(1)}, u32[]{:S(2)}, u32[]{:S(2)}) %all-to-all-start) | async-done | bytes 393248 | tf_op jit(solution)/shard_map/all_to_all | solution.py:1092
  26.7 36.2 %forward.1 = (bf16[768,768]{1,0:T(8,128)(2,1)}, bf16[768,768]{1,0:T(8,128)(2,1)}, bf16[768,2304]{1,0:T(8,128)(2,1)}, bf16[18,256,512]{2,1,0:T(8,128)(2,1)}, bf16...) custom-call(s32[16]{0:T(128)S(1)} %pad_add_fusion.sc_ref.c_ref.b_ref, ...), custom_call_target="tpu_custom_call" | custom-call | flops 30000001024 | bytes 1048576 | tf_op jit(solution)/shard_map/forward/pallas_call | solution.py:319
  63.0 3.8 %ffn_backward.2 = (bf16[768,3072]{1,0:T(8,128)(2,1)S(1)}, f32[768,768]{1,0:T(8,128)S(1)}, bf16[768,768]{1,0:T(8,128)(2,1)S(1)}, f32[8,768]{1,0:T(8,128)S(1)}, f32[8,3072]{1,0:T(8,128)S(1)}) custom-call(s32[16]{0:T(128)S(1)} %pad_add_fusion.sc_ref.c_ref.b_ref, bf16[768,768]{1,0:T(8,128)(2,1)S(1)} %get-tuple-element.249.df_ref, ...), custom_call_target="tpu_custom_call" | custom-call | flops 4000000000 | bytes 1048576 | tf_op jit(solution)/shard_map/ffn_backward/pallas_call | solution.py:432
  67.7 1.2 first_split.3
  69.6 1.4 collective-permute-start.2
  70.9 7.3 %ffn_backward.3 = (bf16[768,3072]{1,0:T(8,128)(2,1)S(1)}, f32[768,768]{1,0:T(8,128)S(1)}, bf16[768,768]{1,0:T(8,128)(2,1)S(1)}, f32[8,768]{1,0:T(8,128)S(1)}, f32[8,3072]{1,0:T(8,128)S(1)}) custom-call(s32[16]{0:T(128)S(1)} %pad_add_fusion.sc_ref.c_ref.b_ref, ...), custom_call_target="tpu_custom_call", output_to_operand_aliasing={{0}: (9, {}), {1}: (10, {}), {2}: (11, {})} | custom-call | flops 8000000000 | bytes 1048576 | tf_op jit(solution)/shard_map/ffn_backward/pallas_call | solution.py:432
  78.2 4.7 %up_gradient.1 = (bf16[768,1536]{1,0:T(8,128)(2,1)S(1)}, bf16[768,1536]{1,0:T(8,128)(2,1)S(1)}) custom-call(s32[16]{0:T(128)S(1)} %pad_add_fusion.sc_ref.c_ref.b_ref, bf16[768,768]{1,0:T(8,128)(2,1)S(1)} %get-tuple-element.278.h_ref, bf16[768,3072]{1,0:T(8,128)(2,1)S(1)} %get-tuple-element.286.d_ref), custom_call_target="tpu_custom_call" | custom-call | flops 100000000 | bytes 1048576 | tf_op jit(solution)/shard_map/up_gradient/pallas_call | solution.py:467
  82.9 1.4 collective-permute-done.1.ar
  85.9 1.2 collective-permute-start.3
  87.1 1.0 collective-permute-start.4
  88.2 7.6 %attention_backward.2 = (bf16[768,2304]{1,0:T(8,128)(2,1)S(1)}, f32[384,768]{1,0:T(8,128)}, f32[256,768]{1,0:T(8,128)S(1)}, f32[8,768]{1,0:T(8,128)S(1)}) custom-call(s32[16]{0:T(128)S(1)} %pad_add_fusion.sc_ref.c_ref.b_ref, bf16[768,768]{1,0:T(8,128)(2,1)S(1)} %get-tuple-element.307.da_ref, f32[768,768]{1,0:T(8,128)S(1)} %get-tuple-element.308.dr_ref, ...), custom_call_target="tpu_custom_call" | custom-call | flops 5000000000 | bytes 1048576 | tf_op jit(solution)/shard_map/attention_backward/pallas_call | solution.py:546
  96.2 1.2 first_split.4
  97.4 1.1 collective-permute-start.6
  98.5 1.0 collective-permute-start.7
  99.5 13.2 %attention_backward.3 = (bf16[768,2304]{1,0:T(8,128)(2,1)S(1)}, f32[384,768]{1,0:T(8,128)}, bf16[256,768]{1,0:T(8,128)(2,1)}, f32[8,768]{1,0:T(8,128)S(1)}) custom-call(s32[16]{0:T(128)S(1)} %pad_add_fusion.sc_ref.c_ref.b_ref, bf16[768,768]{1,0:T(8,128)(2,1)S(1)} %get-tuple-element.307.da_ref, ...), custom_call_target="tpu_custom_call", output_to_operand_aliasing={{0}: (8, {}), {1}: (9, {})} | custom-call | flops 10000000000 | bytes 1048576 | tf_op jit(solution)/shard_map/attention_backward/pallas_call | solution.py:546
  114.8 1.1 collective-permute-start.9
  115.9 6.6 %qkvo_gradient.1 = (bf16[768,1536]{1,0:T(8,128)(2,1)}, bf16[768,1536]{1,0:T(8,128)(2,1)}) custom-call(s32[16]{0:T(128)S(1)} %pad_add_fusion.sc_ref.c_ref.b_ref, bf16[768,768]{1,0:T(8,128)(2,1)S(1)} %copy-done.11, bf16[768,2304]{1,0:T(8,128)(2,1)S(1)} %get-tuple-element.369.dq_ref, bf16[768,768]{1,0:T(8,128)(2,1)S(1)} %copy-done.12, ...), custom_call_target="tpu_custom_call" | custom-call | flops 5000000000 | bytes 1048576 | tf_op jit(solution)/shard_map/qkvo_gradient/pallas_call | solution.py:607
  122.5 1.7 join_split.3
  124.7 2.9 %all-to-all-start.1 = ((bf16[32,8,768]{2,1,0:T(8,128)(2,1)}), bf16[32,8,768]{2,1,0:T(8,128)(2,1)S(1)}, u32[]{:S(2)}, u32[]{:S(2)}) async-start(bf16[32,8,768]{2,1,0:T(8,128)(2,1)} %bitcast.9), calls=%async_computation.1 | async-start | bytes 786432 | tf_op jit(solution)/shard_map/all_to_all | solution.py:1144
  127.6 1.5 collective-permute-done.10
  129.1 4.5 %first_split.5 = (bf16[4,2,96,384]{3,2,1,0:T(8,128)(2,1)}, bf16[4,2,96,384]{3,2,1,0:T(8,128)(2,1)}, bf16[4,2,96,384]{3,2,1,0:T(8,128)(2,1)}, bf16[4,2,96,384]{3,2,1,0:T(8,128)(2,1)}) custom-call(s32[16]{0:T(128)S(1)} %pad_add_fusion.sc_ref.c_ref.b_ref, bf16[4,2,96,1536]{3,2,1,0:T(8,128)(2,1)S(1)} %bitcast.21, bf16[4,2,96,1536]{3,2,1,0:T(8,128)(2,1)} %bitcast.12.r_ref), custom_call_target="tpu_custom_call" | custom-call | flops 1000000000 | bytes 1048576 | tf_op jit(solution)/shard_map/first_split/pallas_call | solution.py:803
  134.5 1.1 collective-permute-start.14
  136.6 3.8 %all-to-all-done.1 = bf16[32,8,768]{2,1,0:T(8,128)(2,1)S(1)} async-done(((bf16[32,8,768]{2,1,0:T(8,128)(2,1)}), bf16[32,8,768]{2,1,0:T(8,128)(2,1)S(1)}, u32[]{:S(2)}, u32[]{:S(2)}) %all-to-all-start.1) | async-done | bytes 393248 | tf_op jit(solution)/shard_map/all_to_all | solution.py:1144
  140.4 3.2 %region_norm_backward.1 = (bf16[256,768]{1,0:T(8,128)(2,1)S(1)}, bf16[320,384]{1,0:T(8,128)(2,1)S(1)}, bf16[256,384]{1,0:T(8,128)(2,1)S(1)}, bf16[8,8,384]{2,1,0:T(8,128)(2,1)S(1)}, f32[4,256]{1,0:T(4,128)}) custom-call(s32[16]{0:T(128)S(1)} %pad_add_fusion.sc_ref.c_ref.b_ref, bf16[256,768]{1,0:T(8,128)(2,1)S(1)} %bitcast.25, s32[1,256]{1,0:T(1,128)} %t_ref.7, ...), custom_call_target="tpu_custom_call" | custom-call | flops 100000000 | bytes 1048576 | tf_op jit(solution)/shard_map/region_norm_backward/pallas_call | solution.py:673
  143.7 1.5 collective-permute-done.12.p_ref
  145.2 3.5 %visual_gradient.1 = (bf16[4,2,72,384]{3,2,1,0:T(8,128)(2,1)S(1)}, bf16[4,2,72,384]{3,2,1,0:T(8,128)(2,1)S(1)}, bf16[4,2,72,384]{3,2,1,0:T(8,128)(2,1)S(1)}, bf16[4,2,72,384]{3,2,1,0:T(8,128)(2,1)S(1)}) custom-call(s32[16]{0:T(128)S(1)} %pad_add_fusion.sc_ref.c_ref.b_ref, bf16[256,2048]{1,0:T(8,128)(2,1)} %f_ref.3, ...), custom_call_target="tpu_custom_call" | custom-call | flops 100000000 | bytes 1048576 | tf_op jit(solution)/shard_map/visual_gradient/pallas_call | solution.py:742
  149.6 1.3 collective-permute-start.17
  152.7 1.2 collective-permute-start.19
  154.6 1.3 collective-permute-start.20
  155.9 5.3 %feature_gradient.1 = f32[256,2048]{1,0:T(8,128)} custom-call(s32[16]{0:T(128)S(1)} %pad_add_fusion.sc_ref.c_ref.b_ref, bf16[256,768]{1,0:T(8,128)(2,1)S(1)} %get-tuple-element.425.d_ref, bf16[2048,768]{1,0:T(8,128)(2,1)} %w_ref.3), custom_call_target="tpu_custom_call" | custom-call | flops 10000000000 | bytes 1048576 | tf_op jit(solution)/shard_map/feature_gradient/pallas_call | solution.py:773
  163.5 1.4 collective-permute-start.21
  164.8 1.2 collective-permute-start.22
  166.0 3.0 %collective-permute-done.18.refs_1_ = bf16[4,96,384]{2,1,0:T(8,128)(2,1)S(1)} collective-permute-done((bf16[4,96,384]{2,1,0:T(8,128)(2,1)S(1)}, bf16[4,96,384]{2,1,0:T(8,128)(2,1)S(1)}, u32[]{:S(2)}, u32[]{:S(2)}) %collective-permute-start.18) | collective-permute-done | bytes 294944 | tf_op jit(solution)/shard_map/ppermute | solution.py:794
  170.5 2.3 %collective-permute-done.21.refs_1_ = bf16[4,72,384]{2,1,0:T(8,128)(2,1)S(1)} collective-permute-done((bf16[4,72,384]{2,1,0:T(8,128)(2,1)S(1)}, bf16[4,72,384]{2,1,0:T(8,128)(2,1)S(1)}, u32[]{:S(2)}, u32[]{:S(2)}) %collective-permute-start.21) | collective-permute-done | bytes 221216 | tf_op jit(solution)/shard_map/ppermute | solution.py:794
  174.2 1.6 collective-permute-start.26
  175.8 2.8 %collective-permute-done.23.r_ref = bf16[2,192,384]{2,1,0:T(8,128)(2,1)S(1)} collective-permute-done((bf16[2,192,384]{2,1,0:T(8,128)(2,1)S(1)}, bf16[2,192,384]{2,1,0:T(8,128)(2,1)S(1)}, u32[]{:S(2)}, u32[]{:S(2)}) %collective-permute-start.23) | collective-permute-done | bytes 294944 | tf_op jit(solution)/shard_map/ppermute | solution.py:794
  180.0 3.3 %collective-permute-done.24.r_ref = bf16[2,144,384]{2,1,0:T(8,128)(2,1)S(1)} collective-permute-done((bf16[2,144,384]{2,1,0:T(8,128)(2,1)S(1)}, bf16[2,144,384]{2,1,0:T(8,128)(2,1)S(1)}, u32[]{:S(2)}, u32[]{:S(2)}) %collective-permute-start.24) | collective-permute-done | bytes 221216 | tf_op jit(solution)/shard_map/ppermute | solution.py:794
  184.3 2.6 %collective-permute-done.29 = bf16[1,192,384]{2,1,0:T(8,128)(2,1)S(1)} collective-permute-done((bf16[1,192,384]{2,1,0:T(8,128)(2,1)S(1)}, bf16[1,192,384]{2,1,0:T(8,128)(2,1)S(1)}, u32[]{:S(2)}, u32[]{:S(2)}) %collective-permute-start.29) | collective-permute-done | bytes 147488 | tf_op jit(solution)/shard_map/ppermute | solution.py:794
  187.0 1.1 collective-permute-start.32
  188.1 2.4 %finish_ffn.1 = (f32[384,768]{1,0:T(8,128)}, f32[96,3072]{1,0:T(8,128)}) custom-call(s32[16]{0:T(128)S(1)} %pad_add_fusion.sc_ref.c_ref.b_ref, bf16[384,384]{1,0:T(8,128)(2,1)S(1)} %add_bitcast_fusion.p0, bf16[384,384]{1,0:T(8,128)(2,1)S(1)} %collective-permute-done.26.p1, bf16[384,384]{1,0:T(8,128)(2,1)S(1)} %collective-permute-done.27.p2, ...), custom_call_target="tpu_custom_call" | custom-call | flops 1000000000 | bytes 1048576 | tf_op jit(solution)/shard_map/finish_ffn/pallas_call | solution.py:803
  190.5 2.3 %collective-permute-done.25 = bf16[1,144,384]{2,1,0:T(8,128)(2,1)S(1)} collective-permute-done((bf16[1,144,384]{2,1,0:T(8,128)(2,1)S(1)}, bf16[1,144,384]{2,1,0:T(8,128)(2,1)S(1)}, u32[]{:S(2)}, u32[]{:S(2)}) %collective-permute-start.25) | collective-permute-done | bytes 110624 | tf_op jit(solution)/shard_map/ppermute | solution.py:794
  194.6 1.7 finish_wide.1
  196.3 2.4 %collective-permute-done.30.p1 = bf16[144,384]{1,0:T(8,128)(2,1)S(1)} collective-permute-done((bf16[144,384]{1,0:T(8,128)(2,1)S(1)}, bf16[144,384]{1,0:T(8,128)(2,1)S(1)}, u32[]{:S(2)}, u32[]{:S(2)}) %collective-permute-start.30) | collective-permute-done | bytes 110624 | tf_op jit(solution)/shard_map/ppermute | solution.py:794
  198.7 1.3 collective-permute-done.35.p3
  200.0 1.6 finish_visual.1
  (98 shorter events, 22.0 us)
Async XLA Ops:
  0.7 12.1 %copy-start.14 = (f32[1536]{0:T(1024)S(1)}, f32[1536]{0:T(1024)}, u32[]{:S(2)}) copy-start(f32[1536]{0:T(1024)} %param.40) | copy-start | bytes 18436
  0.7 12.2 %copy-start.15 = (s32[2]{0:T(128)S(1)}, s32[2]{0:T(128)}, u32[]{:S(2)}) copy-start(s32[2]{0:T(128)} %param.31) | copy-start | bytes 28
  0.7 12.2 %copy-start.16 = (s32[3]{0:T(128)S(1)}, s32[3]{0:T(128)}, u32[]{:S(2)}) copy-start(s32[3]{0:T(128)} %param.30) | copy-start | bytes 40
  0.7 12.2 %copy-start.17 = (s32[3]{0:T(128)S(1)}, s32[3]{0:T(128)}, u32[]{:S(2)}) copy-start(s32[3]{0:T(128)} %param.29) | copy-start | bytes 40
  5.5 20.5 %all-to-all-start = ((bf16[32,8,768]{2,1,0:T(8,128)(2,1)}), bf16[32,8,768]{2,1,0:T(8,128)(2,1)S(1)}, u32[]{:S(2)}, u32[]{:S(2)}) async-start(bf16[32,8,768]{2,1,0:T(8,128)(2,1)} %bitcast.1), calls=%async_computation | async-start | bytes 786432 | tf_op jit(solution)/shard_map/all_to_all | solution.py:1092
  26.7 36.3 %copy-start.3 = (f32[768]{0:T(1024)S(1)}, f32[768]{0:T(1024)}, u32[]{:S(2)}) copy-start(f32[768]{0:T(1024)} %ag_ref.5) | copy-start | bytes 9220
  62.9 4.8 %collective-permute-start = (bf16[8,2,2,96,384]{4,3,2,1,0:T(8,128)(2,1)}, bf16[8,2,2,96,384]{4,3,2,1,0:T(8,128)(2,1)S(1)}, u32[]{:S(2)}, u32[]{:S(2)}) collective-permute-start(bf16[8,2,2,96,384]{4,3,2,1,0:T(8,128)(2,1)} %bitcast.29), channel_id=1, source_target_pairs={{0,1},{1,0},{2,3},{3,2},{4,5},{5,4},{6,7},{7,6},{8,9},{9,8},{10,11... | collective-permute-start | bytes 7077896 | tf_op jit(solution)/shard_map/ppermute | solution.py:794
  68.9 15.4 %collective-permute-start.1 = (bf16[4,2,96,384]{3,2,1,0:T(8,128)(2,1)S(1)}, bf16[4,2,96,384]{3,2,1,0:T(8,128)(2,1)S(1)}, u32[]{:S(2)}, u32[]{:S(2)}) collective-permute-start(bf16[4,2,96,384]{3,2,1,0:T(8,128)(2,1)S(1)} %get-tuple-element.273), channel_id=1, source_target_pairs={{0,2},{1,3},{2,0},{3,1},{4,6},{5,7},{6,4},{7,5},{8,10},{9,11},{10,... | collective-permute-start | bytes 1769480 | tf_op jit(solution)/shard_map/ppermute | solution.py:794
  69.6 15.3 %collective-permute-start.2 = (bf16[4,2,96,384]{3,2,1,0:T(8,128)(2,1)S(1)}, bf16[4,2,96,384]{3,2,1,0:T(8,128)(2,1)S(1)}, u32[]{:S(2)}, u32[]{:S(2)}) collective-permute-start(bf16[4,2,96,384]{3,2,1,0:T(8,128)(2,1)S(1)} %get-tuple-element.275), channel_id=1, source_target_pairs={{0,4},{1,5},{2,6},{3,7},{4,0},{5,1},{6,2},{7,3},{8,12},{9,13},{10,... | collective-permute-start | bytes 1769480 | tf_op jit(solution)/shard_map/ppermute | solution.py:794
  78.2 9.9 %copy-start.5 = (bf16[768,768]{1,0:T(8,128)(2,1)S(1)}, bf16[768,768]{1,0:T(8,128)(2,1)}, u32[]{:S(2)}) copy-start(bf16[768,768]{1,0:T(8,128)(2,1)} %wo_ref.3) | copy-start | bytes 3538948
  78.2 9.9 %copy-start.9 = (bf16[768,2304]{1,0:T(8,128)(2,1)S(1)}, bf16[768,2304]{1,0:T(8,128)(2,1)}, u32[]{:S(2)}) copy-start(bf16[768,2304]{1,0:T(8,128)(2,1)} %get-tuple-element.310.qkv_ref) | copy-start | bytes 10616836
  85.8 10.4 %collective-permute-start.5 = (bf16[768,1536]{1,0:T(8,128)(2,1)S(1)}, bf16[768,1536]{1,0:T(8,128)(2,1)S(1)}, u32[]{:S(2)}, u32[]{:S(2)}) collective-permute-start(bf16[768,1536]{1,0:T(8,128)(2,1)S(1)} %get-tuple-element.304), channel_id=1, source_target_pairs={{0,1},{1,0},{2,3},{3,2},{4,5},{5,4},{6,7},{7,6},{8,9},{9,8},{10,11... | collective-permute-start | bytes 7077896 | tf_op jit(solution)/shard_map/ppermute | solution.py:794
  85.9 9.9 %collective-permute-start.3 = (bf16[4,96,384]{2,1,0:T(8,128)(2,1)S(1)}, bf16[4,96,384]{2,1,0:T(8,128)(2,1)S(1)}, u32[]{:S(2)}, u32[]{:S(2)}) collective-permute-start(bf16[4,96,384]{2,1,0:T(8,128)(2,1)S(1)} %get-tuple-element.300), channel_id=1, source_target_pairs={{0,4},{1,5},{2,6},{3,7},{4,0},{5,1},{6,2},{7,3},{8,12},{9,13},{10,... | collective-permute-start | bytes 884744 | tf_op jit(solution)/shard_map/ppermute | solution.py:794
  87.1 9.1 %collective-permute-start.4 = (bf16[4,96,384]{2,1,0:T(8,128)(2,1)S(1)}, bf16[4,96,384]{2,1,0:T(8,128)(2,1)S(1)}, u32[]{:S(2)}, u32[]{:S(2)}) collective-permute-start(bf16[4,96,384]{2,1,0:T(8,128)(2,1)S(1)} %get-tuple-element.302), channel_id=1, source_target_pairs={{0,2},{1,3},{2,0},{3,1},{4,6},{5,7},{6,4},{7,5},{8,10},{9,11},{10,... | collective-permute-start | bytes 884744 | tf_op jit(solution)/shard_map/ppermute | solution.py:794
  97.4 15.3 %collective-permute-start.6 = (bf16[4,2,96,384]{3,2,1,0:T(8,128)(2,1)S(1)}, bf16[4,2,96,384]{3,2,1,0:T(8,128)(2,1)S(1)}, u32[]{:S(2)}, u32[]{:S(2)}) collective-permute-start(bf16[4,2,96,384]{3,2,1,0:T(8,128)(2,1)S(1)} %get-tuple-element.336), channel_id=1, source_target_pairs={{0,2},{1,3},{2,0},{3,1},{4,6},{5,7},{6,4},{7,5},{8,10},{9,11},{10,... | collective-permute-start | bytes 1769480 | tf_op jit(solution)/shard_map/ppermute | solution.py:794
  98.5 14.4 %collective-permute-start.7 = (bf16[4,2,96,384]{3,2,1,0:T(8,128)(2,1)S(1)}, bf16[4,2,96,384]{3,2,1,0:T(8,128)(2,1)S(1)}, u32[]{:S(2)}, u32[]{:S(2)}) collective-permute-start(bf16[4,2,96,384]{3,2,1,0:T(8,128)(2,1)S(1)} %get-tuple-element.338), channel_id=1, source_target_pairs={{0,4},{1,5},{2,6},{3,7},{4,0},{5,1},{6,2},{7,3},{8,12},{9,13},{10,... | collective-permute-start | bytes 1769480 | tf_op jit(solution)/shard_map/ppermute | solution.py:794
  113.8 8.7 %collective-permute-start.8 = (bf16[4,96,384]{2,1,0:T(8,128)(2,1)S(1)}, bf16[4,96,384]{2,1,0:T(8,128)(2,1)S(1)}, u32[]{:S(2)}, u32[]{:S(2)}) collective-permute-start(bf16[4,96,384]{2,1,0:T(8,128)(2,1)S(1)} %get-tuple-element.359), channel_id=1, source_target_pairs={{0,4},{1,5},{2,6},{3,7},{4,0},{5,1},{6,2},{7,3},{8,12},{9,13},{10,... | collective-permute-start | bytes 884744 | tf_op jit(solution)/shard_map/ppermute | solution.py:794
  114.8 7.7 %collective-permute-start.9 = (bf16[4,96,384]{2,1,0:T(8,128)(2,1)S(1)}, bf16[4,96,384]{2,1,0:T(8,128)(2,1)S(1)}, u32[]{:S(2)}, u32[]{:S(2)}) collective-permute-start(bf16[4,96,384]{2,1,0:T(8,128)(2,1)S(1)} %get-tuple-element.361), channel_id=1, source_target_pairs={{0,2},{1,3},{2,0},{3,1},{4,6},{5,7},{6,4},{7,5},{8,10},{9,11},{10,... | collective-permute-start | bytes 884744 | tf_op jit(solution)/shard_map/ppermute | solution.py:794
  122.5 6.6 %copy-start = (bf16[768,1536]{1,0:T(8,128)(2,1)S(1)}, bf16[768,1536]{1,0:T(8,128)(2,1)}, u32[]{:S(2)}) copy-start(bf16[768,1536]{1,0:T(8,128)(2,1)} %get-tuple-element.390) | copy-start | bytes 7077892
  124.2 4.9 %collective-permute-start.10 = (bf16[768,1536]{1,0:T(8,128)(2,1)}, bf16[768,1536]{1,0:T(8,128)(2,1)}, u32[]{:S(2)}, u32[]{:S(2)}) collective-permute-start(bf16[768,1536]{1,0:T(8,128)(2,1)} %get-tuple-element.391), channel_id=1, source_target_pairs={{0,1},{1,0},{2,3},{3,2},{4,5},{5,4},{6,7},{7,6},{8,9},{9,8},{10,11... | collective-permute-start | bytes 7077896 | tf_op jit(solution)/shard_map/ppermute | solution.py:794
  124.2 19.4 %collective-permute-start.11 = (bf16[256,2048]{1,0:T(8,128)(2,1)}, bf16[256,2048]{1,0:T(8,128)(2,1)}, u32[]{:S(2)}, u32[]{:S(2)}) collective-permute-start(bf16[256,2048]{1,0:T(8,128)(2,1)} %f_ref.3), channel_id=1, source_target_pairs={{0,1},{1,0},{2,3},{3,2},{4,5},{5,4},{6,7},{7,6},{8,9},{9,8},{10,11... | collective-permute-start | bytes 3145736 | tf_op jit(solution)/shard_map/ppermute | solution.py:794
  124.7 15.7 %all-to-all-start.1 = ((bf16[32,8,768]{2,1,0:T(8,128)(2,1)}), bf16[32,8,768]{2,1,0:T(8,128)(2,1)S(1)}, u32[]{:S(2)}, u32[]{:S(2)}) async-start(bf16[32,8,768]{2,1,0:T(8,128)(2,1)} %bitcast.9), calls=%async_computation.1 | async-start | bytes 786432 | tf_op jit(solution)/shard_map/all_to_all | solution.py:1144
  133.6 17.3 %copy-start.6 = (bf16[4,2,96,384]{3,2,1,0:T(8,128)(2,1)S(1)}, bf16[4,2,96,384]{3,2,1,0:T(8,128)(2,1)}, u32[]{:S(2)}) copy-start(bf16[4,2,96,384]{3,2,1,0:T(8,128)(2,1)} %get-tuple-element.393.ak) | copy-start | bytes 1769476
  133.6 17.3 %copy-start.7 = (bf16[4,2,96,384]{3,2,1,0:T(8,128)(2,1)S(1)}, bf16[4,2,96,384]{3,2,1,0:T(8,128)(2,1)}, u32[]{:S(2)}) copy-start(bf16[4,2,96,384]{3,2,1,0:T(8,128)(2,1)} %get-tuple-element.395.bk) | copy-start | bytes 1769476
  133.6 17.3 %collective-permute-start.13 = (bf16[4,2,96,384]{3,2,1,0:T(8,128)(2,1)}, bf16[4,2,96,384]{3,2,1,0:T(8,128)(2,1)S(1)}, u32[]{:S(2)}, u32[]{:S(2)}) collective-permute-start(bf16[4,2,96,384]{3,2,1,0:T(8,128)(2,1)} %get-tuple-element.392), channel_id=1, source_target_pairs={{0,2},{1,3},{2,0},{3,1},{4,6},{5,7},{6,4},{7,5},{8,10},{9,11},{10,... | collective-permute-start | bytes 1769480 | tf_op jit(solution)/shard_map/ppermute | solution.py:794
  134.5 16.3 %collective-permute-start.14 = (bf16[4,2,96,384]{3,2,1,0:T(8,128)(2,1)}, bf16[4,2,96,384]{3,2,1,0:T(8,128)(2,1)S(1)}, u32[]{:S(2)}, u32[]{:S(2)}) collective-permute-start(bf16[4,2,96,384]{3,2,1,0:T(8,128)(2,1)} %get-tuple-element.394), channel_id=1, source_target_pairs={{0,4},{1,5},{2,6},{3,7},{4,0},{5,1},{6,2},{7,3},{8,12},{9,13},{10,... | collective-permute-start | bytes 1769480 | tf_op jit(solution)/shard_map/ppermute | solution.py:794
  135.6 18.3 %collective-permute-start.15 = (bf16[2,384,384]{2,1,0:T(8,128)(2,1)}, bf16[2,384,384]{2,1,0:T(8,128)(2,1)S(1)}, u32[]{:S(2)}, u32[]{:S(2)}) collective-permute-start(bf16[2,384,384]{2,1,0:T(8,128)(2,1)} %get-tuple-element.421), channel_id=1, source_target_pairs={{0,8},{1,9},{2,10},{3,11},{4,12},{5,13},{6,14},{7,15},{8,0},{9,1},... | collective-permute-start | bytes 1769480 | tf_op jit(solution)/shard_map/ppermute | solution.py:794
  143.6 1.5 collective-permute-start.12
  148.7 13.1 %collective-permute-start.16 = (bf16[4,2,72,384]{3,2,1,0:T(8,128)(2,1)S(1)}, bf16[4,2,72,384]{3,2,1,0:T(8,128)(2,1)S(1)}, u32[]{:S(2)}, u32[]{:S(2)}) collective-permute-start(bf16[4,2,72,384]{3,2,1,0:T(8,128)(2,1)S(1)} %get-tuple-element.409), channel_id=1, source_target_pairs={{0,2},{1,3},{2,0},{3,1},{4,6},{5,7},{6,4},{7,5},{8,10},{9,11},{10,... | collective-permute-start | bytes 1327112 | tf_op jit(solution)/shard_map/ppermute | solution.py:794
  149.6 13.0 %collective-permute-start.17 = (bf16[4,2,72,384]{3,2,1,0:T(8,128)(2,1)S(1)}, bf16[4,2,72,384]{3,2,1,0:T(8,128)(2,1)S(1)}, u32[]{:S(2)}, u32[]{:S(2)}) collective-permute-start(bf16[4,2,72,384]{3,2,1,0:T(8,128)(2,1)S(1)} %get-tuple-element.411), channel_id=1, source_target_pairs={{0,4},{1,5},{2,6},{3,7},{4,0},{5,1},{6,2},{7,3},{8,12},{9,13},{10,... | collective-permute-start | bytes 1327112 | tf_op jit(solution)/shard_map/ppermute | solution.py:794
  151.8 17.1 %collective-permute-start.18 = (bf16[4,96,384]{2,1,0:T(8,128)(2,1)S(1)}, bf16[4,96,384]{2,1,0:T(8,128)(2,1)S(1)}, u32[]{:S(2)}, u32[]{:S(2)}) collective-permute-start(bf16[4,96,384]{2,1,0:T(8,128)(2,1)S(1)} %get-tuple-element.414), channel_id=1, source_target_pairs={{0,4},{1,5},{2,6},{3,7},{4,0},{5,1},{6,2},{7,3},{8,12},{9,13},{10,... | collective-permute-start | bytes 884744 | tf_op jit(solution)/shard_map/ppermute | solution.py:794
  152.7 16.3 %collective-permute-start.19 = (bf16[4,96,384]{2,1,0:T(8,128)(2,1)S(1)}, bf16[4,96,384]{2,1,0:T(8,128)(2,1)S(1)}, u32[]{:S(2)}, u32[]{:S(2)}) collective-permute-start(bf16[4,96,384]{2,1,0:T(8,128)(2,1)S(1)} %get-tuple-element.416), channel_id=1, source_target_pairs={{0,2},{1,3},{2,0},{3,1},{4,6},{5,7},{6,4},{7,5},{8,10},{9,11},{10,... | collective-permute-start | bytes 884744 | tf_op jit(solution)/shard_map/ppermute | solution.py:794
  154.6 15.9 %collective-permute-start.20 = (bf16[1,384,384]{2,1,0:T(8,128)(2,1)S(1)}, bf16[1,384,384]{2,1,0:T(8,128)(2,1)S(1)}, u32[]{:S(2)}, u32[]{:S(2)}) collective-permute-start(bf16[1,384,384]{2,1,0:T(8,128)(2,1)S(1)} %get-tuple-element.422), channel_id=1, source_target_pairs={{0,16},{1,17},{2,18},{3,19},{4,20},{5,21},{6,22},{7,23},{8,24},{9,... | collective-permute-start | bytes 884744 | tf_op jit(solution)/shard_map/ppermute | solution.py:794
  163.5 9.3 %collective-permute-start.21 = (bf16[4,72,384]{2,1,0:T(8,128)(2,1)S(1)}, bf16[4,72,384]{2,1,0:T(8,128)(2,1)S(1)}, u32[]{:S(2)}, u32[]{:S(2)}) collective-permute-start(bf16[4,72,384]{2,1,0:T(8,128)(2,1)S(1)} %get-tuple-element.428), channel_id=1, source_target_pairs={{0,4},{1,5},{2,6},{3,7},{4,0},{5,1},{6,2},{7,3},{8,12},{9,13},{10,... | collective-permute-start | bytes 663560 | tf_op jit(solution)/shard_map/ppermute | solution.py:794
  164.8 8.0 %collective-permute-start.22 = (bf16[4,72,384]{2,1,0:T(8,128)(2,1)S(1)}, bf16[4,72,384]{2,1,0:T(8,128)(2,1)S(1)}, u32[]{:S(2)}, u32[]{:S(2)}) collective-permute-start(bf16[4,72,384]{2,1,0:T(8,128)(2,1)S(1)} %get-tuple-element.430), channel_id=1, source_target_pairs={{0,2},{1,3},{2,0},{3,1},{4,6},{5,7},{6,4},{7,5},{8,10},{9,11},{10,... | collective-permute-start | bytes 663560 | tf_op jit(solution)/shard_map/ppermute | solution.py:794
  169.7 8.9 %collective-permute-start.23 = (bf16[2,192,384]{2,1,0:T(8,128)(2,1)S(1)}, bf16[2,192,384]{2,1,0:T(8,128)(2,1)S(1)}, u32[]{:S(2)}, u32[]{:S(2)}) collective-permute-start(bf16[2,192,384]{2,1,0:T(8,128)(2,1)S(1)} %get-tuple-element.433), channel_id=1, source_target_pairs={{0,8},{1,9},{2,10},{3,11},{4,12},{5,13},{6,14},{7,15},{8,0},{9,1},... | collective-permute-start | bytes 884744 | tf_op jit(solution)/shard_map/ppermute | solution.py:794
  173.5 9.7 %collective-permute-start.24 = (bf16[2,144,384]{2,1,0:T(8,128)(2,1)S(1)}, bf16[2,144,384]{2,1,0:T(8,128)(2,1)S(1)}, u32[]{:S(2)}, u32[]{:S(2)}) collective-permute-start(bf16[2,144,384]{2,1,0:T(8,128)(2,1)S(1)} %get-tuple-element.437), channel_id=1, source_target_pairs={{0,8},{1,9},{2,10},{3,11},{4,12},{5,13},{6,14},{7,15},{8,0},{9,1},... | collective-permute-start | bytes 663560 | tf_op jit(solution)/shard_map/ppermute | solution.py:794
  174.2 9.7 %collective-permute-start.26 = (bf16[384,384]{1,0:T(8,128)(2,1)S(1)}, bf16[384,384]{1,0:T(8,128)(2,1)S(1)}, u32[]{:S(2)}, u32[]{:S(2)}) collective-permute-start(bf16[384,384]{1,0:T(8,128)(2,1)S(1)} %add_bitcast_fusion.p0), channel_id=1, source_target_pairs={{0,2},{1,3},{2,0},{3,1},{4,6},{5,7},{6,4},{7,5},{8,10},{9,11},{10,... | collective-permute-start | bytes 884744 | tf_op jit(solution)/shard_map/ppermute | solution.py:794
  175.8 12.3 %collective-permute-start.27 = (bf16[384,384]{1,0:T(8,128)(2,1)S(1)}, bf16[384,384]{1,0:T(8,128)(2,1)S(1)}, u32[]{:S(2)}, u32[]{:S(2)}) collective-permute-start(bf16[384,384]{1,0:T(8,128)(2,1)S(1)} %add_bitcast_fusion.p0), channel_id=1, source_target_pairs={{0,1},{1,0},{2,3},{3,2},{4,5},{5,4},{6,7},{7,6},{8,9},{9,8},{10,11... | collective-permute-start | bytes 884744 | tf_op jit(solution)/shard_map/ppermute | solution.py:794
  179.2 7.7 %collective-permute-start.29 = (bf16[1,192,384]{2,1,0:T(8,128)(2,1)S(1)}, bf16[1,192,384]{2,1,0:T(8,128)(2,1)S(1)}, u32[]{:S(2)}, u32[]{:S(2)}) collective-permute-start(bf16[1,192,384]{2,1,0:T(8,128)(2,1)S(1)} %get-tuple-element.440), channel_id=1, source_target_pairs={{0,16},{1,17},{2,18},{3,19},{4,20},{5,21},{6,22},{7,23},{8,24},{9,... | collective-permute-start | bytes 442376 | tf_op jit(solution)/shard_map/ppermute | solution.py:794
  183.9 4.2 %collective-permute-start.28 = (bf16[384,384]{1,0:T(8,128)(2,1)S(1)}, bf16[384,384]{1,0:T(8,128)(2,1)S(1)}, u32[]{:S(2)}, u32[]{:S(2)}) collective-permute-start(bf16[384,384]{1,0:T(8,128)(2,1)S(1)} %collective-permute-done.26.p1), channel_id=1, source_target_pairs={{0,1},{1,0},{2,3},{3,2},{4,5},{5,4},{6,7},{7,6},{8,9},{9,8},{10,11... | collective-permute-start | bytes 884744 | tf_op jit(solution)/shard_map/ppermute | solution.py:794
  184.0 8.7 %collective-permute-start.25 = (bf16[1,144,384]{2,1,0:T(8,128)(2,1)S(1)}, bf16[1,144,384]{2,1,0:T(8,128)(2,1)S(1)}, u32[]{:S(2)}, u32[]{:S(2)}) collective-permute-start(bf16[1,144,384]{2,1,0:T(8,128)(2,1)S(1)} %get-tuple-element.443), channel_id=1, source_target_pairs={{0,16},{1,17},{2,18},{3,19},{4,20},{5,21},{6,22},{7,23},{8,24},{9,... | collective-permute-start | bytes 331784 | tf_op jit(solution)/shard_map/ppermute | solution.py:794
  186.9 7.6 %collective-permute-start.33 = (bf16[192,384]{1,0:T(8,128)(2,1)S(1)}, bf16[192,384]{1,0:T(8,128)(2,1)S(1)}, u32[]{:S(2)}, u32[]{:S(2)}) collective-permute-start(bf16[192,384]{1,0:T(8,128)(2,1)S(1)} %add_bitcast_fusion.1.p0), channel_id=1, source_target_pairs={{0,1},{1,0},{2,3},{3,2},{4,5},{5,4},{6,7},{7,6},{8,9},{9,8},{10,11... | collective-permute-start | bytes 442376 | tf_op jit(solution)/shard_map/ppermute | solution.py:794
  187.0 6.3 %collective-permute-start.32 = (bf16[192,384]{1,0:T(8,128)(2,1)S(1)}, bf16[192,384]{1,0:T(8,128)(2,1)S(1)}, u32[]{:S(2)}, u32[]{:S(2)}) collective-permute-start(bf16[192,384]{1,0:T(8,128)(2,1)S(1)} %add_bitcast_fusion.1.p0), channel_id=1, source_target_pairs={{0,2},{1,3},{2,0},{3,1},{4,6},{5,7},{6,4},{7,5},{8,10},{9,11},{10,... | collective-permute-start | bytes 442376 | tf_op jit(solution)/shard_map/ppermute | solution.py:794
  193.2 1.4 collective-permute-start.34
  193.2 5.5 %collective-permute-start.30 = (bf16[144,384]{1,0:T(8,128)(2,1)S(1)}, bf16[144,384]{1,0:T(8,128)(2,1)S(1)}, u32[]{:S(2)}, u32[]{:S(2)}) collective-permute-start(bf16[144,384]{1,0:T(8,128)(2,1)S(1)} %add_bitcast_fusion.2.p0), channel_id=1, source_target_pairs={{0,2},{1,3},{2,0},{3,1},{4,6},{5,7},{6,4},{7,5},{8,10},{9,11},{10,... | collective-permute-start | bytes 331784 | tf_op jit(solution)/shard_map/ppermute | solution.py:794
  194.3 4.4 %collective-permute-start.31 = (bf16[144,384]{1,0:T(8,128)(2,1)S(1)}, bf16[144,384]{1,0:T(8,128)(2,1)S(1)}, u32[]{:S(2)}, u32[]{:S(2)}) collective-permute-start(bf16[144,384]{1,0:T(8,128)(2,1)S(1)} %add_bitcast_fusion.2.p0), channel_id=1, source_target_pairs={{0,1},{1,0},{2,3},{3,2},{4,5},{5,4},{6,7},{7,6},{8,9},{9,8},{10,11... | collective-permute-start | bytes 331784 | tf_op jit(solution)/shard_map/ppermute | solution.py:794
  198.7 1.3 collective-permute-start.35
  (8 other events, 32.7 us)
